TPU v7x, 256 devices: a whole 4x4x8 slice. The times are simulated.
256 devices in a mesh: req: 8 (over z), row: 8 (over y, core), col: 4 (over x).
Axes of the slice: x: 4, y: 4, z: 8, core: 2. Of those that a mesh axis runs over, the one named last changes fastest.
Arguments:
- tokens: bfloat16 [16384, 2, 1792], P(('req', 'row'), None, 'col'), may hold values from -6 to 6
- w_query: bfloat16 [1792, 256], P('col', 'row'), may hold values from -0.125 to 0.125
- w_key: bfloat16 [1792, 256], P('col', 'row'), may hold values from -0.125 to 0.125
- w_value: bfloat16 [16, 200704], P('row', 'col'), may hold values from -0.125 to 0.125
- w_out: bfloat16 [1792, 1792], P('row', 'col'), may hold values from -0.125 to 0.125
- cached_state: bfloat16 [32, 273, 57344], P(('req', 'col'), None, 'row'), may hold values from -24 to 24
- cached_norm: bfloat16 [1024, 273, 16], P(('req', 'col'), None, 'row'), as said below
- slot_prompt: int32 [1024], P(('req', 'col')), may hold values from 0 to 1023, as said below
- prompt_of: int32 [16384], P(('req', 'col')), may hold values from 0 to 1023, as said below
- tail_keys: bfloat16 [16384, 2048], P(('req', 'col'), 'row'), may hold values from -6 to 6
- tail_values: bfloat16 [16384, 14336], P(('req', 'col'), 'row'), may hold values from -6 to 6
- tail_length: int32 [16384], P(('req', 'col')), may hold values from 0 to 8, as said below
Outputs:
- layer_out: bfloat16 [16384, 2, 1792], P(('req', 'row'), None, 'col')
Inputs may be any that keep to these rules, and one draw needn't show every extreme that they name: `slot_prompt`: each prompt sits in exactly one slot. The h-th block of 32 slots (holder h) keeps exactly 16 of its own prompts h * 32 to (h + 1) * 32 - 1; its other slots hold prompts of other holders, at most 1 of any one holder. The bound 1 is reached: some holder keeps 1 of one other holder's prompts. `prompt_of`: the h-th aligned block of 512 continuations holds exactly 16 continuations of each prompt h * 32 to (h + 1) * 32 - 1. `tail_length`: each aligned block of 512 continuations holds at least one continuation with a tail of 8 tokens. `cached_norm`: each prompt's column for a head is a sum of phi of some key vectors with positive weights.
All inputs are finite; a program needn't handle non-finite values.
Results may differ from a plain program's by a relative error of at most 0.019.
Values may be sent and summed in bfloat16 or wider, within the bound.
No kernel may reach another device: no remote copies, remote signals or barrier semaphores. Data moves between devices by JAX's collectives and lax.ppermute only.
A program may use at most 128 MiB of HBM per device.

v0:
```python
import functools

import jax
import jax.numpy as jnp
from jax import lax
from jax.experimental import pallas as pl
from jax.experimental.pallas import tpu as pltpu
from jax.sharding import Mesh, PartitionSpec as P

BF = jnp.bfloat16
F32 = jnp.float32
VMEM_LIMIT = 48 * 1024 * 1024
VM = pl.BlockSpec(memory_space=pltpu.VMEM)
SM = pl.BlockSpec(memory_space=pltpu.SMEM)


def dot(a, b):
    return jnp.dot(a, b, preferred_element_type=F32)


def iota(shape, dim):
    return lax.broadcasted_iota(jnp.int32, shape, dim)


def onehot(cond):
    return jnp.where(cond, 1.0, 0.0).astype(BF)


def split(x):
    high = x.astype(BF)
    return high, (x - high.astype(F32)).astype(BF)


def call(kernel, out_shapes, n_smem, n_vmem, **kw):
    return pl.pallas_call(
        kernel,
        out_shape=out_shapes,
        in_specs=[SM] * n_smem + [VM] * n_vmem,
        out_specs=jax.tree.map(lambda _: VM, out_shapes),
        compiler_params=pltpu.CompilerParams(vmem_limit_bytes=VMEM_LIMIT),
        **kw,
    )


def project_kernel(pos_ref, t0, t1, t2, t3, w_ref, out_ref):
    w = w_ref[...]
    for shift, block in enumerate((t0, t1, t2, t3)):
        slot = lax.rem(pos_ref[0] + 4 - shift, 4)
        out_ref[slot] = dot(block[...], w).astype(BF)


def sum_kernel(pos_ref, p_ref, own_ref, oth_ref):
    core = pos_ref[1]

    def total(lo, hi):
        acc = p_ref[0, :, lo:hi].astype(F32)
        for i in range(1, 4):
            acc = acc + p_ref[i, :, lo:hi].astype(F32)
        return acc.astype(BF)

    first, second, keys = total(0, 256), total(256, 512), total(512, 640)
    own_ref[:, 0:256] = jnp.where(core == 0, first, second)
    oth_ref[:, 0:256] = jnp.where(core == 0, second, first)
    own_ref[:, 256:384] = keys
    oth_ref[:, 256:384] = keys


def group_kernel(pos_ref, g_ref, s_ref, own_ref, rec_ref, place_ref, send_ref, keep_ref, grouped):
    core = pos_ref[1]
    me = pos_ref[2]
    rows, cols = iota((256, 128), 0), iota((256, 128), 1)
    acc = None
    for e, ref in enumerate((own_ref, rec_ref)):
        half = core if e == 0 else 1 - core
        queries = None
        for t in range(2):
            pick = onehot((rows >= 224) & (cols == rows - 224 + 32 * t))
            part = dot(ref[t * 256 : (t + 1) * 256, 0:256], pick)
            queries = part if queries is None else queries + part
        hot = onehot(iota((512, 256), 0) == place_ref[half])
        part = dot(hot, queries.astype(BF))
        acc = part if acc is None else acc + part
    grouped[...] = acc.astype(BF)
    send_ref[...] = jnp.zeros_like(send_ref)
    keep_ref[...] = jnp.zeros_like(keep_ref)
    for p in range(32):
        holder, slot = g_ref[p], s_ref[p]

        @pl.when(holder != me)
        def _():
            send_ref[holder] = grouped[p * 16 : (p + 1) * 16, :]

        @pl.when(holder == me)
        def _():
            keep_ref[slot] = grouped[p * 16 : (p + 1) * 16, :]


def slot_kernel(pos_ref, owner_ref, rec_ref, keep_ref, state_ref, send_ref, own_ref, buf):
    me = pos_ref[2]
    step = pl.program_id(0)

    @pl.when(step == 0)
    def _():
        send_ref[...] = jnp.zeros_like(send_ref)
        own_ref[...] = jnp.zeros_like(own_ref)

    for i in range(8):
        slot = step * 8 + i
        owner = owner_ref[slot]

        @pl.when(owner != me)
        def _():
            buf[i * 16 : (i + 1) * 16, :] = rec_ref[owner]

        @pl.when(owner == me)
        def _():
            buf[i * 16 : (i + 1) * 16, :] = keep_ref[slot]

    q = buf[...]
    row, f = iota((128, 384), 0), iota((128, 384), 1)
    lane = iota((1, 384), 1)
    square, line = lane >= 17, (lane >= 1) & (lane < 17)
    unit_a = jnp.where(lane == 0, 1.0, 0.0)
    unit_b = jnp.where(lane < 17, 1.0, 0.0)
    scale = jnp.where(square, 0.5**0.5 / 4.0, jnp.where(line, 0.5, 1.0))
    scale = jnp.where(lane < 273, scale, 0.0)
    a_at = jnp.where(f >= 17, lax.shift_right_logical(f - 17, 4), f - 1)
    b_at = (f - 17) & 15
    live_a = (f >= 1) & (f < 273)
    live_b = (f >= 17) & (f < 273)
    high, low = [], []
    for t in range(2):
        for h in range(2):
            base = t * 32 + h * 16
            left = dot(q, onehot(live_a & (row == a_at + base))) + unit_a
            right = dot(q, onehot(live_b & (row == b_at + base))) + unit_b
            one, two = split(left * right * scale)
            high.append(one)
            low.append(two)
    out_lane = iota((16, 256), 1)
    first_head = (out_lane < 112) | (out_lane == 224) | (out_lane == 226)
    for i in range(8):
        phi = jnp.concatenate([x[i * 16 : (i + 1) * 16, 0:273] for x in high + low], axis=0)
        both = dot(phi, state_ref[i])
        terms = both[0:64] + both[64:128]
        results = []
        for t in range(2):
            r = jnp.where(first_head, terms[t * 32 : t * 32 + 16], terms[t * 32 + 16 : t * 32 + 32])
            rough = r.astype(BF).astype(F32)
            results.append(jnp.where(out_lane >= 226, r - rough, r).astype(BF))
        slot = step * 8 + i
        owner = owner_ref[slot]

        @pl.when(owner != me)
        def _():
            send_ref[owner, :, 0:256] = results[0]
            send_ref[owner, :, 256:512] = results[1]

        @pl.when(owner == me)
        def _():
            own_ref[slot, :, 0:256] = results[0]
            own_ref[slot, :, 256:512] = results[1]


def kappa(s):
    return 1.0 + s + 0.5 * s * s


def tail_kernel(pos_ref, own_ref, rec_ref, tk_ref, tv_ref, len_ref, num_ref, den_ref):
    core = pos_ref[1]
    r, c = iota((256, 256), 0), iota((256, 256), 1)
    expand_q = onehot((r >= 224) & (r - 224 == lax.shift_right_logical(c, 7) * 16 + (c & 15)))
    r, c = iota((256, 128), 0), iota((256, 128), 1)
    sum_a = onehot(lax.shift_right_logical(r, 4) == c)
    pick_q = onehot((r >= 224) & (r - 224 == c))
    r, c = iota((128, 128), 0), iota((128, 128), 1)
    pick_k = onehot((c < 32) & (r == c + 32 * core))
    sum_new = onehot((r < 32) & (lax.shift_right_logical(r, 4) == c))
    r, c = iota((128, 1792), 0), iota((128, 1792), 1)
    expand_w = onehot((r < 16) & (c >= r * 112) & (c < (r + 1) * 112))
    r, c = iota((1792, 256), 0), iota((1792, 256), 1)
    sum_v = onehot(
        functools.reduce(
            jnp.logical_or,
            [(r - c == 112 * (7 * (k // 8) + k % 8)) & (c >= 112 * (k // 8)) & (c < 112 * (k // 8 + 1)) for k in range(16)],
        )
    )
    r, c = iota((128, 256), 0), iota((128, 256), 1)
    spread = onehot((r < 16) & (c < 224) & ((c >= 112) == (r >= 8)))
    spread_new = onehot((r < 2) & (c < 224) & ((c >= 112) == (r >= 1)))
    head_lane = iota((256, 128), 1)
    for e, ref in enumerate((own_ref, rec_ref)):
        half = core if e == 0 else 1 - core
        at = pl.multiple_of(half * 256, 256)
        keys = tk_ref[pl.ds(at, 256), :].astype(F32)
        live = (head_lane & 7) < len_ref[pl.ds(at, 256), :]
        live = live & (head_lane < 16)
        values = tv_ref[pl.ds(at, 256), :]
        new_keys = [dot(ref[t * 256 : (t + 1) * 256, 256:384], pick_k) for t in range(2)]
        for t in range(2):
            vq = ref[t * 256 : (t + 1) * 256, 0:256]
            one, two = split(dot(vq, expand_q) * keys)
            weight = kappa((dot(one, sum_a) + dot(two, sum_a)) * 0.25)
            weight = jnp.where(live, weight, 0.0)
            one, two = split(weight)
            den = dot(one, spread) + dot(two, spread)
            terms = dot(one, expand_w).astype(BF) * values
            num = dot(terms, sum_v)
            query = dot(vq, pick_q)
            for i in range(t + 1):
                one, two = split(query * new_keys[i])
                weight = kappa((dot(one, sum_new) + dot(two, sum_new)) * 0.25)
                one, two = split(weight)
                high = dot(one, spread_new)
                den = den + high + dot(two, spread_new)
                num = num + high * ref[i * 256 : (i + 1) * 256, 0:256].astype(F32)
            num_ref[e, t * 256 : (t + 1) * 256, :] = num
            den_ref[e, t * 256 : (t + 1) * 256, :] = den


def combine_kernel(pos_ref, g_ref, s_ref, num_ref, den_ref, rec_ref, own_ref, place_ref, same_ref, other_ref, buf):
    core = pos_ref[1]
    me = pos_ref[2]
    for p in range(32):
        holder, slot = g_ref[p], s_ref[p]

        @pl.when(holder != me)
        def _():
            buf[p * 16 : (p + 1) * 16, :] = rec_ref[holder]

        @pl.when(holder == me)
        def _():
            buf[p * 16 : (p + 1) * 16, :] = own_ref[slot]

    r, c = iota((256, 256), 0), iota((256, 256), 1)
    spread = onehot((c < 224) & (((c < 112) & ((r == 224) | (r == 226))) | ((c >= 112) & ((r == 225) | (r == 227)))))
    lane = iota((256, 256), 1)
    for e, out_ref in enumerate((same_ref, other_ref)):
        half = core if e == 0 else 1 - core
        at = pl.multiple_of(half * 256, 256)
        hot = onehot(iota((256, 512), 1) == place_ref[pl.ds(at, 256), :])
        prompt = dot(hot, buf[...])
        for t in range(2):
            part = prompt[:, t * 256 : (t + 1) * 256]
            den = den_ref[e, t * 256 : (t + 1) * 256, :] + dot(part.astype(BF), spread)
            num = num_ref[e, t * 256 : (t + 1) * 256, :] + part
            out = jnp.where(lane < 224, num / jnp.where(lane < 224, den, 1.0), 0.0)
            out_ref[t * 256 : (t + 1) * 256, :] = out.astype(BF)


def out_kernel(pos_ref, *refs):
    chunks, w_ref, tok_ref, out_ref = refs[:8], refs[8], refs[9], refs[10]
    core, col = pos_ref[1], pos_ref[3]
    acc = tok_ref[...].astype(F32)
    for s in range(4):
        for d in range(2):
            j = lax.rem(col + 4 - s, 4)
            k = core if d == 0 else 1 - core
            acc = acc + dot(chunks[s * 2 + d][:, 0:224], w_ref[j * 2 + k])
    out_ref[...] = acc.astype(BF)


def body(tokens, w_query, w_key, w_value, w_out, cached_state, cached_norm, slot_prompt, prompt_of, tail_keys, tail_values, tail_length):
    y, core, col = lax.axis_index("y"), lax.axis_index("core"), lax.axis_index("col")
    me = lax.axis_index(("req", "col"))
    pos = jnp.stack([y, core, me, col]).astype(jnp.int32)
    tok = jnp.transpose(tokens, (1, 0, 2)).reshape(512, 448)
    blocks = [tok] + [lax.ppermute(tok, "y", [(i, (i + s) % 4) for i in range(4)]) for s in range(1, 4)]
    value_w = jnp.moveaxis(w_value.reshape(2, 448, 112), 0, 1).reshape(448, 224)
    mine = jnp.concatenate([value_w, w_query, w_key], axis=1)
    theirs = lax.ppermute(mine, "core", [(0, 1), (1, 0)])
    w0, w1 = jnp.where(core == 0, mine, theirs), jnp.where(core == 0, theirs, mine)
    weights = jnp.concatenate(
        [w0[:, :256], w1[:, :256], w0[:, 256:], w1[:, 256:], jnp.zeros((448, 64), BF)], axis=1
    )
    w_all = lax.all_gather(w_out, ("y", "core"), axis=0, tiled=False)
    owner = slot_prompt // 32
    slots = jnp.arange(32, dtype=jnp.int32)
    away = owner != me
    code = jnp.max(
        jnp.where((owner[None, :] == slots[:, None]) & away[None, :], (slots * 32 + slot_prompt % 32 + 1)[None, :], 0), axis=1
    )
    told = lax.all_to_all(code[:, None], ("req", "col"), split_axis=0, concat_axis=0, tiled=True)[:, 0]
    here = (slot_prompt[None, :] == (me * 32 + slots)[:, None])
    there = (told[None, :] > 0) & ((told[None, :] - 1) % 32 == slots[:, None])
    at_slot = jnp.max(jnp.where(here, slots[None, :], 0), axis=1)
    at_holder = jnp.where(jnp.any(here, axis=1), me, jnp.max(jnp.where(there, slots[None, :], 0), axis=1)).astype(jnp.int32)
    index = jnp.arange(512)
    rank = jnp.sum(((prompt_of[None, :] == prompt_of[:, None]) & (index[None, :] < index[:, None])).astype(jnp.int32), axis=1)
    place = (prompt_of - me * 32) * 16 + rank
    norms = jnp.concatenate([cached_norm, cached_norm, jnp.zeros((32, 273, 28), BF)], axis=2)
    states = jnp.transpose(cached_state[0].reshape(273, 224, 32), (2, 0, 1))
    states = jnp.concatenate([states, norms], axis=2)

    partial = call(project_kernel, jax.ShapeDtypeStruct((4, 512, 640), BF), 1, 5)(pos, *blocks, weights)
    partial = lax.all_to_all(partial, "col", split_axis=0, concat_axis=0, tiled=True)
    shape = jax.ShapeDtypeStruct((512, 384), BF)
    own, oth = call(sum_kernel, (shape, shape), 1, 1)(pos, partial)
    rec = lax.ppermute(oth, "core", [(0, 1), (1, 0)])

    shape = jax.ShapeDtypeStruct((32, 16, 128), BF)
    q_send, q_keep = call(group_kernel, (shape, shape), 3, 3, scratch_shapes=[pltpu.VMEM((512, 128), BF)])(
        pos, at_holder, at_slot, own, rec, place.reshape(2, 1, 256)
    )
    q_rec = lax.all_to_all(q_send, ("req", "col"), split_axis=0, concat_axis=0, tiled=True)
    shape = jax.ShapeDtypeStruct((2, 512, 256), F32)
    num, den = call(tail_kernel, (shape, shape), 1, 5)(pos, own, rec, tail_keys, tail_values, tail_length[:, None])
    shape = jax.ShapeDtypeStruct((32, 16, 512), BF)
    whole = pl.BlockSpec((32, 16, 128), lambda i: (0, 0, 0))
    whole_out = pl.BlockSpec((32, 16, 512), lambda i: (0, 0, 0))
    r_send, r_keep = pl.pallas_call(
        slot_kernel,
        grid=(4,),
        out_shape=(shape, shape),
        in_specs=[SM, SM, whole, whole, pl.BlockSpec((8, 273, 256), lambda i: (i, 0, 0))],
        out_specs=(whole_out, whole_out),
        scratch_shapes=[pltpu.VMEM((128, 128), BF)],
        compiler_params=pltpu.CompilerParams(vmem_limit_bytes=VMEM_LIMIT),
    )(pos, owner, q_rec, q_keep, states)
    r_rec = lax.all_to_all(r_send, ("req", "col"), split_axis=0, concat_axis=0, tiled=True)
    shape = jax.ShapeDtypeStruct((512, 256), BF)
    same, other = call(combine_kernel, (shape, shape), 3, 5, scratch_shapes=[pltpu.VMEM((512, 512), BF)])(
        pos, at_holder, at_slot, num, den, r_rec, r_keep, place[:, None]
    )

    def at(y, core, col):
        return (y * 2 + core) * 4 + col

    chunks = []
    for s in range(4):
        for d, part in ((0, same), (1, other)):
            perm = [
                (at(j, k, b), at(b, k ^ d, (j + s) % 4)) for b in range(4) for j in range(4) for k in range(2)
            ]
            chunks.append(lax.ppermute(part, ("y", "core", "col"), perm))
    out = call(out_kernel, jax.ShapeDtypeStruct((512, 448), BF), 1, 10)(pos, *chunks, w_all, tok)
    return jnp.transpose(out.reshape(2, 256, 448), (1, 0, 2))


def solution(mesh):
    inner = Mesh(mesh.devices.reshape(8, 4, 2, 4), ("req", "y", "core", "col"))
    rows = ("y", "core")
    hold = ("req", "col")
    return jax.shard_map(
        body,
        mesh=inner,
        in_specs=(
            P(("req", "y", "core"), None, "col"),
            P("col", rows),
            P("col", rows),
            P(rows, "col"),
            P(rows, "col"),
            P(hold, None, rows),
            P(hold, None, rows),
            P(hold),
            P(hold),
            P(hold, rows),
            P(hold, rows),
            P(hold),
        ),
        out_specs=P(("req", "y", "core"), None, "col"),
        check_vma=False,
    )
```

profile of v0, /device:TPU:9, one launch (start us, length us, event | category | flops | bytes accessed | tf_op | source)
XLA Modules:
  0.0 207.2 jit_solution(12365553193905035715)
XLA Ops:
  6.5 1.2 copy.56
  7.8 1.4 collective-permute-start
  9.1 0.8 collective-permute-start.1
  10.0 2.0 collective-permute-start.2
  11.9 1.2 reshape.66
  13.6 0.9 copy.58
  14.5 0.9 copy.59
  15.5 1.6 collective-permute-start.3
  17.1 0.7 broadcast_compare_fusion
  17.8 0.7 fusion.6
  18.6 0.7 copy.55
  19.3 11.0 %all-to-all-start = ((s32[32,1,1]{2,1,0:T(1,128)}), s32[32,1,1]{2,1,0:T(1,128)S(1)}, u32[]{:S(2)}, u32[]{:S(2)}) async-start(s32[32,1,1]{2,1,0:T(1,128)} %copy.55), calls=%async_computation | async-start | bytes 32768 | tf_op jit(solution)/shard_map/all_to_all | solution.py:283
  31.2 3.1 %collective-permute-done.2.t3 = bf16[512,448]{1,0:T(8,128)(2,1)S(1)} collective-permute-done((bf16[512,448]{1,0:T(8,128)(2,1)S(1)}, bf16[512,448]{1,0:T(8,128)(2,1)S(1)}, u32[]{:S(2)}, u32[]{:S(2)}) %collective-permute-start.2) | collective-permute-done | bytes 458784 | tf_op jit(solution)/shard_map/ppermute | solution.py:268
  34.3 3.9 %shard_map.118 = bf16[4,512,640]{2,1,0:T(8,128)(2,1)} custom-call(s32[4]{0:T(128)S(1)} %pad_add_fusion.pos_ref, bf16[512,448]{1,0:T(8,128)(2,1)S(1)} %bitcast.21, bf16[512,448]{1,0:T(8,128)(2,1)S(1)} %collective-permute-done.t1, bf16[512,448]{1,0:T(8,128)(2,1)S(1)} %collective-permute-done.1.t2, bf16[512,448]{1,0:T(8,128)(2,1)S(1)} %collective-permute-done.2.t3, ...), custom_call_target="tpu_custom_call" | custom-call | tf_op jit(solution)/shard_map/pallas_call | solution.py:295
  38.2 0.7 all-to-all-done
  39.4 3.7 %all-to-all-start.1 = ((bf16[4,512,640]{2,1,0:T(8,128)(2,1)}), bf16[4,512,640]{2,1,0:T(8,128)(2,1)S(1)}, u32[]{:S(2)}, u32[]{:S(2)}) async-start(bf16[4,512,640]{2,1,0:T(8,128)(2,1)} %shard_map.118), calls=%async_computation.1 | async-start | bytes 5242880 | tf_op jit(solution)/shard_map/all_to_all | solution.py:296
  43.2 0.7 all-gather.3.cloned.1.call-update
  43.9 1.4 compare_reduce_fusion.1
  45.5 1.3 fusion.1.s_ref
  46.8 7.3 %copy.61 = bf16[1,273,7168]{1,2,0:T(8,128)(2,1)} copy(bf16[1,273,7168]{2,1,0:T(8,128)(2,1)} %param.17) | data formatting | bytes 7827456 | tf_op args[5]
  54.2 8.4 %copy.62 = bf16[273,224,32]{1,0,2:T(8,128)(2,1)} copy(bf16[273,224,32]{0,2,1:T(8,128)(2,1)} %bitcast.27) | data formatting | bytes 7827456 | tf_op jit(solution)/shard_map/reshape;squeeze | solution.py:292
  62.6 2.0 copy.63
  64.7 0.7 add_reduce_fusion
  65.8 7.8 %all-to-all-done.1.p_ref = bf16[4,512,640]{2,1,0:T(8,128)(2,1)S(1)} async-done(((bf16[4,512,640]{2,1,0:T(8,128)(2,1)}), bf16[4,512,640]{2,1,0:T(8,128)(2,1)S(1)}, u32[]{:S(2)}, u32[]{:S(2)}) %all-to-all-start.1) | async-done | bytes 2621472 | tf_op jit(solution)/shard_map/all_to_all | solution.py:296
  73.6 0.9 shard_map.119
  74.5 2.5 %collective-permute-start.4 = (bf16[512,384]{1,0:T(8,128)(2,1)S(1)}, bf16[512,384]{1,0:T(8,128)(2,1)S(1)}, u32[]{:S(2)}, u32[]{:S(2)}) collective-permute-start(bf16[512,384]{1,0:T(8,128)(2,1)S(1)} %get-tuple-element.16), channel_id=1, source_target_pairs={{0,4},{4,0},{1,5},{5,1},{2,6},{6,2},{3,7},{7,3},{8,12},{12,8},{9,1... | collective-permute-start | bytes 1179656 | tf_op jit(solution)/shard_map/ppermute | solution.py:299
  77.0 1.4 compare_reduce_fusion
  78.3 0.7 select_reduce_fusion
  80.3 2.1 %shard_map.121 = (bf16[32,16,128]{2,1,0:T(8,128)(2,1)}, bf16[32,16,128]{2,1,0:T(8,128)(2,1)S(1)}) custom-call(s32[4]{0:T(128)S(1)} %pad_add_fusion.pos_ref, s32[32]{0:T(128)S(1)} %broadcast_select_fusion.2.g_ref, s32[32]{0:T(128)S(1)} %copy-done.14, bf16[512,384]{1,0:T(8,128)(2,1)S(1)} %get-tuple-element.15.own_ref, ...), custom_call_target="tpu_custom_call" | custom-call | tf_op jit(solution)/shard_map/pallas_call | solution.py:302
  82.4 0.7 copy-done.3
  83.1 9.1 %all-to-all-start.2 = ((bf16[32,16,128]{2,1,0:T(8,128)(2,1)}), bf16[32,16,128]{2,1,0:T(8,128)(2,1)S(1)}, u32[]{:S(2)}, u32[]{:S(2)}) async-start(bf16[32,16,128]{2,1,0:T(8,128)(2,1)} %get-tuple-element.19), calls=%async_computation.2 | async-start | bytes 262144 | tf_op jit(solution)/shard_map/all_to_all | solution.py:305
  92.3 7.6 %maximum_maximum_fusion.state_ref = bf16[32,273,256]{2,1,0:T(8,128)(2,1)} fusion(bf16[32,273,2]{2,1,0:T(8,128)(2,1)} %copy.63, bf16[32,273,224]{2,1,0:T(8,128)(2,1)} %bitcast.28, bf16[256]{0:T(256)(128)(2,1)S(1)} %pad.3.clone), kind=kLoop, calls=%fused_computation | loop fusion | flops 17891328 | bytes 8422016 | tf_op jit(solution)/shard_map/concatenate | solution.py:293
  99.8 2.2 %all-to-all-done.2.rec_ref = bf16[32,16,128]{2,1,0:T(8,128)(2,1)S(1)} async-done(((bf16[32,16,128]{2,1,0:T(8,128)(2,1)}), bf16[32,16,128]{2,1,0:T(8,128)(2,1)S(1)}, u32[]{:S(2)}, u32[]{:S(2)}) %all-to-all-start.2) | async-done | bytes 131104 | tf_op jit(solution)/shard_map/all_to_all | solution.py:305
  102.0 2.3 %copy-done = bf16[32,273,256]{2,1,0:T(8,128)(2,1)S(1)} copy-done((bf16[32,273,256]{2,1,0:T(8,128)(2,1)S(1)}, bf16[32,273,256]{2,1,0:T(8,128)(2,1)}, u32[]{:S(2)}) %copy-start) | copy-done | bytes 4472856
  104.3 9.4 %shard_map.122 = (bf16[32,16,512]{2,1,0:T(8,128)(2,1)S(1)}, bf16[32,16,512]{2,1,0:T(8,128)(2,1)S(1)}) custom-call(s32[4]{0:T(128)S(1)} %pad_add_fusion.pos_ref, s32[32]{0:T(128)S(1)} %get-tuple-element.26.owner_ref, bf16[32,16,128]{2,1,0:T(8,128)(2,1)S(1)} %all-to-all-done.2.rec_ref, bf16[32,16,128]{2,1,0:T(8,128)(2,1)S(1)} %get-tuple-element.20.keep_ref, ...), custom_call_target="tpu_custom_call" | custom-call | tf_op jit(solution)/shard_map/pallas_call | solution.py:311
  113.7 0.8 copy-done.10
  114.5 0.8 copy-done.11
  115.3 7.0 %all-to-all-start.3 = ((bf16[32,16,512]{2,1,0:T(8,128)(2,1)}), bf16[32,16,512]{2,1,0:T(8,128)(2,1)S(1)}, u32[]{:S(2)}, u32[]{:S(2)}) async-start(bf16[32,16,512]{2,1,0:T(8,128)(2,1)} %copy-done.10), calls=%async_computation.3 | async-start | bytes 1048576 | tf_op jit(solution)/shard_map/all_to_all | solution.py:320
  122.4 0.9 copy.60.len_ref
  123.4 1.0 copy-done.4
  124.4 0.9 copy-done.9
  125.3 0.9 copy-done.13
  126.3 5.9 %shard_map.120 = (f32[2,512,256]{2,1,0:T(8,128)S(1)}, f32[2,512,256]{2,1,0:T(8,128)S(1)}) custom-call(s32[4]{0:T(128)S(1)} %pad_add_fusion.pos_ref, bf16[512,384]{1,0:T(8,128)(2,1)S(1)} %get-tuple-element.15.own_ref, bf16[512,384]{1,0:T(8,128)(2,1)S(1)} %copy-done.4, bf16[512,256]{1,0:T(8,128)(2,1)S(1)} %copy-done.13, bf16[512,1792]{1,0:T(8,128)(2,1)S(1)} %copy-done.2, ...), custom_call_target="tpu_custom_call" | custom-call | tf_op jit(solution)/shard_map/pallas_call | solution.py:307
  132.2 1.0 copy-done.5
  133.2 1.0 copy-done.7
  134.2 4.4 %all-to-all-done.3.rec_ref = bf16[32,16,512]{2,1,0:T(8,128)(2,1)S(1)} async-done(((bf16[32,16,512]{2,1,0:T(8,128)(2,1)}), bf16[32,16,512]{2,1,0:T(8,128)(2,1)S(1)}, u32[]{:S(2)}, u32[]{:S(2)}) %all-to-all-start.3) | async-done | bytes 524320 | tf_op jit(solution)/shard_map/all_to_all | solution.py:320
  138.7 1.2 copy-done.6
  139.9 1.2 copy-done.8
  141.1 1.0 copy-done.12
  142.2 1.8 shard_map.123
  144.0 4.1 %collective-permute-start.10 = (bf16[512,256]{1,0:T(8,128)(2,1)S(1)}, bf16[512,256]{1,0:T(8,128)(2,1)S(1)}, u32[]{:S(2)}, u32[]{:S(2)}) collective-permute-start(bf16[512,256]{1,0:T(8,128)(2,1)S(1)} %get-tuple-element.24), channel_id=1, source_target_pairs={{0,6},{4,2},{8,7},{12,3},{16,4},{20,0},{24,5},{28,1},{1,14},{5,10}... | collective-permute-start | bytes 786440 | tf_op jit(solution)/shard_map/ppermute | solution.py:335
  148.6 1.5 collective-permute-start.12
  150.1 4.6 %collective-permute-start.5 = (bf16[512,256]{1,0:T(8,128)(2,1)S(1)}, bf16[512,256]{1,0:T(8,128)(2,1)S(1)}, u32[]{:S(2)}, u32[]{:S(2)}) collective-permute-start(bf16[512,256]{1,0:T(8,128)(2,1)S(1)} %get-tuple-element.23), channel_id=1, source_target_pairs={{0,0},{4,4},{8,1},{12,5},{16,2},{20,6},{24,3},{28,7},{1,8},{5,12},... | collective-permute-start | bytes 786440 | tf_op jit(solution)/shard_map/ppermute | solution.py:335
  154.7 1.8 collective-permute-start.6
  156.5 1.9 collective-permute-done.10.refs_5_
  158.4 4.2 %collective-permute-start.7 = (bf16[512,256]{1,0:T(8,128)(2,1)S(1)}, bf16[512,256]{1,0:T(8,128)(2,1)S(1)}, u32[]{:S(2)}, u32[]{:S(2)}) collective-permute-start(bf16[512,256]{1,0:T(8,128)(2,1)S(1)} %get-tuple-element.23), channel_id=1, source_target_pairs={{0,1},{4,5},{8,2},{12,6},{16,3},{20,7},{24,0},{28,4},{1,9},{5,13},... | collective-permute-start | bytes 786440 | tf_op jit(solution)/shard_map/ppermute | solution.py:335
  162.6 5.9 %collective-permute-start.8 = (bf16[512,256]{1,0:T(8,128)(2,1)S(1)}, bf16[512,256]{1,0:T(8,128)(2,1)S(1)}, u32[]{:S(2)}, u32[]{:S(2)}) collective-permute-start(bf16[512,256]{1,0:T(8,128)(2,1)S(1)} %get-tuple-element.24), channel_id=1, source_target_pairs={{0,5},{4,1},{8,6},{12,2},{16,7},{20,3},{24,4},{28,0},{1,13},{5,9},... | collective-permute-start | bytes 786440 | tf_op jit(solution)/shard_map/ppermute | solution.py:335
  168.5 7.5 %collective-permute-start.9 = (bf16[512,256]{1,0:T(8,128)(2,1)S(1)}, bf16[512,256]{1,0:T(8,128)(2,1)S(1)}, u32[]{:S(2)}, u32[]{:S(2)}) collective-permute-start(bf16[512,256]{1,0:T(8,128)(2,1)S(1)} %get-tuple-element.23), channel_id=1, source_target_pairs={{0,2},{4,6},{8,3},{12,7},{16,0},{20,4},{24,1},{28,5},{1,10},{5,14}... | collective-permute-start | bytes 786440 | tf_op jit(solution)/shard_map/ppermute | solution.py:335
  176.0 5.0 %collective-permute-done.6.refs_1_ = bf16[512,256]{1,0:T(8,128)(2,1)S(1)} collective-permute-done((bf16[512,256]{1,0:T(8,128)(2,1)S(1)}, bf16[512,256]{1,0:T(8,128)(2,1)S(1)}, u32[]{:S(2)}, u32[]{:S(2)}) %collective-permute-start.6) | collective-permute-done | bytes 262176 | tf_op jit(solution)/shard_map/ppermute | solution.py:335
  181.0 4.2 %collective-permute-done.7.refs_2_ = bf16[512,256]{1,0:T(8,128)(2,1)S(1)} collective-permute-done((bf16[512,256]{1,0:T(8,128)(2,1)S(1)}, bf16[512,256]{1,0:T(8,128)(2,1)S(1)}, u32[]{:S(2)}, u32[]{:S(2)}) %collective-permute-start.7) | collective-permute-done | bytes 262176 | tf_op jit(solution)/shard_map/ppermute | solution.py:335
  185.2 10.9 %collective-permute-done.8.refs_3_ = bf16[512,256]{1,0:T(8,128)(2,1)S(1)} collective-permute-done((bf16[512,256]{1,0:T(8,128)(2,1)S(1)}, bf16[512,256]{1,0:T(8,128)(2,1)S(1)}, u32[]{:S(2)}, u32[]{:S(2)}) %collective-permute-start.8) | collective-permute-done | bytes 262176 | tf_op jit(solution)/shard_map/ppermute | solution.py:335
  196.0 1.5 copy-done.1
  197.5 1.8 shard_map.124
  199.3 1.0 copy.66
  (60 shorter events, 4.9 us)
Async XLA Ops:
  7.8 23.4 %collective-permute-start = (bf16[512,448]{1,0:T(8,128)(2,1)S(1)}, bf16[512,448]{1,0:T(8,128)(2,1)S(1)}, u32[]{:S(2)}, u32[]{:S(2)}) collective-permute-start(bf16[512,448]{1,0:T(8,128)(2,1)S(1)} %bitcast.18), channel_id=1, source_target_pairs={{0,8},{8,16},{16,24},{24,0},{1,9},{9,17},{17,25},{25,1},{2,10},{10... | collective-permute-start | bytes 1376264 | tf_op jit(solution)/shard_map/ppermute | solution.py:268
  9.1 22.0 %collective-permute-start.1 = (bf16[512,448]{1,0:T(8,128)(2,1)S(1)}, bf16[512,448]{1,0:T(8,128)(2,1)S(1)}, u32[]{:S(2)}, u32[]{:S(2)}) collective-permute-start(bf16[512,448]{1,0:T(8,128)(2,1)S(1)} %bitcast.19), channel_id=1, source_target_pairs={{0,16},{8,24},{16,0},{24,8},{1,17},{9,25},{17,1},{25,9},{2,18},{10... | collective-permute-start | bytes 1376264 | tf_op jit(solution)/shard_map/ppermute | solution.py:268
  10.0 24.3 %collective-permute-start.2 = (bf16[512,448]{1,0:T(8,128)(2,1)S(1)}, bf16[512,448]{1,0:T(8,128)(2,1)S(1)}, u32[]{:S(2)}, u32[]{:S(2)}) collective-permute-start(bf16[512,448]{1,0:T(8,128)(2,1)S(1)} %bitcast.20), channel_id=1, source_target_pairs={{0,24},{8,0},{16,8},{24,16},{1,25},{9,1},{17,9},{25,17},{2,26},{10... | collective-permute-start | bytes 1376264 | tf_op jit(solution)/shard_map/ppermute | solution.py:268
  15.5 14.9 %collective-permute-start.3 = (bf16[448,288]{1,0:T(8,128)(2,1)S(1)}, bf16[448,288]{1,0:T(8,128)(2,1)S(1)}, u32[]{:S(2)}, u32[]{:S(2)}) collective-permute-start(bf16[448,288]{1,0:T(8,128)(2,1)S(1)} %pad_maximum_fusion), channel_id=1, source_target_pairs={{0,4},{4,0},{1,5},{5,1},{2,6},{6,2},{3,7},{7,3},{8,12},{12,8},{9,1... | collective-permute-start | bytes 774152 | tf_op jit(solution)/shard_map/ppermute | solution.py:271
  19.3 19.6 %all-to-all-start = ((s32[32,1,1]{2,1,0:T(1,128)}), s32[32,1,1]{2,1,0:T(1,128)S(1)}, u32[]{:S(2)}, u32[]{:S(2)}) async-start(s32[32,1,1]{2,1,0:T(1,128)} %copy.55), calls=%async_computation | async-start | bytes 32768 | tf_op jit(solution)/shard_map/all_to_all | solution.py:283
  31.1 14.1 %copy-start.19 = (s32[512]{0:T(512)S(1)}, s32[512]{0:T(512)}, u32[]{:S(2)}) copy-start(s32[512]{0:T(512)} %param.20) | copy-start | bytes 6148
  38.8 0.6 copy-start.16
  39.4 34.2 %all-to-all-start.1 = ((bf16[4,512,640]{2,1,0:T(8,128)(2,1)}), bf16[4,512,640]{2,1,0:T(8,128)(2,1)S(1)}, u32[]{:S(2)}, u32[]{:S(2)}) async-start(bf16[4,512,640]{2,1,0:T(8,128)(2,1)} %shard_map.118), calls=%async_computation.1 | async-start | bytes 5242880 | tf_op jit(solution)/shard_map/all_to_all | solution.py:296
  43.1 132.9 %all-gather.3.cloned.1.call-start = ((), (), s32[]{:S(2)}) async-start(), calls=%async_computation.4 | async-start | bytes 2064384 | tf_op jit(solution)/shard_map/all_gather | solution.py:276
  54.2 8.4 %copy-start.18 = (bf16[32,273,2]{1,2,0:T(2,128)(2,1)S(1)}, bf16[32,273,2]{1,2,0:T(2,128)(2,1)}, u32[]{:S(2)}) copy-start(bf16[32,273,2]{1,2,0:T(2,128)(2,1)} %param.18) | copy-start | bytes 104836
  54.2 10.5 %copy-start.17 = (s32[32,1,1]{2,1,0:T(1,128)S(1)}, s32[32,1,1]{2,1,0:T(1,128)}, u32[]{:S(2)}) copy-start(s32[32,1,1]{2,1,0:T(1,128)} %copy-done.16) | copy-start | bytes 388
  74.5 5.2 %collective-permute-start.4 = (bf16[512,384]{1,0:T(8,128)(2,1)S(1)}, bf16[512,384]{1,0:T(8,128)(2,1)S(1)}, u32[]{:S(2)}, u32[]{:S(2)}) collective-permute-start(bf16[512,384]{1,0:T(8,128)(2,1)S(1)} %get-tuple-element.16), channel_id=1, source_target_pairs={{0,4},{4,0},{1,5},{5,1},{2,6},{6,2},{3,7},{7,3},{8,12},{12,8},{9,1... | collective-permute-start | bytes 1179656 | tf_op jit(solution)/shard_map/ppermute | solution.py:299
  79.7 0.6 copy-start.14
  82.4 0.7 copy-start.3
  83.1 18.9 %all-to-all-start.2 = ((bf16[32,16,128]{2,1,0:T(8,128)(2,1)}), bf16[32,16,128]{2,1,0:T(8,128)(2,1)S(1)}, u32[]{:S(2)}, u32[]{:S(2)}) async-start(bf16[32,16,128]{2,1,0:T(8,128)(2,1)} %get-tuple-element.19), calls=%async_computation.2 | async-start | bytes 262144 | tf_op jit(solution)/shard_map/all_to_all | solution.py:305
  92.2 30.1 %copy-start.20 = (s32[512]{0:T(512)S(1)}, s32[512]{0:T(512)}, u32[]{:S(2)}) copy-start(s32[512]{0:T(512)} %param.23) | copy-start | bytes 6148
  92.3 31.1 %copy-start.2 = (bf16[512,1792]{1,0:T(8,128)(2,1)S(1)}, bf16[512,1792]{1,0:T(8,128)(2,1)}, u32[]{:S(2)}) copy-start(bf16[512,1792]{1,0:T(8,128)(2,1)} %tv_ref.1) | copy-start | bytes 5505028
  102.0 2.3 %copy-start = (bf16[32,273,256]{2,1,0:T(8,128)(2,1)S(1)}, bf16[32,273,256]{2,1,0:T(8,128)(2,1)}, u32[]{:S(2)}) copy-start(bf16[32,273,256]{2,1,0:T(8,128)(2,1)} %maximum_maximum_fusion.state_ref) | copy-start | bytes 13418500
  113.7 0.8 copy-start.10
  114.5 0.8 copy-start.11
  115.3 23.3 %copy-start.15 = (s32[32]{0:T(128)S(1)}, s32[32]{0:T(128)}, u32[]{:S(2)}) copy-start(s32[32]{0:T(128)} %fusion.1.s_ref) | copy-start | bytes 388
  115.3 23.3 %all-to-all-start.3 = ((bf16[32,16,512]{2,1,0:T(8,128)(2,1)}), bf16[32,16,512]{2,1,0:T(8,128)(2,1)S(1)}, u32[]{:S(2)}, u32[]{:S(2)}) async-start(bf16[32,16,512]{2,1,0:T(8,128)(2,1)} %copy-done.10), calls=%async_computation.3 | async-start | bytes 1048576 | tf_op jit(solution)/shard_map/all_to_all | solution.py:320
  123.4 1.0 copy-start.4
  124.4 0.9 copy-start.9
  125.3 0.9 copy-start.13
  132.2 1.0 copy-start.5
  133.2 1.0 copy-start.7
  138.7 1.2 copy-start.6
  139.9 1.2 copy-start.8
  141.1 1.0 copy-start.12
  144.0 14.4 %collective-permute-start.10 = (bf16[512,256]{1,0:T(8,128)(2,1)S(1)}, bf16[512,256]{1,0:T(8,128)(2,1)S(1)}, u32[]{:S(2)}, u32[]{:S(2)}) collective-permute-start(bf16[512,256]{1,0:T(8,128)(2,1)S(1)} %get-tuple-element.24), channel_id=1, source_target_pairs={{0,6},{4,2},{8,7},{12,3},{16,4},{20,0},{24,5},{28,1},{1,14},{5,10}... | collective-permute-start | bytes 786440 | tf_op jit(solution)/shard_map/ppermute | solution.py:335
  148.1 14.6 %collective-permute-start.11 = (bf16[512,256]{1,0:T(8,128)(2,1)S(1)}, bf16[512,256]{1,0:T(8,128)(2,1)S(1)}, u32[]{:S(2)}, u32[]{:S(2)}) collective-permute-start(bf16[512,256]{1,0:T(8,128)(2,1)S(1)} %get-tuple-element.23), channel_id=1, source_target_pairs={{0,3},{4,7},{8,0},{12,4},{16,1},{20,5},{24,2},{28,6},{1,11},{5,15}... | collective-permute-start | bytes 786440 | tf_op jit(solution)/shard_map/ppermute | solution.py:335
  148.6 19.9 %collective-permute-start.12 = (bf16[512,256]{1,0:T(8,128)(2,1)S(1)}, bf16[512,256]{1,0:T(8,128)(2,1)S(1)}, u32[]{:S(2)}, u32[]{:S(2)}) collective-permute-start(bf16[512,256]{1,0:T(8,128)(2,1)S(1)} %get-tuple-element.24), channel_id=1, source_target_pairs={{0,7},{4,3},{8,4},{12,0},{16,5},{20,1},{24,6},{28,2},{1,15},{5,11}... | collective-permute-start | bytes 786440 | tf_op jit(solution)/shard_map/ppermute | solution.py:335
  150.1 25.9 %collective-permute-start.5 = (bf16[512,256]{1,0:T(8,128)(2,1)S(1)}, bf16[512,256]{1,0:T(8,128)(2,1)S(1)}, u32[]{:S(2)}, u32[]{:S(2)}) collective-permute-start(bf16[512,256]{1,0:T(8,128)(2,1)S(1)} %get-tuple-element.23), channel_id=1, source_target_pairs={{0,0},{4,4},{8,1},{12,5},{16,2},{20,6},{24,3},{28,7},{1,8},{5,12},... | collective-permute-start | bytes 786440 | tf_op jit(solution)/shard_map/ppermute | solution.py:335
  154.7 26.3 %collective-permute-start.6 = (bf16[512,256]{1,0:T(8,128)(2,1)S(1)}, bf16[512,256]{1,0:T(8,128)(2,1)S(1)}, u32[]{:S(2)}, u32[]{:S(2)}) collective-permute-start(bf16[512,256]{1,0:T(8,128)(2,1)S(1)} %get-tuple-element.24), channel_id=1, source_target_pairs={{0,4},{4,0},{8,5},{12,1},{16,6},{20,2},{24,7},{28,3},{1,12},{5,8},... | collective-permute-start | bytes 786440 | tf_op jit(solution)/shard_map/ppermute | solution.py:335
  158.4 26.8 %collective-permute-start.7 = (bf16[512,256]{1,0:T(8,128)(2,1)S(1)}, bf16[512,256]{1,0:T(8,128)(2,1)S(1)}, u32[]{:S(2)}, u32[]{:S(2)}) collective-permute-start(bf16[512,256]{1,0:T(8,128)(2,1)S(1)} %get-tuple-element.23), channel_id=1, source_target_pairs={{0,1},{4,5},{8,2},{12,6},{16,3},{20,7},{24,0},{28,4},{1,9},{5,13},... | collective-permute-start | bytes 786440 | tf_op jit(solution)/shard_map/ppermute | solution.py:335
  162.6 33.4 %collective-permute-start.8 = (bf16[512,256]{1,0:T(8,128)(2,1)S(1)}, bf16[512,256]{1,0:T(8,128)(2,1)S(1)}, u32[]{:S(2)}, u32[]{:S(2)}) collective-permute-start(bf16[512,256]{1,0:T(8,128)(2,1)S(1)} %get-tuple-element.24), channel_id=1, source_target_pairs={{0,5},{4,1},{8,6},{12,2},{16,7},{20,3},{24,4},{28,0},{1,13},{5,9},... | collective-permute-start | bytes 786440 | tf_op jit(solution)/shard_map/ppermute | solution.py:335
  168.5 27.5 %collective-permute-start.9 = (bf16[512,256]{1,0:T(8,128)(2,1)S(1)}, bf16[512,256]{1,0:T(8,128)(2,1)S(1)}, u32[]{:S(2)}, u32[]{:S(2)}) collective-permute-start(bf16[512,256]{1,0:T(8,128)(2,1)S(1)} %get-tuple-element.23), channel_id=1, source_target_pairs={{0,2},{4,6},{8,3},{12,7},{16,0},{20,4},{24,1},{28,5},{1,10},{5,14}... | collective-permute-start | bytes 786440 | tf_op jit(solution)/shard_map/ppermute | solution.py:335
  196.0 1.5 copy-start.1
Sparse Core Ops, SparseCore 0:
  45.8 29.9 all-gather.2
where the time goes:
time: 209 us; the launch traced here: 207 us
  starting transfers between devices  69.1 us (33%)
  local copies, waits for them, and re-layouts  41.3 us (20%)
  waiting for transfers between devices  40.9 us (20%)
  Pallas kernels  25.8 us (12%)
  other arithmetic  16.3 us (8%)
  between operations  13.7 us (7%)
    ppermute x8, starting transfers between devices, body(): chunks.append(lax.ppermute(part, ('y', 'core', 'col'), perm))  30.1 us
    unnamed x46, local copies, waits for them, and re-layouts  26.9 us
    ppermute x8, waiting for transfers between devices, body(): chunks.append(lax.ppermute(part, ('y', 'core', 'col'), perm))  22 us
    all_to_all x1, starting transfers between devices, body(): lax.all_to_all(code[:, None], ('req', 'col'), split_axis=0, concat_axis=0...  11 us
    pallas_call x1, Pallas kernels, body(): pl.pallas_call(slot_kernel, grid=(4,), out_shape=(shape, shape), in_specs...  9.39 us
    all_to_all x1, starting transfers between devices, body(): lax.all_to_all(q_send, ('req', 'col'), split_axis=0, concat_axis=0, tiled...  9.1 us
    another operation x1, local copies, waits for them, and re-layouts, body(): states = jnp.transpose(cached_state[0].reshape(273, 224, 32), (2, 0, 1))  8.41 us
    all_to_all x1, waiting for transfers between devices, body(): lax.all_to_all(partial, 'col', split_axis=0, concat_axis=0, tiled=True)  7.76 us
  transfers between devices with their start and end apart: 18, of which 9 were waited for; matrix products, arithmetic and copies ran while one was open for 19% of the time, Pallas kernels for 12%

commit v1 on v0

--- a/solution.py
+++ b/solution.py
@@ -42,27 +42,26 @@
     )
 
 
-def project_kernel(pos_ref, t0, t1, t2, t3, w_ref, out_ref):
-    w = w_ref[...]
+def order_kernel(pos_ref, t0, t1, t2, t3, out_ref):
     for shift, block in enumerate((t0, t1, t2, t3)):
-        slot = lax.rem(pos_ref[0] + 4 - shift, 4)
-        out_ref[slot] = dot(block[...], w).astype(BF)
-
-
-def sum_kernel(pos_ref, p_ref, own_ref, oth_ref):
-    core = pos_ref[1]
-
-    def total(lo, hi):
-        acc = p_ref[0, :, lo:hi].astype(F32)
-        for i in range(1, 4):
-            acc = acc + p_ref[i, :, lo:hi].astype(F32)
-        return acc.astype(BF)
-
-    first, second, keys = total(0, 256), total(256, 512), total(512, 640)
-    own_ref[:, 0:256] = jnp.where(core == 0, first, second)
-    oth_ref[:, 0:256] = jnp.where(core == 0, second, first)
-    own_ref[:, 256:384] = keys
-    oth_ref[:, 256:384] = keys
+        out_ref[lax.rem(pos_ref[0] + 4 - shift, 4)] = block[...]
+
+
+def project_kernel(pos_ref, t_ref, *refs):
+    weights, own_ref, oth_ref, padded = refs[:8], refs[8], refs[9], refs[10]
+    padded[0:64, :] = jnp.zeros((64, 288), BF)
+    for which, out_ref in enumerate((own_ref, oth_ref)):
+        first = second = None
+        for shift in range(4):
+            block = lax.rem(pos_ref[3] + 4 - shift, 4)
+            w = weights[which * 4 + shift][...]
+            padded[64:512, :] = w
+            one = dot(t_ref[block, :, 0:448], w)
+            two = dot(t_ref[block, :, 384:896], padded[...])
+            first = one if first is None else first + one
+            second = two if second is None else second + two
+        out_ref[0:256, :] = first.astype(BF)
+        out_ref[256:512, :] = second.astype(BF)
 
 
 def group_kernel(pos_ref, g_ref, s_ref, own_ref, rec_ref, place_ref, send_ref, keep_ref, grouped):
@@ -174,7 +173,7 @@
     sum_a = onehot(lax.shift_right_logical(r, 4) == c)
     pick_q = onehot((r >= 224) & (r - 224 == c))
     r, c = iota((128, 128), 0), iota((128, 128), 1)
-    pick_k = onehot((c < 32) & (r == c + 32 * core))
+    pick_k = onehot(iota((32, 128), 0) == iota((32, 128), 1))
     sum_new = onehot((r < 32) & (lax.shift_right_logical(r, 4) == c))
     r, c = iota((128, 1792), 0), iota((128, 1792), 1)
     expand_w = onehot((r < 16) & (c >= r * 112) & (c < (r + 1) * 112))
@@ -196,7 +195,7 @@
         live = (head_lane & 7) < len_ref[pl.ds(at, 256), :]
         live = live & (head_lane < 16)
         values = tv_ref[pl.ds(at, 256), :]
-        new_keys = [dot(ref[t * 256 : (t + 1) * 256, 256:384], pick_k) for t in range(2)]
+        new_keys = [dot(ref[t * 256 : (t + 1) * 256, 256:288], pick_k) for t in range(2)]
         for t in range(2):
             vq = ref[t * 256 : (t + 1) * 256, 0:256]
             one, two = split(dot(vq, expand_q) * keys)
@@ -218,7 +217,7 @@
             den_ref[e, t * 256 : (t + 1) * 256, :] = den
 
 
-def combine_kernel(pos_ref, g_ref, s_ref, num_ref, den_ref, rec_ref, own_ref, place_ref, same_ref, other_ref, buf):
+def combine_kernel(pos_ref, g_ref, s_ref, num_ref, den_ref, rec_ref, own_ref, place_ref, out_ref, buf):
     core = pos_ref[1]
     me = pos_ref[2]
     for p in range(32):
@@ -235,7 +234,7 @@
     r, c = iota((256, 256), 0), iota((256, 256), 1)
     spread = onehot((c < 224) & (((c < 112) & ((r == 224) | (r == 226))) | ((c >= 112) & ((r == 225) | (r == 227)))))
     lane = iota((256, 256), 1)
-    for e, out_ref in enumerate((same_ref, other_ref)):
+    for e in range(2):
         half = core if e == 0 else 1 - core
         at = pl.multiple_of(half * 256, 256)
         hot = onehot(iota((256, 512), 1) == place_ref[pl.ds(at, 256), :])
@@ -245,35 +244,37 @@
             den = den_ref[e, t * 256 : (t + 1) * 256, :] + dot(part.astype(BF), spread)
             num = num_ref[e, t * 256 : (t + 1) * 256, :] + part
             out = jnp.where(lane < 224, num / jnp.where(lane < 224, den, 1.0), 0.0)
-            out_ref[t * 256 : (t + 1) * 256, :] = out.astype(BF)
-
-
-def out_kernel(pos_ref, *refs):
-    chunks, w_ref, tok_ref, out_ref = refs[:8], refs[8], refs[9], refs[10]
-    core, col = pos_ref[1], pos_ref[3]
-    acc = tok_ref[...].astype(F32)
-    for s in range(4):
-        for d in range(2):
-            j = lax.rem(col + 4 - s, 4)
-            k = core if d == 0 else 1 - core
-            acc = acc + dot(chunks[s * 2 + d][:, 0:224], w_ref[j * 2 + k])
-    out_ref[...] = acc.astype(BF)
+            out = out.astype(BF)
+            for part in range(2):
+                out_ref[half * 2 + part, t * 128 : (t + 1) * 128, :] = out[part * 128 : (part + 1) * 128]
+
+
+def out_kernel(pos_ref, own_ref, oth_ref, w0, w1, w2, w3, first_ref, second_ref):
+    y, core, col = pos_ref[0], pos_ref[1], pos_ref[3]
+    acc = [None, None]
+    for shift, w_ref in enumerate((w0, w1, w2, w3)):
+        j = lax.rem(y + 4 - shift, 4)
+        for which, ref in enumerate((own_ref, oth_ref)):
+            k = core if which == 0 else 1 - core
+            heads = ref[j, :, 0:224]
+            for e in range(2):
+                part = dot(heads, w_ref[jnp.bitwise_xor(2 * e + k, col)])
+                acc[e] = part if acc[e] is None else acc[e] + part
+    even = lax.rem(y, 2) == 0
+    first_ref[...] = jnp.where(even, acc[0], acc[1]).astype(BF)
+    second_ref[...] = jnp.where(even, acc[1], acc[0]).astype(BF)
 
 
 def body(tokens, w_query, w_key, w_value, w_out, cached_state, cached_norm, slot_prompt, prompt_of, tail_keys, tail_values, tail_length):
     y, core, col = lax.axis_index("y"), lax.axis_index("core"), lax.axis_index("col")
     me = lax.axis_index(("req", "col"))
     pos = jnp.stack([y, core, me, col]).astype(jnp.int32)
-    tok = jnp.transpose(tokens, (1, 0, 2)).reshape(512, 448)
+    tok = tokens.reshape(256, 896)
     blocks = [tok] + [lax.ppermute(tok, "y", [(i, (i + s) % 4) for i in range(4)]) for s in range(1, 4)]
     value_w = jnp.moveaxis(w_value.reshape(2, 448, 112), 0, 1).reshape(448, 224)
     mine = jnp.concatenate([value_w, w_query, w_key], axis=1)
-    theirs = lax.ppermute(mine, "core", [(0, 1), (1, 0)])
-    w0, w1 = jnp.where(core == 0, mine, theirs), jnp.where(core == 0, theirs, mine)
-    weights = jnp.concatenate(
-        [w0[:, :256], w1[:, :256], w0[:, 256:], w1[:, 256:], jnp.zeros((448, 64), BF)], axis=1
-    )
-    w_all = lax.all_gather(w_out, ("y", "core"), axis=0, tiled=False)
+    mine = [mine] + [lax.ppermute(mine, "col", [(i, (i + s) % 4) for i in range(4)]) for s in range(1, 4)]
+    theirs = [lax.ppermute(w, "core", [(0, 1), (1, 0)]) for w in mine]
     owner = slot_prompt // 32
     slots = jnp.arange(32, dtype=jnp.int32)
     away = owner != me
@@ -292,11 +293,20 @@
     states = jnp.transpose(cached_state[0].reshape(273, 224, 32), (2, 0, 1))
     states = jnp.concatenate([states, norms], axis=2)
 
-    partial = call(project_kernel, jax.ShapeDtypeStruct((4, 512, 640), BF), 1, 5)(pos, *blocks, weights)
-    partial = lax.all_to_all(partial, "col", split_axis=0, concat_axis=0, tiled=True)
-    shape = jax.ShapeDtypeStruct((512, 384), BF)
-    own, oth = call(sum_kernel, (shape, shape), 1, 1)(pos, partial)
+    held = call(order_kernel, jax.ShapeDtypeStruct((4, 256, 896), BF), 1, 4)(pos, *blocks)
+    held = lax.all_to_all(held, "col", split_axis=0, concat_axis=0, tiled=True)
+    shape = jax.ShapeDtypeStruct((512, 288), BF)
+    own, oth = call(project_kernel, (shape, shape), 1, 9, scratch_shapes=[pltpu.VMEM((512, 288), BF)])(
+        pos, held, *mine, *theirs
+    )
     rec = lax.ppermute(oth, "core", [(0, 1), (1, 0)])
+    w_out, own = lax.optimization_barrier((w_out, own))
+    pieces = []
+    for s in range(4):
+        perm = [(k * 4 + c, (c >> 1) * 4 + (s ^ (2 * (c & 1) + k))) for k in range(2) for c in range(4)]
+        pieces.append(lax.ppermute(w_out, ("core", "col"), perm))
+    pieces = jnp.stack(pieces)
+    out_w = [pieces] + [lax.ppermute(pieces, "y", [(i, (i + s) % 4) for i in range(4)]) for s in range(1, 4)]
 
     shape = jax.ShapeDtypeStruct((32, 16, 128), BF)
     q_send, q_keep = call(group_kernel, (shape, shape), 3, 3, scratch_shapes=[pltpu.VMEM((512, 128), BF)])(
@@ -318,23 +328,28 @@
         compiler_params=pltpu.CompilerParams(vmem_limit_bytes=VMEM_LIMIT),
     )(pos, owner, q_rec, q_keep, states)
     r_rec = lax.all_to_all(r_send, ("req", "col"), split_axis=0, concat_axis=0, tiled=True)
-    shape = jax.ShapeDtypeStruct((512, 256), BF)
-    same, other = call(combine_kernel, (shape, shape), 3, 5, scratch_shapes=[pltpu.VMEM((512, 512), BF)])(
+    shape = jax.ShapeDtypeStruct((4, 256, 256), BF)
+    heads = call(combine_kernel, shape, 3, 5, scratch_shapes=[pltpu.VMEM((512, 512), BF)])(
         pos, at_holder, at_slot, num, den, r_rec, r_keep, place[:, None]
     )
+    heads = lax.all_to_all(heads, "y", split_axis=0, concat_axis=0, tiled=True)
+    heads_oth = lax.ppermute(heads, "core", [(0, 1), (1, 0)])
+    shape = jax.ShapeDtypeStruct((256, 448), BF)
+    mixed = call(out_kernel, (shape, shape), 1, 6)(pos, heads, heads_oth, *out_w)
 
     def at(y, core, col):
         return (y * 2 + core) * 4 + col
 
-    chunks = []
-    for s in range(4):
-        for d, part in ((0, same), (1, other)):
-            perm = [
-                (at(j, k, b), at(b, k ^ d, (j + s) % 4)) for b in range(4) for j in range(4) for k in range(2)
-            ]
-            chunks.append(lax.ppermute(part, ("y", "core", "col"), perm))
-    out = call(out_kernel, jax.ShapeDtypeStruct((512, 448), BF), 1, 10)(pos, *chunks, w_all, tok)
-    return jnp.transpose(out.reshape(2, 256, 448), (1, 0, 2))
+    got = []
+    for s, part in enumerate(mixed):
+        perm = [
+            (at(j, k, b), at(b, j >> 1, 2 * k + (s ^ (j & 1)))) for b in range(4) for j in range(4) for k in range(2)
+        ]
+        got.append(lax.ppermute(part, ("y", "core", "col"), perm).reshape(2, 128, 448))
+    odd = col % 2 == 1
+    mixed = jnp.concatenate([jnp.where(odd, got[1], got[0]), jnp.where(odd, got[0], got[1])], axis=1)
+    mixed = jnp.transpose(mixed, (1, 0, 2)).astype(F32)
+    return (mixed + tokens.astype(F32)).astype(BF)
 
 
 def solution(mesh):

time: 209 us -> 227 us (1.086)
  waiting for transfers between devices: 40.9 us -> 58.9 us
  between operations: 13.7 us -> 0.36 us
  starting transfers between devices: 69.1 us -> 81.2 us
    ppermute x9 -> x17, waiting for transfers between devices: 22 us -> 45.8 us  [the longest x3 38.2 us: body(): lax.ppermute(pieces, 'y', [(i, (i + s) % 4) for i in range(4)])]
    ppermute x9 -> x17, starting transfers between devices: 31.7 us -> 41.1 us  [the longest x4 12.7 us: body(): theirs = [lax.ppermute(w, 'core', [(0, 1), (1, 0)]) for w in mine]]
    all_to_all x1 -> x2, waiting for transfers between devices: 7.76 us -> 3.16 us  [the longest x1 3.16 us: body(): heads = lax.all_to_all(heads, 'y', split_axis=0, concat_axis=0, tiled=True)]
    all_to_all x1 -> x2, starting transfers between devices: 3.65 us -> 8.2 us  [the longest x1 4.42 us: body(): heads = lax.all_to_all(heads, 'y', split_axis=0, concat_axis=0, tiled=True)]
    all_to_all x1, waiting for transfers between devices: 4.45 us -> 0.01 us  [body(): lax.all_to_all(r_send, ('req', 'col'), split_axis=0, concat_axis=0, tiled...]
    ppermute x3, waiting for transfers between devices: 3.13 us -> 6.25 us  [body(): lax.ppermute(tok, 'y', [(i, (i + s) % 4) for i in range(4)])]
    unnamed x46 -> x58, local copies, waits for them, and re-layouts: 26.9 us -> 29 us
  transfers between devices with their start and end apart: 18 -> 26, of which waited for: 9 -> 11; matrix products, arithmetic and copies ran while one was open for 19% -> 15% of each run, Pallas kernels for 12% -> 4%
where the time goes in v1:
time: 227 us; the launch traced here: 224 us
  starting transfers between devices  81.2 us (36%)
  waiting for transfers between devices  58.9 us (26%)
  local copies, waits for them, and re-layouts  41.5 us (18%)
  Pallas kernels  27.2 us (12%)
  other arithmetic  14.7 us (6%)
    ppermute x3, waiting for transfers between devices, body(): lax.ppermute(pieces, 'y', [(i, (i + s) % 4) for i in range(4)])  38.2 us
    unnamed x58, local copies, waits for them, and re-layouts  29 us
    ppermute x4, starting transfers between devices, body(): theirs = [lax.ppermute(w, 'core', [(0, 1), (1, 0)]) for w in mine]  12.7 us
    ppermute x4, starting transfers between devices, body(): pieces.append(lax.ppermute(w_out, ('core', 'col'), perm))  11.8 us
    all_to_all x1, starting transfers between devices, body(): lax.all_to_all(code[:, None], ('req', 'col'), split_axis=0, concat_axis=0...  11 us
    pallas_call x1, Pallas kernels, body(): pl.pallas_call(slot_kernel, grid=(4,), out_shape=(shape, shape), in_specs...  9.4 us
    all_to_all x1, starting transfers between devices, body(): lax.all_to_all(q_send, ('req', 'col'), split_axis=0, concat_axis=0, tiled...  9.05 us
    another operation x1, local copies, waits for them, and re-layouts, body(): states = jnp.transpose(cached_state[0].reshape(273, 224, 32), (2, 0, 1))  8.34 us
  transfers between devices with their start and end apart: 26, of which 11 were waited for; matrix products, arithmetic and copies ran while one was open for 15% of the time, Pallas kernels for 4%

profile of v1, /device:TPU:9, one launch (start us, length us, event | category | flops | bytes accessed | tf_op | source)
XLA Modules:
  0.0 223.9 jit_solution(5785375479927200687)
XLA Ops:
  0.0 1.3 copy.72.t0
  1.3 1.4 collective-permute-start
  2.7 0.8 collective-permute-start.1
  3.5 2.0 collective-permute-start.2
  7.6 11.0 %all-to-all-start = ((s32[32,1,1]{2,1,0:T(1,128)}), s32[32,1,1]{2,1,0:T(1,128)S(1)}, u32[]{:S(2)}, u32[]{:S(2)}) async-start(s32[32,1,1]{2,1,0:T(1,128)} %copy.68), calls=%async_computation | async-start | bytes 32768 | tf_op jit(solution)/shard_map/all_to_all | solution.py:284
  18.8 6.2 %collective-permute-done.2.t3 = bf16[256,896]{1,0:T(8,128)(2,1)S(1)} collective-permute-done((bf16[256,896]{1,0:T(8,128)(2,1)S(1)}, bf16[256,896]{1,0:T(8,128)(2,1)S(1)}, u32[]{:S(2)}, u32[]{:S(2)}) %collective-permute-start.2) | collective-permute-done | bytes 458784 | tf_op jit(solution)/shard_map/ppermute | solution.py:273
  25.7 1.2 copy-done.1
  27.2 3.8 %all-to-all-start.1 = ((bf16[4,256,896]{2,1,0:T(8,128)(2,1)}), bf16[4,256,896]{2,1,0:T(8,128)(2,1)S(1)}, u32[]{:S(2)}, u32[]{:S(2)}) async-start(bf16[4,256,896]{2,1,0:T(8,128)(2,1)} %copy-done.1), calls=%async_computation.1 | async-start | bytes 3670016 | tf_op jit(solution)/shard_map/all_to_all | solution.py:297
  32.1 1.5 collective-permute-start.3
  33.7 2.4 %collective-permute-start.4 = (bf16[448,288]{1,0:T(8,128)(2,1)S(1)}, bf16[448,288]{1,0:T(8,128)(2,1)S(1)}, u32[]{:S(2)}, u32[]{:S(2)}) collective-permute-start(bf16[448,288]{1,0:T(8,128)(2,1)S(1)} %pad_maximum_fusion.1.refs_0_), channel_id=1, source_target_pairs={{0,2},{1,3},{2,0},{3,1},{4,6},{5,7},{6,4},{7,5},{8,10},{9,11},{10,... | collective-permute-start | bytes 774152 | tf_op jit(solution)/shard_map/ppermute | solution.py:276
  36.1 1.2 collective-permute-start.5
  37.2 3.8 %collective-permute-start.6 = (bf16[448,288]{1,0:T(8,128)(2,1)S(1)}, bf16[448,288]{1,0:T(8,128)(2,1)}, u32[]{:S(2)}, u32[]{:S(2)}) collective-permute-start(bf16[448,288]{1,0:T(8,128)(2,1)S(1)} %pad_maximum_fusion.1.refs_0_), channel_id=1, source_target_pairs={{0,4},{4,0},{1,5},{5,1},{2,6},{6,2},{3,7},{7,3},{8,12},{12,8},{9,1... | collective-permute-start | bytes 774152 | tf_op jit(solution)/shard_map/ppermute | solution.py:277
  41.5 2.1 copy.79
  43.6 7.3 %copy.77 = bf16[1,273,7168]{1,2,0:T(8,128)(2,1)} copy(bf16[1,273,7168]{2,1,0:T(8,128)(2,1)} %param.17) | data formatting | bytes 7827456 | tf_op args[5]
  50.9 8.3 %copy.78 = bf16[273,224,32]{1,0,2:T(8,128)(2,1)} copy(bf16[273,224,32]{0,2,1:T(8,128)(2,1)} %bitcast.26) | data formatting | bytes 7827456 | tf_op jit(solution)/shard_map/reshape;squeeze | solution.py:293
  60.2 5.2 %collective-permute-start.7 = (bf16[448,288]{1,0:T(8,128)(2,1)S(1)}, bf16[448,288]{1,0:T(8,128)(2,1)S(1)}, u32[]{:S(2)}, u32[]{:S(2)}) collective-permute-start(bf16[448,288]{1,0:T(8,128)(2,1)S(1)} %collective-permute-done.3.refs_1_), channel_id=1, source_target_pairs={{0,4},{4,0},{1,5},{5,1},{2,6},{6,2},{3,7},{7,3},{8,12},{12,8},{9,1... | collective-permute-start | bytes 774152 | tf_op jit(solution)/shard_map/ppermute | solution.py:277
  65.4 1.2 collective-permute-done.4.refs_2_
  66.6 3.6 %collective-permute-start.8 = (bf16[448,288]{1,0:T(8,128)(2,1)S(1)}, bf16[448,288]{1,0:T(8,128)(2,1)S(1)}, u32[]{:S(2)}, u32[]{:S(2)}) collective-permute-start(bf16[448,288]{1,0:T(8,128)(2,1)S(1)} %collective-permute-done.4.refs_2_), channel_id=1, source_target_pairs={{0,4},{4,0},{1,5},{5,1},{2,6},{6,2},{3,7},{7,3},{8,12},{12,8},{9,1... | collective-permute-start | bytes 774152 | tf_op jit(solution)/shard_map/ppermute | solution.py:277
  70.3 0.7 copy-done.11
  71.7 0.7 copy-done.13
  72.4 0.7 copy-done.15
  73.1 0.7 copy-done.17
  73.9 1.0 copy-done.12
  74.9 1.0 copy-done.14
  75.8 1.0 copy-done.16
  76.8 1.0 copy-done.18
  77.8 3.3 %shard_map.119 = (bf16[512,288]{1,0:T(8,128)(2,1)S(1)}, bf16[512,288]{1,0:T(8,128)(2,1)S(1)}) custom-call(s32[4]{0:T(128)S(1)} %pad_add_fusion.pos_ref, bf16[4,256,896]{2,1,0:T(8,128)(2,1)S(1)} %all-to-all-done.1.t_ref, bf16[448,288]{1,0:T(8,128)(2,1)S(1)} %pad_maximum_fusion.1.refs_0_, bf16[448,288]{1,0:T(8,128)(2,1)S(1)} %collective-permute-done.3.refs_1_, ...), custom_call_target="tpu_custom_call" | custom-call | tf_op jit(solution)/shard_map/pallas_call | solution.py:299
  81.9 1.2 collective-permute-done.10.rec_ref
  83.1 2.1 shard_map.121
  85.2 9.0 %all-to-all-start.2 = ((bf16[32,16,128]{2,1,0:T(8,128)(2,1)}), bf16[32,16,128]{2,1,0:T(8,128)(2,1)S(1)}, u32[]{:S(2)}, u32[]{:S(2)}) async-start(bf16[32,16,128]{2,1,0:T(8,128)(2,1)} %get-tuple-element.22), calls=%async_computation.2 | async-start | bytes 262144 | tf_op jit(solution)/shard_map/all_to_all | solution.py:315
  94.3 7.6 %maximum_maximum_fusion.state_ref = bf16[32,273,256]{2,1,0:T(8,128)(2,1)} fusion(bf16[32,273,2]{2,1,0:T(8,128)(2,1)} %copy.79, bf16[32,273,224]{2,1,0:T(8,128)(2,1)} %bitcast.27, bf16[256]{0:T(256)(128)(2,1)S(1)} %pad.9.clone), kind=kLoop, calls=%fused_computation | loop fusion | flops 17891328 | bytes 8422016 | tf_op jit(solution)/shard_map/concatenate | solution.py:294
  101.9 2.2 all-to-all-done.2.rec_ref
  104.1 2.3 %copy-done = bf16[32,273,256]{2,1,0:T(8,128)(2,1)S(1)} copy-done((bf16[32,273,256]{2,1,0:T(8,128)(2,1)S(1)}, bf16[32,273,256]{2,1,0:T(8,128)(2,1)}, u32[]{:S(2)}) %copy-start) | copy-done | bytes 4472856
  106.4 9.4 %shard_map.122 = (bf16[32,16,512]{2,1,0:T(8,128)(2,1)S(1)}, bf16[32,16,512]{2,1,0:T(8,128)(2,1)S(1)}) custom-call(s32[4]{0:T(128)S(1)} %pad_add_fusion.pos_ref, s32[32]{0:T(128)S(1)} %get-tuple-element.30.owner_ref, bf16[32,16,128]{2,1,0:T(8,128)(2,1)S(1)} %all-to-all-done.2.rec_ref, bf16[32,16,128]{2,1,0:T(8,128)(2,1)S(1)} %get-tuple-element.23.keep_ref, ...), custom_call_target="tpu_custom_call" | custom-call | tf_op jit(solution)/shard_map/pallas_call | solution.py:321
  115.8 0.8 copy-done.8
  116.6 0.8 copy-done.10
  117.4 7.0 %all-to-all-start.3 = ((bf16[32,16,512]{2,1,0:T(8,128)(2,1)}), bf16[32,16,512]{2,1,0:T(8,128)(2,1)S(1)}, u32[]{:S(2)}, u32[]{:S(2)}) async-start(bf16[32,16,512]{2,1,0:T(8,128)(2,1)} %copy-done.10), calls=%async_computation.3 | async-start | bytes 1048576 | tf_op jit(solution)/shard_map/all_to_all | solution.py:330
  124.5 5.8 %collective-permute-start.15 = (bf16[224,448]{1,0:T(8,128)(2,1)}, bf16[224,448]{1,0:T(8,128)(2,1)}, u32[]{:S(2)}, u32[]{:S(2)}) collective-permute-start(bf16[224,448]{1,0:T(8,128)(2,1)} %param.16), channel_id=1, source_target_pairs={{0,3},{1,1},{2,7},{3,5},{4,2},{5,0},{6,6},{7,4},{8,11},{9,9},{10,1... | collective-permute-start | bytes 602120 | tf_op jit(solution)/shard_map/ppermute | solution.py:307
  130.8 5.5 %collective-permute-start.12 = (bf16[224,448]{1,0:T(8,128)(2,1)}, bf16[224,448]{1,0:T(8,128)(2,1)}, u32[]{:S(2)}, u32[]{:S(2)}) collective-permute-start(bf16[224,448]{1,0:T(8,128)(2,1)} %param.16), channel_id=1, source_target_pairs={{0,0},{1,2},{2,4},{3,6},{4,1},{5,3},{6,5},{7,7},{8,8},{9,10},{10,1... | collective-permute-start | bytes 602120 | tf_op jit(solution)/shard_map/ppermute | solution.py:307
  136.3 0.9 copy.76.len_ref
  137.3 0.9 copy-done.7
  138.3 0.9 copy-done.19
  139.2 5.9 %shard_map.120 = (f32[2,512,256]{2,1,0:T(8,128)S(1)}, f32[2,512,256]{2,1,0:T(8,128)S(1)}) custom-call(s32[4]{0:T(128)S(1)} %pad_add_fusion.pos_ref, bf16[512,288]{1,0:T(8,128)(2,1)S(1)} %get-tuple-element.18.own_ref, bf16[512,288]{1,0:T(8,128)(2,1)S(1)} %collective-permute-done.10.rec_ref, bf16[512,256]{1,0:T(8,128)(2,1)S(1)} %copy-done.19, ...), custom_call_target="tpu_custom_call" | custom-call | tf_op jit(solution)/shard_map/pallas_call | solution.py:317
  145.1 1.0 copy-done.3
  146.1 1.0 copy-done.5
  147.1 1.2 copy-done.4
  148.3 1.2 copy-done.6
  149.5 1.0 copy-done.9
  150.6 2.6 %shard_map.123 = bf16[4,256,256]{2,1,0:T(8,128)(2,1)} custom-call(s32[4]{0:T(128)S(1)} %pad_add_fusion.pos_ref, s32[32]{0:T(128)S(1)} %broadcast_select_fusion.2.g_ref, s32[32]{0:T(128)S(1)} %fusion.2.s_ref, f32[2,512,256]{2,1,0:T(8,128)S(1)} %copy-done.4, f32[2,512,256]{2,1,0:T(8,128)S(1)} %copy-done.6, bf16[32,16,512]{2,1,0:T(8,128)(2,1)S(1)} %all-to-all-done.3.rec_ref, ...), custom_call_target="tpu_custom_call" | custom-call | tf_op jit(solution)/shard_map/pallas_call | solution.py:332
  153.1 4.4 %all-to-all-start.4 = ((bf16[4,256,256]{2,1,0:T(8,128)(2,1)}), bf16[4,256,256]{2,1,0:T(8,128)(2,1)S(1)}, u32[]{:S(2)}, u32[]{:S(2)}) async-start(bf16[4,256,256]{2,1,0:T(8,128)(2,1)} %shard_map.123), calls=%async_computation.4 | async-start | bytes 1048576 | tf_op jit(solution)/shard_map/all_to_all | solution.py:335
  157.6 1.4 pad_maximum_fusion.w0
  159.0 1.3 collective-permute-start.16
  161.0 2.0 collective-permute-start.18
  162.9 3.2 %all-to-all-done.4.own_ref = bf16[4,256,256]{2,1,0:T(8,128)(2,1)S(1)} async-done(((bf16[4,256,256]{2,1,0:T(8,128)(2,1)}), bf16[4,256,256]{2,1,0:T(8,128)(2,1)S(1)}, u32[]{:S(2)}, u32[]{:S(2)}) %all-to-all-start.4) | async-done | bytes 524320 | tf_op jit(solution)/shard_map/all_to_all | solution.py:335
  166.1 1.1 collective-permute-start.11
  167.3 16.9 %collective-permute-done.16.w1 = bf16[4,224,448]{2,1,0:T(8,128)(2,1)S(1)} collective-permute-done((bf16[4,224,448]{2,1,0:T(8,128)(2,1)S(1)}, bf16[4,224,448]{2,1,0:T(8,128)(2,1)S(1)}, u32[]{:S(2)}, u32[]{:S(2)}) %collective-permute-start.16) | collective-permute-done | bytes 802848 | tf_op jit(solution)/shard_map/ppermute | solution.py:309
  184.2 1.6 collective-permute-done.17.w2
  185.8 19.7 %collective-permute-done.18.w3 = bf16[4,224,448]{2,1,0:T(8,128)(2,1)} collective-permute-done((bf16[4,224,448]{2,1,0:T(8,128)(2,1)S(1)}, bf16[4,224,448]{2,1,0:T(8,128)(2,1)}, u32[]{:S(2)}, u32[]{:S(2)}) %collective-permute-start.18) | collective-permute-done | bytes 802848 | tf_op jit(solution)/shard_map/ppermute | solution.py:309
  205.5 3.2 %shard_map.124 = (bf16[256,448]{1,0:T(8,128)(2,1)}, bf16[256,448]{1,0:T(8,128)(2,1)}) custom-call(s32[4]{0:T(128)S(1)} %pad_add_fusion.pos_ref, bf16[4,256,256]{2,1,0:T(8,128)(2,1)S(1)} %all-to-all-done.4.own_ref, bf16[4,256,256]{2,1,0:T(8,128)(2,1)S(1)} %collective-permute-done.11.oth_ref, bf16[4,224,448]{2,1,0:T(8,128)(2,1)S(1)} %pad_maximum_fusion.w0, ...), custom_call_target="tpu_custom_call" | custom-call | tf_op jit(solution)/shard_map/pallas_call | solution.py:338
  208.7 0.7 collective-permute-start.19
  209.4 5.7 %collective-permute-start.20 = (bf16[256,448]{1,0:T(8,128)(2,1)}, bf16[256,448]{1,0:T(8,128)(2,1)S(1)}, u32[]{:S(2)}, u32[]{:S(2)}) collective-permute-start(bf16[256,448]{1,0:T(8,128)(2,1)} %get-tuple-element.28), channel_id=1, source_target_pairs={{0,0},{4,2},{8,1},{12,3},{16,4},{20,6},{24,5},{28,7},{1,8},{5,10},... | collective-permute-start | bytes 688136 | tf_op jit(solution)/shard_map/ppermute | solution.py:348
  215.2 4.7 %collective-permute-done.19 = bf16[256,448]{1,0:T(8,128)(2,1)S(1)} collective-permute-done((bf16[256,448]{1,0:T(8,128)(2,1)}, bf16[256,448]{1,0:T(8,128)(2,1)S(1)}, u32[]{:S(2)}, u32[]{:S(2)}) %collective-permute-start.19) | collective-permute-done | bytes 229408 | tf_op jit(solution)/shard_map/ppermute | solution.py:348
  219.9 1.7 collective-permute-done.20
  221.9 1.9 fusion.1
  (84 shorter events, 8.8 us)
Async XLA Ops:
  0.0 31.0 %copy-start.22 = (bf16[448,32]{0,1:T(8,128)(2,1)S(1)}, bf16[448,32]{0,1:T(8,128)(2,1)}, u32[]{:S(2)}) copy-start(bf16[448,32]{0,1:T(8,128)(2,1)} %param.14) | copy-start | bytes 86020
  0.0 31.1 %copy-start.23 = (bf16[448,32]{0,1:T(8,128)(2,1)S(1)}, bf16[448,32]{0,1:T(8,128)(2,1)}, u32[]{:S(2)}) copy-start(bf16[448,32]{0,1:T(8,128)(2,1)} %param.13) | copy-start | bytes 86020
  0.0 31.3 %copy-start.20 = (bf16[2,50176]{1,0:T(2,128)(2,1)S(1)}, bf16[2,50176]{1,0:T(2,128)(2,1)}, u32[]{:S(2)}) copy-start(bf16[2,50176]{1,0:T(2,128)(2,1)} %param.15) | copy-start | bytes 602116
  1.3 17.5 %collective-permute-start = (bf16[256,896]{1,0:T(8,128)(2,1)S(1)}, bf16[256,896]{1,0:T(8,128)(2,1)S(1)}, u32[]{:S(2)}, u32[]{:S(2)}) collective-permute-start(bf16[256,896]{1,0:T(8,128)(2,1)S(1)} %copy.72.t0), channel_id=1, source_target_pairs={{0,8},{8,16},{16,24},{24,0},{1,9},{9,17},{17,25},{25,1},{2,10},{10... | collective-permute-start | bytes 1376264 | tf_op jit(solution)/shard_map/ppermute | solution.py:273
  2.7 16.1 %collective-permute-start.1 = (bf16[256,896]{1,0:T(8,128)(2,1)S(1)}, bf16[256,896]{1,0:T(8,128)(2,1)S(1)}, u32[]{:S(2)}, u32[]{:S(2)}) collective-permute-start(bf16[256,896]{1,0:T(8,128)(2,1)S(1)} %copy.72.t0), channel_id=1, source_target_pairs={{0,16},{8,24},{16,0},{24,8},{1,17},{9,25},{17,1},{25,9},{2,18},{10... | collective-permute-start | bytes 1376264 | tf_op jit(solution)/shard_map/ppermute | solution.py:273
  3.5 21.5 %collective-permute-start.2 = (bf16[256,896]{1,0:T(8,128)(2,1)S(1)}, bf16[256,896]{1,0:T(8,128)(2,1)S(1)}, u32[]{:S(2)}, u32[]{:S(2)}) collective-permute-start(bf16[256,896]{1,0:T(8,128)(2,1)S(1)} %copy.72.t0), channel_id=1, source_target_pairs={{0,24},{8,0},{16,8},{24,16},{1,25},{9,1},{17,9},{25,17},{2,26},{10... | collective-permute-start | bytes 1376264 | tf_op jit(solution)/shard_map/ppermute | solution.py:273
  7.6 19.6 %all-to-all-start = ((s32[32,1,1]{2,1,0:T(1,128)}), s32[32,1,1]{2,1,0:T(1,128)S(1)}, u32[]{:S(2)}, u32[]{:S(2)}) async-start(s32[32,1,1]{2,1,0:T(1,128)} %copy.68), calls=%async_computation | async-start | bytes 32768 | tf_op jit(solution)/shard_map/all_to_all | solution.py:284
  18.8 22.3 %copy-start.24 = (s32[512]{0:T(512)S(1)}, s32[512]{0:T(512)}, u32[]{:S(2)}) copy-start(s32[512]{0:T(512)} %param.20) | copy-start | bytes 6148
  18.8 22.6 %copy-start.26 = (s32[32]{0:T(128)S(1)}, s32[32]{0:T(128)}, u32[]{:S(2)}) copy-start(s32[32]{0:T(128)} %param.19) | copy-start | bytes 388
  18.8 22.8 %copy-start.21 = (bf16[32,273,2]{1,2,0:T(2,128)(2,1)S(1)}, bf16[32,273,2]{1,2,0:T(2,128)(2,1)}, u32[]{:S(2)}) copy-start(bf16[32,273,2]{1,2,0:T(2,128)(2,1)} %param.18) | copy-start | bytes 104836
  25.7 1.2 copy-start.1
  27.2 46.7 %all-to-all-start.1 = ((bf16[4,256,896]{2,1,0:T(8,128)(2,1)}), bf16[4,256,896]{2,1,0:T(8,128)(2,1)S(1)}, u32[]{:S(2)}, u32[]{:S(2)}) async-start(bf16[4,256,896]{2,1,0:T(8,128)(2,1)} %copy-done.1), calls=%async_computation.1 | async-start | bytes 3670016 | tf_op jit(solution)/shard_map/all_to_all | solution.py:297
  32.1 28.1 %collective-permute-start.3 = (bf16[448,288]{1,0:T(8,128)(2,1)S(1)}, bf16[448,288]{1,0:T(8,128)(2,1)S(1)}, u32[]{:S(2)}, u32[]{:S(2)}) collective-permute-start(bf16[448,288]{1,0:T(8,128)(2,1)S(1)} %pad_maximum_fusion.1.refs_0_), channel_id=1, source_target_pairs={{0,1},{1,2},{2,3},{3,0},{4,5},{5,6},{6,7},{7,4},{8,9},{9,10},{10,1... | collective-permute-start | bytes 774152 | tf_op jit(solution)/shard_map/ppermute | solution.py:276
  33.7 32.9 %collective-permute-start.4 = (bf16[448,288]{1,0:T(8,128)(2,1)S(1)}, bf16[448,288]{1,0:T(8,128)(2,1)S(1)}, u32[]{:S(2)}, u32[]{:S(2)}) collective-permute-start(bf16[448,288]{1,0:T(8,128)(2,1)S(1)} %pad_maximum_fusion.1.refs_0_), channel_id=1, source_target_pairs={{0,2},{1,3},{2,0},{3,1},{4,6},{5,7},{6,4},{7,5},{8,10},{9,11},{10,... | collective-permute-start | bytes 774152 | tf_op jit(solution)/shard_map/ppermute | solution.py:276
  36.1 34.2 %collective-permute-start.5 = (bf16[448,288]{1,0:T(8,128)(2,1)S(1)}, bf16[448,288]{1,0:T(8,128)(2,1)S(1)}, u32[]{:S(2)}, u32[]{:S(2)}) collective-permute-start(bf16[448,288]{1,0:T(8,128)(2,1)S(1)} %pad_maximum_fusion.1.refs_0_), channel_id=1, source_target_pairs={{0,3},{1,0},{2,1},{3,2},{4,7},{5,4},{6,5},{7,6},{8,11},{9,8},{10,9... | collective-permute-start | bytes 774152 | tf_op jit(solution)/shard_map/ppermute | solution.py:276
  37.2 34.4 %collective-permute-start.6 = (bf16[448,288]{1,0:T(8,128)(2,1)S(1)}, bf16[448,288]{1,0:T(8,128)(2,1)}, u32[]{:S(2)}, u32[]{:S(2)}) collective-permute-start(bf16[448,288]{1,0:T(8,128)(2,1)S(1)} %pad_maximum_fusion.1.refs_0_), channel_id=1, source_target_pairs={{0,4},{4,0},{1,5},{5,1},{2,6},{6,2},{3,7},{7,3},{8,12},{12,8},{9,1... | collective-permute-start | bytes 774152 | tf_op jit(solution)/shard_map/ppermute | solution.py:277
  60.2 11.5 %collective-permute-start.7 = (bf16[448,288]{1,0:T(8,128)(2,1)S(1)}, bf16[448,288]{1,0:T(8,128)(2,1)S(1)}, u32[]{:S(2)}, u32[]{:S(2)}) collective-permute-start(bf16[448,288]{1,0:T(8,128)(2,1)S(1)} %collective-permute-done.3.refs_1_), channel_id=1, source_target_pairs={{0,4},{4,0},{1,5},{5,1},{2,6},{6,2},{3,7},{7,3},{8,12},{12,8},{9,1... | collective-permute-start | bytes 774152 | tf_op jit(solution)/shard_map/ppermute | solution.py:277
  66.6 5.8 %collective-permute-start.8 = (bf16[448,288]{1,0:T(8,128)(2,1)S(1)}, bf16[448,288]{1,0:T(8,128)(2,1)S(1)}, u32[]{:S(2)}, u32[]{:S(2)}) collective-permute-start(bf16[448,288]{1,0:T(8,128)(2,1)S(1)} %collective-permute-done.4.refs_2_), channel_id=1, source_target_pairs={{0,4},{4,0},{1,5},{5,1},{2,6},{6,2},{3,7},{7,3},{8,12},{12,8},{9,1... | collective-permute-start | bytes 774152 | tf_op jit(solution)/shard_map/ppermute | solution.py:277
  70.2 2.9 %collective-permute-start.9 = (bf16[448,288]{1,0:T(8,128)(2,1)S(1)}, bf16[448,288]{1,0:T(8,128)(2,1)S(1)}, u32[]{:S(2)}, u32[]{:S(2)}) collective-permute-start(bf16[448,288]{1,0:T(8,128)(2,1)S(1)} %collective-permute-done.5.refs_3_), channel_id=1, source_target_pairs={{0,4},{4,0},{1,5},{5,1},{2,6},{6,2},{3,7},{7,3},{8,12},{12,8},{9,1... | collective-permute-start | bytes 774152 | tf_op jit(solution)/shard_map/ppermute | solution.py:277
  70.3 0.7 copy-start.11
  71.7 0.7 copy-start.13
  72.4 0.7 copy-start.15
  73.1 0.7 copy-start.17
  73.9 1.0 copy-start.12
  74.9 1.0 copy-start.14
  75.8 1.0 copy-start.16
  76.8 1.0 copy-start.18
  81.2 1.9 collective-permute-start.10
  85.2 18.9 %all-to-all-start.2 = ((bf16[32,16,128]{2,1,0:T(8,128)(2,1)}), bf16[32,16,128]{2,1,0:T(8,128)(2,1)S(1)}, u32[]{:S(2)}, u32[]{:S(2)}) async-start(bf16[32,16,128]{2,1,0:T(8,128)(2,1)} %get-tuple-element.22), calls=%async_computation.2 | async-start | bytes 262144 | tf_op jit(solution)/shard_map/all_to_all | solution.py:315
  94.2 42.0 %copy-start.25 = (s32[512]{0:T(512)S(1)}, s32[512]{0:T(512)}, u32[]{:S(2)}) copy-start(s32[512]{0:T(512)} %param.23) | copy-start | bytes 6148
  94.3 43.0 %copy-start.2 = (bf16[512,1792]{1,0:T(8,128)(2,1)S(1)}, bf16[512,1792]{1,0:T(8,128)(2,1)}, u32[]{:S(2)}) copy-start(bf16[512,1792]{1,0:T(8,128)(2,1)} %tv_ref.1) | copy-start | bytes 5505028
  104.1 2.3 %copy-start = (bf16[32,273,256]{2,1,0:T(8,128)(2,1)S(1)}, bf16[32,273,256]{2,1,0:T(8,128)(2,1)}, u32[]{:S(2)}) copy-start(bf16[32,273,256]{2,1,0:T(8,128)(2,1)} %maximum_maximum_fusion.state_ref) | copy-start | bytes 13418500
  115.8 0.8 copy-start.8
  116.6 0.8 copy-start.10
  117.4 29.7 %all-to-all-start.3 = ((bf16[32,16,512]{2,1,0:T(8,128)(2,1)}), bf16[32,16,512]{2,1,0:T(8,128)(2,1)S(1)}, u32[]{:S(2)}, u32[]{:S(2)}) async-start(bf16[32,16,512]{2,1,0:T(8,128)(2,1)} %copy-done.10), calls=%async_computation.3 | async-start | bytes 1048576 | tf_op jit(solution)/shard_map/all_to_all | solution.py:330
  124.5 33.1 %collective-permute-start.15 = (bf16[224,448]{1,0:T(8,128)(2,1)}, bf16[224,448]{1,0:T(8,128)(2,1)}, u32[]{:S(2)}, u32[]{:S(2)}) collective-permute-start(bf16[224,448]{1,0:T(8,128)(2,1)} %param.16), channel_id=1, source_target_pairs={{0,3},{1,1},{2,7},{3,5},{4,2},{5,0},{6,6},{7,4},{8,11},{9,9},{10,1... | collective-permute-start | bytes 602120 | tf_op jit(solution)/shard_map/ppermute | solution.py:307
  130.2 27.3 %collective-permute-start.14 = (bf16[224,448]{1,0:T(8,128)(2,1)}, bf16[224,448]{1,0:T(8,128)(2,1)}, u32[]{:S(2)}, u32[]{:S(2)}) collective-permute-start(bf16[224,448]{1,0:T(8,128)(2,1)} %param.16), channel_id=1, source_target_pairs={{0,2},{1,0},{2,6},{3,4},{4,3},{5,1},{6,7},{7,5},{8,10},{9,8},{10,1... | collective-permute-start | bytes 602120 | tf_op jit(solution)/shard_map/ppermute | solution.py:307
  130.4 27.2 %collective-permute-start.13 = (bf16[224,448]{1,0:T(8,128)(2,1)}, bf16[224,448]{1,0:T(8,128)(2,1)}, u32[]{:S(2)}, u32[]{:S(2)}) collective-permute-start(bf16[224,448]{1,0:T(8,128)(2,1)} %param.16), channel_id=1, source_target_pairs={{0,1},{1,3},{2,5},{3,7},{4,0},{5,2},{6,4},{7,6},{8,9},{9,11},{10,1... | collective-permute-start | bytes 602120 | tf_op jit(solution)/shard_map/ppermute | solution.py:307
  130.8 26.8 %collective-permute-start.12 = (bf16[224,448]{1,0:T(8,128)(2,1)}, bf16[224,448]{1,0:T(8,128)(2,1)}, u32[]{:S(2)}, u32[]{:S(2)}) collective-permute-start(bf16[224,448]{1,0:T(8,128)(2,1)} %param.16), channel_id=1, source_target_pairs={{0,0},{1,2},{2,4},{3,6},{4,1},{5,3},{6,5},{7,7},{8,8},{9,10},{10,1... | collective-permute-start | bytes 602120 | tf_op jit(solution)/shard_map/ppermute | solution.py:307
  137.3 1.0 copy-start.7
  138.3 0.9 copy-start.19
  145.1 1.0 copy-start.3
  146.1 1.0 copy-start.5
  147.1 1.2 copy-start.4
  148.3 1.2 copy-start.6
  149.5 1.0 copy-start.9
  153.1 13.0 %all-to-all-start.4 = ((bf16[4,256,256]{2,1,0:T(8,128)(2,1)}), bf16[4,256,256]{2,1,0:T(8,128)(2,1)S(1)}, u32[]{:S(2)}, u32[]{:S(2)}) async-start(bf16[4,256,256]{2,1,0:T(8,128)(2,1)} %shard_map.123), calls=%async_computation.4 | async-start | bytes 1048576 | tf_op jit(solution)/shard_map/all_to_all | solution.py:335
  159.0 25.2 %collective-permute-start.16 = (bf16[4,224,448]{2,1,0:T(8,128)(2,1)S(1)}, bf16[4,224,448]{2,1,0:T(8,128)(2,1)S(1)}, u32[]{:S(2)}, u32[]{:S(2)}) collective-permute-start(bf16[4,224,448]{2,1,0:T(8,128)(2,1)S(1)} %pad_maximum_fusion.w0), channel_id=1, source_target_pairs={{0,8},{8,16},{16,24},{24,0},{1,9},{9,17},{17,25},{25,1},{2,10},{10... | collective-permute-start | bytes 2408456 | tf_op jit(solution)/shard_map/ppermute | solution.py:309
  160.3 25.5 %collective-permute-start.17 = (bf16[4,224,448]{2,1,0:T(8,128)(2,1)S(1)}, bf16[4,224,448]{2,1,0:T(8,128)(2,1)S(1)}, u32[]{:S(2)}, u32[]{:S(2)}) collective-permute-start(bf16[4,224,448]{2,1,0:T(8,128)(2,1)S(1)} %pad_maximum_fusion.w0), channel_id=1, source_target_pairs={{0,16},{8,24},{16,0},{24,8},{1,17},{9,25},{17,1},{25,9},{2,18},{10... | collective-permute-start | bytes 2408456 | tf_op jit(solution)/shard_map/ppermute | solution.py:309
  161.0 44.5 %collective-permute-start.18 = (bf16[4,224,448]{2,1,0:T(8,128)(2,1)S(1)}, bf16[4,224,448]{2,1,0:T(8,128)(2,1)}, u32[]{:S(2)}, u32[]{:S(2)}) collective-permute-start(bf16[4,224,448]{2,1,0:T(8,128)(2,1)S(1)} %pad_maximum_fusion.w0), channel_id=1, source_target_pairs={{0,24},{8,0},{16,8},{24,16},{1,25},{9,1},{17,9},{25,17},{2,26},{10... | collective-permute-start | bytes 2408456 | tf_op jit(solution)/shard_map/ppermute | solution.py:309
  166.1 39.4 %collective-permute-start.11 = (bf16[4,256,256]{2,1,0:T(8,128)(2,1)S(1)}, bf16[4,256,256]{2,1,0:T(8,128)(2,1)S(1)}, u32[]{:S(2)}, u32[]{:S(2)}) collective-permute-start(bf16[4,256,256]{2,1,0:T(8,128)(2,1)S(1)} %all-to-all-done.4.own_ref), channel_id=1, source_target_pairs={{0,4},{4,0},{1,5},{5,1},{2,6},{6,2},{3,7},{7,3},{8,12},{12,8},{9,1... | collective-permute-start | bytes 1572872 | tf_op jit(solution)/shard_map/ppermute | solution.py:336
  208.7 11.2 %collective-permute-start.19 = (bf16[256,448]{1,0:T(8,128)(2,1)}, bf16[256,448]{1,0:T(8,128)(2,1)S(1)}, u32[]{:S(2)}, u32[]{:S(2)}) collective-permute-start(bf16[256,448]{1,0:T(8,128)(2,1)} %get-tuple-element.27), channel_id=1, source_target_pairs={{0,1},{4,3},{8,0},{12,2},{16,5},{20,7},{24,4},{28,6},{1,9},{5,11},... | collective-permute-start | bytes 688136 | tf_op jit(solution)/shard_map/ppermute | solution.py:348
  209.4 12.2 %collective-permute-start.20 = (bf16[256,448]{1,0:T(8,128)(2,1)}, bf16[256,448]{1,0:T(8,128)(2,1)S(1)}, u32[]{:S(2)}, u32[]{:S(2)}) collective-permute-start(bf16[256,448]{1,0:T(8,128)(2,1)} %get-tuple-element.28), channel_id=1, source_target_pairs={{0,0},{4,2},{8,1},{12,3},{16,4},{20,6},{24,5},{28,7},{1,8},{5,10},... | collective-permute-start | bytes 688136 | tf_op jit(solution)/shard_map/ppermute | solution.py:348

commit v2 on v1

--- a/solution.py
+++ b/solution.py
@@ -10,7 +10,6 @@
 BF = jnp.bfloat16
 F32 = jnp.float32
 VMEM_LIMIT = 48 * 1024 * 1024
-VM = pl.BlockSpec(memory_space=pltpu.VMEM)
 SM = pl.BlockSpec(memory_space=pltpu.SMEM)
 
 
@@ -31,15 +30,20 @@
     return high, (x - high.astype(F32)).astype(BF)
 
 
-def call(kernel, out_shapes, n_smem, n_vmem, **kw):
+def call(kernel, out_shapes, n_smem, *args, scratch=()):
+    def full(shape):
+        zeros = (0,) * len(shape)
+        return pl.BlockSpec(shape, lambda i: zeros)
+
     return pl.pallas_call(
         kernel,
+        grid=(1,),
         out_shape=out_shapes,
-        in_specs=[SM] * n_smem + [VM] * n_vmem,
-        out_specs=jax.tree.map(lambda _: VM, out_shapes),
+        in_specs=[SM] * n_smem + [full(x.shape) for x in args[n_smem:]],
+        out_specs=jax.tree.map(lambda x: full(x.shape), out_shapes),
+        scratch_shapes=scratch,
         compiler_params=pltpu.CompilerParams(vmem_limit_bytes=VMEM_LIMIT),
-        **kw,
-    )
+    )(*args)
 
 
 def order_kernel(pos_ref, t0, t1, t2, t3, out_ref):
@@ -269,12 +273,24 @@
     y, core, col = lax.axis_index("y"), lax.axis_index("core"), lax.axis_index("col")
     me = lax.axis_index(("req", "col"))
     pos = jnp.stack([y, core, me, col]).astype(jnp.int32)
+    def shifts(x, axis):
+        return [x] + [lax.ppermute(x, axis, [(i, (i + s) % 4) for i in range(4)]) for s in range(1, 4)]
+
     tok = tokens.reshape(256, 896)
-    blocks = [tok] + [lax.ppermute(tok, "y", [(i, (i + s) % 4) for i in range(4)]) for s in range(1, 4)]
+    blocks = shifts(tok, "y")
     value_w = jnp.moveaxis(w_value.reshape(2, 448, 112), 0, 1).reshape(448, 224)
-    mine = jnp.concatenate([value_w, w_query, w_key], axis=1)
-    mine = [mine] + [lax.ppermute(mine, "col", [(i, (i + s) % 4) for i in range(4)]) for s in range(1, 4)]
-    theirs = [lax.ppermute(w, "core", [(0, 1), (1, 0)]) for w in mine]
+    mine = shifts(jnp.concatenate([value_w, w_query, w_key], axis=1), "col")
+    pieces = []
+    for s in range(4):
+        perm = [(k * 4 + c, (c >> 1) * 4 + (s ^ (2 * (c & 1) + k))) for k in range(2) for c in range(4)]
+        pieces.append(lax.ppermute(w_out, ("core", "col"), perm))
+    blocks, mine, pieces = lax.optimization_barrier((blocks, mine, pieces))
+    pieces = jnp.stack(pieces)
+
+    def later(x, step):
+        x, held_back = lax.optimization_barrier((x, pieces))
+        return x, lax.ppermute(held_back, "y", [(i, (i + step) % 4) for i in range(4)])
+
     owner = slot_prompt // 32
     slots = jnp.arange(32, dtype=jnp.int32)
     away = owner != me
@@ -293,28 +309,33 @@
     states = jnp.transpose(cached_state[0].reshape(273, 224, 32), (2, 0, 1))
     states = jnp.concatenate([states, norms], axis=2)
 
-    held = call(order_kernel, jax.ShapeDtypeStruct((4, 256, 896), BF), 1, 4)(pos, *blocks)
+    held = call(order_kernel, jax.ShapeDtypeStruct((4, 256, 896), BF), 1, pos, *blocks)
+    held, out_w1 = later(held, 1)
+    theirs = [lax.ppermute(w, "core", [(0, 1), (1, 0)]) for w in mine]
     held = lax.all_to_all(held, "col", split_axis=0, concat_axis=0, tiled=True)
+    held, out_w1 = lax.optimization_barrier((held, out_w1))
     shape = jax.ShapeDtypeStruct((512, 288), BF)
-    own, oth = call(project_kernel, (shape, shape), 1, 9, scratch_shapes=[pltpu.VMEM((512, 288), BF)])(
-        pos, held, *mine, *theirs
-    )
+    own, oth = call(project_kernel, (shape, shape), 1, pos, held, *mine, *theirs, scratch=[pltpu.VMEM((512, 288), BF)])
+    oth, out_w2 = later(oth, 2)
     rec = lax.ppermute(oth, "core", [(0, 1), (1, 0)])
-    w_out, own = lax.optimization_barrier((w_out, own))
-    pieces = []
-    for s in range(4):
-        perm = [(k * 4 + c, (c >> 1) * 4 + (s ^ (2 * (c & 1) + k))) for k in range(2) for c in range(4)]
-        pieces.append(lax.ppermute(w_out, ("core", "col"), perm))
-    pieces = jnp.stack(pieces)
-    out_w = [pieces] + [lax.ppermute(pieces, "y", [(i, (i + s) % 4) for i in range(4)]) for s in range(1, 4)]
 
     shape = jax.ShapeDtypeStruct((32, 16, 128), BF)
-    q_send, q_keep = call(group_kernel, (shape, shape), 3, 3, scratch_shapes=[pltpu.VMEM((512, 128), BF)])(
-        pos, at_holder, at_slot, own, rec, place.reshape(2, 1, 256)
+    q_send, q_keep = call(
+        group_kernel,
+        (shape, shape),
+        3,
+        pos,
+        at_holder,
+        at_slot,
+        own,
+        rec,
+        place.reshape(2, 1, 256),
+        scratch=[pltpu.VMEM((512, 128), BF)],
     )
     q_rec = lax.all_to_all(q_send, ("req", "col"), split_axis=0, concat_axis=0, tiled=True)
+    q_rec, out_w2 = lax.optimization_barrier((q_rec, out_w2))
     shape = jax.ShapeDtypeStruct((2, 512, 256), F32)
-    num, den = call(tail_kernel, (shape, shape), 1, 5)(pos, own, rec, tail_keys, tail_values, tail_length[:, None])
+    num, den = call(tail_kernel, (shape, shape), 1, pos, own, rec, tail_keys, tail_values, tail_length[:, None])
     shape = jax.ShapeDtypeStruct((32, 16, 512), BF)
     whole = pl.BlockSpec((32, 16, 128), lambda i: (0, 0, 0))
     whole_out = pl.BlockSpec((32, 16, 512), lambda i: (0, 0, 0))
@@ -327,15 +348,27 @@
         scratch_shapes=[pltpu.VMEM((128, 128), BF)],
         compiler_params=pltpu.CompilerParams(vmem_limit_bytes=VMEM_LIMIT),
     )(pos, owner, q_rec, q_keep, states)
+    r_send, out_w3 = later(r_send, 3)
     r_rec = lax.all_to_all(r_send, ("req", "col"), split_axis=0, concat_axis=0, tiled=True)
-    shape = jax.ShapeDtypeStruct((4, 256, 256), BF)
-    heads = call(combine_kernel, shape, 3, 5, scratch_shapes=[pltpu.VMEM((512, 512), BF)])(
-        pos, at_holder, at_slot, num, den, r_rec, r_keep, place[:, None]
+    r_rec, out_w3 = lax.optimization_barrier((r_rec, out_w3))
+    heads = call(
+        combine_kernel,
+        jax.ShapeDtypeStruct((4, 256, 256), BF),
+        3,
+        pos,
+        at_holder,
+        at_slot,
+        num,
+        den,
+        r_rec,
+        r_keep,
+        place[:, None],
+        scratch=[pltpu.VMEM((512, 512), BF)],
     )
     heads = lax.all_to_all(heads, "y", split_axis=0, concat_axis=0, tiled=True)
     heads_oth = lax.ppermute(heads, "core", [(0, 1), (1, 0)])
     shape = jax.ShapeDtypeStruct((256, 448), BF)
-    mixed = call(out_kernel, (shape, shape), 1, 6)(pos, heads, heads_oth, *out_w)
+    mixed = call(out_kernel, (shape, shape), 1, pos, heads, heads_oth, pieces, out_w1, out_w2, out_w3)
 
     def at(y, core, col):
         return (y * 2 + core) * 4 + col

time: 227 us -> 213 us (0.938)
  waiting for transfers between devices: 58.9 us -> 36.5 us
  blocking collectives: 0 us -> 10.9 us
  starting transfers between devices: 81.2 us -> 78.7 us
  local copies, waits for them, and re-layouts: 41.5 us -> 43.8 us
    ppermute x9, waiting for transfers between devices: 45.6 us -> 22.7 us  [the longest x3 20.8 us: later(): lax.ppermute(held_back, 'y', [(i, (i + step) % 4) for i in range(4)])]
    all_to_all x0 -> x1, blocking collectives: none -> 10.9 us  [body(): heads = lax.all_to_all(heads, 'y', split_axis=0, concat_axis=0, tiled=True)]
    ppermute x4, starting transfers between devices: 12.7 us -> 4.1 us  [body(): theirs = [lax.ppermute(w, 'core', [(0, 1), (1, 0)]) for w in mine]]
    all_to_all x1 -> x0, starting transfers between devices: 4.42 us -> none  [body(): heads = lax.all_to_all(heads, 'y', split_axis=0, concat_axis=0, tiled=True)]
    ppermute x1, starting transfers between devices: 0.59 us -> 4.22 us  [body(): rec = lax.ppermute(oth, 'core', [(0, 1), (1, 0)])]
    all_to_all x1, starting transfers between devices: 7.03 us -> 10.6 us  [body(): lax.all_to_all(r_send, ('req', 'col'), split_axis=0, concat_axis=0, tiled...]
    all_to_all x1 -> x0, waiting for transfers between devices: 3.16 us -> none  [body(): heads = lax.all_to_all(heads, 'y', split_axis=0, concat_axis=0, tiled=True)]
    ppermute x4, waiting for transfers between devices: 0.01 us -> 2.59 us  [body(): pieces.append(lax.ppermute(w_out, ('core', 'col'), perm))]
  transfers between devices with their start and end apart: 26 -> 25, of which waited for: 11 -> 10; matrix products, arithmetic and copies ran while one was open for 15% -> 18% of each run, Pallas kernels for 4% -> 4%
where the time goes in v2:
time: 213 us; the launch traced here: 210 us
  starting transfers between devices  78.7 us (37%)
  local copies, waits for them, and re-layouts  43.8 us (21%)
  waiting for transfers between devices  36.5 us (17%)
  Pallas kernels  25.9 us (12%)
  other arithmetic  13.6 us (6%)
  blocking collectives  10.9 us (5%)
    unnamed x66, local copies, waits for them, and re-layouts  29.9 us
    ppermute x3, waiting for transfers between devices, later(): lax.ppermute(held_back, 'y', [(i, (i + step) % 4) for i in range(4)])  20.8 us
    pallas_call x6, Pallas kernels, call(): pl.pallas_call(kernel, grid=(1,), out_shape=out_shapes, in_specs=[SM] * n...  16.6 us
    all_to_all x1, starting transfers between devices, body(): lax.all_to_all(q_send, ('req', 'col'), split_axis=0, concat_axis=0, tiled...  11.3 us
    all_to_all x1, blocking collectives, body(): heads = lax.all_to_all(heads, 'y', split_axis=0, concat_axis=0, tiled=True)  10.9 us
    ppermute x4, starting transfers between devices, body(): pieces.append(lax.ppermute(w_out, ('core', 'col'), perm))  10.8 us
    all_to_all x1, starting transfers between devices, body(): lax.all_to_all(r_send, ('req', 'col'), split_axis=0, concat_axis=0, tiled...  10.6 us
    ppermute x6, starting transfers between devices, shifts(): lax.ppermute(x, axis, [(i, (i + s) % 4) for i in range(4)])  10.4 us
  transfers between devices with their start and end apart: 25, of which 10 were waited for; matrix products, arithmetic and copies ran while one was open for 18% of the time, Pallas kernels for 4%

profile of v2, /device:TPU:9, one launch (start us, length us, event | category | flops | bytes accessed | tf_op | source)
XLA Modules:
  0.0 209.8 jit_solution(10655236840876545593)
XLA Ops:
  0.0 3.7 %collective-permute-start.6 = (bf16[224,448]{1,0:T(8,128)(2,1)}, bf16[224,448]{1,0:T(8,128)(2,1)S(1)}, u32[]{:S(2)}, u32[]{:S(2)}) collective-permute-start(bf16[224,448]{1,0:T(8,128)(2,1)} %param.16), channel_id=1, source_target_pairs={{0,0},{1,2},{2,4},{3,6},{4,1},{5,3},{6,5},{7,7},{8,8},{9,10},{10,1... | collective-permute-start | bytes 602120 | tf_op jit(solution)/shard_map/ppermute | solution.py:286
  3.8 1.6 collective-permute-start.8
  5.4 1.2 reshape.69
  7.0 0.9 copy.73
  7.9 0.9 copy.74
  9.0 1.0 collective-permute-start.3
  9.9 1.3 copy.69
  11.2 1.4 collective-permute-start
  12.6 0.8 collective-permute-start.1
  13.4 1.9 collective-permute-start.2
  15.4 5.4 %collective-permute-start.9 = (bf16[224,448]{1,0:T(8,128)(2,1)}, bf16[224,448]{1,0:T(8,128)(2,1)S(1)}, u32[]{:S(2)}, u32[]{:S(2)}) collective-permute-start(bf16[224,448]{1,0:T(8,128)(2,1)} %param.16), channel_id=1, source_target_pairs={{0,3},{1,1},{2,7},{3,5},{4,2},{5,0},{6,6},{7,4},{8,11},{9,9},{10,1... | collective-permute-start | bytes 602120 | tf_op jit(solution)/shard_map/ppermute | solution.py:286
  21.5 2.6 %collective-permute-done.9 = bf16[224,448]{1,0:T(8,128)(2,1)S(1)} collective-permute-done((bf16[224,448]{1,0:T(8,128)(2,1)}, bf16[224,448]{1,0:T(8,128)(2,1)S(1)}, u32[]{:S(2)}, u32[]{:S(2)}) %collective-permute-start.9) | collective-permute-done | bytes 200736 | tf_op jit(solution)/shard_map/ppermute | solution.py:286
  24.8 5.3 %collective-permute-start.5 = (bf16[448,288]{1,0:T(8,128)(2,1)S(1)}, bf16[448,288]{1,0:T(8,128)(2,1)S(1)}, u32[]{:S(2)}, u32[]{:S(2)}) collective-permute-start(bf16[448,288]{1,0:T(8,128)(2,1)S(1)} %pad_maximum_fusion.1.refs_0_), channel_id=1, source_target_pairs={{0,3},{1,0},{2,1},{3,2},{4,7},{5,4},{6,5},{7,6},{8,11},{9,8},{10,9... | collective-permute-start | bytes 774152 | tf_op jit(solution)/shard_map/ppermute | solution.py:277
  30.8 0.7 copy.68
  31.5 8.6 %all-to-all-start = ((s32[32,1,1]{2,1,0:T(1,128)}), s32[32,1,1]{2,1,0:T(1,128)S(1)}, u32[]{:S(2)}, u32[]{:S(2)}) async-start(s32[32,1,1]{2,1,0:T(1,128)} %copy.68), calls=%async_computation | async-start | bytes 32768 | tf_op jit(solution)/shard_map/all_to_all | solution.py:300
  40.2 1.9 collective-permute-done.5.refs_3_
  42.1 0.7 copy-done.19
  42.8 1.3 copy.75.t0
  44.1 1.4 pad_maximum_fusion.w0
  45.5 0.7 shard_map.118
  46.2 1.2 copy-done.1
  47.5 1.2 all-to-all-done
  48.7 4.7 %all-to-all-start.1 = ((bf16[4,256,896]{2,1,0:T(8,128)(2,1)}), bf16[4,256,896]{2,1,0:T(8,128)(2,1)S(1)}, u32[]{:S(2)}, u32[]{:S(2)}) async-start(bf16[4,256,896]{2,1,0:T(8,128)(2,1)} %copy-done.1), calls=%async_computation.1 | async-start | bytes 3670016 | tf_op jit(solution)/shard_map/all_to_all | solution.py:315
  53.4 7.3 %copy.77 = bf16[1,273,7168]{1,2,0:T(8,128)(2,1)} copy(bf16[1,273,7168]{2,1,0:T(8,128)(2,1)} %param.17) | data formatting | bytes 7827456 | tf_op args[5]
  60.7 8.4 %copy.78 = bf16[273,224,32]{1,0,2:T(8,128)(2,1)} copy(bf16[273,224,32]{0,2,1:T(8,128)(2,1)} %bitcast.26) | data formatting | bytes 7827456 | tf_op jit(solution)/shard_map/reshape;squeeze | solution.py:309
  69.1 2.0 copy.79
  72.6 3.3 %collective-permute-start.11 = (bf16[448,288]{1,0:T(8,128)(2,1)S(1)}, bf16[448,288]{1,0:T(8,128)(2,1)}, u32[]{:S(2)}, u32[]{:S(2)}) collective-permute-start(bf16[448,288]{1,0:T(8,128)(2,1)S(1)} %pad_maximum_fusion.1.refs_0_), channel_id=1, source_target_pairs={{0,4},{4,0},{1,5},{5,1},{2,6},{6,2},{3,7},{7,3},{8,12},{12,8},{9,1... | collective-permute-start | bytes 774152 | tf_op jit(solution)/shard_map/ppermute | solution.py:314
  77.4 12.9 %collective-permute-done.10.w1 = bf16[4,224,448]{2,1,0:T(8,128)(2,1)S(1)} collective-permute-done((bf16[4,224,448]{2,1,0:T(8,128)(2,1)S(1)}, bf16[4,224,448]{2,1,0:T(8,128)(2,1)S(1)}, u32[]{:S(2)}, u32[]{:S(2)}) %collective-permute-start.10) | collective-permute-done | bytes 802848 | tf_op jit(solution)/shard_map/ppermute | solution.py:292
  90.3 1.0 copy-done.7
  91.3 1.0 copy-done.16
  92.3 1.0 copy-done.18
  93.3 1.0 copy-done.20
  94.2 3.7 %shard_map.119 = (bf16[512,288]{1,0:T(8,128)(2,1)S(1)}, bf16[512,288]{1,0:T(8,128)(2,1)S(1)}) custom-call(s32[4]{0:T(128)S(1)} %pad_add_fusion.pos_ref, bf16[4,256,896]{2,1,0:T(8,128)(2,1)S(1)} %all-to-all-done.1.t_ref, bf16[448,288]{1,0:T(8,128)(2,1)S(1)} %pad_maximum_fusion.1.refs_0_, bf16[448,288]{1,0:T(8,128)(2,1)S(1)} %copy-done.16, ...), custom_call_target="tpu_custom_call" | custom-call | tf_op jit(solution)/shard_map/pallas_call | solution.py:38
  97.9 4.2 %collective-permute-start.15 = (bf16[512,288]{1,0:T(8,128)(2,1)S(1)}, bf16[512,288]{1,0:T(8,128)(2,1)S(1)}, u32[]{:S(2)}, u32[]{:S(2)}) collective-permute-start(bf16[512,288]{1,0:T(8,128)(2,1)S(1)} %get-tuple-element.56), channel_id=1, source_target_pairs={{0,4},{4,0},{1,5},{5,1},{2,6},{6,2},{3,7},{7,3},{8,12},{12,8},{9,1... | collective-permute-start | bytes 884744 | tf_op jit(solution)/shard_map/ppermute | solution.py:320
  102.1 0.7 collective-permute-start.16
  103.5 2.1 %shard_map.121 = (bf16[32,16,128]{2,1,0:T(8,128)(2,1)}, bf16[32,16,128]{2,1,0:T(8,128)(2,1)S(1)}) custom-call(s32[4]{0:T(128)S(1)} %pad_add_fusion.pos_ref, s32[32]{0:T(128)S(1)} %broadcast_select_fusion.2.g_ref, s32[32]{0:T(128)S(1)} %fusion.2.s_ref, bf16[512,288]{1,0:T(8,128)(2,1)S(1)} %get-tuple-element.54.own_ref, ...), custom_call_target="tpu_custom_call" | custom-call | tf_op jit(solution)/shard_map/pallas_call | solution.py:38
  105.6 11.3 %all-to-all-start.2 = ((bf16[32,16,128]{2,1,0:T(8,128)(2,1)}), bf16[32,16,128]{2,1,0:T(8,128)(2,1)S(1)}, u32[]{:S(2)}, u32[]{:S(2)}) async-start(bf16[32,16,128]{2,1,0:T(8,128)(2,1)} %get-tuple-element.59), calls=%async_computation.2 | async-start | bytes 262144 | tf_op jit(solution)/shard_map/all_to_all | solution.py:335
  116.9 7.5 %maximum_maximum_fusion.state_ref = bf16[32,273,256]{2,1,0:T(8,128)(2,1)} fusion(bf16[32,273,2]{2,1,0:T(8,128)(2,1)} %copy.79, bf16[32,273,224]{2,1,0:T(8,128)(2,1)} %bitcast.27, bf16[256]{0:T(256)(128)(2,1)S(1)} %pad.5.clone), kind=kLoop, calls=%fused_computation | loop fusion | flops 17891328 | bytes 8422016 | tf_op jit(solution)/shard_map/concatenate | solution.py:310
  124.4 1.9 all-to-all-done.2.rec_ref
  126.3 2.6 %copy-done = bf16[32,273,256]{2,1,0:T(8,128)(2,1)S(1)} copy-done((bf16[32,273,256]{2,1,0:T(8,128)(2,1)S(1)}, bf16[32,273,256]{2,1,0:T(8,128)(2,1)}, u32[]{:S(2)}) %copy-start) | copy-done | bytes 4472856
  128.9 9.4 %shard_map.122 = (bf16[32,16,512]{2,1,0:T(8,128)(2,1)S(1)}, bf16[32,16,512]{2,1,0:T(8,128)(2,1)S(1)}) custom-call(s32[4]{0:T(128)S(1)} %pad_add_fusion.pos_ref, s32[32]{0:T(128)S(1)} %get-tuple-element.74.owner_ref, bf16[32,16,128]{2,1,0:T(8,128)(2,1)S(1)} %all-to-all-done.2.rec_ref, bf16[32,16,128]{2,1,0:T(8,128)(2,1)S(1)} %get-tuple-element.62.keep_ref, ...), custom_call_target="tpu_custom_call" | custom-call | tf_op jit(solution)/shard_map/pallas_call | solution.py:342
  138.3 0.8 copy-done.11
  139.1 0.8 copy-done.13
  139.9 10.6 %all-to-all-start.3 = ((bf16[32,16,512]{2,1,0:T(8,128)(2,1)}), bf16[32,16,512]{2,1,0:T(8,128)(2,1)S(1)}, u32[]{:S(2)}, u32[]{:S(2)}) async-start(bf16[32,16,512]{2,1,0:T(8,128)(2,1)} %copy-done.13), calls=%async_computation.3 | async-start | bytes 1048576 | tf_op jit(solution)/shard_map/all_to_all | solution.py:352
  150.5 2.6 %collective-permute-start.17 = (bf16[4,224,448]{2,1,0:T(8,128)(2,1)S(1)}, bf16[4,224,448]{2,1,0:T(8,128)(2,1)}, u32[]{:S(2)}, u32[]{:S(2)}) collective-permute-start(bf16[4,224,448]{2,1,0:T(8,128)(2,1)S(1)} %pad_maximum_fusion.w0), channel_id=1, source_target_pairs={{0,24},{8,0},{16,8},{24,16},{1,25},{9,1},{17,9},{25,17},{2,26},{10... | collective-permute-start | bytes 2408456 | tf_op jit(solution)/shard_map/ppermute | solution.py:292
  153.4 1.5 copy-done.2
  154.9 0.9 copy-done.21
  155.9 5.9 %shard_map.120 = (f32[2,512,256]{2,1,0:T(8,128)S(1)}, f32[2,512,256]{2,1,0:T(8,128)S(1)}) custom-call(s32[4]{0:T(128)S(1)} %pad_add_fusion.pos_ref, bf16[512,288]{1,0:T(8,128)(2,1)S(1)} %get-tuple-element.54.own_ref, bf16[512,288]{1,0:T(8,128)(2,1)S(1)} %collective-permute-done.15.rec_ref, bf16[512,256]{1,0:T(8,128)(2,1)S(1)} %copy-done.21, ...), custom_call_target="tpu_custom_call" | custom-call | tf_op jit(solution)/shard_map/pallas_call | solution.py:38
  161.8 1.0 copy-done.3
  162.8 1.0 copy-done.5
  163.8 7.9 %collective-permute-done.17.w3 = bf16[4,224,448]{2,1,0:T(8,128)(2,1)} collective-permute-done((bf16[4,224,448]{2,1,0:T(8,128)(2,1)S(1)}, bf16[4,224,448]{2,1,0:T(8,128)(2,1)}, u32[]{:S(2)}, u32[]{:S(2)}) %collective-permute-start.17) | collective-permute-done | bytes 802848 | tf_op jit(solution)/shard_map/ppermute | solution.py:292
  171.7 1.2 copy-done.4
  172.9 1.2 copy-done.6
  174.1 1.0 copy-done.12
  175.2 1.8 shard_map.123
  177.0 10.9 %all_to_all.29.own_ref = bf16[4,256,256]{2,1,0:T(8,128)(2,1)S(1)} all-to-all(bf16[4,256,256]{2,1,0:T(8,128)(2,1)S(1)} %shard_map.123), channel_id=1, replica_groups=mesh['req'=8,'y'=4,'core'=2,'col'=4] {'y'}, dimensions={0} | all-to-all | bytes 1048576 | tf_op jit(solution)/shard_map/all_to_all | solution.py:368
  187.9 3.3 %collective-permute-start.18 = (bf16[4,256,256]{2,1,0:T(8,128)(2,1)S(1)}, bf16[4,256,256]{2,1,0:T(8,128)(2,1)S(1)}, u32[]{:S(2)}, u32[]{:S(2)}) collective-permute-start(bf16[4,256,256]{2,1,0:T(8,128)(2,1)S(1)} %all_to_all.29.own_ref), channel_id=1, source_target_pairs={{0,4},{4,0},{1,5},{5,1},{2,6},{6,2},{3,7},{7,3},{8,12},{12,8},{9,1... | collective-permute-start | bytes 1572872 | tf_op jit(solution)/shard_map/ppermute | solution.py:369
  191.2 1.5 collective-permute-done.18.oth_ref
  192.7 2.4 %shard_map.124 = (bf16[256,448]{1,0:T(8,128)(2,1)S(1)}, bf16[256,448]{1,0:T(8,128)(2,1)S(1)}) custom-call(s32[4]{0:T(128)S(1)} %pad_add_fusion.pos_ref, bf16[4,256,256]{2,1,0:T(8,128)(2,1)S(1)} %all_to_all.29.own_ref, bf16[4,256,256]{2,1,0:T(8,128)(2,1)S(1)} %collective-permute-done.18.oth_ref, bf16[4,224,448]{2,1,0:T(8,128)(2,1)S(1)} %pad_maximum_fusion.w0, ...), custom_call_target="tpu_custom_call" | custom-call | tf_op jit(solution)/shard_map/pallas_call | solution.py:38
  195.2 3.7 %collective-permute-start.19 = (bf16[256,448]{1,0:T(8,128)(2,1)S(1)}, bf16[256,448]{1,0:T(8,128)(2,1)S(1)}, u32[]{:S(2)}, u32[]{:S(2)}) collective-permute-start(bf16[256,448]{1,0:T(8,128)(2,1)S(1)} %get-tuple-element.71), channel_id=1, source_target_pairs={{0,1},{4,3},{8,0},{12,2},{16,5},{20,7},{24,4},{28,6},{1,9},{5,11},... | collective-permute-start | bytes 688136 | tf_op jit(solution)/shard_map/ppermute | solution.py:381
  198.8 3.7 %collective-permute-start.20 = (bf16[256,448]{1,0:T(8,128)(2,1)S(1)}, bf16[256,448]{1,0:T(8,128)(2,1)S(1)}, u32[]{:S(2)}, u32[]{:S(2)}) collective-permute-start(bf16[256,448]{1,0:T(8,128)(2,1)S(1)} %get-tuple-element.72), channel_id=1, source_target_pairs={{0,0},{4,2},{8,1},{12,3},{16,4},{20,6},{24,5},{28,7},{1,8},{5,10},... | collective-permute-start | bytes 688136 | tf_op jit(solution)/shard_map/ppermute | solution.py:381
  202.5 4.4 %collective-permute-done.19 = bf16[256,448]{1,0:T(8,128)(2,1)S(1)} collective-permute-done((bf16[256,448]{1,0:T(8,128)(2,1)S(1)}, bf16[256,448]{1,0:T(8,128)(2,1)S(1)}, u32[]{:S(2)}, u32[]{:S(2)}) %collective-permute-start.19) | collective-permute-done | bytes 229408 | tf_op jit(solution)/shard_map/ppermute | solution.py:381
  206.9 1.7 collective-permute-done.20
  208.9 0.9 fusion.1
  (92 shorter events, 7.2 us)
Async XLA Ops:
  0.0 12.6 %collective-permute-start.6 = (bf16[224,448]{1,0:T(8,128)(2,1)}, bf16[224,448]{1,0:T(8,128)(2,1)S(1)}, u32[]{:S(2)}, u32[]{:S(2)}) collective-permute-start(bf16[224,448]{1,0:T(8,128)(2,1)} %param.16), channel_id=1, source_target_pairs={{0,0},{1,2},{2,4},{3,6},{4,1},{5,3},{6,5},{7,7},{8,8},{9,10},{10,1... | collective-permute-start | bytes 602120 | tf_op jit(solution)/shard_map/ppermute | solution.py:286
  3.7 9.7 %collective-permute-start.7 = (bf16[224,448]{1,0:T(8,128)(2,1)}, bf16[224,448]{1,0:T(8,128)(2,1)S(1)}, u32[]{:S(2)}, u32[]{:S(2)}) collective-permute-start(bf16[224,448]{1,0:T(8,128)(2,1)} %param.16), channel_id=1, source_target_pairs={{0,1},{1,3},{2,5},{3,7},{4,0},{5,2},{6,4},{7,6},{8,9},{9,11},{10,1... | collective-permute-start | bytes 602120 | tf_op jit(solution)/shard_map/ppermute | solution.py:286
  3.8 11.6 %collective-permute-start.8 = (bf16[224,448]{1,0:T(8,128)(2,1)}, bf16[224,448]{1,0:T(8,128)(2,1)S(1)}, u32[]{:S(2)}, u32[]{:S(2)}) collective-permute-start(bf16[224,448]{1,0:T(8,128)(2,1)} %param.16), channel_id=1, source_target_pairs={{0,2},{1,0},{2,6},{3,4},{4,3},{5,1},{6,7},{7,5},{8,10},{9,8},{10,1... | collective-permute-start | bytes 602120 | tf_op jit(solution)/shard_map/ppermute | solution.py:286
  9.0 15.1 %collective-permute-start.3 = (bf16[448,288]{1,0:T(8,128)(2,1)S(1)}, bf16[448,288]{1,0:T(8,128)(2,1)S(1)}, u32[]{:S(2)}, u32[]{:S(2)}) collective-permute-start(bf16[448,288]{1,0:T(8,128)(2,1)S(1)} %pad_maximum_fusion.1.refs_0_), channel_id=1, source_target_pairs={{0,1},{1,2},{2,3},{3,0},{4,5},{5,6},{6,7},{7,4},{8,9},{9,10},{10,1... | collective-permute-start | bytes 774152 | tf_op jit(solution)/shard_map/ppermute | solution.py:277
  11.2 30.9 %collective-permute-start = (bf16[256,896]{1,0:T(8,128)(2,1)S(1)}, bf16[256,896]{1,0:T(8,128)(2,1)S(1)}, u32[]{:S(2)}, u32[]{:S(2)}) collective-permute-start(bf16[256,896]{1,0:T(8,128)(2,1)S(1)} %copy.69), channel_id=1, source_target_pairs={{0,8},{8,16},{16,24},{24,0},{1,9},{9,17},{17,25},{25,1},{2,10},{10... | collective-permute-start | bytes 1376264 | tf_op jit(solution)/shard_map/ppermute | solution.py:277
  12.6 31.5 %copy-start.23 = (bf16[224,448]{1,0:T(8,128)(2,1)}, bf16[224,448]{1,0:T(8,128)(2,1)S(1)}, u32[]{:S(2)}) copy-start(bf16[224,448]{1,0:T(8,128)(2,1)S(1)} %collective-permute-done.6) | copy-start | bytes 602116
  12.6 29.5 %collective-permute-start.1 = (bf16[256,896]{1,0:T(8,128)(2,1)S(1)}, bf16[256,896]{1,0:T(8,128)(2,1)S(1)}, u32[]{:S(2)}, u32[]{:S(2)}) collective-permute-start(bf16[256,896]{1,0:T(8,128)(2,1)S(1)} %copy.69), channel_id=1, source_target_pairs={{0,16},{8,24},{16,0},{24,8},{1,17},{9,25},{17,1},{25,9},{2,18},{10... | collective-permute-start | bytes 1376264 | tf_op jit(solution)/shard_map/ppermute | solution.py:277
  13.4 8.1 %copy-start.24 = (bf16[224,448]{1,0:T(8,128)(2,1)}, bf16[224,448]{1,0:T(8,128)(2,1)S(1)}, u32[]{:S(2)}) copy-start(bf16[224,448]{1,0:T(8,128)(2,1)S(1)} %collective-permute-done.7) | copy-start | bytes 602116
  13.4 29.4 %collective-permute-start.2 = (bf16[256,896]{1,0:T(8,128)(2,1)S(1)}, bf16[256,896]{1,0:T(8,128)(2,1)S(1)}, u32[]{:S(2)}, u32[]{:S(2)}) collective-permute-start(bf16[256,896]{1,0:T(8,128)(2,1)S(1)} %copy.69), channel_id=1, source_target_pairs={{0,24},{8,0},{16,8},{24,16},{1,25},{9,1},{17,9},{25,17},{2,26},{10... | collective-permute-start | bytes 1376264 | tf_op jit(solution)/shard_map/ppermute | solution.py:277
  15.4 8.7 %copy-start.25 = (bf16[224,448]{1,0:T(8,128)(2,1)}, bf16[224,448]{1,0:T(8,128)(2,1)S(1)}, u32[]{:S(2)}) copy-start(bf16[224,448]{1,0:T(8,128)(2,1)S(1)} %collective-permute-done.8) | copy-start | bytes 602116
  15.4 8.7 %collective-permute-start.9 = (bf16[224,448]{1,0:T(8,128)(2,1)}, bf16[224,448]{1,0:T(8,128)(2,1)S(1)}, u32[]{:S(2)}, u32[]{:S(2)}) collective-permute-start(bf16[224,448]{1,0:T(8,128)(2,1)} %param.16), channel_id=1, source_target_pairs={{0,3},{1,1},{2,7},{3,5},{4,2},{5,0},{6,6},{7,4},{8,11},{9,9},{10,1... | collective-permute-start | bytes 602120 | tf_op jit(solution)/shard_map/ppermute | solution.py:286
  24.1 0.7 copy-start.26
  24.1 16.1 %collective-permute-start.4 = (bf16[448,288]{1,0:T(8,128)(2,1)S(1)}, bf16[448,288]{1,0:T(8,128)(2,1)S(1)}, u32[]{:S(2)}, u32[]{:S(2)}) collective-permute-start(bf16[448,288]{1,0:T(8,128)(2,1)S(1)} %pad_maximum_fusion.1.refs_0_), channel_id=1, source_target_pairs={{0,2},{1,3},{2,0},{3,1},{4,6},{5,7},{6,4},{7,5},{8,10},{9,11},{10,... | collective-permute-start | bytes 774152 | tf_op jit(solution)/shard_map/ppermute | solution.py:277
  24.8 19.3 %copy-start.14 = (bf16[448,288]{1,0:T(8,128)(2,1)}, bf16[448,288]{1,0:T(8,128)(2,1)S(1)}, u32[]{:S(2)}) copy-start(bf16[448,288]{1,0:T(8,128)(2,1)S(1)} %collective-permute-done.3.refs_1_) | copy-start | bytes 774148
  24.8 17.3 %collective-permute-start.5 = (bf16[448,288]{1,0:T(8,128)(2,1)S(1)}, bf16[448,288]{1,0:T(8,128)(2,1)S(1)}, u32[]{:S(2)}, u32[]{:S(2)}) collective-permute-start(bf16[448,288]{1,0:T(8,128)(2,1)S(1)} %pad_maximum_fusion.1.refs_0_), channel_id=1, source_target_pairs={{0,3},{1,0},{2,1},{3,2},{4,7},{5,4},{6,5},{7,6},{8,11},{9,8},{10,9... | collective-permute-start | bytes 774152 | tf_op jit(solution)/shard_map/ppermute | solution.py:277
  31.5 17.2 %all-to-all-start = ((s32[32,1,1]{2,1,0:T(1,128)}), s32[32,1,1]{2,1,0:T(1,128)S(1)}, u32[]{:S(2)}, u32[]{:S(2)}) async-start(s32[32,1,1]{2,1,0:T(1,128)} %copy.68), calls=%async_computation | async-start | bytes 32768 | tf_op jit(solution)/shard_map/all_to_all | solution.py:300
  40.2 3.9 %copy-start.17 = (bf16[448,288]{1,0:T(8,128)(2,1)}, bf16[448,288]{1,0:T(8,128)(2,1)S(1)}, u32[]{:S(2)}) copy-start(bf16[448,288]{1,0:T(8,128)(2,1)S(1)} %collective-permute-done.4.refs_2_) | copy-start | bytes 774148
  42.1 0.8 copy-start.19
  46.2 1.2 copy-start.1
  48.7 42.6 %all-to-all-start.1 = ((bf16[4,256,896]{2,1,0:T(8,128)(2,1)}), bf16[4,256,896]{2,1,0:T(8,128)(2,1)S(1)}, u32[]{:S(2)}, u32[]{:S(2)}) async-start(bf16[4,256,896]{2,1,0:T(8,128)(2,1)} %copy-done.1), calls=%async_computation.1 | async-start | bytes 3670016 | tf_op jit(solution)/shard_map/all_to_all | solution.py:315
  60.7 8.4 %copy-start.27 = (bf16[32,273,2]{1,2,0:T(2,128)(2,1)S(1)}, bf16[32,273,2]{1,2,0:T(2,128)(2,1)}, u32[]{:S(2)}) copy-start(bf16[32,273,2]{1,2,0:T(2,128)(2,1)} %param.18) | copy-start | bytes 104836
  60.7 10.5 %copy-start.30 = (s32[32]{0:T(128)S(1)}, s32[32]{0:T(128)}, u32[]{:S(2)}) copy-start(s32[32]{0:T(128)} %param.19) | copy-start | bytes 388
  60.7 11.0 %copy-start.28 = (s32[512]{0:T(512)S(1)}, s32[512]{0:T(512)}, u32[]{:S(2)}) copy-start(s32[512]{0:T(512)} %param.20) | copy-start | bytes 6148
  60.7 15.2 %copy-start.15 = (bf16[448,288]{1,0:T(8,128)(2,1)S(1)}, bf16[448,288]{1,0:T(8,128)(2,1)}, u32[]{:S(2)}) copy-start(bf16[448,288]{1,0:T(8,128)(2,1)} %copy-done.14) | copy-start | bytes 774148
  71.6 18.7 %collective-permute-start.10 = (bf16[4,224,448]{2,1,0:T(8,128)(2,1)S(1)}, bf16[4,224,448]{2,1,0:T(8,128)(2,1)S(1)}, u32[]{:S(2)}, u32[]{:S(2)}) collective-permute-start(bf16[4,224,448]{2,1,0:T(8,128)(2,1)S(1)} %pad_maximum_fusion.w0), channel_id=1, source_target_pairs={{0,8},{8,16},{16,24},{24,0},{1,9},{9,17},{17,25},{25,1},{2,10},{10... | collective-permute-start | bytes 2408456 | tf_op jit(solution)/shard_map/ppermute | solution.py:292
  72.6 18.7 %collective-permute-start.11 = (bf16[448,288]{1,0:T(8,128)(2,1)S(1)}, bf16[448,288]{1,0:T(8,128)(2,1)}, u32[]{:S(2)}, u32[]{:S(2)}) collective-permute-start(bf16[448,288]{1,0:T(8,128)(2,1)S(1)} %pad_maximum_fusion.1.refs_0_), channel_id=1, source_target_pairs={{0,4},{4,0},{1,5},{5,1},{2,6},{6,2},{3,7},{7,3},{8,12},{12,8},{9,1... | collective-permute-start | bytes 774152 | tf_op jit(solution)/shard_map/ppermute | solution.py:314
  75.9 15.4 %collective-permute-start.12 = (bf16[448,288]{1,0:T(8,128)(2,1)S(1)}, bf16[448,288]{1,0:T(8,128)(2,1)}, u32[]{:S(2)}, u32[]{:S(2)}) collective-permute-start(bf16[448,288]{1,0:T(8,128)(2,1)S(1)} %copy-done.15), channel_id=1, source_target_pairs={{0,4},{4,0},{1,5},{5,1},{2,6},{6,2},{3,7},{7,3},{8,12},{12,8},{9,1... | collective-permute-start | bytes 774152 | tf_op jit(solution)/shard_map/ppermute | solution.py:314
  76.2 15.1 %collective-permute-start.13 = (bf16[448,288]{1,0:T(8,128)(2,1)}, bf16[448,288]{1,0:T(8,128)(2,1)}, u32[]{:S(2)}, u32[]{:S(2)}) collective-permute-start(bf16[448,288]{1,0:T(8,128)(2,1)} %copy-done.17), channel_id=1, source_target_pairs={{0,4},{4,0},{1,5},{5,1},{2,6},{6,2},{3,7},{7,3},{8,12},{12,8},{9,1... | collective-permute-start | bytes 774152 | tf_op jit(solution)/shard_map/ppermute | solution.py:314
  76.4 14.9 %collective-permute-start.14 = (bf16[448,288]{1,0:T(8,128)(2,1)}, bf16[448,288]{1,0:T(8,128)(2,1)}, u32[]{:S(2)}, u32[]{:S(2)}) collective-permute-start(bf16[448,288]{1,0:T(8,128)(2,1)} %copy-done.19), channel_id=1, source_target_pairs={{0,4},{4,0},{1,5},{5,1},{2,6},{6,2},{3,7},{7,3},{8,12},{12,8},{9,1... | collective-permute-start | bytes 774152 | tf_op jit(solution)/shard_map/ppermute | solution.py:314
  90.3 1.0 copy-start.7
  91.3 1.0 copy-start.16
  92.3 1.0 copy-start.18
  93.3 1.0 copy-start.20
  97.9 5.6 %collective-permute-start.15 = (bf16[512,288]{1,0:T(8,128)(2,1)S(1)}, bf16[512,288]{1,0:T(8,128)(2,1)S(1)}, u32[]{:S(2)}, u32[]{:S(2)}) collective-permute-start(bf16[512,288]{1,0:T(8,128)(2,1)S(1)} %get-tuple-element.56), channel_id=1, source_target_pairs={{0,4},{4,0},{1,5},{5,1},{2,6},{6,2},{3,7},{7,3},{8,12},{12,8},{9,1... | collective-permute-start | bytes 884744 | tf_op jit(solution)/shard_map/ppermute | solution.py:320
  102.1 24.1 %collective-permute-start.16 = (bf16[4,224,448]{2,1,0:T(8,128)(2,1)S(1)}, bf16[4,224,448]{2,1,0:T(8,128)(2,1)S(1)}, u32[]{:S(2)}, u32[]{:S(2)}) collective-permute-start(bf16[4,224,448]{2,1,0:T(8,128)(2,1)S(1)} %pad_maximum_fusion.w0), channel_id=1, source_target_pairs={{0,16},{8,24},{16,0},{24,8},{1,17},{9,25},{17,1},{25,9},{2,18},{10... | collective-permute-start | bytes 2408456 | tf_op jit(solution)/shard_map/ppermute | solution.py:292
  105.6 20.7 %all-to-all-start.2 = ((bf16[32,16,128]{2,1,0:T(8,128)(2,1)}), bf16[32,16,128]{2,1,0:T(8,128)(2,1)S(1)}, u32[]{:S(2)}, u32[]{:S(2)}) async-start(bf16[32,16,128]{2,1,0:T(8,128)(2,1)} %get-tuple-element.59), calls=%async_computation.2 | async-start | bytes 262144 | tf_op jit(solution)/shard_map/all_to_all | solution.py:335
  116.9 36.2 %copy-start.29 = (s32[512]{0:T(512)S(1)}, s32[512]{0:T(512)}, u32[]{:S(2)}) copy-start(s32[512]{0:T(512)} %param.23) | copy-start | bytes 6148
  126.3 26.8 %copy-start.9 = (bf16[4,224,448]{2,1,0:T(8,128)(2,1)}, bf16[4,224,448]{2,1,0:T(8,128)(2,1)S(1)}, u32[]{:S(2)}) copy-start(bf16[4,224,448]{2,1,0:T(8,128)(2,1)S(1)} %collective-permute-done.16.w2) | copy-start | bytes 2408452
  126.3 2.6 %copy-start = (bf16[32,273,256]{2,1,0:T(8,128)(2,1)S(1)}, bf16[32,273,256]{2,1,0:T(8,128)(2,1)}, u32[]{:S(2)}) copy-start(bf16[32,273,256]{2,1,0:T(8,128)(2,1)} %maximum_maximum_fusion.state_ref) | copy-start | bytes 13418500
  138.3 0.8 copy-start.11
  139.1 0.8 copy-start.13
  139.9 31.8 %all-to-all-start.3 = ((bf16[32,16,512]{2,1,0:T(8,128)(2,1)}), bf16[32,16,512]{2,1,0:T(8,128)(2,1)S(1)}, u32[]{:S(2)}, u32[]{:S(2)}) async-start(bf16[32,16,512]{2,1,0:T(8,128)(2,1)} %copy-done.13), calls=%async_computation.3 | async-start | bytes 1048576 | tf_op jit(solution)/shard_map/all_to_all | solution.py:352
  150.5 21.1 %collective-permute-start.17 = (bf16[4,224,448]{2,1,0:T(8,128)(2,1)S(1)}, bf16[4,224,448]{2,1,0:T(8,128)(2,1)}, u32[]{:S(2)}, u32[]{:S(2)}) collective-permute-start(bf16[4,224,448]{2,1,0:T(8,128)(2,1)S(1)} %pad_maximum_fusion.w0), channel_id=1, source_target_pairs={{0,24},{8,0},{16,8},{24,16},{1,25},{9,1},{17,9},{25,17},{2,26},{10... | collective-permute-start | bytes 2408456 | tf_op jit(solution)/shard_map/ppermute | solution.py:292
  153.4 1.5 copy-start.2
  154.9 0.9 copy-start.21
  161.8 1.0 copy-start.3
  162.8 1.0 copy-start.5
  171.7 1.2 copy-start.4
  172.9 1.2 copy-start.6
  174.1 1.0 copy-start.12
  175.2 17.6 %copy-start.8 = (bf16[4,224,448]{2,1,0:T(8,128)(2,1)S(1)}, bf16[4,224,448]{2,1,0:T(8,128)(2,1)}, u32[]{:S(2)}) copy-start(bf16[4,224,448]{2,1,0:T(8,128)(2,1)} %copy-done.7) | copy-start | bytes 2408452
  175.2 17.6 %copy-start.10 = (bf16[4,224,448]{2,1,0:T(8,128)(2,1)S(1)}, bf16[4,224,448]{2,1,0:T(8,128)(2,1)}, u32[]{:S(2)}) copy-start(bf16[4,224,448]{2,1,0:T(8,128)(2,1)} %copy-done.9) | copy-start | bytes 2408452
  177.0 32.0 %copy-start.22 = (bf16[256,2,448]{0,2,1:T(8,128)(2,1)S(1)}, bf16[256,2,448]{0,2,1:T(8,128)(2,1)}, u32[]{:S(2)}) copy-start(bf16[256,2,448]{0,2,1:T(8,128)(2,1)} %param.12) | copy-start | bytes 1376260
  187.9 4.8 %collective-permute-start.18 = (bf16[4,256,256]{2,1,0:T(8,128)(2,1)S(1)}, bf16[4,256,256]{2,1,0:T(8,128)(2,1)S(1)}, u32[]{:S(2)}, u32[]{:S(2)}) collective-permute-start(bf16[4,256,256]{2,1,0:T(8,128)(2,1)S(1)} %all_to_all.29.own_ref), channel_id=1, source_target_pairs={{0,4},{4,0},{1,5},{5,1},{2,6},{6,2},{3,7},{7,3},{8,12},{12,8},{9,1... | collective-permute-start | bytes 1572872 | tf_op jit(solution)/shard_map/ppermute | solution.py:369
  195.2 11.7 %collective-permute-start.19 = (bf16[256,448]{1,0:T(8,128)(2,1)S(1)}, bf16[256,448]{1,0:T(8,128)(2,1)S(1)}, u32[]{:S(2)}, u32[]{:S(2)}) collective-permute-start(bf16[256,448]{1,0:T(8,128)(2,1)S(1)} %get-tuple-element.71), channel_id=1, source_target_pairs={{0,1},{4,3},{8,0},{12,2},{16,5},{20,7},{24,4},{28,6},{1,9},{5,11},... | collective-permute-start | bytes 688136 | tf_op jit(solution)/shard_map/ppermute | solution.py:381
  198.8 9.7 %collective-permute-start.20 = (bf16[256,448]{1,0:T(8,128)(2,1)S(1)}, bf16[256,448]{1,0:T(8,128)(2,1)S(1)}, u32[]{:S(2)}, u32[]{:S(2)}) collective-permute-start(bf16[256,448]{1,0:T(8,128)(2,1)S(1)} %get-tuple-element.72), channel_id=1, source_target_pairs={{0,0},{4,2},{8,1},{12,3},{16,4},{20,6},{24,5},{28,7},{1,8},{5,10},... | collective-permute-start | bytes 688136 | tf_op jit(solution)/shard_map/ppermute | solution.py:381

commit v3 on v2

--- a/solution.py
+++ b/solution.py
@@ -30,6 +30,10 @@
     return high, (x - high.astype(F32)).astype(BF)
 
 
+def in_hbm(x):
+    return pltpu.with_memory_space_constraint(x, pltpu.HBM)
+
+
 def call(kernel, out_shapes, n_smem, *args, scratch=()):
     def full(shape):
         zeros = (0,) * len(shape)
@@ -38,12 +42,12 @@
     return pl.pallas_call(
         kernel,
         grid=(1,),
-        out_shape=out_shapes,
+        out_shape=jax.tree.map(lambda x: pltpu.HBM(x.shape, x.dtype), out_shapes),
         in_specs=[SM] * n_smem + [full(x.shape) for x in args[n_smem:]],
         out_specs=jax.tree.map(lambda x: full(x.shape), out_shapes),
         scratch_shapes=scratch,
         compiler_params=pltpu.CompilerParams(vmem_limit_bytes=VMEM_LIMIT),
-    )(*args)
+    )(*args[:n_smem], *[in_hbm(x) for x in args[n_smem:]])
 
 
 def order_kernel(pos_ref, t0, t1, t2, t3, out_ref):
@@ -98,7 +102,7 @@
             keep_ref[slot] = grouped[p * 16 : (p + 1) * 16, :]
 
 
-def slot_kernel(pos_ref, owner_ref, rec_ref, keep_ref, state_ref, send_ref, own_ref, buf):
+def slot_kernel(pos_ref, owner_ref, rec_ref, keep_ref, state_ref, norm_ref, send_ref, own_ref, buf, both_ref):
     me = pos_ref[2]
     step = pl.program_id(0)
 
@@ -144,7 +148,9 @@
     first_head = (out_lane < 112) | (out_lane == 224) | (out_lane == 226)
     for i in range(8):
         phi = jnp.concatenate([x[i * 16 : (i + 1) * 16, 0:273] for x in high + low], axis=0)
-        both = dot(phi, state_ref[i])
+        both_ref[:, 0:224] = state_ref[i]
+        both_ref[:, 224:256] = norm_ref[i]
+        both = dot(phi, both_ref[...])
         terms = both[0:64] + both[64:128]
         results = []
         for t in range(2):
@@ -253,10 +259,12 @@
                 out_ref[half * 2 + part, t * 128 : (t + 1) * 128, :] = out[part * 128 : (part + 1) * 128]
 
 
-def out_kernel(pos_ref, own_ref, oth_ref, w0, w1, w2, w3, first_ref, second_ref):
+def out_kernel(pos_ref, own_ref, oth_ref, w0, w1, w3, far_1, far_3, first_ref, second_ref, far):
     y, core, col = pos_ref[0], pos_ref[1], pos_ref[3]
     acc = [None, None]
-    for shift, w_ref in enumerate((w0, w1, w2, w3)):
+    far[0:2] = far_1[...]
+    far[2:4] = far_3[...]
+    for shift, w_ref in enumerate((w0, w1, far, w3)):
         j = lax.rem(y + 4 - shift, 4)
         for which, ref in enumerate((own_ref, oth_ref)):
             k = core if which == 0 else 1 - core
@@ -276,20 +284,19 @@
     def shifts(x, axis):
         return [x] + [lax.ppermute(x, axis, [(i, (i + s) % 4) for i in range(4)]) for s in range(1, 4)]
 
-    tok = tokens.reshape(256, 896)
-    blocks = shifts(tok, "y")
+    blocks = shifts(tokens.reshape(256, 896), "y")
+    blocks, w_out = lax.optimization_barrier((blocks, w_out))
     value_w = jnp.moveaxis(w_value.reshape(2, 448, 112), 0, 1).reshape(448, 224)
     mine = shifts(jnp.concatenate([value_w, w_query, w_key], axis=1), "col")
     pieces = []
     for s in range(4):
         perm = [(k * 4 + c, (c >> 1) * 4 + (s ^ (2 * (c & 1) + k))) for k in range(2) for c in range(4)]
         pieces.append(lax.ppermute(w_out, ("core", "col"), perm))
-    blocks, mine, pieces = lax.optimization_barrier((blocks, mine, pieces))
+    blocks, mine = lax.optimization_barrier((blocks, mine))
     pieces = jnp.stack(pieces)
 
-    def later(x, step):
-        x, held_back = lax.optimization_barrier((x, pieces))
-        return x, lax.ppermute(held_back, "y", [(i, (i + step) % 4) for i in range(4)])
+    def over_y(x, step):
+        return lax.ppermute(x, "y", [(i, (i + step) % 4) for i in range(4)])
 
     owner = slot_prompt // 32
     slots = jnp.arange(32, dtype=jnp.int32)
@@ -307,16 +314,15 @@
     place = (prompt_of - me * 32) * 16 + rank
     norms = jnp.concatenate([cached_norm, cached_norm, jnp.zeros((32, 273, 28), BF)], axis=2)
     states = jnp.transpose(cached_state[0].reshape(273, 224, 32), (2, 0, 1))
-    states = jnp.concatenate([states, norms], axis=2)
 
     held = call(order_kernel, jax.ShapeDtypeStruct((4, 256, 896), BF), 1, pos, *blocks)
-    held, out_w1 = later(held, 1)
     theirs = [lax.ppermute(w, "core", [(0, 1), (1, 0)]) for w in mine]
     held = lax.all_to_all(held, "col", split_axis=0, concat_axis=0, tiled=True)
-    held, out_w1 = lax.optimization_barrier((held, out_w1))
+    held, states, norms = lax.optimization_barrier((held, states, norms))
     shape = jax.ShapeDtypeStruct((512, 288), BF)
     own, oth = call(project_kernel, (shape, shape), 1, pos, held, *mine, *theirs, scratch=[pltpu.VMEM((512, 288), BF)])
-    oth, out_w2 = later(oth, 2)
+    oth, pieces = lax.optimization_barrier((oth, pieces))
+    out_w1, out_w3 = over_y(pieces, 1), over_y(pieces, 3)
     rec = lax.ppermute(oth, "core", [(0, 1), (1, 0)])
 
     shape = jax.ShapeDtypeStruct((32, 16, 128), BF)
@@ -333,7 +339,7 @@
         scratch=[pltpu.VMEM((512, 128), BF)],
     )
     q_rec = lax.all_to_all(q_send, ("req", "col"), split_axis=0, concat_axis=0, tiled=True)
-    q_rec, out_w2 = lax.optimization_barrier((q_rec, out_w2))
+    q_rec, out_w1, out_w3 = lax.optimization_barrier((q_rec, out_w1, out_w3))
     shape = jax.ShapeDtypeStruct((2, 512, 256), F32)
     num, den = call(tail_kernel, (shape, shape), 1, pos, own, rec, tail_keys, tail_values, tail_length[:, None])
     shape = jax.ShapeDtypeStruct((32, 16, 512), BF)
@@ -342,15 +348,23 @@
     r_send, r_keep = pl.pallas_call(
         slot_kernel,
         grid=(4,),
-        out_shape=(shape, shape),
-        in_specs=[SM, SM, whole, whole, pl.BlockSpec((8, 273, 256), lambda i: (i, 0, 0))],
+        out_shape=(pltpu.HBM(shape.shape, BF), pltpu.HBM(shape.shape, BF)),
+        in_specs=[
+            SM,
+            SM,
+            whole,
+            whole,
+            pl.BlockSpec((8, 273, 224), lambda i: (i, 0, 0)),
+            pl.BlockSpec((8, 273, 32), lambda i: (i, 0, 0)),
+        ],
         out_specs=(whole_out, whole_out),
-        scratch_shapes=[pltpu.VMEM((128, 128), BF)],
+        scratch_shapes=[pltpu.VMEM((128, 128), BF), pltpu.VMEM((273, 256), BF)],
         compiler_params=pltpu.CompilerParams(vmem_limit_bytes=VMEM_LIMIT),
-    )(pos, owner, q_rec, q_keep, states)
-    r_send, out_w3 = later(r_send, 3)
+    )(pos, owner, in_hbm(q_rec), in_hbm(q_keep), in_hbm(states), in_hbm(norms))
+    r_send, far_1, far_3 = lax.optimization_barrier((r_send, out_w1[:2], out_w3[2:]))
+    far_1, far_3 = over_y(far_1, 1), over_y(far_3, 3)
     r_rec = lax.all_to_all(r_send, ("req", "col"), split_axis=0, concat_axis=0, tiled=True)
-    r_rec, out_w3 = lax.optimization_barrier((r_rec, out_w3))
+    r_rec, far_1, far_3 = lax.optimization_barrier((r_rec, far_1, far_3))
     heads = call(
         combine_kernel,
         jax.ShapeDtypeStruct((4, 256, 256), BF),
@@ -368,7 +382,7 @@
     heads = lax.all_to_all(heads, "y", split_axis=0, concat_axis=0, tiled=True)
     heads_oth = lax.ppermute(heads, "core", [(0, 1), (1, 0)])
     shape = jax.ShapeDtypeStruct((256, 448), BF)
-    mixed = call(out_kernel, (shape, shape), 1, pos, heads, heads_oth, pieces, out_w1, out_w2, out_w3)
+    mixed = call(out_kernel, (shape, shape), 1, pos, heads, heads_oth, pieces, out_w1, out_w3, far_1, far_3, scratch=[pltpu.VMEM((4, 224, 448), BF)])
 
     def at(y, core, col):
         return (y * 2 + core) * 4 + col

time: 213 us -> 192 us (0.901)
  Pallas kernels: 25.9 us -> 42 us
  local copies, waits for them, and re-layouts: 43.8 us -> 31.9 us
  starting transfers between devices: 78.7 us -> 68.9 us
  other arithmetic: 13.6 us -> 5.97 us
  waiting for transfers between devices: 36.5 us -> 29.9 us
    unnamed x66 -> x47, local copies, waits for them, and re-layouts: 29.9 us -> 11.3 us
    ppermute x3 -> x4, waiting for transfers between devices: 20.8 us -> 2.25 us  [over_y(): return lax.ppermute(x, 'y', [(i, (i + step) % 4) for i in range(4)])]
    pallas_call x7, Pallas kernels: 25.9 us -> 42 us  [the longest x6 27.7 us: call(): pl.pallas_call(kernel, grid=(1,), out_shape=jax.tree.map(lambda x: pltpu....]
    ppermute x3 -> x4, starting transfers between devices: 3.32 us -> 11.5 us  [over_y(): return lax.ppermute(x, 'y', [(i, (i + step) % 4) for i in range(4)])]
    all_to_all x1, starting transfers between devices: 10.6 us -> 3.9 us  [body(): lax.all_to_all(r_send, ('req', 'col'), split_axis=0, concat_axis=0, tiled...]
    all_to_all x1, starting transfers between devices: 11.3 us -> 4.89 us  [body(): lax.all_to_all(q_send, ('req', 'col'), split_axis=0, concat_axis=0, tiled...]
    concatenate x1, other arithmetic: 7.48 us -> 1.11 us  [body(): jnp.concatenate([cached_norm, cached_norm, jnp.zeros((32, 273, 28), BF)],...]
    all_to_all x1, waiting for transfers between devices: 1.86 us -> 6.52 us  [body(): lax.all_to_all(q_send, ('req', 'col'), split_axis=0, concat_axis=0, tiled...]
  transfers between devices with their start and end apart: 25 -> 26, of which waited for: 10 -> 14; matrix products, arithmetic and copies ran while one was open for 18% -> 15% of each run, Pallas kernels for 4% -> 7%
where the time goes in v3:
time: 192 us; the launch traced here: 189 us
  starting transfers between devices  68.9 us (36%)
  Pallas kernels  42 us (22%)
  local copies, waits for them, and re-layouts  31.9 us (17%)
  waiting for transfers between devices  29.9 us (16%)
  blocking collectives  10.1 us (5%)
  other arithmetic  5.97 us (3%)
    pallas_call x6, Pallas kernels, call(): pl.pallas_call(kernel, grid=(1,), out_shape=jax.tree.map(lambda x: pltpu....  27.7 us
    pallas_call x1, Pallas kernels, body(): pl.pallas_call(slot_kernel, grid=(4,), out_shape=(pltpu.HBM(shape.shape,...  14.3 us
    ppermute x4, starting transfers between devices, over_y(): return lax.ppermute(x, 'y', [(i, (i + step) % 4) for i in range(4)])  11.5 us
    ppermute x4, starting transfers between devices, body(): pieces.append(lax.ppermute(w_out, ('core', 'col'), perm))  11.3 us
    unnamed x47, local copies, waits for them, and re-layouts  11.3 us
    ppermute x6, starting transfers between devices, shifts(): lax.ppermute(x, axis, [(i, (i + s) % 4) for i in range(4)])  10.5 us
    all_to_all x1, blocking collectives, body(): heads = lax.all_to_all(heads, 'y', split_axis=0, concat_axis=0, tiled=True)  10.1 us
    all_to_all x1, starting transfers between devices, body(): lax.all_to_all(code[:, None], ('req', 'col'), split_axis=0, concat_axis=0...  8.84 us
  transfers between devices with their start and end apart: 26, of which 14 were waited for; matrix products, arithmetic and copies ran while one was open for 15% of the time, Pallas kernels for 7%

profile of v3, /device:TPU:9, one launch (start us, length us, event | category | flops | bytes accessed | tf_op | source)
XLA Modules:
  0.0 189.0 jit_solution(7983700075168012865)
XLA Ops:
  0.0 1.3 copy.67
  1.3 1.4 collective-permute-start
  2.7 0.8 collective-permute-start.1
  3.5 2.0 %collective-permute-start.2 = (bf16[256,896]{1,0:T(8,128)(2,1)S(1)}, bf16[256,896]{1,0:T(8,128)(2,1)S(1)}, u32[]{:S(2)}, u32[]{:S(2)}) collective-permute-start(bf16[256,896]{1,0:T(8,128)(2,1)S(1)} %copy.67), channel_id=1, source_target_pairs={{0,24},{8,0},{16,8},{24,16},{1,25},{9,1},{17,9},{25,17},{2,26},{10... | collective-permute-start | bytes 1376264 | tf_op jit(solution)/shard_map/ppermute | solution.py:285
  5.5 1.2 reshape.69
  7.4 0.9 pad_maximum_fusion.1.refs_0_
  8.3 1.2 collective-permute-start.3
  9.6 2.5 %collective-permute-start.4 = (bf16[448,288]{1,0:T(8,128)(2,1)}, bf16[448,288]{1,0:T(8,128)(2,1)}, u32[]{:S(2)}, u32[]{:S(2)}) collective-permute-start(bf16[448,288]{1,0:T(8,128)(2,1)} %pad_maximum_fusion.1.refs_0_), channel_id=1, source_target_pairs={{0,2},{1,3},{2,0},{3,1},{4,6},{5,7},{6,4},{7,5},{8,10},{9,11},{10,... | collective-permute-start | bytes 774152 | tf_op jit(solution)/shard_map/ppermute | solution.py:285
  12.0 0.6 collective-permute-done.t1
  12.6 2.7 %collective-permute-start.5 = (bf16[448,288]{1,0:T(8,128)(2,1)}, bf16[448,288]{1,0:T(8,128)(2,1)}, u32[]{:S(2)}, u32[]{:S(2)}) collective-permute-start(bf16[448,288]{1,0:T(8,128)(2,1)} %pad_maximum_fusion.1.refs_0_), channel_id=1, source_target_pairs={{0,3},{1,0},{2,1},{3,2},{4,7},{5,4},{6,5},{7,6},{8,11},{9,8},{10,9... | collective-permute-start | bytes 774152 | tf_op jit(solution)/shard_map/ppermute | solution.py:285
  15.4 0.7 copy.66
  16.1 8.8 %all-to-all-start = ((s32[32,1,1]{2,1,0:T(1,128)}), s32[32,1,1]{2,1,0:T(1,128)S(1)}, u32[]{:S(2)}, u32[]{:S(2)}) async-start(s32[32,1,1]{2,1,0:T(1,128)} %copy.66), calls=%async_computation | async-start | bytes 32768 | tf_op jit(solution)/shard_map/all_to_all | solution.py:307
  25.2 1.1 collective-permute-done.4.refs_2_
  26.3 1.0 copy.73.t0
  27.3 2.8 %shard_map.118 = bf16[4,256,896]{2,1,0:T(8,128)(2,1)} custom-call(s32[4]{0:T(128)S(1)} %pad_add_fusion.pos_ref, bf16[256,896]{1,0:T(8,128)(2,1)} %copy.73.t0, bf16[256,896]{1,0:T(8,128)(2,1)} %copy-done.11, bf16[256,896]{1,0:T(8,128)(2,1)} %copy-done.12, bf16[256,896]{1,0:T(8,128)(2,1)} %copy-done.13), custom_call_target="tpu_custom_call" | custom-call | tf_op jit(solution)/shard_map/pallas_call | solution.py:42
  30.1 3.5 %all-to-all-done = s32[32,1,1]{2,1,0:T(1,128)S(1)} async-done(((s32[32,1,1]{2,1,0:T(1,128)}), s32[32,1,1]{2,1,0:T(1,128)S(1)}, u32[]{:S(2)}, u32[]{:S(2)}) %all-to-all-start) | async-done | bytes 160 | tf_op jit(solution)/shard_map/all_to_all | solution.py:307
  33.5 3.6 %all-to-all-start.1 = ((bf16[4,256,896]{2,1,0:T(8,128)(2,1)}), bf16[4,256,896]{2,1,0:T(8,128)(2,1)S(1)}, u32[]{:S(2)}, u32[]{:S(2)}) async-start(bf16[4,256,896]{2,1,0:T(8,128)(2,1)} %shard_map.118), calls=%async_computation.1 | async-start | bytes 3670016 | tf_op jit(solution)/shard_map/all_to_all | solution.py:320
  37.1 7.3 %copy.74 = bf16[1,273,7168]{1,2,0:T(8,128)(2,1)} copy(bf16[1,273,7168]{2,1,0:T(8,128)(2,1)} %param.17) | data formatting | bytes 7827456 | tf_op args[5]
  44.5 8.4 %copy.75 = bf16[273,224,32]{1,0,2:T(8,128)(2,1)} copy(bf16[273,224,32]{0,2,1:T(8,128)(2,1)} %bitcast.24) | data formatting | bytes 7827456 | tf_op jit(solution)/shard_map/reshape;squeeze | solution.py:316
  53.6 1.1 maximum_maximum_fusion
  54.7 4.4 %collective-permute-start.11 = (bf16[224,448]{1,0:T(8,128)(2,1)S(1)}, bf16[224,448]{1,0:T(8,128)(2,1)S(1)}, u32[]{:S(2)}, u32[]{:S(2)}) collective-permute-start(bf16[224,448]{1,0:T(8,128)(2,1)S(1)} %copy-done.21), channel_id=1, source_target_pairs={{0,1},{1,3},{2,5},{3,7},{4,0},{5,2},{6,4},{7,6},{8,9},{9,11},{10,1... | collective-permute-start | bytes 602120 | tf_op jit(solution)/shard_map/ppermute | solution.py:294
  59.1 2.8 %collective-permute-start.12 = (bf16[224,448]{1,0:T(8,128)(2,1)S(1)}, bf16[224,448]{1,0:T(8,128)(2,1)S(1)}, u32[]{:S(2)}, u32[]{:S(2)}) collective-permute-start(bf16[224,448]{1,0:T(8,128)(2,1)S(1)} %copy-done.21), channel_id=1, source_target_pairs={{0,2},{1,0},{2,6},{3,4},{4,3},{5,1},{6,7},{7,5},{8,10},{9,8},{10,1... | collective-permute-start | bytes 602120 | tf_op jit(solution)/shard_map/ppermute | solution.py:294
  62.0 2.2 %collective-permute-start.13 = (bf16[224,448]{1,0:T(8,128)(2,1)S(1)}, bf16[224,448]{1,0:T(8,128)(2,1)S(1)}, u32[]{:S(2)}, u32[]{:S(2)}) collective-permute-start(bf16[224,448]{1,0:T(8,128)(2,1)S(1)} %copy-done.21), channel_id=1, source_target_pairs={{0,3},{1,1},{2,7},{3,5},{4,2},{5,0},{6,6},{7,4},{8,11},{9,9},{10,1... | collective-permute-start | bytes 602120 | tf_op jit(solution)/shard_map/ppermute | solution.py:294
  64.2 0.6 multiply_add_fusion
  64.8 1.9 %collective-permute-start.10 = (bf16[224,448]{1,0:T(8,128)(2,1)S(1)}, bf16[224,448]{1,0:T(8,128)(2,1)S(1)}, u32[]{:S(2)}, u32[]{:S(2)}) collective-permute-start(bf16[224,448]{1,0:T(8,128)(2,1)S(1)} %copy-done.21), channel_id=1, source_target_pairs={{0,0},{1,2},{2,4},{3,6},{4,1},{5,3},{6,5},{7,7},{8,8},{9,10},{10,1... | collective-permute-start | bytes 602120 | tf_op jit(solution)/shard_map/ppermute | solution.py:294
  66.8 0.5 collective-permute-start.7
  67.3 1.5 collective-permute-done.12
  68.8 3.0 %collective-permute-start.8 = (bf16[448,288]{1,0:T(8,128)(2,1)}, bf16[448,288]{1,0:T(8,128)(2,1)}, u32[]{:S(2)}, u32[]{:S(2)}) collective-permute-start(bf16[448,288]{1,0:T(8,128)(2,1)} %collective-permute-done.4.refs_2_), channel_id=1, source_target_pairs={{0,4},{4,0},{1,5},{5,1},{2,6},{6,2},{3,7},{7,3},{8,12},{12,8},{9,1... | collective-permute-start | bytes 774152 | tf_op jit(solution)/shard_map/ppermute | solution.py:319
  71.8 0.3 collective-permute-start.9
  72.2 0.7 add_reduce_fusion
  72.8 0.7 compare_reduce_fusion
  73.5 0.4 collective-permute-done.10
  74.1 1.2 copy-done
  75.3 5.4 %shard_map.119 = (bf16[512,288]{1,0:T(8,128)(2,1)}, bf16[512,288]{1,0:T(8,128)(2,1)}) custom-call(s32[4]{0:T(128)S(1)} %pad_add_fusion.pos_ref, bf16[4,256,896]{2,1,0:T(8,128)(2,1)} %copy-done, bf16[448,288]{1,0:T(8,128)(2,1)} %pad_maximum_fusion.1.refs_0_, bf16[448,288]{1,0:T(8,128)(2,1)} %collective-permute-done.3.refs_1_, ...), custom_call_target="tpu_custom_call" | custom-call | tf_op jit(solution)/shard_map/pallas_call | solution.py:42
  80.7 10.0 %collective-permute-start.15 = (bf16[4,224,448]{2,1,0:T(8,128)(2,1)S(1)}, bf16[4,224,448]{2,1,0:T(8,128)(2,1)S(1)}, u32[]{:S(2)}, u32[]{:S(2)}) collective-permute-start(bf16[4,224,448]{2,1,0:T(8,128)(2,1)S(1)} %pad_maximum_fusion.w0), channel_id=1, source_target_pairs={{0,8},{8,16},{16,24},{24,0},{1,9},{9,17},{17,25},{25,1},{2,10},{10... | collective-permute-start | bytes 2408456 | tf_op jit(solution)/shard_map/ppermute | solution.py:299
  91.0 1.7 collective-permute-done.14.rec_ref
  92.7 0.8 copy-done.6
  93.5 2.7 %shard_map.121 = (bf16[32,16,128]{2,1,0:T(8,128)(2,1)}, bf16[32,16,128]{2,1,0:T(8,128)(2,1)}) custom-call(s32[4]{0:T(128)S(1)} %pad_add_fusion.pos_ref, s32[32]{0:T(128)S(1)} %broadcast_select_fusion.2.g_ref, s32[32]{0:T(128)S(1)} %fusion.2.s_ref, bf16[512,288]{1,0:T(8,128)(2,1)} %get-tuple-element.55.own_ref, bf16[512,288]{1,0:T(8,128)(2,1)} %copy-done.6, ...), custom_call_target="tpu_custom_call" | custom-call | tf_op jit(solution)/shard_map/pallas_call | solution.py:42
  96.2 4.9 %all-to-all-start.2 = ((bf16[32,16,128]{2,1,0:T(8,128)(2,1)}), bf16[32,16,128]{2,1,0:T(8,128)(2,1)S(1)}, u32[]{:S(2)}, u32[]{:S(2)}) async-start(bf16[32,16,128]{2,1,0:T(8,128)(2,1)} %get-tuple-element.61), calls=%async_computation.2 | async-start | bytes 262144 | tf_op jit(solution)/shard_map/all_to_all | solution.py:341
  101.1 2.8 %copy.77.norm_ref = bf16[32,273,32]{2,1,0:T(8,128)(2,1)} copy(bf16[32,273,32]{1,2,0:T(8,128)(2,1)} %maximum_maximum_fusion) | data formatting | bytes 1118208 | tf_op jit(solution)/shard_map/optimization_barrier | solution.py:321
  103.9 6.5 %all-to-all-done.2.rec_ref = bf16[32,16,128]{2,1,0:T(8,128)(2,1)S(1)} async-done(((bf16[32,16,128]{2,1,0:T(8,128)(2,1)}), bf16[32,16,128]{2,1,0:T(8,128)(2,1)S(1)}, u32[]{:S(2)}, u32[]{:S(2)}) %all-to-all-start.2) | async-done | bytes 131104 | tf_op jit(solution)/shard_map/all_to_all | solution.py:341
  110.6 2.1 %collective-permute-done.16.w3 = bf16[4,224,448]{2,1,0:T(8,128)(2,1)} collective-permute-done((bf16[4,224,448]{2,1,0:T(8,128)(2,1)S(1)}, bf16[4,224,448]{2,1,0:T(8,128)(2,1)}, u32[]{:S(2)}, u32[]{:S(2)}) %collective-permute-start.16) | collective-permute-done | bytes 802848 | tf_op jit(solution)/shard_map/ppermute | solution.py:299
  112.7 0.8 slice.6
  113.5 1.8 slice.7
  115.3 14.3 %shard_map.122 = (bf16[32,16,512]{2,1,0:T(8,128)(2,1)}, bf16[32,16,512]{2,1,0:T(8,128)(2,1)}) custom-call(s32[4]{0:T(128)S(1)} %pad_add_fusion.pos_ref, s32[32]{0:T(128)S(1)} %get-tuple-element.80.owner_ref, bf16[32,16,128]{2,1,0:T(8,128)(2,1)} %copy-done.8, bf16[32,16,128]{2,1,0:T(8,128)(2,1)} %get-tuple-element.64.keep_ref, ...), custom_call_target="tpu_custom_call" | custom-call | tf_op jit(solution)/shard_map/pallas_call | solution.py:348
  129.6 3.9 %all-to-all-start.3 = ((bf16[32,16,512]{2,1,0:T(8,128)(2,1)}), bf16[32,16,512]{2,1,0:T(8,128)(2,1)S(1)}, u32[]{:S(2)}, u32[]{:S(2)}) async-start(bf16[32,16,512]{2,1,0:T(8,128)(2,1)} %get-tuple-element.70), calls=%async_computation.3 | async-start | bytes 1048576 | tf_op jit(solution)/shard_map/all_to_all | solution.py:366
  133.5 0.3 collective-permute-start.17
  133.8 1.2 collective-permute-start.18
  135.1 0.8 copy.76.len_ref
  135.9 0.9 copy.78.place_ref
  136.8 8.5 %shard_map.120 = (f32[2,512,256]{2,1,0:T(8,128)}, f32[2,512,256]{2,1,0:T(8,128)}) custom-call(s32[4]{0:T(128)S(1)} %pad_add_fusion.pos_ref, bf16[512,288]{1,0:T(8,128)(2,1)} %get-tuple-element.55.own_ref, bf16[512,288]{1,0:T(8,128)(2,1)} %copy-done.6, bf16[512,256]{1,0:T(8,128)(2,1)} %tk_ref.1, bf16[512,1792]{1,0:T(8,128)(2,1)} %tv_ref.1, s32[512,1]{1,0:T(8,128)} %copy.76.len_ref), custom_call_target="tpu_custom_call" | custom-call | tf_op jit(solution)/shard_map/pallas_call | solution.py:42
  145.3 4.3 %all-to-all-done.3.rec_ref = bf16[32,16,512]{2,1,0:T(8,128)(2,1)S(1)} async-done(((bf16[32,16,512]{2,1,0:T(8,128)(2,1)}), bf16[32,16,512]{2,1,0:T(8,128)(2,1)S(1)}, u32[]{:S(2)}, u32[]{:S(2)}) %all-to-all-start.3) | async-done | bytes 524320 | tf_op jit(solution)/shard_map/all_to_all | solution.py:366
  149.6 0.8 copy-done.3
  150.4 4.0 %shard_map.123 = bf16[4,256,256]{2,1,0:T(8,128)(2,1)} custom-call(s32[4]{0:T(128)S(1)} %pad_add_fusion.pos_ref, s32[32]{0:T(128)S(1)} %broadcast_select_fusion.2.g_ref, s32[32]{0:T(128)S(1)} %fusion.2.s_ref, f32[2,512,256]{2,1,0:T(8,128)} %get-tuple-element.59.num_ref, f32[2,512,256]{2,1,0:T(8,128)} %get-tuple-element.60.den_ref, ...), custom_call_target="tpu_custom_call" | custom-call | tf_op jit(solution)/shard_map/pallas_call | solution.py:42
  154.3 10.1 %all_to_all.29.own_ref = bf16[4,256,256]{2,1,0:T(8,128)(2,1)S(1)} all-to-all(bf16[4,256,256]{2,1,0:T(8,128)(2,1)} %shard_map.123), channel_id=1, replica_groups=mesh['req'=8,'y'=4,'core'=2,'col'=4] {'y'}, dimensions={0} | all-to-all | bytes 1048576 | tf_op jit(solution)/shard_map/all_to_all | solution.py:382
  164.4 3.3 %collective-permute-start.19 = (bf16[4,256,256]{2,1,0:T(8,128)(2,1)S(1)}, bf16[4,256,256]{2,1,0:T(8,128)(2,1)S(1)}, u32[]{:S(2)}, u32[]{:S(2)}) collective-permute-start(bf16[4,256,256]{2,1,0:T(8,128)(2,1)S(1)} %all_to_all.29.own_ref), channel_id=1, source_target_pairs={{0,4},{4,0},{1,5},{5,1},{2,6},{6,2},{3,7},{7,3},{8,12},{12,8},{9,1... | collective-permute-start | bytes 1572872 | tf_op jit(solution)/shard_map/ppermute | solution.py:383
  167.7 1.5 collective-permute-done.19.oth_ref
  169.3 0.8 copy-done.7
  170.1 4.4 %shard_map.124 = (bf16[256,448]{1,0:T(8,128)(2,1)}, bf16[256,448]{1,0:T(8,128)(2,1)}) custom-call(s32[4]{0:T(128)S(1)} %pad_add_fusion.pos_ref, bf16[4,256,256]{2,1,0:T(8,128)(2,1)} %copy-done.4, bf16[4,256,256]{2,1,0:T(8,128)(2,1)} %copy-done.7, bf16[4,224,448]{2,1,0:T(8,128)(2,1)} %copy-done.2, bf16[4,224,448]{2,1,0:T(8,128)(2,1)} %copy-done.5, ...), custom_call_target="tpu_custom_call" | custom-call | tf_op jit(solution)/shard_map/pallas_call | solution.py:42
  174.5 3.2 %collective-permute-start.20 = (bf16[256,448]{1,0:T(8,128)(2,1)}, bf16[256,448]{1,0:T(8,128)(2,1)S(1)}, u32[]{:S(2)}, u32[]{:S(2)}) collective-permute-start(bf16[256,448]{1,0:T(8,128)(2,1)} %get-tuple-element.77), channel_id=1, source_target_pairs={{0,1},{4,3},{8,0},{12,2},{16,5},{20,7},{24,4},{28,6},{1,9},{5,11},... | collective-permute-start | bytes 688136 | tf_op jit(solution)/shard_map/ppermute | solution.py:395
  177.7 3.6 %collective-permute-start.21 = (bf16[256,448]{1,0:T(8,128)(2,1)}, bf16[256,448]{1,0:T(8,128)(2,1)S(1)}, u32[]{:S(2)}, u32[]{:S(2)}) collective-permute-start(bf16[256,448]{1,0:T(8,128)(2,1)} %get-tuple-element.78), channel_id=1, source_target_pairs={{0,0},{4,2},{8,1},{12,3},{16,4},{20,6},{24,5},{28,7},{1,8},{5,10},... | collective-permute-start | bytes 688136 | tf_op jit(solution)/shard_map/ppermute | solution.py:395
  181.3 5.0 %collective-permute-done.20 = bf16[256,448]{1,0:T(8,128)(2,1)S(1)} collective-permute-done((bf16[256,448]{1,0:T(8,128)(2,1)}, bf16[256,448]{1,0:T(8,128)(2,1)S(1)}, u32[]{:S(2)}, u32[]{:S(2)}) %collective-permute-start.20) | collective-permute-done | bytes 229408 | tf_op jit(solution)/shard_map/ppermute | solution.py:395
  186.3 1.4 collective-permute-done.21
  188.1 0.9 fusion.1
  (78 shorter events, 2.8 us)
Async XLA Ops:
  0.0 26.3 %copy-start.1 = (bf16[256,2,448]{0,2,1:T(8,128)(2,1)S(1)}, bf16[256,2,448]{0,2,1:T(8,128)(2,1)}, u32[]{:S(2)}) copy-start(bf16[256,2,448]{0,2,1:T(8,128)(2,1)} %param.12) | copy-start | bytes 1376260
  0.0 7.1 %copy-start.15 = (bf16[448,32]{0,1:T(8,128)(2,1)S(1)}, bf16[448,32]{0,1:T(8,128)(2,1)}, u32[]{:S(2)}) copy-start(bf16[448,32]{0,1:T(8,128)(2,1)} %param.13) | copy-start | bytes 86020
  0.0 7.3 %copy-start.16 = (bf16[448,32]{0,1:T(8,128)(2,1)S(1)}, bf16[448,32]{0,1:T(8,128)(2,1)}, u32[]{:S(2)}) copy-start(bf16[448,32]{0,1:T(8,128)(2,1)} %param.14) | copy-start | bytes 86020
  0.0 12.0 %copy-start.20 = (s32[32]{0:T(128)S(1)}, s32[32]{0:T(128)}, u32[]{:S(2)}) copy-start(s32[32]{0:T(128)} %param.19) | copy-start | bytes 388
  1.3 11.3 %collective-permute-start = (bf16[256,896]{1,0:T(8,128)(2,1)S(1)}, bf16[256,896]{1,0:T(8,128)(2,1)S(1)}, u32[]{:S(2)}, u32[]{:S(2)}) collective-permute-start(bf16[256,896]{1,0:T(8,128)(2,1)S(1)} %copy.67), channel_id=1, source_target_pairs={{0,8},{8,16},{16,24},{24,0},{1,9},{9,17},{17,25},{25,1},{2,10},{10... | collective-permute-start | bytes 1376264 | tf_op jit(solution)/shard_map/ppermute | solution.py:285
  2.7 22.3 %collective-permute-start.1 = (bf16[256,896]{1,0:T(8,128)(2,1)S(1)}, bf16[256,896]{1,0:T(8,128)(2,1)S(1)}, u32[]{:S(2)}, u32[]{:S(2)}) collective-permute-start(bf16[256,896]{1,0:T(8,128)(2,1)S(1)} %copy.67), channel_id=1, source_target_pairs={{0,16},{8,24},{16,0},{24,8},{1,17},{9,25},{17,1},{25,9},{2,18},{10... | collective-permute-start | bytes 1376264 | tf_op jit(solution)/shard_map/ppermute | solution.py:285
  3.5 21.6 %collective-permute-start.2 = (bf16[256,896]{1,0:T(8,128)(2,1)S(1)}, bf16[256,896]{1,0:T(8,128)(2,1)S(1)}, u32[]{:S(2)}, u32[]{:S(2)}) collective-permute-start(bf16[256,896]{1,0:T(8,128)(2,1)S(1)} %copy.67), channel_id=1, source_target_pairs={{0,24},{8,0},{16,8},{24,16},{1,25},{9,1},{17,9},{25,17},{2,26},{10... | collective-permute-start | bytes 1376264 | tf_op jit(solution)/shard_map/ppermute | solution.py:285
  8.3 16.8 %collective-permute-start.3 = (bf16[448,288]{1,0:T(8,128)(2,1)}, bf16[448,288]{1,0:T(8,128)(2,1)}, u32[]{:S(2)}, u32[]{:S(2)}) collective-permute-start(bf16[448,288]{1,0:T(8,128)(2,1)} %pad_maximum_fusion.1.refs_0_), channel_id=1, source_target_pairs={{0,1},{1,2},{2,3},{3,0},{4,5},{5,6},{6,7},{7,4},{8,9},{9,10},{10,1... | collective-permute-start | bytes 774152 | tf_op jit(solution)/shard_map/ppermute | solution.py:285
  9.6 16.7 %collective-permute-start.4 = (bf16[448,288]{1,0:T(8,128)(2,1)}, bf16[448,288]{1,0:T(8,128)(2,1)}, u32[]{:S(2)}, u32[]{:S(2)}) collective-permute-start(bf16[448,288]{1,0:T(8,128)(2,1)} %pad_maximum_fusion.1.refs_0_), channel_id=1, source_target_pairs={{0,2},{1,3},{2,0},{3,1},{4,6},{5,7},{6,4},{7,5},{8,10},{9,11},{10,... | collective-permute-start | bytes 774152 | tf_op jit(solution)/shard_map/ppermute | solution.py:285
  12.6 14.6 %copy-start.11 = (bf16[256,896]{1,0:T(8,128)(2,1)}, bf16[256,896]{1,0:T(8,128)(2,1)S(1)}, u32[]{:S(2)}) copy-start(bf16[256,896]{1,0:T(8,128)(2,1)S(1)} %collective-permute-done.t1) | copy-start | bytes 1376260
  12.6 13.7 %collective-permute-start.5 = (bf16[448,288]{1,0:T(8,128)(2,1)}, bf16[448,288]{1,0:T(8,128)(2,1)}, u32[]{:S(2)}, u32[]{:S(2)}) collective-permute-start(bf16[448,288]{1,0:T(8,128)(2,1)} %pad_maximum_fusion.1.refs_0_), channel_id=1, source_target_pairs={{0,3},{1,0},{2,1},{3,2},{4,7},{5,4},{6,5},{7,6},{8,11},{9,8},{10,9... | collective-permute-start | bytes 774152 | tf_op jit(solution)/shard_map/ppermute | solution.py:285
  16.1 17.4 %all-to-all-start = ((s32[32,1,1]{2,1,0:T(1,128)}), s32[32,1,1]{2,1,0:T(1,128)S(1)}, u32[]{:S(2)}, u32[]{:S(2)}) async-start(s32[32,1,1]{2,1,0:T(1,128)} %copy.66), calls=%async_computation | async-start | bytes 32768 | tf_op jit(solution)/shard_map/all_to_all | solution.py:307
  25.0 2.2 %copy-start.12 = (bf16[256,896]{1,0:T(8,128)(2,1)}, bf16[256,896]{1,0:T(8,128)(2,1)S(1)}, u32[]{:S(2)}) copy-start(bf16[256,896]{1,0:T(8,128)(2,1)S(1)} %collective-permute-done.1.t2) | copy-start | bytes 1376260
  25.2 2.1 %copy-start.13 = (bf16[256,896]{1,0:T(8,128)(2,1)}, bf16[256,896]{1,0:T(8,128)(2,1)S(1)}, u32[]{:S(2)}) copy-start(bf16[256,896]{1,0:T(8,128)(2,1)S(1)} %collective-permute-done.2.t3) | copy-start | bytes 1376260
  33.5 40.5 %all-to-all-start.1 = ((bf16[4,256,896]{2,1,0:T(8,128)(2,1)}), bf16[4,256,896]{2,1,0:T(8,128)(2,1)S(1)}, u32[]{:S(2)}, u32[]{:S(2)}) async-start(bf16[4,256,896]{2,1,0:T(8,128)(2,1)} %shard_map.118), calls=%async_computation.1 | async-start | bytes 3670016 | tf_op jit(solution)/shard_map/all_to_all | solution.py:320
  44.4 8.9 %copy-start.18 = (s32[512]{0:T(512)S(1)}, s32[512]{0:T(512)}, u32[]{:S(2)}) copy-start(s32[512]{0:T(512)} %param.20) | copy-start | bytes 6148
  44.4 9.2 %copy-start.14 = (bf16[32,273,2]{1,2,0:T(2,128)(2,1)S(1)}, bf16[32,273,2]{1,2,0:T(2,128)(2,1)}, u32[]{:S(2)}) copy-start(bf16[32,273,2]{1,2,0:T(2,128)(2,1)} %param.18) | copy-start | bytes 104836
  44.5 10.3 %copy-start.21 = (bf16[224,448]{1,0:T(8,128)(2,1)S(1)}, bf16[224,448]{1,0:T(8,128)(2,1)}, u32[]{:S(2)}) copy-start(bf16[224,448]{1,0:T(8,128)(2,1)} %param.16) | copy-start | bytes 602116
  54.7 12.1 %collective-permute-start.11 = (bf16[224,448]{1,0:T(8,128)(2,1)S(1)}, bf16[224,448]{1,0:T(8,128)(2,1)S(1)}, u32[]{:S(2)}, u32[]{:S(2)}) collective-permute-start(bf16[224,448]{1,0:T(8,128)(2,1)S(1)} %copy-done.21), channel_id=1, source_target_pairs={{0,1},{1,3},{2,5},{3,7},{4,0},{5,2},{6,4},{7,6},{8,9},{9,11},{10,1... | collective-permute-start | bytes 602120 | tf_op jit(solution)/shard_map/ppermute | solution.py:294
  59.1 9.7 %collective-permute-start.12 = (bf16[224,448]{1,0:T(8,128)(2,1)S(1)}, bf16[224,448]{1,0:T(8,128)(2,1)S(1)}, u32[]{:S(2)}, u32[]{:S(2)}) collective-permute-start(bf16[224,448]{1,0:T(8,128)(2,1)S(1)} %copy-done.21), channel_id=1, source_target_pairs={{0,2},{1,0},{2,6},{3,4},{4,3},{5,1},{6,7},{7,5},{8,10},{9,8},{10,1... | collective-permute-start | bytes 602120 | tf_op jit(solution)/shard_map/ppermute | solution.py:294
  62.0 9.9 %collective-permute-start.13 = (bf16[224,448]{1,0:T(8,128)(2,1)S(1)}, bf16[224,448]{1,0:T(8,128)(2,1)S(1)}, u32[]{:S(2)}, u32[]{:S(2)}) collective-permute-start(bf16[224,448]{1,0:T(8,128)(2,1)S(1)} %copy-done.21), channel_id=1, source_target_pairs={{0,3},{1,1},{2,7},{3,5},{4,2},{5,0},{6,6},{7,4},{8,11},{9,9},{10,1... | collective-permute-start | bytes 602120 | tf_op jit(solution)/shard_map/ppermute | solution.py:294
  64.8 9.1 %collective-permute-start.10 = (bf16[224,448]{1,0:T(8,128)(2,1)S(1)}, bf16[224,448]{1,0:T(8,128)(2,1)S(1)}, u32[]{:S(2)}, u32[]{:S(2)}) collective-permute-start(bf16[224,448]{1,0:T(8,128)(2,1)S(1)} %copy-done.21), channel_id=1, source_target_pairs={{0,0},{1,2},{2,4},{3,6},{4,1},{5,3},{6,5},{7,7},{8,8},{9,10},{10,1... | collective-permute-start | bytes 602120 | tf_op jit(solution)/shard_map/ppermute | solution.py:294
  66.7 7.4 %collective-permute-start.6 = (bf16[448,288]{1,0:T(8,128)(2,1)}, bf16[448,288]{1,0:T(8,128)(2,1)}, u32[]{:S(2)}, u32[]{:S(2)}) collective-permute-start(bf16[448,288]{1,0:T(8,128)(2,1)} %pad_maximum_fusion.1.refs_0_), channel_id=1, source_target_pairs={{0,4},{4,0},{1,5},{5,1},{2,6},{6,2},{3,7},{7,3},{8,12},{12,8},{9,1... | collective-permute-start | bytes 774152 | tf_op jit(solution)/shard_map/ppermute | solution.py:319
  66.8 7.3 %collective-permute-start.7 = (bf16[448,288]{1,0:T(8,128)(2,1)}, bf16[448,288]{1,0:T(8,128)(2,1)}, u32[]{:S(2)}, u32[]{:S(2)}) collective-permute-start(bf16[448,288]{1,0:T(8,128)(2,1)} %collective-permute-done.3.refs_1_), channel_id=1, source_target_pairs={{0,4},{4,0},{1,5},{5,1},{2,6},{6,2},{3,7},{7,3},{8,12},{12,8},{9,1... | collective-permute-start | bytes 774152 | tf_op jit(solution)/shard_map/ppermute | solution.py:319
  68.8 5.3 %collective-permute-start.8 = (bf16[448,288]{1,0:T(8,128)(2,1)}, bf16[448,288]{1,0:T(8,128)(2,1)}, u32[]{:S(2)}, u32[]{:S(2)}) collective-permute-start(bf16[448,288]{1,0:T(8,128)(2,1)} %collective-permute-done.4.refs_2_), channel_id=1, source_target_pairs={{0,4},{4,0},{1,5},{5,1},{2,6},{6,2},{3,7},{7,3},{8,12},{12,8},{9,1... | collective-permute-start | bytes 774152 | tf_op jit(solution)/shard_map/ppermute | solution.py:319
  71.8 2.3 %collective-permute-start.9 = (bf16[448,288]{1,0:T(8,128)(2,1)}, bf16[448,288]{1,0:T(8,128)(2,1)}, u32[]{:S(2)}, u32[]{:S(2)}) collective-permute-start(bf16[448,288]{1,0:T(8,128)(2,1)} %collective-permute-done.5.refs_3_), channel_id=1, source_target_pairs={{0,4},{4,0},{1,5},{5,1},{2,6},{6,2},{3,7},{7,3},{8,12},{12,8},{9,1... | collective-permute-start | bytes 774152 | tf_op jit(solution)/shard_map/ppermute | solution.py:319
  74.0 55.6 %copy-start.2 = (bf16[4,224,448]{2,1,0:T(8,128)(2,1)}, bf16[4,224,448]{2,1,0:T(8,128)(2,1)S(1)}, u32[]{:S(2)}) copy-start(bf16[4,224,448]{2,1,0:T(8,128)(2,1)S(1)} %pad_maximum_fusion.w0) | copy-start | bytes 2408452
  74.0 1.3 copy-start
  80.7 29.9 %collective-permute-start.15 = (bf16[4,224,448]{2,1,0:T(8,128)(2,1)S(1)}, bf16[4,224,448]{2,1,0:T(8,128)(2,1)S(1)}, u32[]{:S(2)}, u32[]{:S(2)}) collective-permute-start(bf16[4,224,448]{2,1,0:T(8,128)(2,1)S(1)} %pad_maximum_fusion.w0), channel_id=1, source_target_pairs={{0,8},{8,16},{16,24},{24,0},{1,9},{9,17},{17,25},{25,1},{2,10},{10... | collective-permute-start | bytes 2408456 | tf_op jit(solution)/shard_map/ppermute | solution.py:299
  90.7 22.0 %collective-permute-start.16 = (bf16[4,224,448]{2,1,0:T(8,128)(2,1)S(1)}, bf16[4,224,448]{2,1,0:T(8,128)(2,1)}, u32[]{:S(2)}, u32[]{:S(2)}) collective-permute-start(bf16[4,224,448]{2,1,0:T(8,128)(2,1)S(1)} %pad_maximum_fusion.w0), channel_id=1, source_target_pairs={{0,24},{8,0},{16,8},{24,16},{1,25},{9,1},{17,9},{25,17},{2,26},{10... | collective-permute-start | bytes 2408456 | tf_op jit(solution)/shard_map/ppermute | solution.py:299
  90.7 2.0 %collective-permute-start.14 = (bf16[512,288]{1,0:T(8,128)(2,1)}, bf16[512,288]{1,0:T(8,128)(2,1)S(1)}, u32[]{:S(2)}, u32[]{:S(2)}) collective-permute-start(bf16[512,288]{1,0:T(8,128)(2,1)} %get-tuple-element.58), channel_id=1, source_target_pairs={{0,4},{4,0},{1,5},{5,1},{2,6},{6,2},{3,7},{7,3},{8,12},{12,8},{9,1... | collective-permute-start | bytes 884744 | tf_op jit(solution)/shard_map/ppermute | solution.py:326
  92.7 0.8 copy-start.6
  96.2 14.2 %all-to-all-start.2 = ((bf16[32,16,128]{2,1,0:T(8,128)(2,1)}), bf16[32,16,128]{2,1,0:T(8,128)(2,1)S(1)}, u32[]{:S(2)}, u32[]{:S(2)}) async-start(bf16[32,16,128]{2,1,0:T(8,128)(2,1)} %get-tuple-element.61), calls=%async_computation.2 | async-start | bytes 262144 | tf_op jit(solution)/shard_map/all_to_all | solution.py:341
  110.4 4.9 %copy-start.8 = (bf16[32,16,128]{2,1,0:T(8,128)(2,1)}, bf16[32,16,128]{2,1,0:T(8,128)(2,1)S(1)}, u32[]{:S(2)}) copy-start(bf16[32,16,128]{2,1,0:T(8,128)(2,1)S(1)} %all-to-all-done.2.rec_ref) | copy-start | bytes 393220
  110.6 19.0 %copy-start.5 = (bf16[4,224,448]{2,1,0:T(8,128)(2,1)}, bf16[4,224,448]{2,1,0:T(8,128)(2,1)S(1)}, u32[]{:S(2)}) copy-start(bf16[4,224,448]{2,1,0:T(8,128)(2,1)S(1)} %collective-permute-done.15.w1) | copy-start | bytes 2408452
  115.3 19.7 %copy-start.19 = (s32[512]{0:T(512)S(1)}, s32[512]{0:T(512)}, u32[]{:S(2)}) copy-start(s32[512]{0:T(512)} %param.23) | copy-start | bytes 6148
  115.3 20.6 %copy-start.17 = (s32[512]{0:T(512)S(1)}, s32[512]{0:T(512)}, u32[]{:S(2)}) copy-start(s32[512]{0:T(512)} %multiply_add_fusion) | copy-start | bytes 6148
  129.6 20.0 %all-to-all-start.3 = ((bf16[32,16,512]{2,1,0:T(8,128)(2,1)}), bf16[32,16,512]{2,1,0:T(8,128)(2,1)S(1)}, u32[]{:S(2)}, u32[]{:S(2)}) async-start(bf16[32,16,512]{2,1,0:T(8,128)(2,1)} %get-tuple-element.70), calls=%async_computation.3 | async-start | bytes 1048576 | tf_op jit(solution)/shard_map/all_to_all | solution.py:366
  133.5 11.8 %collective-permute-start.17 = (bf16[2,224,448]{2,1,0:T(8,128)(2,1)}, bf16[2,224,448]{2,1,0:T(8,128)(2,1)S(1)}, u32[]{:S(2)}, u32[]{:S(2)}) collective-permute-start(bf16[2,224,448]{2,1,0:T(8,128)(2,1)} %slice.6), channel_id=1, source_target_pairs={{0,8},{8,16},{16,24},{24,0},{1,9},{9,17},{17,25},{25,1},{2,10},{10... | collective-permute-start | bytes 1204232 | tf_op jit(solution)/shard_map/ppermute | solution.py:299
  133.8 11.4 %collective-permute-start.18 = (bf16[2,224,448]{2,1,0:T(8,128)(2,1)}, bf16[2,224,448]{2,1,0:T(8,128)(2,1)S(1)}, u32[]{:S(2)}, u32[]{:S(2)}) collective-permute-start(bf16[2,224,448]{2,1,0:T(8,128)(2,1)} %slice.7), channel_id=1, source_target_pairs={{0,24},{8,0},{16,8},{24,16},{1,25},{9,1},{17,9},{25,17},{2,26},{10... | collective-permute-start | bytes 1204232 | tf_op jit(solution)/shard_map/ppermute | solution.py:299
  145.3 24.0 %copy-start.9 = (bf16[2,224,448]{2,1,0:T(8,128)(2,1)}, bf16[2,224,448]{2,1,0:T(8,128)(2,1)S(1)}, u32[]{:S(2)}) copy-start(bf16[2,224,448]{2,1,0:T(8,128)(2,1)S(1)} %collective-permute-done.17.far_1) | copy-start | bytes 1204228
  145.3 24.0 %copy-start.10 = (bf16[2,224,448]{2,1,0:T(8,128)(2,1)}, bf16[2,224,448]{2,1,0:T(8,128)(2,1)S(1)}, u32[]{:S(2)}) copy-start(bf16[2,224,448]{2,1,0:T(8,128)(2,1)S(1)} %collective-permute-done.18.far_3) | copy-start | bytes 1204228
  149.6 0.8 copy-start.3
  164.4 4.9 %copy-start.4 = (bf16[4,256,256]{2,1,0:T(8,128)(2,1)}, bf16[4,256,256]{2,1,0:T(8,128)(2,1)S(1)}, u32[]{:S(2)}) copy-start(bf16[4,256,256]{2,1,0:T(8,128)(2,1)S(1)} %all_to_all.29.own_ref) | copy-start | bytes 1572868
  164.4 4.9 %collective-permute-start.19 = (bf16[4,256,256]{2,1,0:T(8,128)(2,1)S(1)}, bf16[4,256,256]{2,1,0:T(8,128)(2,1)S(1)}, u32[]{:S(2)}, u32[]{:S(2)}) collective-permute-start(bf16[4,256,256]{2,1,0:T(8,128)(2,1)S(1)} %all_to_all.29.own_ref), channel_id=1, source_target_pairs={{0,4},{4,0},{1,5},{5,1},{2,6},{6,2},{3,7},{7,3},{8,12},{12,8},{9,1... | collective-permute-start | bytes 1572872 | tf_op jit(solution)/shard_map/ppermute | solution.py:383
  169.3 0.8 copy-start.7
  174.5 11.9 %collective-permute-start.20 = (bf16[256,448]{1,0:T(8,128)(2,1)}, bf16[256,448]{1,0:T(8,128)(2,1)S(1)}, u32[]{:S(2)}, u32[]{:S(2)}) collective-permute-start(bf16[256,448]{1,0:T(8,128)(2,1)} %get-tuple-element.77), channel_id=1, source_target_pairs={{0,1},{4,3},{8,0},{12,2},{16,5},{20,7},{24,4},{28,6},{1,9},{5,11},... | collective-permute-start | bytes 688136 | tf_op jit(solution)/shard_map/ppermute | solution.py:395
  177.7 10.0 %collective-permute-start.21 = (bf16[256,448]{1,0:T(8,128)(2,1)}, bf16[256,448]{1,0:T(8,128)(2,1)S(1)}, u32[]{:S(2)}, u32[]{:S(2)}) collective-permute-start(bf16[256,448]{1,0:T(8,128)(2,1)} %get-tuple-element.78), channel_id=1, source_target_pairs={{0,0},{4,2},{8,1},{12,3},{16,4},{20,6},{24,5},{28,7},{1,8},{5,10},... | collective-permute-start | bytes 688136 | tf_op jit(solution)/shard_map/ppermute | solution.py:395

commit v4 on v3

--- a/solution.py
+++ b/solution.py
@@ -50,9 +50,12 @@
     )(*args[:n_smem], *[in_hbm(x) for x in args[n_smem:]])
 
 
-def order_kernel(pos_ref, t0, t1, t2, t3, out_ref):
-    for shift, block in enumerate((t0, t1, t2, t3)):
-        out_ref[lax.rem(pos_ref[0] + 4 - shift, 4)] = block[...]
+def order_kernel(pos_ref, *refs):
+    out_ref = refs[8]
+    for shift in range(4):
+        slot = lax.rem(pos_ref[0] + 4 - shift, 4)
+        out_ref[slot, 0:128, :] = refs[2 * shift][...]
+        out_ref[slot, 128:256, :] = refs[2 * shift + 1][...]
 
 
 def project_kernel(pos_ref, t_ref, *refs):
@@ -102,7 +105,7 @@
             keep_ref[slot] = grouped[p * 16 : (p + 1) * 16, :]
 
 
-def slot_kernel(pos_ref, owner_ref, rec_ref, keep_ref, state_ref, norm_ref, send_ref, own_ref, buf, both_ref):
+def slot_kernel(pos_ref, owner_ref, rec_ref, keep_ref, state_ref, norm_ref, send_ref, own_ref, buf):
     me = pos_ref[2]
     step = pl.program_id(0)
 
@@ -135,47 +138,51 @@
     b_at = (f - 17) & 15
     live_a = (f >= 1) & (f < 273)
     live_b = (f >= 17) & (f < 273)
-    high, low = [], []
+    r, c = iota((128, 16), 0), iota((128, 16), 1)
+    den_lane = iota((128, 32), 1)
+    phis, dens = [], []
     for t in range(2):
+        tile = jnp.zeros((128, 32), F32)
         for h in range(2):
             base = t * 32 + h * 16
             left = dot(q, onehot(live_a & (row == a_at + base))) + unit_a
             right = dot(q, onehot(live_b & (row == b_at + base))) + unit_b
-            one, two = split(left * right * scale)
-            high.append(one)
-            low.append(two)
-    out_lane = iota((16, 256), 1)
-    first_head = (out_lane < 112) | (out_lane == 224) | (out_lane == 226)
+            phi = left * right * scale
+            norm = dot(onehot(2 * lax.shift_right_logical(r, 4) + h == c), norm_ref[...])
+            den = jnp.sum(phi * norm, axis=1, keepdims=True)
+            rough = den.astype(BF).astype(F32)
+            tile = jnp.where(den_lane == h, rough, jnp.where(den_lane == h + 2, den - rough, tile))
+            phis.append(phi.astype(BF))
+        dens.append(tile.astype(BF))
+    first_head = iota((16, 224), 1) < 112
     for i in range(8):
-        phi = jnp.concatenate([x[i * 16 : (i + 1) * 16, 0:273] for x in high + low], axis=0)
-        both_ref[:, 0:224] = state_ref[i]
-        both_ref[:, 224:256] = norm_ref[i]
-        both = dot(phi, both_ref[...])
-        terms = both[0:64] + both[64:128]
-        results = []
-        for t in range(2):
-            r = jnp.where(first_head, terms[t * 32 : t * 32 + 16], terms[t * 32 + 16 : t * 32 + 32])
-            rough = r.astype(BF).astype(F32)
-            results.append(jnp.where(out_lane >= 226, r - rough, r).astype(BF))
+        at = slice(i * 16, (i + 1) * 16)
+        phi = jnp.concatenate([x[at, 0:273] for x in phis], axis=0)
+        terms = dot(phi, state_ref[i])
+        results = [
+            jnp.where(first_head, terms[t * 32 : t * 32 + 16], terms[t * 32 + 16 : t * 32 + 32]).astype(BF) for t in range(2)
+        ]
         slot = step * 8 + i
         owner = owner_ref[slot]
 
         @pl.when(owner != me)
         def _():
-            send_ref[owner, :, 0:256] = results[0]
-            send_ref[owner, :, 256:512] = results[1]
+            for t in range(2):
+                send_ref[owner, :, t * 256 : t * 256 + 224] = results[t]
+                send_ref[owner, :, t * 256 + 224 : t * 256 + 256] = dens[t][at]
 
         @pl.when(owner == me)
         def _():
-            own_ref[slot, :, 0:256] = results[0]
-            own_ref[slot, :, 256:512] = results[1]
+            for t in range(2):
+                own_ref[slot, :, t * 256 : t * 256 + 224] = results[t]
+                own_ref[slot, :, t * 256 + 224 : t * 256 + 256] = dens[t][at]
 
 
 def kappa(s):
     return 1.0 + s + 0.5 * s * s
 
 
-def tail_kernel(pos_ref, own_ref, rec_ref, tk_ref, tv_ref, len_ref, num_ref, den_ref):
+def tail_kernel(pos_ref, own_ref, rec_ref, tk_ref, tv_ref, len_ref, num_ref):
     core = pos_ref[1]
     r, c = iota((256, 256), 0), iota((256, 256), 1)
     expand_q = onehot((r >= 224) & (r - 224 == lax.shift_right_logical(c, 7) * 16 + (c & 15)))
@@ -195,7 +202,8 @@
         )
     )
     r, c = iota((128, 256), 0), iota((128, 256), 1)
-    spread = onehot((r < 16) & (c < 224) & ((c >= 112) == (r >= 8)))
+    den_at = onehot((r < 16) & (c == 224 + lax.shift_right_logical(r, 3)))
+    den_new = onehot((r < 2) & (c == 224 + r))
     spread_new = onehot((r < 2) & (c < 224) & ((c >= 112) == (r >= 1)))
     head_lane = iota((256, 128), 1)
     for e, ref in enumerate((own_ref, rec_ref)):
@@ -212,22 +220,19 @@
             weight = kappa((dot(one, sum_a) + dot(two, sum_a)) * 0.25)
             weight = jnp.where(live, weight, 0.0)
             one, two = split(weight)
-            den = dot(one, spread) + dot(two, spread)
             terms = dot(one, expand_w).astype(BF) * values
-            num = dot(terms, sum_v)
+            num = dot(terms, sum_v) + (dot(one, den_at) + dot(two, den_at))
             query = dot(vq, pick_q)
             for i in range(t + 1):
                 one, two = split(query * new_keys[i])
                 weight = kappa((dot(one, sum_new) + dot(two, sum_new)) * 0.25)
                 one, two = split(weight)
-                high = dot(one, spread_new)
-                den = den + high + dot(two, spread_new)
-                num = num + high * ref[i * 256 : (i + 1) * 256, 0:256].astype(F32)
+                num = num + dot(one, spread_new) * ref[i * 256 : (i + 1) * 256, 0:256].astype(F32)
+                num = num + (dot(one, den_new) + dot(two, den_new))
             num_ref[e, t * 256 : (t + 1) * 256, :] = num
-            den_ref[e, t * 256 : (t + 1) * 256, :] = den
-
-
-def combine_kernel(pos_ref, g_ref, s_ref, num_ref, den_ref, rec_ref, own_ref, place_ref, out_ref, buf):
+
+
+def combine_kernel(pos_ref, g_ref, s_ref, num_ref, rec_ref, own_ref, place_ref, out_ref, buf):
     core = pos_ref[1]
     me = pos_ref[2]
     for p in range(32):
@@ -250,27 +255,28 @@
         hot = onehot(iota((256, 512), 1) == place_ref[pl.ds(at, 256), :])
         prompt = dot(hot, buf[...])
         for t in range(2):
-            part = prompt[:, t * 256 : (t + 1) * 256]
-            den = den_ref[e, t * 256 : (t + 1) * 256, :] + dot(part.astype(BF), spread)
-            num = num_ref[e, t * 256 : (t + 1) * 256, :] + part
+            num = num_ref[e, t * 256 : (t + 1) * 256, :] + prompt[:, t * 256 : (t + 1) * 256]
+            one, two = split(num)
+            den = dot(one, spread) + dot(two, spread)
             out = jnp.where(lane < 224, num / jnp.where(lane < 224, den, 1.0), 0.0)
             out = out.astype(BF)
             for part in range(2):
                 out_ref[half * 2 + part, t * 128 : (t + 1) * 128, :] = out[part * 128 : (part + 1) * 128]
 
 
-def out_kernel(pos_ref, own_ref, oth_ref, w0, w1, w3, far_1, far_3, first_ref, second_ref, far):
+def out_kernel(pos_ref, own_ref, oth_ref, *refs):
+    parts, first_ref, second_ref, weights = refs[:8], refs[8], refs[9], refs[10]
     y, core, col = pos_ref[0], pos_ref[1], pos_ref[3]
     acc = [None, None]
-    far[0:2] = far_1[...]
-    far[2:4] = far_3[...]
-    for shift, w_ref in enumerate((w0, w1, far, w3)):
+    for shift in range(4):
+        weights[shift, 0:2] = parts[2 * shift][...]
+        weights[shift, 2:4] = parts[2 * shift + 1][...]
         j = lax.rem(y + 4 - shift, 4)
         for which, ref in enumerate((own_ref, oth_ref)):
             k = core if which == 0 else 1 - core
             heads = ref[j, :, 0:224]
             for e in range(2):
-                part = dot(heads, w_ref[jnp.bitwise_xor(2 * e + k, col)])
+                part = dot(heads, weights[shift, jnp.bitwise_xor(2 * e + k, col)])
                 acc[e] = part if acc[e] is None else acc[e] + part
     even = lax.rem(y, 2) == 0
     first_ref[...] = jnp.where(even, acc[0], acc[1]).astype(BF)
@@ -284,8 +290,14 @@
     def shifts(x, axis):
         return [x] + [lax.ppermute(x, axis, [(i, (i + s) % 4) for i in range(4)]) for s in range(1, 4)]
 
-    blocks = shifts(tokens.reshape(256, 896), "y")
-    blocks, w_out = lax.optimization_barrier((blocks, w_out))
+    def over_y(x, step):
+        return lax.ppermute(x, "y", [(i, (i + step) % 4) for i in range(4)])
+
+    top, low = tokens[:128].reshape(128, 896), tokens[128:].reshape(128, 896)
+    top_1, low_3 = over_y(top, 1), over_y(low, 3)
+    low_1, top_3 = over_y(low, 1), over_y(top, 3)
+    top_1, low_3, w_out = lax.optimization_barrier((top_1, low_3, w_out))
+    blocks = [top, low, top_1, low_1, over_y(top_1, 1), over_y(low_3, 3), top_3, low_3]
     value_w = jnp.moveaxis(w_value.reshape(2, 448, 112), 0, 1).reshape(448, 224)
     mine = shifts(jnp.concatenate([value_w, w_query, w_key], axis=1), "col")
     pieces = []
@@ -293,10 +305,7 @@
         perm = [(k * 4 + c, (c >> 1) * 4 + (s ^ (2 * (c & 1) + k))) for k in range(2) for c in range(4)]
         pieces.append(lax.ppermute(w_out, ("core", "col"), perm))
     blocks, mine = lax.optimization_barrier((blocks, mine))
-    pieces = jnp.stack(pieces)
-
-    def over_y(x, step):
-        return lax.ppermute(x, "y", [(i, (i + step) % 4) for i in range(4)])
+    pieces = [jnp.stack(pieces[:2]), jnp.stack(pieces[2:])]
 
     owner = slot_prompt // 32
     slots = jnp.arange(32, dtype=jnp.int32)
@@ -312,18 +321,19 @@
     index = jnp.arange(512)
     rank = jnp.sum(((prompt_of[None, :] == prompt_of[:, None]) & (index[None, :] < index[:, None])).astype(jnp.int32), axis=1)
     place = (prompt_of - me * 32) * 16 + rank
-    norms = jnp.concatenate([cached_norm, cached_norm, jnp.zeros((32, 273, 28), BF)], axis=2)
-    states = jnp.transpose(cached_state[0].reshape(273, 224, 32), (2, 0, 1))
+    norms = jnp.pad(jnp.transpose(cached_norm, (0, 2, 1)).reshape(64, 273), ((0, 0), (0, 111)))
+    states = cached_state[0].reshape(273, 224, 32)
 
     held = call(order_kernel, jax.ShapeDtypeStruct((4, 256, 896), BF), 1, pos, *blocks)
     theirs = [lax.ppermute(w, "core", [(0, 1), (1, 0)]) for w in mine]
     held = lax.all_to_all(held, "col", split_axis=0, concat_axis=0, tiled=True)
     held, states, norms = lax.optimization_barrier((held, states, norms))
+    states = jnp.transpose(states, (2, 0, 1))
     shape = jax.ShapeDtypeStruct((512, 288), BF)
     own, oth = call(project_kernel, (shape, shape), 1, pos, held, *mine, *theirs, scratch=[pltpu.VMEM((512, 288), BF)])
-    oth, pieces = lax.optimization_barrier((oth, pieces))
-    out_w1, out_w3 = over_y(pieces, 1), over_y(pieces, 3)
     rec = lax.ppermute(oth, "core", [(0, 1), (1, 0)])
+    rec, pieces = lax.optimization_barrier((rec, pieces))
+    out_w = [over_y(x, step) for step in (1, 3) for x in pieces]
 
     shape = jax.ShapeDtypeStruct((32, 16, 128), BF)
     q_send, q_keep = call(
@@ -339,9 +349,9 @@
         scratch=[pltpu.VMEM((512, 128), BF)],
     )
     q_rec = lax.all_to_all(q_send, ("req", "col"), split_axis=0, concat_axis=0, tiled=True)
-    q_rec, out_w1, out_w3 = lax.optimization_barrier((q_rec, out_w1, out_w3))
+    q_rec, out_w = lax.optimization_barrier((q_rec, out_w))
     shape = jax.ShapeDtypeStruct((2, 512, 256), F32)
-    num, den = call(tail_kernel, (shape, shape), 1, pos, own, rec, tail_keys, tail_values, tail_length[:, None])
+    num = call(tail_kernel, shape, 1, pos, own, rec, tail_keys, tail_values, tail_length[:, None])
     shape = jax.ShapeDtypeStruct((32, 16, 512), BF)
     whole = pl.BlockSpec((32, 16, 128), lambda i: (0, 0, 0))
     whole_out = pl.BlockSpec((32, 16, 512), lambda i: (0, 0, 0))
@@ -355,13 +365,13 @@
             whole,
             whole,
             pl.BlockSpec((8, 273, 224), lambda i: (i, 0, 0)),
-            pl.BlockSpec((8, 273, 32), lambda i: (i, 0, 0)),
+            pl.BlockSpec((16, 384), lambda i: (i, 0)),
         ],
         out_specs=(whole_out, whole_out),
-        scratch_shapes=[pltpu.VMEM((128, 128), BF), pltpu.VMEM((273, 256), BF)],
+        scratch_shapes=[pltpu.VMEM((128, 128), BF)],
         compiler_params=pltpu.CompilerParams(vmem_limit_bytes=VMEM_LIMIT),
     )(pos, owner, in_hbm(q_rec), in_hbm(q_keep), in_hbm(states), in_hbm(norms))
-    r_send, far_1, far_3 = lax.optimization_barrier((r_send, out_w1[:2], out_w3[2:]))
+    r_send, far_1, far_3 = lax.optimization_barrier((r_send, out_w[0], out_w[3]))
     far_1, far_3 = over_y(far_1, 1), over_y(far_3, 3)
     r_rec = lax.all_to_all(r_send, ("req", "col"), split_axis=0, concat_axis=0, tiled=True)
     r_rec, far_1, far_3 = lax.optimization_barrier((r_rec, far_1, far_3))
@@ -373,7 +383,6 @@
         at_holder,
         at_slot,
         num,
-        den,
         r_rec,
         r_keep,
         place[:, None],
@@ -382,7 +391,7 @@
     heads = lax.all_to_all(heads, "y", split_axis=0, concat_axis=0, tiled=True)
     heads_oth = lax.ppermute(heads, "core", [(0, 1), (1, 0)])
     shape = jax.ShapeDtypeStruct((256, 448), BF)
-    mixed = call(out_kernel, (shape, shape), 1, pos, heads, heads_oth, pieces, out_w1, out_w3, far_1, far_3, scratch=[pltpu.VMEM((4, 224, 448), BF)])
+    mixed = call(out_kernel, (shape, shape), 1, pos, heads, heads_oth, *pieces, out_w[0], out_w[1], far_1, far_3, out_w[2], out_w[3], scratch=[pltpu.VMEM((4, 4, 224, 448), BF)])
 
     def at(y, core, col):
         return (y * 2 + core) * 4 + col

time: 192 us -> 188 us (0.979)
  starting transfers between devices: 68.9 us -> 80 us
  waiting for transfers between devices: 29.9 us -> 19.7 us
  local copies, waits for them, and re-layouts: 31.9 us -> 28.8 us
  Pallas kernels: 42 us -> 39.5 us
  other arithmetic: 5.97 us -> 4.03 us
    another operation x1 -> x0, local copies, waits for them, and re-layouts: 8.43 us -> none  [body(): states = jnp.transpose(cached_state[0].reshape(273, 224, 32), (2, 0, 1))]
    all_to_all x1, starting transfers between devices: 4.89 us -> 10.6 us  [body(): lax.all_to_all(q_send, ('req', 'col'), split_axis=0, concat_axis=0, tiled...]
    optimization_barrier x1, local copies, waits for them, and re-layouts: 2.83 us -> 8.35 us  [body(): held, states, norms = lax.optimization_barrier((held, states, norms))]
    all_to_all x1, waiting for transfers between devices: 6.52 us -> 1.04 us  [body(): lax.all_to_all(q_send, ('req', 'col'), split_axis=0, concat_axis=0, tiled...]
    ppermute x6 -> x3, starting transfers between devices: 10.5 us -> 5.58 us  [shifts(): lax.ppermute(x, axis, [(i, (i + s) % 4) for i in range(4)])]
    all_to_all x1, starting transfers between devices: 3.9 us -> 8.25 us  [body(): lax.all_to_all(r_send, ('req', 'col'), split_axis=0, concat_axis=0, tiled...]
    pallas_call x1, Pallas kernels: 14.3 us -> 11.7 us  [body(): pl.pallas_call(slot_kernel, grid=(4,), out_shape=(pltpu.HBM(shape.shape,...]
    all_to_all x1, waiting for transfers between devices: 4.28 us -> 1.83 us  [body(): lax.all_to_all(r_send, ('req', 'col'), split_axis=0, concat_axis=0, tiled...]
  transfers between devices with their start and end apart: 26 -> 31, of which waited for: 14 -> 10; matrix products, arithmetic and copies ran while one was open for 15% -> 15% of each run, Pallas kernels for 7% -> 11%
where the time goes in v4:
time: 188 us; the launch traced here: 184 us
  starting transfers between devices  80 us (43%)
  Pallas kernels  39.5 us (21%)
  local copies, waits for them, and re-layouts  28.8 us (15%)
  waiting for transfers between devices  19.7 us (10%)
  blocking collectives  11.8 us (6%)
  other arithmetic  4.03 us (2%)
    pallas_call x6, Pallas kernels, call(): pl.pallas_call(kernel, grid=(1,), out_shape=jax.tree.map(lambda x: pltpu....  27.8 us
    ppermute x12, starting transfers between devices, over_y(): return lax.ppermute(x, 'y', [(i, (i + step) % 4) for i in range(4)])  13.6 us
    unnamed x61, local copies, waits for them, and re-layouts  12.1 us
    all_to_all x1, blocking collectives, body(): heads = lax.all_to_all(heads, 'y', split_axis=0, concat_axis=0, tiled=True)  11.8 us
    pallas_call x1, Pallas kernels, body(): pl.pallas_call(slot_kernel, grid=(4,), out_shape=(pltpu.HBM(shape.shape,...  11.7 us
    ppermute x4, starting transfers between devices, body(): pieces.append(lax.ppermute(w_out, ('core', 'col'), perm))  11.5 us
    all_to_all x1, starting transfers between devices, body(): lax.all_to_all(q_send, ('req', 'col'), split_axis=0, concat_axis=0, tiled...  10.6 us
    all_to_all x1, starting transfers between devices, body(): lax.all_to_all(code[:, None], ('req', 'col'), split_axis=0, concat_axis=0...  9.53 us
  transfers between devices with their start and end apart: 31, of which 10 were waited for; matrix products, arithmetic and copies ran while one was open for 15% of the time, Pallas kernels for 11%

profile of v4, /device:TPU:9, one launch (start us, length us, event | category | flops | bytes accessed | tf_op | source)
XLA Modules:
  0.0 184.3 jit_solution(11936045315093713542)
XLA Ops:
  0.0 1.1 fusion.8
  1.4 1.5 collective-permute-start.2
  3.0 1.4 collective-permute-start
  4.4 0.2 collective-permute-start.5
  4.6 1.2 reshape.76
  5.8 0.2 copy.84
  6.2 0.9 copy.73
  7.1 0.9 copy.74
  8.2 1.3 collective-permute-start.6
  9.5 4.0 %collective-permute-done.refs_2_ = bf16[128,896]{1,0:T(8,128)(2,1)S(1)} collective-permute-done((bf16[128,896]{1,0:T(8,128)(2,1)S(1)}, bf16[128,896]{1,0:T(8,128)(2,1)S(1)}, u32[]{:S(2)}, u32[]{:S(2)}) %collective-permute-start) | collective-permute-done | bytes 229408 | tf_op jit(solution)/shard_map/ppermute | solution.py:294
  13.5 3.4 %collective-permute-start.7 = (bf16[448,288]{1,0:T(8,128)(2,1)S(1)}, bf16[448,288]{1,0:T(8,128)(2,1)S(1)}, u32[]{:S(2)}, u32[]{:S(2)}) collective-permute-start(bf16[448,288]{1,0:T(8,128)(2,1)S(1)} %pad_maximum_fusion.2.refs_0_), channel_id=1, source_target_pairs={{0,2},{1,3},{2,0},{3,1},{4,6},{5,7},{6,4},{7,5},{8,10},{9,11},{10,... | collective-permute-start | bytes 774152 | tf_op jit(solution)/shard_map/ppermute | solution.py:291
  16.9 0.9 collective-permute-start.8
  17.8 2.4 %collective-permute-start.4 = (bf16[128,896]{1,0:T(8,128)(2,1)S(1)}, bf16[128,896]{1,0:T(8,128)(2,1)S(1)}, u32[]{:S(2)}, u32[]{:S(2)}) collective-permute-start(bf16[128,896]{1,0:T(8,128)(2,1)S(1)} %collective-permute-done.1.refs_7_), channel_id=1, source_target_pairs={{0,24},{8,0},{16,8},{24,16},{1,25},{9,1},{17,9},{25,17},{2,26},{10... | collective-permute-start | bytes 688136 | tf_op jit(solution)/shard_map/ppermute | solution.py:294
  20.4 0.7 copy.67
  21.1 9.5 %all-to-all-start = ((s32[32,1,1]{2,1,0:T(1,128)}), s32[32,1,1]{2,1,0:T(1,128)S(1)}, u32[]{:S(2)}, u32[]{:S(2)}) async-start(s32[32,1,1]{2,1,0:T(1,128)} %copy.67), calls=%async_computation | async-start | bytes 32768 | tf_op jit(solution)/shard_map/all_to_all | solution.py:316
  30.7 1.4 collective-permute-done.8.refs_3_
  32.1 1.0 copy.75.refs_0_
  33.2 0.8 copy.76.refs_1_
  34.0 3.0 %shard_map.118 = bf16[4,256,896]{2,1,0:T(8,128)(2,1)} custom-call(s32[4]{0:T(128)S(1)} %pad_add_fusion.pos_ref, bf16[128,896]{1,0:T(8,128)(2,1)} %copy.75.refs_0_, bf16[128,896]{1,0:T(8,128)(2,1)} %copy.76.refs_1_, bf16[128,896]{1,0:T(8,128)(2,1)} %copy-done.21, bf16[128,896]{1,0:T(8,128)(2,1)} %copy-done.20, bf16[128,896]{1,0:T(8,128)(2,1)} %copy-done.22, ...), custom_call_target="tpu_custom_call" | custom-call | tf_op jit(solution)/shard_map/pallas_call | solution.py:42
  37.0 2.2 %all-to-all-done = s32[32,1,1]{2,1,0:T(1,128)S(1)} async-done(((s32[32,1,1]{2,1,0:T(1,128)}), s32[32,1,1]{2,1,0:T(1,128)S(1)}, u32[]{:S(2)}, u32[]{:S(2)}) %all-to-all-start) | async-done | bytes 160 | tf_op jit(solution)/shard_map/all_to_all | solution.py:316
  39.2 3.6 %all-to-all-start.1 = ((bf16[4,256,896]{2,1,0:T(8,128)(2,1)}), bf16[4,256,896]{2,1,0:T(8,128)(2,1)S(1)}, u32[]{:S(2)}, u32[]{:S(2)}) async-start(bf16[4,256,896]{2,1,0:T(8,128)(2,1)} %shard_map.118), calls=%async_computation.1 | async-start | bytes 3670016 | tf_op jit(solution)/shard_map/all_to_all | solution.py:329
  42.8 7.3 %copy.77 = bf16[1,273,7168]{1,2,0:T(8,128)(2,1)} copy(bf16[1,273,7168]{2,1,0:T(8,128)(2,1)} %param.17) | data formatting | bytes 7827456 | tf_op args[5]
  50.2 0.6 pad.4.norm_ref
  51.2 0.2 convert_reduce_fusion
  51.5 0.6 multiply_add_fusion
  52.0 4.1 %collective-permute-start.10 = (bf16[448,288]{1,0:T(8,128)(2,1)S(1)}, bf16[448,288]{1,0:T(8,128)(2,1)S(1)}, u32[]{:S(2)}, u32[]{:S(2)}) collective-permute-start(bf16[448,288]{1,0:T(8,128)(2,1)S(1)} %collective-permute-done.6.refs_1_), channel_id=1, source_target_pairs={{0,4},{4,0},{1,5},{5,1},{2,6},{6,2},{3,7},{7,3},{8,12},{12,8},{9,1... | collective-permute-start | bytes 774152 | tf_op jit(solution)/shard_map/ppermute | solution.py:328
  56.2 0.7 add_reduce_fusion
  56.9 0.5 collective-permute-start.12
  57.4 0.3 collective-permute-start.9
  57.7 3.7 %collective-permute-start.14 = (bf16[224,448]{1,0:T(8,128)(2,1)}, bf16[224,448]{1,0:T(8,128)(2,1)S(1)}, u32[]{:S(2)}, u32[]{:S(2)}) collective-permute-start(bf16[224,448]{1,0:T(8,128)(2,1)} %param.16), channel_id=1, source_target_pairs={{0,0},{1,2},{2,4},{3,6},{4,1},{5,3},{6,5},{7,7},{8,8},{9,10},{10,1... | collective-permute-start | bytes 602120 | tf_op jit(solution)/shard_map/ppermute | solution.py:306
  61.5 0.6 copy-done.18
  62.2 0.7 compare_reduce_fusion
  62.8 5.8 %collective-permute-start.16 = (bf16[224,448]{1,0:T(8,128)(2,1)}, bf16[224,448]{1,0:T(8,128)(2,1)S(1)}, u32[]{:S(2)}, u32[]{:S(2)}) collective-permute-start(bf16[224,448]{1,0:T(8,128)(2,1)} %param.16), channel_id=1, source_target_pairs={{0,2},{1,0},{2,6},{3,4},{4,3},{5,1},{6,7},{7,5},{8,10},{9,8},{10,1... | collective-permute-start | bytes 602120 | tf_op jit(solution)/shard_map/ppermute | solution.py:306
  68.6 1.9 %collective-permute-start.17 = (bf16[224,448]{1,0:T(8,128)(2,1)}, bf16[224,448]{1,0:T(8,128)(2,1)S(1)}, u32[]{:S(2)}, u32[]{:S(2)}) collective-permute-start(bf16[224,448]{1,0:T(8,128)(2,1)} %param.16), channel_id=1, source_target_pairs={{0,3},{1,1},{2,7},{3,5},{4,2},{5,0},{6,6},{7,4},{8,11},{9,9},{10,1... | collective-permute-start | bytes 602120 | tf_op jit(solution)/shard_map/ppermute | solution.py:306
  70.5 5.4 %shard_map.119 = (bf16[512,288]{1,0:T(8,128)(2,1)}, bf16[512,288]{1,0:T(8,128)(2,1)}) custom-call(s32[4]{0:T(128)S(1)} %pad_add_fusion.pos_ref, bf16[4,256,896]{2,1,0:T(8,128)(2,1)} %copy-done, bf16[448,288]{1,0:T(8,128)(2,1)} %copy-done.7, bf16[448,288]{1,0:T(8,128)(2,1)} %copy-done.15, bf16[448,288]{1,0:T(8,128)(2,1)} %copy-done.16, ...), custom_call_target="tpu_custom_call" | custom-call | tf_op jit(solution)/shard_map/pallas_call | solution.py:42
  76.0 0.4 collective-permute-start.13
  76.8 1.1 collective-permute-done.13.rec_ref
  78.0 2.3 %collective-permute-start.20 = (bf16[2,224,448]{2,1,0:T(8,128)(2,1)S(1)}, bf16[2,224,448]{2,1,0:T(8,128)(2,1)S(1)}, u32[]{:S(2)}, u32[]{:S(2)}) collective-permute-start(bf16[2,224,448]{2,1,0:T(8,128)(2,1)S(1)} %pad_maximum_fusion.refs_0_), channel_id=1, source_target_pairs={{0,24},{8,0},{16,8},{24,16},{1,25},{9,1},{17,9},{25,17},{2,26},{10... | collective-permute-start | bytes 1204232 | tf_op jit(solution)/shard_map/ppermute | solution.py:294
  80.3 2.7 %collective-permute-start.21 = (bf16[2,224,448]{2,1,0:T(8,128)(2,1)S(1)}, bf16[2,224,448]{2,1,0:T(8,128)(2,1)}, u32[]{:S(2)}, u32[]{:S(2)}) collective-permute-start(bf16[2,224,448]{2,1,0:T(8,128)(2,1)S(1)} %pad_maximum_fusion.1.refs_1_), channel_id=1, source_target_pairs={{0,24},{8,0},{16,8},{24,16},{1,25},{9,1},{17,9},{25,17},{2,26},{10... | collective-permute-start | bytes 1204232 | tf_op jit(solution)/shard_map/ppermute | solution.py:294
  82.9 2.7 %shard_map.121 = (bf16[32,16,128]{2,1,0:T(8,128)(2,1)}, bf16[32,16,128]{2,1,0:T(8,128)(2,1)}) custom-call(s32[4]{0:T(128)S(1)} %pad_add_fusion.pos_ref, s32[32]{0:T(128)S(1)} %broadcast_select_fusion.2.g_ref, s32[32]{0:T(128)S(1)} %fusion.2.s_ref, bf16[512,288]{1,0:T(8,128)(2,1)} %get-tuple-element.60.own_ref, bf16[512,288]{1,0:T(8,128)(2,1)} %copy-done.6, ...), custom_call_target="tpu_custom_call" | custom-call | tf_op jit(solution)/shard_map/pallas_call | solution.py:42
  85.7 10.6 %all-to-all-start.2 = ((bf16[32,16,128]{2,1,0:T(8,128)(2,1)}), bf16[32,16,128]{2,1,0:T(8,128)(2,1)S(1)}, u32[]{:S(2)}, u32[]{:S(2)}) async-start(bf16[32,16,128]{2,1,0:T(8,128)(2,1)} %get-tuple-element.64), calls=%async_computation.2 | async-start | bytes 262144 | tf_op jit(solution)/shard_map/all_to_all | solution.py:351
  96.3 8.3 %copy.79 = bf16[273,224,32]{1,0,2:T(8,128)(2,1)} copy(bf16[273,224,32]{0,2,1:T(8,128)(2,1)} %bitcast.26) | data formatting | bytes 7827456 | tf_op jit(solution)/shard_map/optimization_barrier | solution.py:330
  104.7 1.0 all-to-all-done.2.rec_ref
  105.8 0.6 copy-done.9
  106.4 11.7 %shard_map.122 = (bf16[32,16,512]{2,1,0:T(8,128)(2,1)}, bf16[32,16,512]{2,1,0:T(8,128)(2,1)}) custom-call(s32[4]{0:T(128)S(1)} %pad_add_fusion.pos_ref, s32[32]{0:T(128)S(1)} %get-tuple-element.86.owner_ref, bf16[32,16,128]{2,1,0:T(8,128)(2,1)} %copy-done.9, bf16[32,16,128]{2,1,0:T(8,128)(2,1)} %get-tuple-element.68.keep_ref, ...), custom_call_target="tpu_custom_call" | custom-call | tf_op jit(solution)/shard_map/pallas_call | solution.py:358
  118.1 8.3 %all-to-all-start.3 = ((bf16[32,16,512]{2,1,0:T(8,128)(2,1)}), bf16[32,16,512]{2,1,0:T(8,128)(2,1)S(1)}, u32[]{:S(2)}, u32[]{:S(2)}) async-start(bf16[32,16,512]{2,1,0:T(8,128)(2,1)} %get-tuple-element.74), calls=%async_computation.3 | async-start | bytes 1048576 | tf_op jit(solution)/shard_map/all_to_all | solution.py:376
  126.4 0.3 collective-permute-start.22
  126.7 2.8 %collective-permute-start.23 = (bf16[2,224,448]{2,1,0:T(8,128)(2,1)}, bf16[2,224,448]{2,1,0:T(8,128)(2,1)S(1)}, u32[]{:S(2)}, u32[]{:S(2)}) collective-permute-start(bf16[2,224,448]{2,1,0:T(8,128)(2,1)} %collective-permute-done.21.refs_7_), channel_id=1, source_target_pairs={{0,24},{8,0},{16,8},{24,16},{1,25},{9,1},{17,9},{25,17},{2,26},{10... | collective-permute-start | bytes 1204232 | tf_op jit(solution)/shard_map/ppermute | solution.py:294
  129.5 0.9 copy.78.len_ref
  130.4 0.9 copy.80.place_ref
  131.2 8.4 %shard_map.120.num_ref = f32[2,512,256]{2,1,0:T(8,128)} custom-call(s32[4]{0:T(128)S(1)} %pad_add_fusion.pos_ref, bf16[512,288]{1,0:T(8,128)(2,1)} %get-tuple-element.60.own_ref, bf16[512,288]{1,0:T(8,128)(2,1)} %copy-done.6, bf16[512,256]{1,0:T(8,128)(2,1)} %tk_ref.1, bf16[512,1792]{1,0:T(8,128)(2,1)} %tv_ref.1, s32[512,1]{1,0:T(8,128)} %copy.78.len_ref), custom_call_target="tpu_custom_call" | custom-call | tf_op jit(solution)/shard_map/pallas_call | solution.py:42
  139.7 1.8 all-to-all-done.3.rec_ref
  141.5 0.8 copy-done.2
  142.3 3.7 %shard_map.123 = bf16[4,256,256]{2,1,0:T(8,128)(2,1)} custom-call(s32[4]{0:T(128)S(1)} %pad_add_fusion.pos_ref, s32[32]{0:T(128)S(1)} %broadcast_select_fusion.2.g_ref, s32[32]{0:T(128)S(1)} %fusion.2.s_ref, f32[2,512,256]{2,1,0:T(8,128)} %shard_map.120.num_ref, bf16[32,16,512]{2,1,0:T(8,128)(2,1)} %copy-done.2, ...), custom_call_target="tpu_custom_call" | custom-call | tf_op jit(solution)/shard_map/pallas_call | solution.py:42
  146.0 11.8 %all_to_all.29.own_ref = bf16[4,256,256]{2,1,0:T(8,128)(2,1)S(1)} all-to-all(bf16[4,256,256]{2,1,0:T(8,128)(2,1)} %shard_map.123), channel_id=1, replica_groups=mesh['req'=8,'y'=4,'core'=2,'col'=4] {'y'}, dimensions={0} | all-to-all | bytes 1048576 | tf_op jit(solution)/shard_map/all_to_all | solution.py:391
  157.8 5.1 %collective-permute-start.24 = (bf16[4,256,256]{2,1,0:T(8,128)(2,1)S(1)}, bf16[4,256,256]{2,1,0:T(8,128)(2,1)S(1)}, u32[]{:S(2)}, u32[]{:S(2)}) collective-permute-start(bf16[4,256,256]{2,1,0:T(8,128)(2,1)S(1)} %all_to_all.29.own_ref), channel_id=1, source_target_pairs={{0,4},{4,0},{1,5},{5,1},{2,6},{6,2},{3,7},{7,3},{8,12},{12,8},{9,1... | collective-permute-start | bytes 1572872 | tf_op jit(solution)/shard_map/ppermute | solution.py:392
  162.9 1.5 collective-permute-done.24.oth_ref
  164.5 0.8 copy-done.8
  165.3 4.5 %shard_map.124 = (bf16[256,448]{1,0:T(8,128)(2,1)}, bf16[256,448]{1,0:T(8,128)(2,1)}) custom-call(s32[4]{0:T(128)S(1)} %pad_add_fusion.pos_ref, bf16[4,256,256]{2,1,0:T(8,128)(2,1)} %copy-done.1, bf16[4,256,256]{2,1,0:T(8,128)(2,1)} %copy-done.8, bf16[2,224,448]{2,1,0:T(8,128)(2,1)} %copy-done.3, bf16[2,224,448]{2,1,0:T(8,128)(2,1)} %copy-done.4, ...), custom_call_target="tpu_custom_call" | custom-call | tf_op jit(solution)/shard_map/pallas_call | solution.py:42
  169.8 3.1 %collective-permute-start.25 = (bf16[256,448]{1,0:T(8,128)(2,1)}, bf16[256,448]{1,0:T(8,128)(2,1)S(1)}, u32[]{:S(2)}, u32[]{:S(2)}) collective-permute-start(bf16[256,448]{1,0:T(8,128)(2,1)} %get-tuple-element.83), channel_id=1, source_target_pairs={{0,1},{4,3},{8,0},{12,2},{16,5},{20,7},{24,4},{28,6},{1,9},{5,11},... | collective-permute-start | bytes 688136 | tf_op jit(solution)/shard_map/ppermute | solution.py:404
  172.9 3.7 %collective-permute-start.26 = (bf16[256,448]{1,0:T(8,128)(2,1)}, bf16[256,448]{1,0:T(8,128)(2,1)S(1)}, u32[]{:S(2)}, u32[]{:S(2)}) collective-permute-start(bf16[256,448]{1,0:T(8,128)(2,1)} %get-tuple-element.84), channel_id=1, source_target_pairs={{0,0},{4,2},{8,1},{12,3},{16,4},{20,6},{24,5},{28,7},{1,8},{5,10},... | collective-permute-start | bytes 688136 | tf_op jit(solution)/shard_map/ppermute | solution.py:404
  176.6 5.0 %collective-permute-done.25 = bf16[256,448]{1,0:T(8,128)(2,1)S(1)} collective-permute-done((bf16[256,448]{1,0:T(8,128)(2,1)}, bf16[256,448]{1,0:T(8,128)(2,1)S(1)}, u32[]{:S(2)}, u32[]{:S(2)}) %collective-permute-start.25) | collective-permute-done | bytes 229408 | tf_op jit(solution)/shard_map/ppermute | solution.py:404
  181.6 1.4 collective-permute-done.26
  183.4 0.9 fusion.1
  (102 shorter events, 2.5 us)
Async XLA Ops:
  0.0 9.5 %copy-start.28 = (s32[32]{0:T(128)S(1)}, s32[32]{0:T(128)}, u32[]{:S(2)}) copy-start(s32[32]{0:T(128)} %param.19) | copy-start | bytes 388
  1.3 15.7 %collective-permute-start.1 = (bf16[128,896]{1,0:T(8,128)(2,1)S(1)}, bf16[128,896]{1,0:T(8,128)(2,1)S(1)}, u32[]{:S(2)}, u32[]{:S(2)}) collective-permute-start(bf16[128,896]{1,0:T(8,128)(2,1)S(1)} %copy.69), channel_id=1, source_target_pairs={{0,24},{8,0},{16,8},{24,16},{1,25},{9,1},{17,9},{25,17},{2,26},{10... | collective-permute-start | bytes 688136 | tf_op jit(solution)/shard_map/ppermute | solution.py:294
  1.4 16.4 %collective-permute-start.2 = (bf16[128,896]{1,0:T(8,128)(2,1)S(1)}, bf16[128,896]{1,0:T(8,128)(2,1)S(1)}, u32[]{:S(2)}, u32[]{:S(2)}) collective-permute-start(bf16[128,896]{1,0:T(8,128)(2,1)S(1)} %copy.69), channel_id=1, source_target_pairs={{0,8},{8,16},{16,24},{24,0},{1,9},{9,17},{17,25},{25,1},{2,10},{10... | collective-permute-start | bytes 688136 | tf_op jit(solution)/shard_map/ppermute | solution.py:294
  3.0 10.5 %collective-permute-start = (bf16[128,896]{1,0:T(8,128)(2,1)S(1)}, bf16[128,896]{1,0:T(8,128)(2,1)S(1)}, u32[]{:S(2)}, u32[]{:S(2)}) collective-permute-start(bf16[128,896]{1,0:T(8,128)(2,1)S(1)} %copy.68), channel_id=1, source_target_pairs={{0,8},{8,16},{16,24},{24,0},{1,9},{9,17},{17,25},{25,1},{2,10},{10... | collective-permute-start | bytes 688136 | tf_op jit(solution)/shard_map/ppermute | solution.py:294
  4.4 13.4 %collective-permute-start.5 = (bf16[128,896]{1,0:T(8,128)(2,1)S(1)}, bf16[128,896]{1,0:T(8,128)(2,1)}, u32[]{:S(2)}, u32[]{:S(2)}) collective-permute-start(bf16[128,896]{1,0:T(8,128)(2,1)S(1)} %copy.68), channel_id=1, source_target_pairs={{0,24},{8,0},{16,8},{24,16},{1,25},{9,1},{17,9},{25,17},{2,26},{10... | collective-permute-start | bytes 688136 | tf_op jit(solution)/shard_map/ppermute | solution.py:294
  8.2 49.2 %copy-start.7 = (bf16[448,288]{1,0:T(8,128)(2,1)}, bf16[448,288]{1,0:T(8,128)(2,1)S(1)}, u32[]{:S(2)}) copy-start(bf16[448,288]{1,0:T(8,128)(2,1)S(1)} %pad_maximum_fusion.2.refs_0_) | copy-start | bytes 774148
  8.2 22.5 %collective-permute-start.6 = (bf16[448,288]{1,0:T(8,128)(2,1)S(1)}, bf16[448,288]{1,0:T(8,128)(2,1)S(1)}, u32[]{:S(2)}, u32[]{:S(2)}) collective-permute-start(bf16[448,288]{1,0:T(8,128)(2,1)S(1)} %pad_maximum_fusion.2.refs_0_), channel_id=1, source_target_pairs={{0,1},{1,2},{2,3},{3,0},{4,5},{5,6},{6,7},{7,4},{8,9},{9,10},{10,1... | collective-permute-start | bytes 774152 | tf_op jit(solution)/shard_map/ppermute | solution.py:291
  13.5 20.5 %copy-start.21 = (bf16[128,896]{1,0:T(8,128)(2,1)}, bf16[128,896]{1,0:T(8,128)(2,1)S(1)}, u32[]{:S(2)}) copy-start(bf16[128,896]{1,0:T(8,128)(2,1)S(1)} %collective-permute-done.refs_2_) | copy-start | bytes 688132
  13.5 17.2 %collective-permute-start.7 = (bf16[448,288]{1,0:T(8,128)(2,1)S(1)}, bf16[448,288]{1,0:T(8,128)(2,1)S(1)}, u32[]{:S(2)}, u32[]{:S(2)}) collective-permute-start(bf16[448,288]{1,0:T(8,128)(2,1)S(1)} %pad_maximum_fusion.2.refs_0_), channel_id=1, source_target_pairs={{0,2},{1,3},{2,0},{3,1},{4,6},{5,7},{6,4},{7,5},{8,10},{9,11},{10,... | collective-permute-start | bytes 774152 | tf_op jit(solution)/shard_map/ppermute | solution.py:291
  16.9 17.1 %copy-start.19 = (bf16[128,896]{1,0:T(8,128)(2,1)}, bf16[128,896]{1,0:T(8,128)(2,1)S(1)}, u32[]{:S(2)}) copy-start(bf16[128,896]{1,0:T(8,128)(2,1)S(1)} %collective-permute-done.1.refs_7_) | copy-start | bytes 688132
  16.9 15.2 %collective-permute-start.8 = (bf16[448,288]{1,0:T(8,128)(2,1)S(1)}, bf16[448,288]{1,0:T(8,128)(2,1)S(1)}, u32[]{:S(2)}, u32[]{:S(2)}) collective-permute-start(bf16[448,288]{1,0:T(8,128)(2,1)S(1)} %pad_maximum_fusion.2.refs_0_), channel_id=1, source_target_pairs={{0,3},{1,0},{2,1},{3,2},{4,7},{5,4},{6,5},{7,6},{8,11},{9,8},{10,9... | collective-permute-start | bytes 774152 | tf_op jit(solution)/shard_map/ppermute | solution.py:291
  17.8 16.2 %copy-start.20 = (bf16[128,896]{1,0:T(8,128)(2,1)}, bf16[128,896]{1,0:T(8,128)(2,1)S(1)}, u32[]{:S(2)}) copy-start(bf16[128,896]{1,0:T(8,128)(2,1)S(1)} %collective-permute-done.2.refs_3_) | copy-start | bytes 688132
  17.8 14.3 %collective-permute-start.3 = (bf16[128,896]{1,0:T(8,128)(2,1)S(1)}, bf16[128,896]{1,0:T(8,128)(2,1)S(1)}, u32[]{:S(2)}, u32[]{:S(2)}) collective-permute-start(bf16[128,896]{1,0:T(8,128)(2,1)S(1)} %collective-permute-done.refs_2_), channel_id=1, source_target_pairs={{0,8},{8,16},{16,24},{24,0},{1,9},{9,17},{17,25},{25,1},{2,10},{10... | collective-permute-start | bytes 688136 | tf_op jit(solution)/shard_map/ppermute | solution.py:294
  17.8 14.3 %collective-permute-start.4 = (bf16[128,896]{1,0:T(8,128)(2,1)S(1)}, bf16[128,896]{1,0:T(8,128)(2,1)S(1)}, u32[]{:S(2)}, u32[]{:S(2)}) collective-permute-start(bf16[128,896]{1,0:T(8,128)(2,1)S(1)} %collective-permute-done.1.refs_7_), channel_id=1, source_target_pairs={{0,24},{8,0},{16,8},{24,16},{1,25},{9,1},{17,9},{25,17},{2,26},{10... | collective-permute-start | bytes 688136 | tf_op jit(solution)/shard_map/ppermute | solution.py:294
  21.1 18.1 %all-to-all-start = ((s32[32,1,1]{2,1,0:T(1,128)}), s32[32,1,1]{2,1,0:T(1,128)S(1)}, u32[]{:S(2)}, u32[]{:S(2)}) async-start(s32[32,1,1]{2,1,0:T(1,128)} %copy.67), calls=%async_computation | async-start | bytes 32768 | tf_op jit(solution)/shard_map/all_to_all | solution.py:316
  30.7 21.3 %copy-start.15 = (bf16[448,288]{1,0:T(8,128)(2,1)}, bf16[448,288]{1,0:T(8,128)(2,1)S(1)}, u32[]{:S(2)}) copy-start(bf16[448,288]{1,0:T(8,128)(2,1)S(1)} %collective-permute-done.6.refs_1_) | copy-start | bytes 774148
  30.7 26.1 %copy-start.16 = (bf16[448,288]{1,0:T(8,128)(2,1)}, bf16[448,288]{1,0:T(8,128)(2,1)S(1)}, u32[]{:S(2)}) copy-start(bf16[448,288]{1,0:T(8,128)(2,1)S(1)} %collective-permute-done.7.refs_2_) | copy-start | bytes 774148
  32.1 24.8 %copy-start.17 = (bf16[448,288]{1,0:T(8,128)(2,1)}, bf16[448,288]{1,0:T(8,128)(2,1)S(1)}, u32[]{:S(2)}) copy-start(bf16[448,288]{1,0:T(8,128)(2,1)S(1)} %collective-permute-done.8.refs_3_) | copy-start | bytes 774148
  32.1 1.9 %copy-start.22 = (bf16[128,896]{1,0:T(8,128)(2,1)}, bf16[128,896]{1,0:T(8,128)(2,1)S(1)}, u32[]{:S(2)}) copy-start(bf16[128,896]{1,0:T(8,128)(2,1)S(1)} %collective-permute-done.3.refs_4_) | copy-start | bytes 688132
  32.1 1.9 %copy-start.23 = (bf16[128,896]{1,0:T(8,128)(2,1)}, bf16[128,896]{1,0:T(8,128)(2,1)S(1)}, u32[]{:S(2)}) copy-start(bf16[128,896]{1,0:T(8,128)(2,1)S(1)} %collective-permute-done.4.refs_5_) | copy-start | bytes 688132
  39.2 23.6 %all-to-all-start.1 = ((bf16[4,256,896]{2,1,0:T(8,128)(2,1)}), bf16[4,256,896]{2,1,0:T(8,128)(2,1)S(1)}, u32[]{:S(2)}, u32[]{:S(2)}) async-start(bf16[4,256,896]{2,1,0:T(8,128)(2,1)} %shard_map.118), calls=%async_computation.1 | async-start | bytes 3670016 | tf_op jit(solution)/shard_map/all_to_all | solution.py:329
  42.8 7.4 %copy-start.24 = (bf16[32,273,2]{1,2,0:T(2,128)(2,1)S(1)}, bf16[32,273,2]{1,2,0:T(2,128)(2,1)}, u32[]{:S(2)}) copy-start(bf16[32,273,2]{1,2,0:T(2,128)(2,1)} %param.18) | copy-start | bytes 104836
  42.8 8.4 %copy-start.26 = (s32[512]{0:T(512)S(1)}, s32[512]{0:T(512)}, u32[]{:S(2)}) copy-start(s32[512]{0:T(512)} %param.20) | copy-start | bytes 6148
  52.0 9.4 %collective-permute-start.10 = (bf16[448,288]{1,0:T(8,128)(2,1)S(1)}, bf16[448,288]{1,0:T(8,128)(2,1)S(1)}, u32[]{:S(2)}, u32[]{:S(2)}) collective-permute-start(bf16[448,288]{1,0:T(8,128)(2,1)S(1)} %collective-permute-done.6.refs_1_), channel_id=1, source_target_pairs={{0,4},{4,0},{1,5},{5,1},{2,6},{6,2},{3,7},{7,3},{8,12},{12,8},{9,1... | collective-permute-start | bytes 774152 | tf_op jit(solution)/shard_map/ppermute | solution.py:328
  56.8 6.0 %collective-permute-start.11 = (bf16[448,288]{1,0:T(8,128)(2,1)S(1)}, bf16[448,288]{1,0:T(8,128)(2,1)}, u32[]{:S(2)}, u32[]{:S(2)}) collective-permute-start(bf16[448,288]{1,0:T(8,128)(2,1)S(1)} %collective-permute-done.7.refs_2_), channel_id=1, source_target_pairs={{0,4},{4,0},{1,5},{5,1},{2,6},{6,2},{3,7},{7,3},{8,12},{12,8},{9,1... | collective-permute-start | bytes 774152 | tf_op jit(solution)/shard_map/ppermute | solution.py:328
  56.9 11.7 %collective-permute-start.12 = (bf16[448,288]{1,0:T(8,128)(2,1)S(1)}, bf16[448,288]{1,0:T(8,128)(2,1)}, u32[]{:S(2)}, u32[]{:S(2)}) collective-permute-start(bf16[448,288]{1,0:T(8,128)(2,1)S(1)} %collective-permute-done.8.refs_3_), channel_id=1, source_target_pairs={{0,4},{4,0},{1,5},{5,1},{2,6},{6,2},{3,7},{7,3},{8,12},{12,8},{9,1... | collective-permute-start | bytes 774152 | tf_op jit(solution)/shard_map/ppermute | solution.py:328
  57.4 13.1 %collective-permute-start.9 = (bf16[448,288]{1,0:T(8,128)(2,1)S(1)}, bf16[448,288]{1,0:T(8,128)(2,1)}, u32[]{:S(2)}, u32[]{:S(2)}) collective-permute-start(bf16[448,288]{1,0:T(8,128)(2,1)S(1)} %pad_maximum_fusion.2.refs_0_), channel_id=1, source_target_pairs={{0,4},{4,0},{1,5},{5,1},{2,6},{6,2},{3,7},{7,3},{8,12},{12,8},{9,1... | collective-permute-start | bytes 774152 | tf_op jit(solution)/shard_map/ppermute | solution.py:328
  57.7 18.8 %collective-permute-start.14 = (bf16[224,448]{1,0:T(8,128)(2,1)}, bf16[224,448]{1,0:T(8,128)(2,1)S(1)}, u32[]{:S(2)}, u32[]{:S(2)}) collective-permute-start(bf16[224,448]{1,0:T(8,128)(2,1)} %param.16), channel_id=1, source_target_pairs={{0,0},{1,2},{2,4},{3,6},{4,1},{5,3},{6,5},{7,7},{8,8},{9,10},{10,1... | collective-permute-start | bytes 602120 | tf_op jit(solution)/shard_map/ppermute | solution.py:306
  61.4 0.7 copy-start.18
  61.4 15.1 %collective-permute-start.15 = (bf16[224,448]{1,0:T(8,128)(2,1)}, bf16[224,448]{1,0:T(8,128)(2,1)S(1)}, u32[]{:S(2)}, u32[]{:S(2)}) collective-permute-start(bf16[224,448]{1,0:T(8,128)(2,1)} %param.16), channel_id=1, source_target_pairs={{0,1},{1,3},{2,5},{3,7},{4,0},{5,2},{6,4},{7,6},{8,9},{9,11},{10,1... | collective-permute-start | bytes 602120 | tf_op jit(solution)/shard_map/ppermute | solution.py:306
  62.8 7.7 %copy-start = (bf16[4,256,896]{2,1,0:T(8,128)(2,1)}, bf16[4,256,896]{2,1,0:T(8,128)(2,1)S(1)}, u32[]{:S(2)}) copy-start(bf16[4,256,896]{2,1,0:T(8,128)(2,1)S(1)} %all-to-all-done.1.t_ref) | copy-start | bytes 5505028
  62.8 13.8 %collective-permute-start.16 = (bf16[224,448]{1,0:T(8,128)(2,1)}, bf16[224,448]{1,0:T(8,128)(2,1)S(1)}, u32[]{:S(2)}, u32[]{:S(2)}) collective-permute-start(bf16[224,448]{1,0:T(8,128)(2,1)} %param.16), channel_id=1, source_target_pairs={{0,2},{1,0},{2,6},{3,4},{4,3},{5,1},{6,7},{7,5},{8,10},{9,8},{10,1... | collective-permute-start | bytes 602120 | tf_op jit(solution)/shard_map/ppermute | solution.py:306
  68.6 8.2 %collective-permute-start.17 = (bf16[224,448]{1,0:T(8,128)(2,1)}, bf16[224,448]{1,0:T(8,128)(2,1)S(1)}, u32[]{:S(2)}, u32[]{:S(2)}) collective-permute-start(bf16[224,448]{1,0:T(8,128)(2,1)} %param.16), channel_id=1, source_target_pairs={{0,3},{1,1},{2,7},{3,5},{4,2},{5,0},{6,6},{7,4},{8,11},{9,9},{10,1... | collective-permute-start | bytes 602120 | tf_op jit(solution)/shard_map/ppermute | solution.py:306
  76.0 2.0 %collective-permute-start.13 = (bf16[512,288]{1,0:T(8,128)(2,1)}, bf16[512,288]{1,0:T(8,128)(2,1)S(1)}, u32[]{:S(2)}, u32[]{:S(2)}) collective-permute-start(bf16[512,288]{1,0:T(8,128)(2,1)} %get-tuple-element.61), channel_id=1, source_target_pairs={{0,4},{4,0},{1,5},{5,1},{2,6},{6,2},{3,7},{7,3},{8,12},{12,8},{9,1... | collective-permute-start | bytes 884744 | tf_op jit(solution)/shard_map/ppermute | solution.py:334
  76.6 28.1 %copy-start.3 = (bf16[2,224,448]{2,1,0:T(8,128)(2,1)}, bf16[2,224,448]{2,1,0:T(8,128)(2,1)S(1)}, u32[]{:S(2)}) copy-start(bf16[2,224,448]{2,1,0:T(8,128)(2,1)S(1)} %pad_maximum_fusion.refs_0_) | copy-start | bytes 1204228
  76.8 27.9 %copy-start.4 = (bf16[2,224,448]{2,1,0:T(8,128)(2,1)}, bf16[2,224,448]{2,1,0:T(8,128)(2,1)S(1)}, u32[]{:S(2)}) copy-start(bf16[2,224,448]{2,1,0:T(8,128)(2,1)S(1)} %pad_maximum_fusion.1.refs_1_) | copy-start | bytes 1204228
  78.0 5.0 %copy-start.6 = (bf16[512,288]{1,0:T(8,128)(2,1)}, bf16[512,288]{1,0:T(8,128)(2,1)S(1)}, u32[]{:S(2)}) copy-start(bf16[512,288]{1,0:T(8,128)(2,1)S(1)} %collective-permute-done.13.rec_ref) | copy-start | bytes 884740
  78.0 27.8 %collective-permute-start.18 = (bf16[2,224,448]{2,1,0:T(8,128)(2,1)S(1)}, bf16[2,224,448]{2,1,0:T(8,128)(2,1)S(1)}, u32[]{:S(2)}, u32[]{:S(2)}) collective-permute-start(bf16[2,224,448]{2,1,0:T(8,128)(2,1)S(1)} %pad_maximum_fusion.refs_0_), channel_id=1, source_target_pairs={{0,8},{8,16},{16,24},{24,0},{1,9},{9,17},{17,25},{25,1},{2,10},{10... | collective-permute-start | bytes 1204232 | tf_op jit(solution)/shard_map/ppermute | solution.py:294
  78.0 27.8 %collective-permute-start.20 = (bf16[2,224,448]{2,1,0:T(8,128)(2,1)S(1)}, bf16[2,224,448]{2,1,0:T(8,128)(2,1)S(1)}, u32[]{:S(2)}, u32[]{:S(2)}) collective-permute-start(bf16[2,224,448]{2,1,0:T(8,128)(2,1)S(1)} %pad_maximum_fusion.refs_0_), channel_id=1, source_target_pairs={{0,24},{8,0},{16,8},{24,16},{1,25},{9,1},{17,9},{25,17},{2,26},{10... | collective-permute-start | bytes 1204232 | tf_op jit(solution)/shard_map/ppermute | solution.py:294
  80.3 25.5 %collective-permute-start.19 = (bf16[2,224,448]{2,1,0:T(8,128)(2,1)S(1)}, bf16[2,224,448]{2,1,0:T(8,128)(2,1)S(1)}, u32[]{:S(2)}, u32[]{:S(2)}) collective-permute-start(bf16[2,224,448]{2,1,0:T(8,128)(2,1)S(1)} %pad_maximum_fusion.1.refs_1_), channel_id=1, source_target_pairs={{0,8},{8,16},{16,24},{24,0},{1,9},{9,17},{17,25},{25,1},{2,10},{10... | collective-permute-start | bytes 1204232 | tf_op jit(solution)/shard_map/ppermute | solution.py:294
  80.3 25.5 %collective-permute-start.21 = (bf16[2,224,448]{2,1,0:T(8,128)(2,1)S(1)}, bf16[2,224,448]{2,1,0:T(8,128)(2,1)}, u32[]{:S(2)}, u32[]{:S(2)}) collective-permute-start(bf16[2,224,448]{2,1,0:T(8,128)(2,1)S(1)} %pad_maximum_fusion.1.refs_1_), channel_id=1, source_target_pairs={{0,24},{8,0},{16,8},{24,16},{1,25},{9,1},{17,9},{25,17},{2,26},{10... | collective-permute-start | bytes 1204232 | tf_op jit(solution)/shard_map/ppermute | solution.py:294
  85.7 20.0 %all-to-all-start.2 = ((bf16[32,16,128]{2,1,0:T(8,128)(2,1)}), bf16[32,16,128]{2,1,0:T(8,128)(2,1)S(1)}, u32[]{:S(2)}, u32[]{:S(2)}) async-start(bf16[32,16,128]{2,1,0:T(8,128)(2,1)} %get-tuple-element.64), calls=%async_computation.2 | async-start | bytes 262144 | tf_op jit(solution)/shard_map/all_to_all | solution.py:351
  104.7 24.8 %copy-start.27 = (s32[512]{0:T(512)S(1)}, s32[512]{0:T(512)}, u32[]{:S(2)}) copy-start(s32[512]{0:T(512)} %param.23) | copy-start | bytes 6148
  104.7 25.7 %copy-start.25 = (s32[512]{0:T(512)S(1)}, s32[512]{0:T(512)}, u32[]{:S(2)}) copy-start(s32[512]{0:T(512)} %multiply_add_fusion) | copy-start | bytes 6148
  105.7 0.7 copy-start.9
  105.8 33.9 %copy-start.10 = (bf16[2,224,448]{2,1,0:T(8,128)(2,1)}, bf16[2,224,448]{2,1,0:T(8,128)(2,1)S(1)}, u32[]{:S(2)}) copy-start(bf16[2,224,448]{2,1,0:T(8,128)(2,1)S(1)} %collective-permute-done.18.refs_2_) | copy-start | bytes 1204228
  105.8 33.9 %copy-start.12 = (bf16[2,224,448]{2,1,0:T(8,128)(2,1)}, bf16[2,224,448]{2,1,0:T(8,128)(2,1)S(1)}, u32[]{:S(2)}) copy-start(bf16[2,224,448]{2,1,0:T(8,128)(2,1)S(1)} %collective-permute-done.19.refs_3_) | copy-start | bytes 1204228
  105.8 33.8 %copy-start.11 = (bf16[2,224,448]{2,1,0:T(8,128)(2,1)}, bf16[2,224,448]{2,1,0:T(8,128)(2,1)S(1)}, u32[]{:S(2)}) copy-start(bf16[2,224,448]{2,1,0:T(8,128)(2,1)S(1)} %collective-permute-done.20.refs_6_) | copy-start | bytes 1204228
  118.1 23.4 %all-to-all-start.3 = ((bf16[32,16,512]{2,1,0:T(8,128)(2,1)}), bf16[32,16,512]{2,1,0:T(8,128)(2,1)S(1)}, u32[]{:S(2)}, u32[]{:S(2)}) async-start(bf16[32,16,512]{2,1,0:T(8,128)(2,1)} %get-tuple-element.74), calls=%async_computation.3 | async-start | bytes 1048576 | tf_op jit(solution)/shard_map/all_to_all | solution.py:376
  126.4 13.2 %collective-permute-start.22 = (bf16[2,224,448]{2,1,0:T(8,128)(2,1)S(1)}, bf16[2,224,448]{2,1,0:T(8,128)(2,1)S(1)}, u32[]{:S(2)}, u32[]{:S(2)}) collective-permute-start(bf16[2,224,448]{2,1,0:T(8,128)(2,1)S(1)} %collective-permute-done.18.refs_2_), channel_id=1, source_target_pairs={{0,8},{8,16},{16,24},{24,0},{1,9},{9,17},{17,25},{25,1},{2,10},{10... | collective-permute-start | bytes 1204232 | tf_op jit(solution)/shard_map/ppermute | solution.py:294
  126.7 12.9 %collective-permute-start.23 = (bf16[2,224,448]{2,1,0:T(8,128)(2,1)}, bf16[2,224,448]{2,1,0:T(8,128)(2,1)S(1)}, u32[]{:S(2)}, u32[]{:S(2)}) collective-permute-start(bf16[2,224,448]{2,1,0:T(8,128)(2,1)} %collective-permute-done.21.refs_7_), channel_id=1, source_target_pairs={{0,24},{8,0},{16,8},{24,16},{1,25},{9,1},{17,9},{25,17},{2,26},{10... | collective-permute-start | bytes 1204232 | tf_op jit(solution)/shard_map/ppermute | solution.py:294
  139.6 24.8 %copy-start.13 = (bf16[2,224,448]{2,1,0:T(8,128)(2,1)}, bf16[2,224,448]{2,1,0:T(8,128)(2,1)S(1)}, u32[]{:S(2)}) copy-start(bf16[2,224,448]{2,1,0:T(8,128)(2,1)S(1)} %collective-permute-done.22.refs_4_) | copy-start | bytes 1204228
  139.7 24.8 %copy-start.14 = (bf16[2,224,448]{2,1,0:T(8,128)(2,1)}, bf16[2,224,448]{2,1,0:T(8,128)(2,1)S(1)}, u32[]{:S(2)}) copy-start(bf16[2,224,448]{2,1,0:T(8,128)(2,1)S(1)} %collective-permute-done.23.refs_5_) | copy-start | bytes 1204228
  141.5 0.8 copy-start.2
  146.0 37.4 %copy-start.5 = (bf16[256,2,448]{0,2,1:T(8,128)(2,1)S(1)}, bf16[256,2,448]{0,2,1:T(8,128)(2,1)}, u32[]{:S(2)}) copy-start(bf16[256,2,448]{0,2,1:T(8,128)(2,1)} %param.12) | copy-start | bytes 1376260
  157.8 6.6 %copy-start.1 = (bf16[4,256,256]{2,1,0:T(8,128)(2,1)}, bf16[4,256,256]{2,1,0:T(8,128)(2,1)S(1)}, u32[]{:S(2)}) copy-start(bf16[4,256,256]{2,1,0:T(8,128)(2,1)S(1)} %all_to_all.29.own_ref) | copy-start | bytes 1572868
  157.8 6.6 %collective-permute-start.24 = (bf16[4,256,256]{2,1,0:T(8,128)(2,1)S(1)}, bf16[4,256,256]{2,1,0:T(8,128)(2,1)S(1)}, u32[]{:S(2)}, u32[]{:S(2)}) collective-permute-start(bf16[4,256,256]{2,1,0:T(8,128)(2,1)S(1)} %all_to_all.29.own_ref), channel_id=1, source_target_pairs={{0,4},{4,0},{1,5},{5,1},{2,6},{6,2},{3,7},{7,3},{8,12},{12,8},{9,1... | collective-permute-start | bytes 1572872 | tf_op jit(solution)/shard_map/ppermute | solution.py:392
  164.5 0.8 copy-start.8
  169.8 11.9 %collective-permute-start.25 = (bf16[256,448]{1,0:T(8,128)(2,1)}, bf16[256,448]{1,0:T(8,128)(2,1)S(1)}, u32[]{:S(2)}, u32[]{:S(2)}) collective-permute-start(bf16[256,448]{1,0:T(8,128)(2,1)} %get-tuple-element.83), channel_id=1, source_target_pairs={{0,1},{4,3},{8,0},{12,2},{16,5},{20,7},{24,4},{28,6},{1,9},{5,11},... | collective-permute-start | bytes 688136 | tf_op jit(solution)/shard_map/ppermute | solution.py:404
  172.9 10.1 %collective-permute-start.26 = (bf16[256,448]{1,0:T(8,128)(2,1)}, bf16[256,448]{1,0:T(8,128)(2,1)S(1)}, u32[]{:S(2)}, u32[]{:S(2)}) collective-permute-start(bf16[256,448]{1,0:T(8,128)(2,1)} %get-tuple-element.84), channel_id=1, source_target_pairs={{0,0},{4,2},{8,1},{12,3},{16,4},{20,6},{24,5},{28,7},{1,8},{5,10},... | collective-permute-start | bytes 688136 | tf_op jit(solution)/shard_map/ppermute | solution.py:404

commit v5 on v4

--- a/solution.py
+++ b/solution.py
@@ -34,7 +34,7 @@
     return pltpu.with_memory_space_constraint(x, pltpu.HBM)
 
 
-def call(kernel, out_shapes, n_smem, *args, scratch=()):
+def call(kernel, out_shapes, n_smem, *args, scratch=(), free=()):
     def full(shape):
         zeros = (0,) * len(shape)
         return pl.BlockSpec(shape, lambda i: zeros)
@@ -47,32 +47,51 @@
         out_specs=jax.tree.map(lambda x: full(x.shape), out_shapes),
         scratch_shapes=scratch,
         compiler_params=pltpu.CompilerParams(vmem_limit_bytes=VMEM_LIMIT),
-    )(*args[:n_smem], *[in_hbm(x) for x in args[n_smem:]])
-
-
-def order_kernel(pos_ref, *refs):
-    out_ref = refs[8]
+    )(*args[:n_smem], *[x if i + n_smem in free else in_hbm(x) for i, x in enumerate(args[n_smem:])])
+
+
+def project_kernel(pos_ref, *refs):
+    blocks, mine_ref, theirs_ref, out_ref, first, second = refs[:8], refs[8], refs[9], refs[10], refs[11], refs[12]
+    core = pos_ref[1]
+    one = jnp.where(core == 0, mine_ref[...], theirs_ref[...])
+    two = jnp.where(core == 0, theirs_ref[...], mine_ref[...])
+    first[:, 0:256] = one[:, 0:256]
+    first[:, 256:512] = two[:, 0:256]
+    first[:, 512:640] = jnp.concatenate([one[:, 256:288], two[:, 256:288], jnp.zeros((448, 64), BF)], axis=1)
+    second[0:64, :] = jnp.zeros((64, 640), BF)
+    second[64:512, 0:128] = jnp.concatenate([jnp.zeros((448, 64), BF), one[:, 256:288], two[:, 256:288]], axis=1)
+    second[64:512, 128:384] = one[:, 0:256]
+    second[64:512, 384:640] = two[:, 0:256]
     for shift in range(4):
         slot = lax.rem(pos_ref[0] + 4 - shift, 4)
-        out_ref[slot, 0:128, :] = refs[2 * shift][...]
-        out_ref[slot, 128:256, :] = refs[2 * shift + 1][...]
-
-
-def project_kernel(pos_ref, t_ref, *refs):
-    weights, own_ref, oth_ref, padded = refs[:8], refs[8], refs[9], refs[10]
-    padded[0:64, :] = jnp.zeros((64, 288), BF)
-    for which, out_ref in enumerate((own_ref, oth_ref)):
-        first = second = None
-        for shift in range(4):
-            block = lax.rem(pos_ref[3] + 4 - shift, 4)
-            w = weights[which * 4 + shift][...]
-            padded[64:512, :] = w
-            one = dot(t_ref[block, :, 0:448], w)
-            two = dot(t_ref[block, :, 384:896], padded[...])
-            first = one if first is None else first + one
-            second = two if second is None else second + two
-        out_ref[0:256, :] = first.astype(BF)
-        out_ref[256:512, :] = second.astype(BF)
+        for part in range(2):
+            block = blocks[2 * shift + part]
+            a = dot(block[:, 0:448], first[...])
+            b = dot(block[:, 384:896], second[...])
+            at = slice(part * 128, (part + 1) * 128)
+            out_ref[slot, at, 0:512] = a[:, 0:512].astype(BF)
+            out_ref[slot, at, 512:640] = (a[:, 512:640] + b[:, 0:128]).astype(BF)
+            out_ref[slot, at, 640:1152] = b[:, 128:640].astype(BF)
+
+
+def sum_kernel(pos_ref, p_ref, own_ref, oth_ref):
+    core = pos_ref[1]
+
+    def total(lo, hi):
+        acc = p_ref[0, :, lo:hi].astype(F32)
+        for i in range(1, 4):
+            acc = acc + p_ref[i, :, lo:hi].astype(F32)
+        return acc.astype(BF)
+
+    keys = total(512, 640)
+    for t in range(2):
+        at = slice(t * 256, (t + 1) * 256)
+        one, two = total(t * 640, t * 640 + 256), total(t * 640 + 256, t * 640 + 512)
+        own_ref[at, 0:256] = jnp.where(core == 0, one, two)
+        oth_ref[at, 0:256] = jnp.where(core == 0, two, one)
+        one, two = keys[:, t * 64 : t * 64 + 32], keys[:, t * 64 + 32 : t * 64 + 64]
+        own_ref[at, 256:288] = jnp.where(core == 0, one, two)
+        oth_ref[at, 256:288] = jnp.where(core == 0, two, one)
 
 
 def group_kernel(pos_ref, g_ref, s_ref, own_ref, rec_ref, place_ref, send_ref, keep_ref, grouped):
@@ -265,31 +284,26 @@
 
 
 def out_kernel(pos_ref, own_ref, oth_ref, *refs):
-    parts, first_ref, second_ref, weights = refs[:8], refs[8], refs[9], refs[10]
+    parts, first_ref, second_ref = refs[:8], refs[8], refs[9]
     y, core, col = pos_ref[0], pos_ref[1], pos_ref[3]
     acc = [None, None]
     for shift in range(4):
-        weights[shift, 0:2] = parts[2 * shift][...]
-        weights[shift, 2:4] = parts[2 * shift + 1][...]
         j = lax.rem(y + 4 - shift, 4)
         for which, ref in enumerate((own_ref, oth_ref)):
             k = core if which == 0 else 1 - core
             heads = ref[j, :, 0:224]
             for e in range(2):
-                part = dot(heads, weights[shift, jnp.bitwise_xor(2 * e + k, col)])
+                part = dot(heads, parts[2 * shift + e][jnp.bitwise_xor(k, lax.rem(col, 2))])
                 acc[e] = part if acc[e] is None else acc[e] + part
-    even = lax.rem(y, 2) == 0
-    first_ref[...] = jnp.where(even, acc[0], acc[1]).astype(BF)
-    second_ref[...] = jnp.where(even, acc[1], acc[0]).astype(BF)
+    same = lax.rem(y, 2) == lax.div(col, 2)
+    first_ref[...] = jnp.where(same, acc[0], acc[1]).astype(BF)
+    second_ref[...] = jnp.where(same, acc[1], acc[0]).astype(BF)
 
 
 def body(tokens, w_query, w_key, w_value, w_out, cached_state, cached_norm, slot_prompt, prompt_of, tail_keys, tail_values, tail_length):
     y, core, col = lax.axis_index("y"), lax.axis_index("core"), lax.axis_index("col")
     me = lax.axis_index(("req", "col"))
     pos = jnp.stack([y, core, me, col]).astype(jnp.int32)
-    def shifts(x, axis):
-        return [x] + [lax.ppermute(x, axis, [(i, (i + s) % 4) for i in range(4)]) for s in range(1, 4)]
-
     def over_y(x, step):
         return lax.ppermute(x, "y", [(i, (i + step) % 4) for i in range(4)])
 
@@ -299,12 +313,12 @@
     top_1, low_3, w_out = lax.optimization_barrier((top_1, low_3, w_out))
     blocks = [top, low, top_1, low_1, over_y(top_1, 1), over_y(low_3, 3), top_3, low_3]
     value_w = jnp.moveaxis(w_value.reshape(2, 448, 112), 0, 1).reshape(448, 224)
-    mine = shifts(jnp.concatenate([value_w, w_query, w_key], axis=1), "col")
+    mine = jnp.concatenate([value_w, w_query, w_key], axis=1)
+    theirs = lax.ppermute(mine, "core", [(0, 1), (1, 0)])
     pieces = []
     for s in range(4):
         perm = [(k * 4 + c, (c >> 1) * 4 + (s ^ (2 * (c & 1) + k))) for k in range(2) for c in range(4)]
         pieces.append(lax.ppermute(w_out, ("core", "col"), perm))
-    blocks, mine = lax.optimization_barrier((blocks, mine))
     pieces = [jnp.stack(pieces[:2]), jnp.stack(pieces[2:])]
 
     owner = slot_prompt // 32
@@ -324,16 +338,23 @@
     norms = jnp.pad(jnp.transpose(cached_norm, (0, 2, 1)).reshape(64, 273), ((0, 0), (0, 111)))
     states = cached_state[0].reshape(273, 224, 32)
 
-    held = call(order_kernel, jax.ShapeDtypeStruct((4, 256, 896), BF), 1, pos, *blocks)
-    theirs = [lax.ppermute(w, "core", [(0, 1), (1, 0)]) for w in mine]
-    held = lax.all_to_all(held, "col", split_axis=0, concat_axis=0, tiled=True)
-    held, states, norms = lax.optimization_barrier((held, states, norms))
+    partial = call(
+        project_kernel,
+        jax.ShapeDtypeStruct((4, 256, 1152), BF),
+        1,
+        pos,
+        *blocks,
+        mine,
+        theirs,
+        scratch=[pltpu.VMEM((448, 640), BF), pltpu.VMEM((512, 640), BF)],
+        free=range(1, 11),
+    )
+    partial = lax.all_to_all(partial, "col", split_axis=0, concat_axis=0, tiled=True)
     states = jnp.transpose(states, (2, 0, 1))
+    partial, states, norms = lax.optimization_barrier((partial, states, norms))
     shape = jax.ShapeDtypeStruct((512, 288), BF)
-    own, oth = call(project_kernel, (shape, shape), 1, pos, held, *mine, *theirs, scratch=[pltpu.VMEM((512, 288), BF)])
+    own, oth = call(sum_kernel, (shape, shape), 1, pos, partial, free=(1,))
     rec = lax.ppermute(oth, "core", [(0, 1), (1, 0)])
-    rec, pieces = lax.optimization_barrier((rec, pieces))
-    out_w = [over_y(x, step) for step in (1, 3) for x in pieces]
 
     shape = jax.ShapeDtypeStruct((32, 16, 128), BF)
     q_send, q_keep = call(
@@ -347,11 +368,14 @@
         rec,
         place.reshape(2, 1, 256),
         scratch=[pltpu.VMEM((512, 128), BF)],
-    )
+        free=(3, 4),
+    )
+    q_send, pieces = lax.optimization_barrier((q_send, pieces))
+    out_w = [over_y(x, step) for step in (1, 3) for x in pieces]
     q_rec = lax.all_to_all(q_send, ("req", "col"), split_axis=0, concat_axis=0, tiled=True)
-    q_rec, out_w = lax.optimization_barrier((q_rec, out_w))
     shape = jax.ShapeDtypeStruct((2, 512, 256), F32)
     num = call(tail_kernel, shape, 1, pos, own, rec, tail_keys, tail_values, tail_length[:, None])
+    q_rec, num = lax.optimization_barrier((q_rec, num))
     shape = jax.ShapeDtypeStruct((32, 16, 512), BF)
     whole = pl.BlockSpec((32, 16, 128), lambda i: (0, 0, 0))
     whole_out = pl.BlockSpec((32, 16, 512), lambda i: (0, 0, 0))
@@ -371,8 +395,8 @@
         scratch_shapes=[pltpu.VMEM((128, 128), BF)],
         compiler_params=pltpu.CompilerParams(vmem_limit_bytes=VMEM_LIMIT),
     )(pos, owner, in_hbm(q_rec), in_hbm(q_keep), in_hbm(states), in_hbm(norms))
-    r_send, far_1, far_3 = lax.optimization_barrier((r_send, out_w[0], out_w[3]))
-    far_1, far_3 = over_y(far_1, 1), over_y(far_3, 3)
+    r_send, out_w = lax.optimization_barrier((r_send, out_w))
+    far_1, far_3 = over_y(out_w[0], 1), over_y(out_w[3], 3)
     r_rec = lax.all_to_all(r_send, ("req", "col"), split_axis=0, concat_axis=0, tiled=True)
     r_rec, far_1, far_3 = lax.optimization_barrier((r_rec, far_1, far_3))
     heads = call(
@@ -387,11 +411,12 @@
         r_keep,
         place[:, None],
         scratch=[pltpu.VMEM((512, 512), BF)],
+        free=(4,),
     )
     heads = lax.all_to_all(heads, "y", split_axis=0, concat_axis=0, tiled=True)
     heads_oth = lax.ppermute(heads, "core", [(0, 1), (1, 0)])
     shape = jax.ShapeDtypeStruct((256, 448), BF)
-    mixed = call(out_kernel, (shape, shape), 1, pos, heads, heads_oth, *pieces, out_w[0], out_w[1], far_1, far_3, out_w[2], out_w[3], scratch=[pltpu.VMEM((4, 4, 224, 448), BF)])
+    mixed = call(out_kernel, (shape, shape), 1, pos, heads, heads_oth, *pieces, out_w[0], out_w[1], far_1, far_3, out_w[2], out_w[3], free=(1, 2))
 
     def at(y, core, col):
         return (y * 2 + core) * 4 + col

time: 188 us -> 181 us (0.963)
  waiting for transfers between devices: 19.7 us -> 31.8 us
  starting transfers between devices: 80 us -> 69.1 us
  Pallas kernels: 39.5 us -> 36 us
  local copies, waits for them, and re-layouts: 28.8 us -> 26.1 us
    optimization_barrier x3 -> x0, local copies, waits for them, and re-layouts: 10.2 us -> none  [the longest x1 8.35 us: body(): held, states, norms = lax.optimization_barrier((held, states, norms))]
    ppermute x7 -> x1, starting transfers between devices: 10.6 us -> 2.07 us  [body(): theirs = lax.ppermute(mine, 'core', [(0, 1), (1, 0)])]
    another operation x0 -> x1, local copies, waits for them, and re-layouts: none -> 8.46 us  [body(): states = cached_state[0].reshape(273, 224, 32)]
    all_to_all x1, starting transfers between devices: 10.6 us -> 3.85 us  [body(): lax.all_to_all(q_send, ('req', 'col'), split_axis=0, concat_axis=0, tiled...]
    ppermute x12, waiting for transfers between devices: 4 us -> 10.2 us  [over_y(): return lax.ppermute(x, 'y', [(i, (i + step) % 4) for i in range(4)])]
    ppermute x4, waiting for transfers between devices: 0.17 us -> 4.59 us  [body(): pieces.append(lax.ppermute(w_out, ('core', 'col'), perm))]
    pallas_call x6, Pallas kernels: 27.8 us -> 24.2 us  [call(): pl.pallas_call(kernel, grid=(1,), out_shape=jax.tree.map(lambda x: pltpu....]
    all_to_all x1, waiting for transfers between devices: 1.83 us -> 4.46 us  [body(): lax.all_to_all(r_send, ('req', 'col'), split_axis=0, concat_axis=0, tiled...]
  transfers between devices with their start and end apart: 31 -> 25, of which waited for: 10 -> 11; matrix products, arithmetic and copies ran while one was open for 15% -> 14% of each run, Pallas kernels for 11% -> 15%
where the time goes in v5:
time: 181 us; the launch traced here: 178 us
  starting transfers between devices  69.1 us (38%)
  Pallas kernels  36 us (20%)
  waiting for transfers between devices  31.8 us (18%)
  local copies, waits for them, and re-layouts  26.1 us (14%)
  blocking collectives  10.5 us (6%)
  other arithmetic  4.04 us (2%)
    pallas_call x6, Pallas kernels, call(): pl.pallas_call(kernel, grid=(1,), out_shape=jax.tree.map(lambda x: pltpu....  24.2 us
    ppermute x12, starting transfers between devices, over_y(): return lax.ppermute(x, 'y', [(i, (i + step) % 4) for i in range(4)])  13.5 us
    ppermute x4, starting transfers between devices, body(): pieces.append(lax.ppermute(w_out, ('core', 'col'), perm))  12.9 us
    pallas_call x1, Pallas kernels, body(): pl.pallas_call(slot_kernel, grid=(4,), out_shape=(pltpu.HBM(shape.shape,...  11.8 us
    unnamed x39, local copies, waits for them, and re-layouts  11.1 us
    all_to_all x1, starting transfers between devices, body(): lax.all_to_all(code[:, None], ('req', 'col'), split_axis=0, concat_axis=0...  11 us
    all_to_all x1, blocking collectives, body(): heads = lax.all_to_all(heads, 'y', split_axis=0, concat_axis=0, tiled=True)  10.5 us
    ppermute x12, waiting for transfers between devices, over_y(): return lax.ppermute(x, 'y', [(i, (i + step) % 4) for i in range(4)])  10.2 us
  transfers between devices with their start and end apart: 25, of which 11 were waited for; matrix products, arithmetic and copies ran while one was open for 14% of the time, Pallas kernels for 15%

profile of v5, /device:TPU:9, one launch (start us, length us, event | category | flops | bytes accessed | tf_op | source)
XLA Modules:
  0.0 177.9 jit_solution(8654343950088372354)
XLA Ops:
  0.0 1.1 fusion.8
  1.1 0.2 copy.76.refs_1_
  1.4 1.5 collective-permute-start.2
  2.8 0.2 copy.75.refs_0_
  3.0 1.4 collective-permute-start
  4.4 0.2 collective-permute-start.5
  4.6 1.2 reshape.76
  5.8 0.2 copy.84
  6.1 0.1 reshape.77
  6.2 0.9 copy.73
  7.1 0.9 copy.74
  8.2 2.1 %collective-permute-start.6 = (bf16[448,288]{1,0:T(8,128)(2,1)S(1)}, bf16[448,288]{1,0:T(8,128)(2,1)S(1)}, u32[]{:S(2)}, u32[]{:S(2)}) collective-permute-start(bf16[448,288]{1,0:T(8,128)(2,1)S(1)} %pad_maximum_fusion.2.refs_8_), channel_id=1, source_target_pairs={{0,4},{4,0},{1,5},{5,1},{2,6},{6,2},{3,7},{7,3},{8,12},{12,8},{9,1... | collective-permute-start | bytes 774152 | tf_op jit(solution)/shard_map/ppermute | solution.py:317
  10.3 3.1 %collective-permute-done.refs_2_ = bf16[128,896]{1,0:T(8,128)(2,1)S(1)} collective-permute-done((bf16[128,896]{1,0:T(8,128)(2,1)S(1)}, bf16[128,896]{1,0:T(8,128)(2,1)S(1)}, u32[]{:S(2)}, u32[]{:S(2)}) %collective-permute-start) | collective-permute-done | bytes 229408 | tf_op jit(solution)/shard_map/ppermute | solution.py:308
  13.4 0.3 collective-permute-start.3
  13.7 2.8 %collective-permute-start.4 = (bf16[128,896]{1,0:T(8,128)(2,1)S(1)}, bf16[128,896]{1,0:T(8,128)(2,1)S(1)}, u32[]{:S(2)}, u32[]{:S(2)}) collective-permute-start(bf16[128,896]{1,0:T(8,128)(2,1)S(1)} %collective-permute-done.1.refs_7_), channel_id=1, source_target_pairs={{0,24},{8,0},{16,8},{24,16},{1,25},{9,1},{17,9},{25,17},{2,26},{10... | collective-permute-start | bytes 688136 | tf_op jit(solution)/shard_map/ppermute | solution.py:308
  16.7 0.7 copy.67
  17.4 11.0 %all-to-all-start = ((s32[32,1,1]{2,1,0:T(1,128)}), s32[32,1,1]{2,1,0:T(1,128)S(1)}, u32[]{:S(2)}, u32[]{:S(2)}) async-start(s32[32,1,1]{2,1,0:T(1,128)} %copy.67), calls=%async_computation | async-start | bytes 32768 | tf_op jit(solution)/shard_map/all_to_all | solution.py:330
  28.5 4.0 %shard_map.118 = bf16[4,256,1152]{2,1,0:T(8,128)(2,1)} custom-call(s32[4]{0:T(128)S(1)} %pad_add_fusion.pos_ref, bf16[128,896]{1,0:T(8,128)(2,1)S(1)} %copy.75.refs_0_, bf16[128,896]{1,0:T(8,128)(2,1)S(1)} %copy.76.refs_1_, bf16[128,896]{1,0:T(8,128)(2,1)S(1)} %collective-permute-done.refs_2_, bf16[128,896]{1,0:T(8,128)(2,1)S(1)} %collective-permute-done.2.refs_3_, ...), custom_call_target="tpu_custom_call" | custom-call | tf_op jit(solution)/shard_map/pallas_call | solution.py:42
  32.5 4.4 %all-to-all-done = s32[32,1,1]{2,1,0:T(1,128)S(1)} async-done(((s32[32,1,1]{2,1,0:T(1,128)}), s32[32,1,1]{2,1,0:T(1,128)S(1)}, u32[]{:S(2)}, u32[]{:S(2)}) %all-to-all-start) | async-done | bytes 160 | tf_op jit(solution)/shard_map/all_to_all | solution.py:330
  36.9 3.6 %all-to-all-start.1 = ((bf16[4,256,1152]{2,1,0:T(8,128)(2,1)}), bf16[4,256,1152]{2,1,0:T(8,128)(2,1)S(1)}, u32[]{:S(2)}, u32[]{:S(2)}) async-start(bf16[4,256,1152]{2,1,0:T(8,128)(2,1)} %shard_map.118), calls=%async_computation.1 | async-start | bytes 4718592 | tf_op jit(solution)/shard_map/all_to_all | solution.py:352
  40.6 7.3 %copy.77 = bf16[1,273,7168]{1,2,0:T(8,128)(2,1)} copy(bf16[1,273,7168]{2,1,0:T(8,128)(2,1)} %param.17) | data formatting | bytes 7827456 | tf_op args[5]
  47.9 8.5 %copy.78 = bf16[273,224,32]{1,0,2:T(8,128)(2,1)} copy(bf16[273,224,32]{0,2,1:T(8,128)(2,1)} %bitcast.26) | data formatting | bytes 7827456 | tf_op jit(solution)/shard_map/reshape;squeeze | solution.py:339
  56.4 0.6 pad.4.norm_ref
  57.0 0.2 compare_reduce_fusion.1
  57.2 0.2 fusion.2.s_ref
  57.4 0.2 convert_reduce_fusion
  57.7 0.6 multiply_add_fusion
  58.2 0.7 add_reduce_fusion
  58.9 0.7 compare_reduce_fusion
  59.7 7.1 %collective-permute-start.8 = (bf16[224,448]{1,0:T(8,128)(2,1)S(1)}, bf16[224,448]{1,0:T(8,128)(2,1)S(1)}, u32[]{:S(2)}, u32[]{:S(2)}) collective-permute-start(bf16[224,448]{1,0:T(8,128)(2,1)S(1)} %copy-done.17), channel_id=1, source_target_pairs={{0,0},{1,2},{2,4},{3,6},{4,1},{5,3},{6,5},{7,7},{8,8},{9,10},{10,1... | collective-permute-start | bytes 602120 | tf_op jit(solution)/shard_map/ppermute | solution.py:321
  66.9 1.5 collective-permute-start.10
  68.4 4.3 %collective-permute-start.11 = (bf16[224,448]{1,0:T(8,128)(2,1)S(1)}, bf16[224,448]{1,0:T(8,128)(2,1)S(1)}, u32[]{:S(2)}, u32[]{:S(2)}) collective-permute-start(bf16[224,448]{1,0:T(8,128)(2,1)S(1)} %copy-done.17), channel_id=1, source_target_pairs={{0,3},{1,1},{2,7},{3,5},{4,2},{5,0},{6,6},{7,4},{8,11},{9,9},{10,1... | collective-permute-start | bytes 602120 | tf_op jit(solution)/shard_map/ppermute | solution.py:321
  72.6 2.0 %shard_map.119 = (bf16[512,288]{1,0:T(8,128)(2,1)}, bf16[512,288]{1,0:T(8,128)(2,1)}) custom-call(s32[4]{0:T(128)S(1)} %pad_add_fusion.pos_ref, bf16[4,256,1152]{2,1,0:T(8,128)(2,1)S(1)} %all-to-all-done.1.p_ref), custom_call_target="tpu_custom_call" | custom-call | tf_op jit(solution)/shard_map/pallas_call | solution.py:42
  74.7 0.4 collective-permute-start.7
  75.2 4.5 %collective-permute-done.10 = bf16[224,448]{1,0:T(8,128)(2,1)S(1)} collective-permute-done((bf16[224,448]{1,0:T(8,128)(2,1)S(1)}, bf16[224,448]{1,0:T(8,128)(2,1)S(1)}, u32[]{:S(2)}, u32[]{:S(2)}) %collective-permute-start.10) | collective-permute-done | bytes 200736 | tf_op jit(solution)/shard_map/ppermute | solution.py:321
  79.9 1.3 copy-done
  81.1 2.3 %shard_map.120 = (bf16[32,16,128]{2,1,0:T(8,128)(2,1)}, bf16[32,16,128]{2,1,0:T(8,128)(2,1)}) custom-call(s32[4]{0:T(128)S(1)} %pad_add_fusion.pos_ref, s32[32]{0:T(128)S(1)} %broadcast_select_fusion.2.g_ref, s32[32]{0:T(128)S(1)} %fusion.2.s_ref, bf16[512,288]{1,0:T(8,128)(2,1)S(1)} %copy-done, bf16[512,288]{1,0:T(8,128)(2,1)S(1)} %collective-permute-done.7.rec_ref, ...), custom_call_target="tpu_custom_call" | custom-call | tf_op jit(solution)/shard_map/pallas_call | solution.py:42
  83.4 2.1 %collective-permute-start.13 = (bf16[2,224,448]{2,1,0:T(8,128)(2,1)S(1)}, bf16[2,224,448]{2,1,0:T(8,128)(2,1)S(1)}, u32[]{:S(2)}, u32[]{:S(2)}) collective-permute-start(bf16[2,224,448]{2,1,0:T(8,128)(2,1)S(1)} %pad_maximum_fusion.1.refs_1_), channel_id=1, source_target_pairs={{0,8},{8,16},{16,24},{24,0},{1,9},{9,17},{17,25},{25,1},{2,10},{10... | collective-permute-start | bytes 1204232 | tf_op jit(solution)/shard_map/ppermute | solution.py:308
  85.5 0.7 collective-permute-start.14
  86.2 2.6 %collective-permute-start.15 = (bf16[2,224,448]{2,1,0:T(8,128)(2,1)S(1)}, bf16[2,224,448]{2,1,0:T(8,128)(2,1)S(1)}, u32[]{:S(2)}, u32[]{:S(2)}) collective-permute-start(bf16[2,224,448]{2,1,0:T(8,128)(2,1)S(1)} %pad_maximum_fusion.1.refs_1_), channel_id=1, source_target_pairs={{0,24},{8,0},{16,8},{24,16},{1,25},{9,1},{17,9},{25,17},{2,26},{10... | collective-permute-start | bytes 1204232 | tf_op jit(solution)/shard_map/ppermute | solution.py:308
  88.8 3.9 %all-to-all-start.2 = ((bf16[32,16,128]{2,1,0:T(8,128)(2,1)}), bf16[32,16,128]{2,1,0:T(8,128)(2,1)S(1)}, u32[]{:S(2)}, u32[]{:S(2)}) async-start(bf16[32,16,128]{2,1,0:T(8,128)(2,1)} %get-tuple-element.39), calls=%async_computation.2 | async-start | bytes 262144 | tf_op jit(solution)/shard_map/all_to_all | solution.py:375
  92.7 0.9 copy.79.len_ref
  93.5 8.3 %shard_map.121.num_ref = f32[2,512,256]{2,1,0:T(8,128)} custom-call(s32[4]{0:T(128)S(1)} %pad_add_fusion.pos_ref, bf16[512,288]{1,0:T(8,128)(2,1)} %get-tuple-element.35.own_ref, bf16[512,288]{1,0:T(8,128)(2,1)} %copy-done.1, bf16[512,256]{1,0:T(8,128)(2,1)} %tk_ref.1, bf16[512,1792]{1,0:T(8,128)(2,1)} %tv_ref.1, s32[512,1]{1,0:T(8,128)} %copy.79.len_ref), custom_call_target="tpu_custom_call" | custom-call | tf_op jit(solution)/shard_map/pallas_call | solution.py:42
  101.8 0.2 all-to-all-done.2.rec_ref
  102.1 0.6 copy-done.5
  102.7 11.8 %shard_map.122 = (bf16[32,16,512]{2,1,0:T(8,128)(2,1)}, bf16[32,16,512]{2,1,0:T(8,128)(2,1)}) custom-call(s32[4]{0:T(128)S(1)} %pad_add_fusion.pos_ref, s32[32]{0:T(128)S(1)} %get-tuple-element.60.owner_ref, bf16[32,16,128]{2,1,0:T(8,128)(2,1)} %copy-done.5, bf16[32,16,128]{2,1,0:T(8,128)(2,1)} %get-tuple-element.42.keep_ref, ...), custom_call_target="tpu_custom_call" | custom-call | tf_op jit(solution)/shard_map/pallas_call | solution.py:382
  114.6 8.8 %all-to-all-start.3 = ((bf16[32,16,512]{2,1,0:T(8,128)(2,1)}), bf16[32,16,512]{2,1,0:T(8,128)(2,1)S(1)}, u32[]{:S(2)}, u32[]{:S(2)}) async-start(bf16[32,16,512]{2,1,0:T(8,128)(2,1)} %get-tuple-element.48), calls=%async_computation.3 | async-start | bytes 1048576 | tf_op jit(solution)/shard_map/all_to_all | solution.py:400
  123.4 0.3 collective-permute-start.16
  123.7 1.5 collective-permute-start.17
  125.3 0.9 copy.80.place_ref
  126.1 7.0 %collective-permute-done.16.refs_4_ = bf16[2,224,448]{2,1,0:T(8,128)(2,1)S(1)} collective-permute-done((bf16[2,224,448]{2,1,0:T(8,128)(2,1)S(1)}, bf16[2,224,448]{2,1,0:T(8,128)(2,1)S(1)}, u32[]{:S(2)}, u32[]{:S(2)}) %collective-permute-start.16) | collective-permute-done | bytes 401440 | tf_op jit(solution)/shard_map/ppermute | solution.py:308
  133.2 4.5 %all-to-all-done.3.rec_ref = bf16[32,16,512]{2,1,0:T(8,128)(2,1)S(1)} async-done(((bf16[32,16,512]{2,1,0:T(8,128)(2,1)}), bf16[32,16,512]{2,1,0:T(8,128)(2,1)S(1)}, u32[]{:S(2)}, u32[]{:S(2)}) %all-to-all-start.3) | async-done | bytes 524320 | tf_op jit(solution)/shard_map/all_to_all | solution.py:400
  137.6 3.6 %shard_map.123 = bf16[4,256,256]{2,1,0:T(8,128)(2,1)} custom-call(s32[4]{0:T(128)S(1)} %pad_add_fusion.pos_ref, s32[32]{0:T(128)S(1)} %broadcast_select_fusion.2.g_ref, s32[32]{0:T(128)S(1)} %fusion.2.s_ref, f32[2,512,256]{2,1,0:T(8,128)} %shard_map.121.num_ref, bf16[32,16,512]{2,1,0:T(8,128)(2,1)S(1)} %all-to-all-done.3.rec_ref, ...), custom_call_target="tpu_custom_call" | custom-call | tf_op jit(solution)/shard_map/pallas_call | solution.py:42
  141.2 10.5 %all_to_all.29.own_ref = bf16[4,256,256]{2,1,0:T(8,128)(2,1)S(1)} all-to-all(bf16[4,256,256]{2,1,0:T(8,128)(2,1)} %shard_map.123), channel_id=1, replica_groups=mesh['req'=8,'y'=4,'core'=2,'col'=4] {'y'}, dimensions={0} | all-to-all | bytes 1048576 | tf_op jit(solution)/shard_map/all_to_all | solution.py:416
  151.7 6.2 %collective-permute-start.18 = (bf16[4,256,256]{2,1,0:T(8,128)(2,1)S(1)}, bf16[4,256,256]{2,1,0:T(8,128)(2,1)S(1)}, u32[]{:S(2)}, u32[]{:S(2)}) collective-permute-start(bf16[4,256,256]{2,1,0:T(8,128)(2,1)S(1)} %all_to_all.29.own_ref), channel_id=1, source_target_pairs={{0,4},{4,0},{1,5},{5,1},{2,6},{6,2},{3,7},{7,3},{8,12},{12,8},{9,1... | collective-permute-start | bytes 1572872 | tf_op jit(solution)/shard_map/ppermute | solution.py:417
  157.9 1.5 collective-permute-done.18.oth_ref
  159.5 4.0 %shard_map.124 = (bf16[256,448]{1,0:T(8,128)(2,1)}, bf16[256,448]{1,0:T(8,128)(2,1)}) custom-call(s32[4]{0:T(128)S(1)} %pad_add_fusion.pos_ref, bf16[4,256,256]{2,1,0:T(8,128)(2,1)S(1)} %all_to_all.29.own_ref, bf16[4,256,256]{2,1,0:T(8,128)(2,1)S(1)} %collective-permute-done.18.oth_ref, bf16[2,224,448]{2,1,0:T(8,128)(2,1)} %copy-done.2, ...), custom_call_target="tpu_custom_call" | custom-call | tf_op jit(solution)/shard_map/pallas_call | solution.py:42
  163.5 3.0 %collective-permute-start.19 = (bf16[256,448]{1,0:T(8,128)(2,1)}, bf16[256,448]{1,0:T(8,128)(2,1)S(1)}, u32[]{:S(2)}, u32[]{:S(2)}) collective-permute-start(bf16[256,448]{1,0:T(8,128)(2,1)} %get-tuple-element.57), channel_id=1, source_target_pairs={{0,1},{4,3},{8,0},{12,2},{16,5},{20,7},{24,4},{28,6},{1,9},{5,11},... | collective-permute-start | bytes 688136 | tf_op jit(solution)/shard_map/ppermute | solution.py:429
  166.5 3.7 %collective-permute-start.20 = (bf16[256,448]{1,0:T(8,128)(2,1)}, bf16[256,448]{1,0:T(8,128)(2,1)S(1)}, u32[]{:S(2)}, u32[]{:S(2)}) collective-permute-start(bf16[256,448]{1,0:T(8,128)(2,1)} %get-tuple-element.58), channel_id=1, source_target_pairs={{0,0},{4,2},{8,1},{12,3},{16,4},{20,6},{24,5},{28,7},{1,8},{5,10},... | collective-permute-start | bytes 688136 | tf_op jit(solution)/shard_map/ppermute | solution.py:429
  170.2 5.2 %collective-permute-done.19 = bf16[256,448]{1,0:T(8,128)(2,1)S(1)} collective-permute-done((bf16[256,448]{1,0:T(8,128)(2,1)}, bf16[256,448]{1,0:T(8,128)(2,1)S(1)}, u32[]{:S(2)}, u32[]{:S(2)}) %collective-permute-start.19) | collective-permute-done | bytes 229408 | tf_op jit(solution)/shard_map/ppermute | solution.py:429
  175.4 1.3 collective-permute-done.20
  176.7 0.2 copy.81
  176.8 0.2 copy.82
  177.0 0.9 fusion.1
  (66 shorter events, 1.2 us)
Async XLA Ops:
  0.0 10.3 %copy-start.16 = (s32[32]{0:T(128)S(1)}, s32[32]{0:T(128)}, u32[]{:S(2)}) copy-start(s32[32]{0:T(128)} %param.19) | copy-start | bytes 388
  1.3 12.1 %collective-permute-start.1 = (bf16[128,896]{1,0:T(8,128)(2,1)S(1)}, bf16[128,896]{1,0:T(8,128)(2,1)S(1)}, u32[]{:S(2)}, u32[]{:S(2)}) collective-permute-start(bf16[128,896]{1,0:T(8,128)(2,1)S(1)} %copy.76.refs_1_), channel_id=1, source_target_pairs={{0,24},{8,0},{16,8},{24,16},{1,25},{9,1},{17,9},{25,17},{2,26},{10... | collective-permute-start | bytes 688136 | tf_op jit(solution)/shard_map/ppermute | solution.py:308
  1.4 27.1 %collective-permute-start.2 = (bf16[128,896]{1,0:T(8,128)(2,1)S(1)}, bf16[128,896]{1,0:T(8,128)(2,1)S(1)}, u32[]{:S(2)}, u32[]{:S(2)}) collective-permute-start(bf16[128,896]{1,0:T(8,128)(2,1)S(1)} %copy.76.refs_1_), channel_id=1, source_target_pairs={{0,8},{8,16},{16,24},{24,0},{1,9},{9,17},{17,25},{25,1},{2,10},{10... | collective-permute-start | bytes 688136 | tf_op jit(solution)/shard_map/ppermute | solution.py:308
  3.0 10.4 %collective-permute-start = (bf16[128,896]{1,0:T(8,128)(2,1)S(1)}, bf16[128,896]{1,0:T(8,128)(2,1)S(1)}, u32[]{:S(2)}, u32[]{:S(2)}) collective-permute-start(bf16[128,896]{1,0:T(8,128)(2,1)S(1)} %copy.75.refs_0_), channel_id=1, source_target_pairs={{0,8},{8,16},{16,24},{24,0},{1,9},{9,17},{17,25},{25,1},{2,10},{10... | collective-permute-start | bytes 688136 | tf_op jit(solution)/shard_map/ppermute | solution.py:308
  4.4 24.1 %collective-permute-start.5 = (bf16[128,896]{1,0:T(8,128)(2,1)S(1)}, bf16[128,896]{1,0:T(8,128)(2,1)S(1)}, u32[]{:S(2)}, u32[]{:S(2)}) collective-permute-start(bf16[128,896]{1,0:T(8,128)(2,1)S(1)} %copy.75.refs_0_), channel_id=1, source_target_pairs={{0,24},{8,0},{16,8},{24,16},{1,25},{9,1},{17,9},{25,17},{2,26},{10... | collective-permute-start | bytes 688136 | tf_op jit(solution)/shard_map/ppermute | solution.py:308
  8.2 20.3 %collective-permute-start.6 = (bf16[448,288]{1,0:T(8,128)(2,1)S(1)}, bf16[448,288]{1,0:T(8,128)(2,1)S(1)}, u32[]{:S(2)}, u32[]{:S(2)}) collective-permute-start(bf16[448,288]{1,0:T(8,128)(2,1)S(1)} %pad_maximum_fusion.2.refs_8_), channel_id=1, source_target_pairs={{0,4},{4,0},{1,5},{5,1},{2,6},{6,2},{3,7},{7,3},{8,12},{12,8},{9,1... | collective-permute-start | bytes 774152 | tf_op jit(solution)/shard_map/ppermute | solution.py:317
  13.4 15.1 %collective-permute-start.3 = (bf16[128,896]{1,0:T(8,128)(2,1)S(1)}, bf16[128,896]{1,0:T(8,128)(2,1)S(1)}, u32[]{:S(2)}, u32[]{:S(2)}) collective-permute-start(bf16[128,896]{1,0:T(8,128)(2,1)S(1)} %collective-permute-done.refs_2_), channel_id=1, source_target_pairs={{0,8},{8,16},{16,24},{24,0},{1,9},{9,17},{17,25},{25,1},{2,10},{10... | collective-permute-start | bytes 688136 | tf_op jit(solution)/shard_map/ppermute | solution.py:308
  13.7 14.8 %collective-permute-start.4 = (bf16[128,896]{1,0:T(8,128)(2,1)S(1)}, bf16[128,896]{1,0:T(8,128)(2,1)S(1)}, u32[]{:S(2)}, u32[]{:S(2)}) collective-permute-start(bf16[128,896]{1,0:T(8,128)(2,1)S(1)} %collective-permute-done.1.refs_7_), channel_id=1, source_target_pairs={{0,24},{8,0},{16,8},{24,16},{1,25},{9,1},{17,9},{25,17},{2,26},{10... | collective-permute-start | bytes 688136 | tf_op jit(solution)/shard_map/ppermute | solution.py:308
  17.4 19.6 %all-to-all-start = ((s32[32,1,1]{2,1,0:T(1,128)}), s32[32,1,1]{2,1,0:T(1,128)S(1)}, u32[]{:S(2)}, u32[]{:S(2)}) async-start(s32[32,1,1]{2,1,0:T(1,128)} %copy.67), calls=%async_computation | async-start | bytes 32768 | tf_op jit(solution)/shard_map/all_to_all | solution.py:330
  36.9 35.7 %all-to-all-start.1 = ((bf16[4,256,1152]{2,1,0:T(8,128)(2,1)}), bf16[4,256,1152]{2,1,0:T(8,128)(2,1)S(1)}, u32[]{:S(2)}, u32[]{:S(2)}) async-start(bf16[4,256,1152]{2,1,0:T(8,128)(2,1)} %shard_map.118), calls=%async_computation.1 | async-start | bytes 4718592 | tf_op jit(solution)/shard_map/all_to_all | solution.py:352
  47.9 8.5 %copy-start.12 = (bf16[32,273,2]{1,2,0:T(2,128)(2,1)S(1)}, bf16[32,273,2]{1,2,0:T(2,128)(2,1)}, u32[]{:S(2)}) copy-start(bf16[32,273,2]{1,2,0:T(2,128)(2,1)} %param.18) | copy-start | bytes 104836
  47.9 9.5 %copy-start.14 = (s32[512]{0:T(512)S(1)}, s32[512]{0:T(512)}, u32[]{:S(2)}) copy-start(s32[512]{0:T(512)} %param.20) | copy-start | bytes 6148
  47.9 11.8 %copy-start.17 = (bf16[224,448]{1,0:T(8,128)(2,1)S(1)}, bf16[224,448]{1,0:T(8,128)(2,1)}, u32[]{:S(2)}) copy-start(bf16[224,448]{1,0:T(8,128)(2,1)} %param.16) | copy-start | bytes 602116
  56.4 36.3 %copy-start.15 = (s32[512]{0:T(512)S(1)}, s32[512]{0:T(512)}, u32[]{:S(2)}) copy-start(s32[512]{0:T(512)} %param.23) | copy-start | bytes 6148
  59.7 15.4 %collective-permute-start.8 = (bf16[224,448]{1,0:T(8,128)(2,1)S(1)}, bf16[224,448]{1,0:T(8,128)(2,1)S(1)}, u32[]{:S(2)}, u32[]{:S(2)}) collective-permute-start(bf16[224,448]{1,0:T(8,128)(2,1)S(1)} %copy-done.17), channel_id=1, source_target_pairs={{0,0},{1,2},{2,4},{3,6},{4,1},{5,3},{6,5},{7,7},{8,8},{9,10},{10,1... | collective-permute-start | bytes 602120 | tf_op jit(solution)/shard_map/ppermute | solution.py:321
  66.8 8.3 %collective-permute-start.9 = (bf16[224,448]{1,0:T(8,128)(2,1)S(1)}, bf16[224,448]{1,0:T(8,128)(2,1)S(1)}, u32[]{:S(2)}, u32[]{:S(2)}) collective-permute-start(bf16[224,448]{1,0:T(8,128)(2,1)S(1)} %copy-done.17), channel_id=1, source_target_pairs={{0,1},{1,3},{2,5},{3,7},{4,0},{5,2},{6,4},{7,6},{8,9},{9,11},{10,1... | collective-permute-start | bytes 602120 | tf_op jit(solution)/shard_map/ppermute | solution.py:321
  66.9 12.8 %collective-permute-start.10 = (bf16[224,448]{1,0:T(8,128)(2,1)S(1)}, bf16[224,448]{1,0:T(8,128)(2,1)S(1)}, u32[]{:S(2)}, u32[]{:S(2)}) collective-permute-start(bf16[224,448]{1,0:T(8,128)(2,1)S(1)} %copy-done.17), channel_id=1, source_target_pairs={{0,2},{1,0},{2,6},{3,4},{4,3},{5,1},{6,7},{7,5},{8,10},{9,8},{10,1... | collective-permute-start | bytes 602120 | tf_op jit(solution)/shard_map/ppermute | solution.py:321
  68.4 11.4 %collective-permute-start.11 = (bf16[224,448]{1,0:T(8,128)(2,1)S(1)}, bf16[224,448]{1,0:T(8,128)(2,1)S(1)}, u32[]{:S(2)}, u32[]{:S(2)}) collective-permute-start(bf16[224,448]{1,0:T(8,128)(2,1)S(1)} %copy-done.17), channel_id=1, source_target_pairs={{0,3},{1,1},{2,7},{3,5},{4,2},{5,0},{6,6},{7,4},{8,11},{9,9},{10,1... | collective-permute-start | bytes 602120 | tf_op jit(solution)/shard_map/ppermute | solution.py:321
  74.7 5.1 %collective-permute-start.7 = (bf16[512,288]{1,0:T(8,128)(2,1)}, bf16[512,288]{1,0:T(8,128)(2,1)S(1)}, u32[]{:S(2)}, u32[]{:S(2)}) collective-permute-start(bf16[512,288]{1,0:T(8,128)(2,1)} %get-tuple-element.36), channel_id=1, source_target_pairs={{0,4},{4,0},{1,5},{5,1},{2,6},{6,2},{3,7},{7,3},{8,12},{12,8},{9,1... | collective-permute-start | bytes 884744 | tf_op jit(solution)/shard_map/ppermute | solution.py:357
  75.2 39.4 %copy-start.2 = (bf16[2,224,448]{2,1,0:T(8,128)(2,1)}, bf16[2,224,448]{2,1,0:T(8,128)(2,1)S(1)}, u32[]{:S(2)}) copy-start(bf16[2,224,448]{2,1,0:T(8,128)(2,1)S(1)} %pad_maximum_fusion.refs_0_) | copy-start | bytes 1204228
  79.8 34.7 %copy-start.3 = (bf16[2,224,448]{2,1,0:T(8,128)(2,1)}, bf16[2,224,448]{2,1,0:T(8,128)(2,1)S(1)}, u32[]{:S(2)}) copy-start(bf16[2,224,448]{2,1,0:T(8,128)(2,1)S(1)} %pad_maximum_fusion.1.refs_1_) | copy-start | bytes 1204228
  79.8 13.7 %copy-start.1 = (bf16[512,288]{1,0:T(8,128)(2,1)}, bf16[512,288]{1,0:T(8,128)(2,1)S(1)}, u32[]{:S(2)}) copy-start(bf16[512,288]{1,0:T(8,128)(2,1)S(1)} %collective-permute-done.7.rec_ref) | copy-start | bytes 884740
  79.8 1.3 copy-start
  83.4 31.1 %collective-permute-start.12 = (bf16[2,224,448]{2,1,0:T(8,128)(2,1)S(1)}, bf16[2,224,448]{2,1,0:T(8,128)(2,1)S(1)}, u32[]{:S(2)}, u32[]{:S(2)}) collective-permute-start(bf16[2,224,448]{2,1,0:T(8,128)(2,1)S(1)} %pad_maximum_fusion.refs_0_), channel_id=1, source_target_pairs={{0,8},{8,16},{16,24},{24,0},{1,9},{9,17},{17,25},{25,1},{2,10},{10... | collective-permute-start | bytes 1204232 | tf_op jit(solution)/shard_map/ppermute | solution.py:308
  83.4 31.1 %collective-permute-start.13 = (bf16[2,224,448]{2,1,0:T(8,128)(2,1)S(1)}, bf16[2,224,448]{2,1,0:T(8,128)(2,1)S(1)}, u32[]{:S(2)}, u32[]{:S(2)}) collective-permute-start(bf16[2,224,448]{2,1,0:T(8,128)(2,1)S(1)} %pad_maximum_fusion.1.refs_1_), channel_id=1, source_target_pairs={{0,8},{8,16},{16,24},{24,0},{1,9},{9,17},{17,25},{25,1},{2,10},{10... | collective-permute-start | bytes 1204232 | tf_op jit(solution)/shard_map/ppermute | solution.py:308
  85.5 29.1 %collective-permute-start.14 = (bf16[2,224,448]{2,1,0:T(8,128)(2,1)S(1)}, bf16[2,224,448]{2,1,0:T(8,128)(2,1)S(1)}, u32[]{:S(2)}, u32[]{:S(2)}) collective-permute-start(bf16[2,224,448]{2,1,0:T(8,128)(2,1)S(1)} %pad_maximum_fusion.refs_0_), channel_id=1, source_target_pairs={{0,24},{8,0},{16,8},{24,16},{1,25},{9,1},{17,9},{25,17},{2,26},{10... | collective-permute-start | bytes 1204232 | tf_op jit(solution)/shard_map/ppermute | solution.py:308
  86.2 28.4 %collective-permute-start.15 = (bf16[2,224,448]{2,1,0:T(8,128)(2,1)S(1)}, bf16[2,224,448]{2,1,0:T(8,128)(2,1)S(1)}, u32[]{:S(2)}, u32[]{:S(2)}) collective-permute-start(bf16[2,224,448]{2,1,0:T(8,128)(2,1)S(1)} %pad_maximum_fusion.1.refs_1_), channel_id=1, source_target_pairs={{0,24},{8,0},{16,8},{24,16},{1,25},{9,1},{17,9},{25,17},{2,26},{10... | collective-permute-start | bytes 1204232 | tf_op jit(solution)/shard_map/ppermute | solution.py:308
  88.8 13.3 %all-to-all-start.2 = ((bf16[32,16,128]{2,1,0:T(8,128)(2,1)}), bf16[32,16,128]{2,1,0:T(8,128)(2,1)S(1)}, u32[]{:S(2)}, u32[]{:S(2)}) async-start(bf16[32,16,128]{2,1,0:T(8,128)(2,1)} %get-tuple-element.39), calls=%async_computation.2 | async-start | bytes 262144 | tf_op jit(solution)/shard_map/all_to_all | solution.py:375
  101.8 23.5 %copy-start.13 = (s32[512]{0:T(512)S(1)}, s32[512]{0:T(512)}, u32[]{:S(2)}) copy-start(s32[512]{0:T(512)} %multiply_add_fusion) | copy-start | bytes 6148
  102.1 0.7 copy-start.5
  114.5 44.9 %copy-start.6 = (bf16[2,224,448]{2,1,0:T(8,128)(2,1)}, bf16[2,224,448]{2,1,0:T(8,128)(2,1)S(1)}, u32[]{:S(2)}) copy-start(bf16[2,224,448]{2,1,0:T(8,128)(2,1)S(1)} %collective-permute-done.12.refs_2_) | copy-start | bytes 1204228
  114.6 44.9 %copy-start.7 = (bf16[2,224,448]{2,1,0:T(8,128)(2,1)}, bf16[2,224,448]{2,1,0:T(8,128)(2,1)S(1)}, u32[]{:S(2)}) copy-start(bf16[2,224,448]{2,1,0:T(8,128)(2,1)S(1)} %collective-permute-done.13.refs_3_) | copy-start | bytes 1204228
  114.6 44.9 %copy-start.8 = (bf16[2,224,448]{2,1,0:T(8,128)(2,1)}, bf16[2,224,448]{2,1,0:T(8,128)(2,1)S(1)}, u32[]{:S(2)}) copy-start(bf16[2,224,448]{2,1,0:T(8,128)(2,1)S(1)} %collective-permute-done.14.refs_6_) | copy-start | bytes 1204228
  114.6 44.9 %copy-start.9 = (bf16[2,224,448]{2,1,0:T(8,128)(2,1)}, bf16[2,224,448]{2,1,0:T(8,128)(2,1)S(1)}, u32[]{:S(2)}) copy-start(bf16[2,224,448]{2,1,0:T(8,128)(2,1)S(1)} %collective-permute-done.15.refs_7_) | copy-start | bytes 1204228
  114.6 23.0 %all-to-all-start.3 = ((bf16[32,16,512]{2,1,0:T(8,128)(2,1)}), bf16[32,16,512]{2,1,0:T(8,128)(2,1)S(1)}, u32[]{:S(2)}, u32[]{:S(2)}) async-start(bf16[32,16,512]{2,1,0:T(8,128)(2,1)} %get-tuple-element.48), calls=%async_computation.3 | async-start | bytes 1048576 | tf_op jit(solution)/shard_map/all_to_all | solution.py:400
  123.4 9.7 %collective-permute-start.16 = (bf16[2,224,448]{2,1,0:T(8,128)(2,1)S(1)}, bf16[2,224,448]{2,1,0:T(8,128)(2,1)S(1)}, u32[]{:S(2)}, u32[]{:S(2)}) collective-permute-start(bf16[2,224,448]{2,1,0:T(8,128)(2,1)S(1)} %collective-permute-done.12.refs_2_), channel_id=1, source_target_pairs={{0,8},{8,16},{16,24},{24,0},{1,9},{9,17},{17,25},{25,1},{2,10},{10... | collective-permute-start | bytes 1204232 | tf_op jit(solution)/shard_map/ppermute | solution.py:308
  123.7 9.4 %collective-permute-start.17 = (bf16[2,224,448]{2,1,0:T(8,128)(2,1)S(1)}, bf16[2,224,448]{2,1,0:T(8,128)(2,1)S(1)}, u32[]{:S(2)}, u32[]{:S(2)}) collective-permute-start(bf16[2,224,448]{2,1,0:T(8,128)(2,1)S(1)} %collective-permute-done.15.refs_7_), channel_id=1, source_target_pairs={{0,24},{8,0},{16,8},{24,16},{1,25},{9,1},{17,9},{25,17},{2,26},{10... | collective-permute-start | bytes 1204232 | tf_op jit(solution)/shard_map/ppermute | solution.py:308
  133.1 26.4 %copy-start.10 = (bf16[2,224,448]{2,1,0:T(8,128)(2,1)}, bf16[2,224,448]{2,1,0:T(8,128)(2,1)S(1)}, u32[]{:S(2)}) copy-start(bf16[2,224,448]{2,1,0:T(8,128)(2,1)S(1)} %collective-permute-done.16.refs_4_) | copy-start | bytes 1204228
  133.2 26.3 %copy-start.11 = (bf16[2,224,448]{2,1,0:T(8,128)(2,1)}, bf16[2,224,448]{2,1,0:T(8,128)(2,1)S(1)}, u32[]{:S(2)}) copy-start(bf16[2,224,448]{2,1,0:T(8,128)(2,1)S(1)} %collective-permute-done.17.refs_5_) | copy-start | bytes 1204228
  141.2 35.8 %copy-start.4 = (bf16[256,2,448]{0,2,1:T(8,128)(2,1)S(1)}, bf16[256,2,448]{0,2,1:T(8,128)(2,1)}, u32[]{:S(2)}) copy-start(bf16[256,2,448]{0,2,1:T(8,128)(2,1)} %param.12) | copy-start | bytes 1376260
  151.7 7.8 %collective-permute-start.18 = (bf16[4,256,256]{2,1,0:T(8,128)(2,1)S(1)}, bf16[4,256,256]{2,1,0:T(8,128)(2,1)S(1)}, u32[]{:S(2)}, u32[]{:S(2)}) collective-permute-start(bf16[4,256,256]{2,1,0:T(8,128)(2,1)S(1)} %all_to_all.29.own_ref), channel_id=1, source_target_pairs={{0,4},{4,0},{1,5},{5,1},{2,6},{6,2},{3,7},{7,3},{8,12},{12,8},{9,1... | collective-permute-start | bytes 1572872 | tf_op jit(solution)/shard_map/ppermute | solution.py:417
  163.5 11.8 %collective-permute-start.19 = (bf16[256,448]{1,0:T(8,128)(2,1)}, bf16[256,448]{1,0:T(8,128)(2,1)S(1)}, u32[]{:S(2)}, u32[]{:S(2)}) collective-permute-start(bf16[256,448]{1,0:T(8,128)(2,1)} %get-tuple-element.57), channel_id=1, source_target_pairs={{0,1},{4,3},{8,0},{12,2},{16,5},{20,7},{24,4},{28,6},{1,9},{5,11},... | collective-permute-start | bytes 688136 | tf_op jit(solution)/shard_map/ppermute | solution.py:429
  166.5 10.1 %collective-permute-start.20 = (bf16[256,448]{1,0:T(8,128)(2,1)}, bf16[256,448]{1,0:T(8,128)(2,1)S(1)}, u32[]{:S(2)}, u32[]{:S(2)}) collective-permute-start(bf16[256,448]{1,0:T(8,128)(2,1)} %get-tuple-element.58), channel_id=1, source_target_pairs={{0,0},{4,2},{8,1},{12,3},{16,4},{20,6},{24,5},{28,7},{1,8},{5,10},... | collective-permute-start | bytes 688136 | tf_op jit(solution)/shard_map/ppermute | solution.py:429

commit v6 on v5

--- a/solution.py
+++ b/solution.py
@@ -124,7 +124,7 @@
             keep_ref[slot] = grouped[p * 16 : (p + 1) * 16, :]
 
 
-def slot_kernel(pos_ref, owner_ref, rec_ref, keep_ref, state_ref, norm_ref, send_ref, own_ref, buf):
+def slot_kernel(pos_ref, owner_ref, rec_ref, keep_ref, state_ref, norm_ref, send_ref, own_ref, buf, spread):
     me = pos_ref[2]
     step = pl.program_id(0)
 
@@ -132,6 +132,14 @@
     def _():
         send_ref[...] = jnp.zeros_like(send_ref)
         own_ref[...] = jnp.zeros_like(own_ref)
+        row, f = iota((128, 384), 0), iota((128, 384), 1)
+        a_at = jnp.where(f >= 17, lax.shift_right_logical(f - 17, 4), f - 1)
+        b_at = (f - 17) & 15
+        live_a = (f >= 1) & (f < 273)
+        live_b = (f >= 17) & (f < 273)
+        for base in range(4):
+            spread[base * 2] = onehot(live_a & (row == a_at + base * 16))
+            spread[base * 2 + 1] = onehot(live_b & (row == b_at + base * 16))
 
     for i in range(8):
         slot = step * 8 + i
@@ -146,26 +154,20 @@
             buf[i * 16 : (i + 1) * 16, :] = keep_ref[slot]
 
     q = buf[...]
-    row, f = iota((128, 384), 0), iota((128, 384), 1)
     lane = iota((1, 384), 1)
     square, line = lane >= 17, (lane >= 1) & (lane < 17)
     unit_a = jnp.where(lane == 0, 1.0, 0.0)
     unit_b = jnp.where(lane < 17, 1.0, 0.0)
     scale = jnp.where(square, 0.5**0.5 / 4.0, jnp.where(line, 0.5, 1.0))
     scale = jnp.where(lane < 273, scale, 0.0)
-    a_at = jnp.where(f >= 17, lax.shift_right_logical(f - 17, 4), f - 1)
-    b_at = (f - 17) & 15
-    live_a = (f >= 1) & (f < 273)
-    live_b = (f >= 17) & (f < 273)
     r, c = iota((128, 16), 0), iota((128, 16), 1)
     den_lane = iota((128, 32), 1)
     phis, dens = [], []
     for t in range(2):
         tile = jnp.zeros((128, 32), F32)
         for h in range(2):
-            base = t * 32 + h * 16
-            left = dot(q, onehot(live_a & (row == a_at + base))) + unit_a
-            right = dot(q, onehot(live_b & (row == b_at + base))) + unit_b
+            left = dot(q, spread[t * 4 + h * 2]) + unit_a
+            right = dot(q, spread[t * 4 + h * 2 + 1]) + unit_b
             phi = left * right * scale
             norm = dot(onehot(2 * lax.shift_right_logical(r, 4) + h == c), norm_ref[...])
             den = jnp.sum(phi * norm, axis=1, keepdims=True)
@@ -304,23 +306,6 @@
     y, core, col = lax.axis_index("y"), lax.axis_index("core"), lax.axis_index("col")
     me = lax.axis_index(("req", "col"))
     pos = jnp.stack([y, core, me, col]).astype(jnp.int32)
-    def over_y(x, step):
-        return lax.ppermute(x, "y", [(i, (i + step) % 4) for i in range(4)])
-
-    top, low = tokens[:128].reshape(128, 896), tokens[128:].reshape(128, 896)
-    top_1, low_3 = over_y(top, 1), over_y(low, 3)
-    low_1, top_3 = over_y(low, 1), over_y(top, 3)
-    top_1, low_3, w_out = lax.optimization_barrier((top_1, low_3, w_out))
-    blocks = [top, low, top_1, low_1, over_y(top_1, 1), over_y(low_3, 3), top_3, low_3]
-    value_w = jnp.moveaxis(w_value.reshape(2, 448, 112), 0, 1).reshape(448, 224)
-    mine = jnp.concatenate([value_w, w_query, w_key], axis=1)
-    theirs = lax.ppermute(mine, "core", [(0, 1), (1, 0)])
-    pieces = []
-    for s in range(4):
-        perm = [(k * 4 + c, (c >> 1) * 4 + (s ^ (2 * (c & 1) + k))) for k in range(2) for c in range(4)]
-        pieces.append(lax.ppermute(w_out, ("core", "col"), perm))
-    pieces = [jnp.stack(pieces[:2]), jnp.stack(pieces[2:])]
-
     owner = slot_prompt // 32
     slots = jnp.arange(32, dtype=jnp.int32)
     away = owner != me
@@ -328,6 +313,18 @@
         jnp.where((owner[None, :] == slots[:, None]) & away[None, :], (slots * 32 + slot_prompt % 32 + 1)[None, :], 0), axis=1
     )
     told = lax.all_to_all(code[:, None], ("req", "col"), split_axis=0, concat_axis=0, tiled=True)[:, 0]
+    def over_y(x, step):
+        return lax.ppermute(x, "y", [(i, (i + step) % 4) for i in range(4)])
+
+    top, low = tokens[:128].reshape(128, 896), tokens[128:].reshape(128, 896)
+    top_1, low_3 = over_y(top, 1), over_y(low, 3)
+    low_1, top_3 = over_y(low, 1), over_y(top, 3)
+    top_1, low_3, w_value, w_query, w_key = lax.optimization_barrier((top_1, low_3, w_value, w_query, w_key))
+    top_1, low_3, low_1, top_3, told = lax.optimization_barrier((top_1, low_3, low_1, top_3, told))
+    blocks = [top, low, top_1, low_1, over_y(top_1, 1), over_y(low_3, 3), top_3, low_3]
+    value_w = jnp.moveaxis(w_value.reshape(2, 448, 112), 0, 1).reshape(448, 224)
+    mine = jnp.concatenate([value_w, w_query, w_key], axis=1)
+    theirs = lax.ppermute(mine, "core", [(0, 1), (1, 0)])
     here = (slot_prompt[None, :] == (me * 32 + slots)[:, None])
     there = (told[None, :] > 0) & ((told[None, :] - 1) % 32 == slots[:, None])
     at_slot = jnp.max(jnp.where(here, slots[None, :], 0), axis=1)
@@ -370,12 +367,17 @@
         scratch=[pltpu.VMEM((512, 128), BF)],
         free=(3, 4),
     )
-    q_send, pieces = lax.optimization_barrier((q_send, pieces))
-    out_w = [over_y(x, step) for step in (1, 3) for x in pieces]
+    q_send, w_out = lax.optimization_barrier((q_send, w_out))
+    pieces = []
+    for s in range(4):
+        perm = [(k * 4 + c, (c >> 1) * 4 + (s ^ (2 * (c & 1) + k))) for k in range(2) for c in range(4)]
+        pieces.append(lax.ppermute(w_out, ("core", "col"), perm))
+    pieces = [jnp.stack(pieces[:2]), jnp.stack(pieces[2:])]
     q_rec = lax.all_to_all(q_send, ("req", "col"), split_axis=0, concat_axis=0, tiled=True)
+    q_rec, pieces = lax.optimization_barrier((q_rec, pieces))
+    near_1, near_3 = over_y(pieces[0], 1), over_y(pieces[1], 3)
     shape = jax.ShapeDtypeStruct((2, 512, 256), F32)
     num = call(tail_kernel, shape, 1, pos, own, rec, tail_keys, tail_values, tail_length[:, None])
-    q_rec, num = lax.optimization_barrier((q_rec, num))
     shape = jax.ShapeDtypeStruct((32, 16, 512), BF)
     whole = pl.BlockSpec((32, 16, 128), lambda i: (0, 0, 0))
     whole_out = pl.BlockSpec((32, 16, 512), lambda i: (0, 0, 0))
@@ -392,13 +394,14 @@
             pl.BlockSpec((16, 384), lambda i: (i, 0)),
         ],
         out_specs=(whole_out, whole_out),
-        scratch_shapes=[pltpu.VMEM((128, 128), BF)],
+        scratch_shapes=[pltpu.VMEM((128, 128), BF), pltpu.VMEM((8, 128, 384), BF)],
         compiler_params=pltpu.CompilerParams(vmem_limit_bytes=VMEM_LIMIT),
     )(pos, owner, in_hbm(q_rec), in_hbm(q_keep), in_hbm(states), in_hbm(norms))
-    r_send, out_w = lax.optimization_barrier((r_send, out_w))
-    far_1, far_3 = over_y(out_w[0], 1), over_y(out_w[3], 3)
+    r_send, near_1, near_3 = lax.optimization_barrier((r_send, near_1, near_3))
+    out_w = [near_1, over_y(pieces[1], 1), over_y(pieces[0], 3), near_3]
+    far_1, far_3 = over_y(near_1, 1), over_y(near_3, 3)
     r_rec = lax.all_to_all(r_send, ("req", "col"), split_axis=0, concat_axis=0, tiled=True)
-    r_rec, far_1, far_3 = lax.optimization_barrier((r_rec, far_1, far_3))
+    r_rec, num, out_w, far_1, far_3 = lax.optimization_barrier((r_rec, num, out_w, far_1, far_3))
     heads = call(
         combine_kernel,
         jax.ShapeDtypeStruct((4, 256, 256), BF),

time: 181 us -> 195 us (1.077)
  blocking collectives: 10.5 us -> 31.1 us
  starting transfers between devices: 69.1 us -> 50.8 us
  waiting for transfers between devices: 31.8 us -> 44.1 us
    all_to_all x0 -> x1, blocking collectives: none -> 19.4 us  [body(): lax.all_to_all(code[:, None], ('req', 'col'), split_axis=0, concat_axis=0...]
    all_to_all x1 -> x0, starting transfers between devices: 11 us -> none  [body(): lax.all_to_all(code[:, None], ('req', 'col'), split_axis=0, concat_axis=0...]
    all_to_all x1, waiting for transfers between devices: 0.01 us -> 9.37 us  [body(): lax.all_to_all(partial, 'col', split_axis=0, concat_axis=0, tiled=True)]
    ppermute x4, starting transfers between devices: 12.9 us -> 6.06 us  [body(): pieces.append(lax.ppermute(w_out, ('core', 'col'), perm))]
    ppermute x12, waiting for transfers between devices: 10.2 us -> 16.3 us  [over_y(): return lax.ppermute(x, 'y', [(i, (i + step) % 4) for i in range(4)])]
    all_to_all x1, starting transfers between devices: 8.81 us -> 3.9 us  [body(): lax.all_to_all(r_send, ('req', 'col'), split_axis=0, concat_axis=0, tiled...]
    all_to_all x1, waiting for transfers between devices: 0.23 us -> 4.74 us  [body(): lax.all_to_all(q_send, ('req', 'col'), split_axis=0, concat_axis=0, tiled...]
    all_to_all x1, waiting for transfers between devices: 4.46 us -> 0.01 us  [body(): lax.all_to_all(r_send, ('req', 'col'), split_axis=0, concat_axis=0, tiled...]
  transfers between devices with their start and end apart: 25 -> 24, of which waited for: 11 -> 11; matrix products, arithmetic and copies ran while one was open for 14% -> 13% of each run, Pallas kernels for 15% -> 11%
where the time goes in v6:
time: 195 us; the launch traced here: 192 us
  starting transfers between devices  50.8 us (26%)
  waiting for transfers between devices  44.1 us (23%)
  Pallas kernels  36.3 us (19%)
  blocking collectives  31.1 us (16%)
  local copies, waits for them, and re-layouts  24.6 us (13%)
  other arithmetic  4.7 us (2%)
    pallas_call x6, Pallas kernels, call(): pl.pallas_call(kernel, grid=(1,), out_shape=jax.tree.map(lambda x: pltpu....  24.4 us
    all_to_all x1, blocking collectives, body(): lax.all_to_all(code[:, None], ('req', 'col'), split_axis=0, concat_axis=0...  19.4 us
    ppermute x12, waiting for transfers between devices, over_y(): return lax.ppermute(x, 'y', [(i, (i + step) % 4) for i in range(4)])  16.3 us
    ppermute x12, starting transfers between devices, over_y(): return lax.ppermute(x, 'y', [(i, (i + step) % 4) for i in range(4)])  13.8 us
    pallas_call x1, Pallas kernels, body(): pl.pallas_call(slot_kernel, grid=(4,), out_shape=(pltpu.HBM(shape.shape,...  11.9 us
    all_to_all x1, blocking collectives, body(): heads = lax.all_to_all(heads, 'y', split_axis=0, concat_axis=0, tiled=True)  11.6 us
    all_to_all x1, waiting for transfers between devices, body(): lax.all_to_all(partial, 'col', split_axis=0, concat_axis=0, tiled=True)  9.37 us
    unnamed x31, local copies, waits for them, and re-layouts  8.52 us
  transfers between devices with their start and end apart: 24, of which 11 were waited for; matrix products, arithmetic and copies ran while one was open for 13% of the time, Pallas kernels for 11%

profile of v6, /device:TPU:9, one launch (start us, length us, event | category | flops | bytes accessed | tf_op | source)
XLA Modules:
  0.0 191.8 jit_solution(5915229181280287066)
XLA Ops:
  0.0 1.1 fusion.8
  1.1 0.2 copy.68.refs_1_
  1.3 1.5 collective-permute-start.2
  2.8 0.2 copy.67.refs_0_
  3.0 1.4 collective-permute-start
  4.3 0.2 collective-permute-start.3
  4.6 0.7 fusion.7
  5.2 0.7 broadcast_compare_fusion.1
  5.9 7.5 %collective-permute-done.refs_2_ = bf16[128,896]{1,0:T(8,128)(2,1)S(1)} collective-permute-done((bf16[128,896]{1,0:T(8,128)(2,1)S(1)}, bf16[128,896]{1,0:T(8,128)(2,1)S(1)}, u32[]{:S(2)}, u32[]{:S(2)}) %collective-permute-start) | collective-permute-done | bytes 229408 | tf_op jit(solution)/shard_map/ppermute | solution.py:317
  13.4 1.2 reshape.50
  14.6 0.2 copy.84
  15.0 0.9 copy.73
  15.9 0.9 copy.74
  17.0 2.4 %collective-permute-start.6 = (bf16[448,288]{1,0:T(8,128)(2,1)S(1)}, bf16[448,288]{1,0:T(8,128)(2,1)S(1)}, u32[]{:S(2)}, u32[]{:S(2)}) collective-permute-start(bf16[448,288]{1,0:T(8,128)(2,1)S(1)} %pad_maximum_fusion.2.refs_8_), channel_id=1, source_target_pairs={{0,4},{4,0},{1,5},{5,1},{2,6},{6,2},{3,7},{7,3},{8,12},{12,8},{9,1... | collective-permute-start | bytes 774152 | tf_op jit(solution)/shard_map/ppermute | solution.py:327
  19.6 19.4 %all_to_all.29 = s32[32,1,1]{2,1,0:T(1,128)S(1)} all-to-all(s32[32,1,1]{2,1,0:T(1,128)S(1)} %copy.71), channel_id=1, replica_groups=mesh['req'=8,'y'=4,'core'=2,'col'=4] {'req','col'}, dimensions={0} | all-to-all | bytes 256 | tf_op jit(solution)/shard_map/all_to_all | solution.py:315
  39.0 0.7 reduce
  39.8 2.7 %collective-permute-start.5 = (bf16[128,896]{1,0:T(8,128)(2,1)S(1)}, bf16[128,896]{1,0:T(8,128)(2,1)S(1)}, u32[]{:S(2)}, u32[]{:S(2)}) collective-permute-start(bf16[128,896]{1,0:T(8,128)(2,1)S(1)} %collective-permute-done.1.refs_7_), channel_id=1, source_target_pairs={{0,24},{8,0},{16,8},{24,16},{1,25},{9,1},{17,9},{25,17},{2,26},{10... | collective-permute-start | bytes 688136 | tf_op jit(solution)/shard_map/ppermute | solution.py:317
  42.6 4.3 %collective-permute-done.4.refs_4_ = bf16[128,896]{1,0:T(8,128)(2,1)S(1)} collective-permute-done((bf16[128,896]{1,0:T(8,128)(2,1)S(1)}, bf16[128,896]{1,0:T(8,128)(2,1)S(1)}, u32[]{:S(2)}, u32[]{:S(2)}) %collective-permute-start.4) | collective-permute-done | bytes 229408 | tf_op jit(solution)/shard_map/ppermute | solution.py:317
  46.9 4.0 %shard_map.118 = bf16[4,256,1152]{2,1,0:T(8,128)(2,1)} custom-call(s32[4]{0:T(128)S(1)} %pad_add_fusion.pos_ref, bf16[128,896]{1,0:T(8,128)(2,1)S(1)} %copy.67.refs_0_, bf16[128,896]{1,0:T(8,128)(2,1)S(1)} %copy.68.refs_1_, bf16[128,896]{1,0:T(8,128)(2,1)S(1)} %collective-permute-done.refs_2_, bf16[128,896]{1,0:T(8,128)(2,1)S(1)} %collective-permute-done.2.refs_3_, ...), custom_call_target="tpu_custom_call" | custom-call | tf_op jit(solution)/shard_map/pallas_call | solution.py:42
  50.9 3.6 %all-to-all-start.1 = ((bf16[4,256,1152]{2,1,0:T(8,128)(2,1)}), bf16[4,256,1152]{2,1,0:T(8,128)(2,1)S(1)}, u32[]{:S(2)}, u32[]{:S(2)}) async-start(bf16[4,256,1152]{2,1,0:T(8,128)(2,1)} %shard_map.118), calls=%async_computation.1 | async-start | bytes 4718592 | tf_op jit(solution)/shard_map/all_to_all | solution.py:349
  54.5 7.3 %copy.77 = bf16[1,273,7168]{1,2,0:T(8,128)(2,1)} copy(bf16[1,273,7168]{2,1,0:T(8,128)(2,1)} %param.17) | data formatting | bytes 7827456 | tf_op args[5]
  61.9 8.4 %copy.78 = bf16[273,224,32]{1,0,2:T(8,128)(2,1)} copy(bf16[273,224,32]{0,2,1:T(8,128)(2,1)} %bitcast.26) | data formatting | bytes 7827456 | tf_op jit(solution)/shard_map/reshape;squeeze | solution.py:336
  70.3 0.6 pad.4.norm_ref
  71.0 0.2 compare_reduce_fusion
  71.1 0.2 fusion.2.s_ref
  71.3 0.2 convert_reduce_fusion
  71.6 0.6 multiply_add_fusion
  72.2 9.4 %all-to-all-done.1.p_ref = bf16[4,256,1152]{2,1,0:T(8,128)(2,1)S(1)} async-done(((bf16[4,256,1152]{2,1,0:T(8,128)(2,1)}), bf16[4,256,1152]{2,1,0:T(8,128)(2,1)S(1)}, u32[]{:S(2)}, u32[]{:S(2)}) %all-to-all-start.1) | async-done | bytes 2359328 | tf_op jit(solution)/shard_map/all_to_all | solution.py:349
  81.6 2.0 %shard_map.119 = (bf16[512,288]{1,0:T(8,128)(2,1)}, bf16[512,288]{1,0:T(8,128)(2,1)}) custom-call(s32[4]{0:T(128)S(1)} %pad_add_fusion.pos_ref, bf16[4,256,1152]{2,1,0:T(8,128)(2,1)S(1)} %all-to-all-done.1.p_ref), custom_call_target="tpu_custom_call" | custom-call | tf_op jit(solution)/shard_map/pallas_call | solution.py:42
  83.6 3.0 %collective-permute-start.7 = (bf16[512,288]{1,0:T(8,128)(2,1)}, bf16[512,288]{1,0:T(8,128)(2,1)S(1)}, u32[]{:S(2)}, u32[]{:S(2)}) collective-permute-start(bf16[512,288]{1,0:T(8,128)(2,1)} %get-tuple-element.54), channel_id=1, source_target_pairs={{0,4},{4,0},{1,5},{5,1},{2,6},{6,2},{3,7},{7,3},{8,12},{12,8},{9,1... | collective-permute-start | bytes 884744 | tf_op jit(solution)/shard_map/ppermute | solution.py:354
  86.7 1.4 collective-permute-done.7.rec_ref
  88.2 1.1 copy-done
  89.3 2.4 %shard_map.120 = (bf16[32,16,128]{2,1,0:T(8,128)(2,1)}, bf16[32,16,128]{2,1,0:T(8,128)(2,1)}) custom-call(s32[4]{0:T(128)S(1)} %pad_add_fusion.pos_ref, s32[32]{0:T(128)S(1)} %broadcast_select_fusion.2.g_ref, s32[32]{0:T(128)S(1)} %fusion.2.s_ref, bf16[512,288]{1,0:T(8,128)(2,1)S(1)} %copy-done, bf16[512,288]{1,0:T(8,128)(2,1)S(1)} %collective-permute-done.7.rec_ref, ...), custom_call_target="tpu_custom_call" | custom-call | tf_op jit(solution)/shard_map/pallas_call | solution.py:42
  91.7 1.2 collective-permute-start.10
  92.9 1.9 collective-permute-start.11
  94.9 1.9 %collective-permute-start.8 = (bf16[224,448]{1,0:T(8,128)(2,1)S(1)}, bf16[224,448]{1,0:T(8,128)(2,1)S(1)}, u32[]{:S(2)}, u32[]{:S(2)}) collective-permute-start(bf16[224,448]{1,0:T(8,128)(2,1)S(1)} %copy-done.14), channel_id=1, source_target_pairs={{0,0},{1,2},{2,4},{3,6},{4,1},{5,3},{6,5},{7,7},{8,8},{9,10},{10,1... | collective-permute-start | bytes 602120 | tf_op jit(solution)/shard_map/ppermute | solution.py:374
  96.8 1.0 collective-permute-start.9
  97.8 4.1 %all-to-all-start.2 = ((bf16[32,16,128]{2,1,0:T(8,128)(2,1)}), bf16[32,16,128]{2,1,0:T(8,128)(2,1)S(1)}, u32[]{:S(2)}, u32[]{:S(2)}) async-start(bf16[32,16,128]{2,1,0:T(8,128)(2,1)} %get-tuple-element.56), calls=%async_computation.2 | async-start | bytes 262144 | tf_op jit(solution)/shard_map/all_to_all | solution.py:376
  102.0 4.5 %collective-permute-done.8 = bf16[224,448]{1,0:T(8,128)(2,1)S(1)} collective-permute-done((bf16[224,448]{1,0:T(8,128)(2,1)S(1)}, bf16[224,448]{1,0:T(8,128)(2,1)S(1)}, u32[]{:S(2)}, u32[]{:S(2)}) %collective-permute-start.8) | collective-permute-done | bytes 200736 | tf_op jit(solution)/shard_map/ppermute | solution.py:374
  106.6 4.7 %all-to-all-done.2.rec_ref = bf16[32,16,128]{2,1,0:T(8,128)(2,1)S(1)} async-done(((bf16[32,16,128]{2,1,0:T(8,128)(2,1)}), bf16[32,16,128]{2,1,0:T(8,128)(2,1)S(1)}, u32[]{:S(2)}, u32[]{:S(2)}) %all-to-all-start.2) | async-done | bytes 131104 | tf_op jit(solution)/shard_map/all_to_all | solution.py:376
  111.3 1.8 collective-permute-start.12
  113.1 0.6 collective-permute-start.13
  113.7 11.9 %shard_map.121 = (bf16[32,16,512]{2,1,0:T(8,128)(2,1)}, bf16[32,16,512]{2,1,0:T(8,128)(2,1)}) custom-call(s32[4]{0:T(128)S(1)} %pad_add_fusion.pos_ref, s32[32]{0:T(128)S(1)} %get-tuple-element.80.owner_ref, bf16[32,16,128]{2,1,0:T(8,128)(2,1)} %copy-done.5, bf16[32,16,128]{2,1,0:T(8,128)(2,1)} %get-tuple-element.59.keep_ref, ...), custom_call_target="tpu_custom_call" | custom-call | tf_op jit(solution)/shard_map/pallas_call | solution.py:384
  125.7 3.9 %all-to-all-start.3 = ((bf16[32,16,512]{2,1,0:T(8,128)(2,1)}), bf16[32,16,512]{2,1,0:T(8,128)(2,1)S(1)}, u32[]{:S(2)}, u32[]{:S(2)}) async-start(bf16[32,16,512]{2,1,0:T(8,128)(2,1)} %get-tuple-element.65), calls=%async_computation.3 | async-start | bytes 1048576 | tf_op jit(solution)/shard_map/all_to_all | solution.py:403
  129.6 1.9 collective-permute-start.14
  131.5 1.0 collective-permute-start.15
  132.5 0.5 collective-permute-start.16
  133.0 2.1 %collective-permute-start.17 = (bf16[2,224,448]{2,1,0:T(8,128)(2,1)S(1)}, bf16[2,224,448]{2,1,0:T(8,128)(2,1)}, u32[]{:S(2)}, u32[]{:S(2)}) collective-permute-start(bf16[2,224,448]{2,1,0:T(8,128)(2,1)S(1)} %collective-permute-done.13.refs_7_), channel_id=1, source_target_pairs={{0,24},{8,0},{16,8},{24,16},{1,25},{9,1},{17,9},{25,17},{2,26},{10... | collective-permute-start | bytes 1204232 | tf_op jit(solution)/shard_map/ppermute | solution.py:317
  135.1 0.9 copy.79.len_ref
  135.9 0.9 copy.80.place_ref
  136.8 8.3 %shard_map.122.num_ref = f32[2,512,256]{2,1,0:T(8,128)} custom-call(s32[4]{0:T(128)S(1)} %pad_add_fusion.pos_ref, bf16[512,288]{1,0:T(8,128)(2,1)} %get-tuple-element.53.own_ref, bf16[512,288]{1,0:T(8,128)(2,1)} %copy-done.1, bf16[512,256]{1,0:T(8,128)(2,1)} %tk_ref.1, bf16[512,1792]{1,0:T(8,128)(2,1)} %tv_ref.1, s32[512,1]{1,0:T(8,128)} %copy.79.len_ref), custom_call_target="tpu_custom_call" | custom-call | tf_op jit(solution)/shard_map/pallas_call | solution.py:42
  145.1 4.2 %collective-permute-done.16.refs_4_ = bf16[2,224,448]{2,1,0:T(8,128)(2,1)} collective-permute-done((bf16[2,224,448]{2,1,0:T(8,128)(2,1)S(1)}, bf16[2,224,448]{2,1,0:T(8,128)(2,1)}, u32[]{:S(2)}, u32[]{:S(2)}) %collective-permute-start.16) | collective-permute-done | bytes 401440 | tf_op jit(solution)/shard_map/ppermute | solution.py:317
  149.3 0.3 collective-permute-done.17.refs_5_
  149.6 3.6 %shard_map.123 = bf16[4,256,256]{2,1,0:T(8,128)(2,1)} custom-call(s32[4]{0:T(128)S(1)} %pad_add_fusion.pos_ref, s32[32]{0:T(128)S(1)} %broadcast_select_fusion.2.g_ref, s32[32]{0:T(128)S(1)} %fusion.2.s_ref, f32[2,512,256]{2,1,0:T(8,128)} %shard_map.122.num_ref, bf16[32,16,512]{2,1,0:T(8,128)(2,1)S(1)} %all-to-all-done.3.rec_ref, ...), custom_call_target="tpu_custom_call" | custom-call | tf_op jit(solution)/shard_map/pallas_call | solution.py:42
  153.2 11.6 %all_to_all.30.own_ref = bf16[4,256,256]{2,1,0:T(8,128)(2,1)S(1)} all-to-all(bf16[4,256,256]{2,1,0:T(8,128)(2,1)} %shard_map.123), channel_id=1, replica_groups=mesh['req'=8,'y'=4,'core'=2,'col'=4] {'y'}, dimensions={0} | all-to-all | bytes 1048576 | tf_op jit(solution)/shard_map/all_to_all | solution.py:419
  164.9 6.4 %collective-permute-start.18 = (bf16[4,256,256]{2,1,0:T(8,128)(2,1)S(1)}, bf16[4,256,256]{2,1,0:T(8,128)(2,1)S(1)}, u32[]{:S(2)}, u32[]{:S(2)}) collective-permute-start(bf16[4,256,256]{2,1,0:T(8,128)(2,1)S(1)} %all_to_all.30.own_ref), channel_id=1, source_target_pairs={{0,4},{4,0},{1,5},{5,1},{2,6},{6,2},{3,7},{7,3},{8,12},{12,8},{9,1... | collective-permute-start | bytes 1572872 | tf_op jit(solution)/shard_map/ppermute | solution.py:420
  171.3 1.5 collective-permute-done.18.oth_ref
  172.9 4.1 %shard_map.124 = (bf16[256,448]{1,0:T(8,128)(2,1)}, bf16[256,448]{1,0:T(8,128)(2,1)}) custom-call(s32[4]{0:T(128)S(1)} %pad_add_fusion.pos_ref, bf16[4,256,256]{2,1,0:T(8,128)(2,1)S(1)} %all_to_all.30.own_ref, bf16[4,256,256]{2,1,0:T(8,128)(2,1)S(1)} %collective-permute-done.18.oth_ref, bf16[2,224,448]{2,1,0:T(8,128)(2,1)} %copy-done.3, ...), custom_call_target="tpu_custom_call" | custom-call | tf_op jit(solution)/shard_map/pallas_call | solution.py:42
  176.9 3.8 %collective-permute-start.19 = (bf16[256,448]{1,0:T(8,128)(2,1)}, bf16[256,448]{1,0:T(8,128)(2,1)S(1)}, u32[]{:S(2)}, u32[]{:S(2)}) collective-permute-start(bf16[256,448]{1,0:T(8,128)(2,1)} %get-tuple-element.77), channel_id=1, source_target_pairs={{0,1},{4,3},{8,0},{12,2},{16,5},{20,7},{24,4},{28,6},{1,9},{5,11},... | collective-permute-start | bytes 688136 | tf_op jit(solution)/shard_map/ppermute | solution.py:432
  180.7 3.7 %collective-permute-start.20 = (bf16[256,448]{1,0:T(8,128)(2,1)}, bf16[256,448]{1,0:T(8,128)(2,1)S(1)}, u32[]{:S(2)}, u32[]{:S(2)}) collective-permute-start(bf16[256,448]{1,0:T(8,128)(2,1)} %get-tuple-element.78), channel_id=1, source_target_pairs={{0,0},{4,2},{8,1},{12,3},{16,4},{20,6},{24,5},{28,7},{1,8},{5,10},... | collective-permute-start | bytes 688136 | tf_op jit(solution)/shard_map/ppermute | solution.py:432
  184.4 4.4 %collective-permute-done.19 = bf16[256,448]{1,0:T(8,128)(2,1)S(1)} collective-permute-done((bf16[256,448]{1,0:T(8,128)(2,1)}, bf16[256,448]{1,0:T(8,128)(2,1)S(1)}, u32[]{:S(2)}, u32[]{:S(2)}) %collective-permute-start.19) | collective-permute-done | bytes 229408 | tf_op jit(solution)/shard_map/ppermute | solution.py:432
  188.8 1.8 collective-permute-done.20
  190.8 0.2 copy.82
  190.9 0.9 fusion.1
  (59 shorter events, 1.3 us)
Async XLA Ops:
  1.3 12.1 %collective-permute-start.1 = (bf16[128,896]{1,0:T(8,128)(2,1)S(1)}, bf16[128,896]{1,0:T(8,128)(2,1)S(1)}, u32[]{:S(2)}, u32[]{:S(2)}) collective-permute-start(bf16[128,896]{1,0:T(8,128)(2,1)S(1)} %copy.68.refs_1_), channel_id=1, source_target_pairs={{0,24},{8,0},{16,8},{24,16},{1,25},{9,1},{17,9},{25,17},{2,26},{10... | collective-permute-start | bytes 688136 | tf_op jit(solution)/shard_map/ppermute | solution.py:317
  1.3 38.3 %collective-permute-start.2 = (bf16[128,896]{1,0:T(8,128)(2,1)S(1)}, bf16[128,896]{1,0:T(8,128)(2,1)S(1)}, u32[]{:S(2)}, u32[]{:S(2)}) collective-permute-start(bf16[128,896]{1,0:T(8,128)(2,1)S(1)} %copy.68.refs_1_), channel_id=1, source_target_pairs={{0,8},{8,16},{16,24},{24,0},{1,9},{9,17},{17,25},{25,1},{2,10},{10... | collective-permute-start | bytes 688136 | tf_op jit(solution)/shard_map/ppermute | solution.py:317
  3.0 10.4 %collective-permute-start = (bf16[128,896]{1,0:T(8,128)(2,1)S(1)}, bf16[128,896]{1,0:T(8,128)(2,1)S(1)}, u32[]{:S(2)}, u32[]{:S(2)}) collective-permute-start(bf16[128,896]{1,0:T(8,128)(2,1)S(1)} %copy.67.refs_0_), channel_id=1, source_target_pairs={{0,8},{8,16},{16,24},{24,0},{1,9},{9,17},{17,25},{25,1},{2,10},{10... | collective-permute-start | bytes 688136 | tf_op jit(solution)/shard_map/ppermute | solution.py:317
  4.3 35.3 %collective-permute-start.3 = (bf16[128,896]{1,0:T(8,128)(2,1)S(1)}, bf16[128,896]{1,0:T(8,128)(2,1)S(1)}, u32[]{:S(2)}, u32[]{:S(2)}) collective-permute-start(bf16[128,896]{1,0:T(8,128)(2,1)S(1)} %copy.67.refs_0_), channel_id=1, source_target_pairs={{0,24},{8,0},{16,8},{24,16},{1,25},{9,1},{17,9},{25,17},{2,26},{10... | collective-permute-start | bytes 688136 | tf_op jit(solution)/shard_map/ppermute | solution.py:317
  17.0 30.0 %collective-permute-start.6 = (bf16[448,288]{1,0:T(8,128)(2,1)S(1)}, bf16[448,288]{1,0:T(8,128)(2,1)S(1)}, u32[]{:S(2)}, u32[]{:S(2)}) collective-permute-start(bf16[448,288]{1,0:T(8,128)(2,1)S(1)} %pad_maximum_fusion.2.refs_8_), channel_id=1, source_target_pairs={{0,4},{4,0},{1,5},{5,1},{2,6},{6,2},{3,7},{7,3},{8,12},{12,8},{9,1... | collective-permute-start | bytes 774152 | tf_op jit(solution)/shard_map/ppermute | solution.py:327
  39.7 7.2 %collective-permute-start.4 = (bf16[128,896]{1,0:T(8,128)(2,1)S(1)}, bf16[128,896]{1,0:T(8,128)(2,1)S(1)}, u32[]{:S(2)}, u32[]{:S(2)}) collective-permute-start(bf16[128,896]{1,0:T(8,128)(2,1)S(1)} %collective-permute-done.refs_2_), channel_id=1, source_target_pairs={{0,8},{8,16},{16,24},{24,0},{1,9},{9,17},{17,25},{25,1},{2,10},{10... | collective-permute-start | bytes 688136 | tf_op jit(solution)/shard_map/ppermute | solution.py:317
  39.8 7.1 %collective-permute-start.5 = (bf16[128,896]{1,0:T(8,128)(2,1)S(1)}, bf16[128,896]{1,0:T(8,128)(2,1)S(1)}, u32[]{:S(2)}, u32[]{:S(2)}) collective-permute-start(bf16[128,896]{1,0:T(8,128)(2,1)S(1)} %collective-permute-done.1.refs_7_), channel_id=1, source_target_pairs={{0,24},{8,0},{16,8},{24,16},{1,25},{9,1},{17,9},{25,17},{2,26},{10... | collective-permute-start | bytes 688136 | tf_op jit(solution)/shard_map/ppermute | solution.py:317
  50.9 30.7 %all-to-all-start.1 = ((bf16[4,256,1152]{2,1,0:T(8,128)(2,1)}), bf16[4,256,1152]{2,1,0:T(8,128)(2,1)S(1)}, u32[]{:S(2)}, u32[]{:S(2)}) async-start(bf16[4,256,1152]{2,1,0:T(8,128)(2,1)} %shard_map.118), calls=%async_computation.1 | async-start | bytes 4718592 | tf_op jit(solution)/shard_map/all_to_all | solution.py:349
  61.8 8.4 %copy-start.9 = (bf16[32,273,2]{1,2,0:T(2,128)(2,1)S(1)}, bf16[32,273,2]{1,2,0:T(2,128)(2,1)}, u32[]{:S(2)}) copy-start(bf16[32,273,2]{1,2,0:T(2,128)(2,1)} %param.18) | copy-start | bytes 104836
  61.8 9.1 %copy-start.13 = (s32[32]{0:T(128)S(1)}, s32[32]{0:T(128)}, u32[]{:S(2)}) copy-start(s32[32]{0:T(128)} %param.19) | copy-start | bytes 388
  61.8 9.5 %copy-start.11 = (s32[512]{0:T(512)S(1)}, s32[512]{0:T(512)}, u32[]{:S(2)}) copy-start(s32[512]{0:T(512)} %param.20) | copy-start | bytes 6148
  61.8 29.9 %copy-start.14 = (bf16[224,448]{1,0:T(8,128)(2,1)S(1)}, bf16[224,448]{1,0:T(8,128)(2,1)}, u32[]{:S(2)}) copy-start(bf16[224,448]{1,0:T(8,128)(2,1)} %param.16) | copy-start | bytes 602116
  83.6 4.6 %collective-permute-start.7 = (bf16[512,288]{1,0:T(8,128)(2,1)}, bf16[512,288]{1,0:T(8,128)(2,1)S(1)}, u32[]{:S(2)}, u32[]{:S(2)}) collective-permute-start(bf16[512,288]{1,0:T(8,128)(2,1)} %get-tuple-element.54), channel_id=1, source_target_pairs={{0,4},{4,0},{1,5},{5,1},{2,6},{6,2},{3,7},{7,3},{8,12},{12,8},{9,1... | collective-permute-start | bytes 884744 | tf_op jit(solution)/shard_map/ppermute | solution.py:354
  88.2 37.6 %copy-start.1 = (bf16[512,288]{1,0:T(8,128)(2,1)}, bf16[512,288]{1,0:T(8,128)(2,1)S(1)}, u32[]{:S(2)}) copy-start(bf16[512,288]{1,0:T(8,128)(2,1)S(1)} %collective-permute-done.7.rec_ref) | copy-start | bytes 884740
  88.2 1.1 copy-start
  91.7 43.3 %copy-start.12 = (s32[512]{0:T(512)S(1)}, s32[512]{0:T(512)}, u32[]{:S(2)}) copy-start(s32[512]{0:T(512)} %param.23) | copy-start | bytes 6148
  91.7 10.2 %collective-permute-start.10 = (bf16[224,448]{1,0:T(8,128)(2,1)S(1)}, bf16[224,448]{1,0:T(8,128)(2,1)S(1)}, u32[]{:S(2)}, u32[]{:S(2)}) collective-permute-start(bf16[224,448]{1,0:T(8,128)(2,1)S(1)} %copy-done.14), channel_id=1, source_target_pairs={{0,2},{1,0},{2,6},{3,4},{4,3},{5,1},{6,7},{7,5},{8,10},{9,8},{10,1... | collective-permute-start | bytes 602120 | tf_op jit(solution)/shard_map/ppermute | solution.py:374
  92.9 9.0 %collective-permute-start.11 = (bf16[224,448]{1,0:T(8,128)(2,1)S(1)}, bf16[224,448]{1,0:T(8,128)(2,1)S(1)}, u32[]{:S(2)}, u32[]{:S(2)}) collective-permute-start(bf16[224,448]{1,0:T(8,128)(2,1)S(1)} %copy-done.14), channel_id=1, source_target_pairs={{0,3},{1,1},{2,7},{3,5},{4,2},{5,0},{6,6},{7,4},{8,11},{9,9},{10,1... | collective-permute-start | bytes 602120 | tf_op jit(solution)/shard_map/ppermute | solution.py:374
  94.9 11.7 %collective-permute-start.8 = (bf16[224,448]{1,0:T(8,128)(2,1)S(1)}, bf16[224,448]{1,0:T(8,128)(2,1)S(1)}, u32[]{:S(2)}, u32[]{:S(2)}) collective-permute-start(bf16[224,448]{1,0:T(8,128)(2,1)S(1)} %copy-done.14), channel_id=1, source_target_pairs={{0,0},{1,2},{2,4},{3,6},{4,1},{5,3},{6,5},{7,7},{8,8},{9,10},{10,1... | collective-permute-start | bytes 602120 | tf_op jit(solution)/shard_map/ppermute | solution.py:374
  96.8 9.7 %collective-permute-start.9 = (bf16[224,448]{1,0:T(8,128)(2,1)S(1)}, bf16[224,448]{1,0:T(8,128)(2,1)S(1)}, u32[]{:S(2)}, u32[]{:S(2)}) collective-permute-start(bf16[224,448]{1,0:T(8,128)(2,1)S(1)} %copy-done.14), channel_id=1, source_target_pairs={{0,1},{1,3},{2,5},{3,7},{4,0},{5,2},{6,4},{7,6},{8,9},{9,11},{10,1... | collective-permute-start | bytes 602120 | tf_op jit(solution)/shard_map/ppermute | solution.py:374
  97.8 13.5 %all-to-all-start.2 = ((bf16[32,16,128]{2,1,0:T(8,128)(2,1)}), bf16[32,16,128]{2,1,0:T(8,128)(2,1)S(1)}, u32[]{:S(2)}, u32[]{:S(2)}) async-start(bf16[32,16,128]{2,1,0:T(8,128)(2,1)} %get-tuple-element.56), calls=%async_computation.2 | async-start | bytes 262144 | tf_op jit(solution)/shard_map/all_to_all | solution.py:376
  101.9 34.0 %copy-start.10 = (s32[512]{0:T(512)S(1)}, s32[512]{0:T(512)}, u32[]{:S(2)}) copy-start(s32[512]{0:T(512)} %multiply_add_fusion) | copy-start | bytes 6148
  102.0 43.1 %copy-start.2 = (bf16[2,224,448]{2,1,0:T(8,128)(2,1)}, bf16[2,224,448]{2,1,0:T(8,128)(2,1)S(1)}, u32[]{:S(2)}) copy-start(bf16[2,224,448]{2,1,0:T(8,128)(2,1)S(1)} %pad_maximum_fusion.1.refs_1_) | copy-start | bytes 1204228
  106.6 38.5 %copy-start.3 = (bf16[2,224,448]{2,1,0:T(8,128)(2,1)}, bf16[2,224,448]{2,1,0:T(8,128)(2,1)S(1)}, u32[]{:S(2)}) copy-start(bf16[2,224,448]{2,1,0:T(8,128)(2,1)S(1)} %pad_maximum_fusion.refs_0_) | copy-start | bytes 1204228
  111.3 2.4 %copy-start.5 = (bf16[32,16,128]{2,1,0:T(8,128)(2,1)}, bf16[32,16,128]{2,1,0:T(8,128)(2,1)S(1)}, u32[]{:S(2)}) copy-start(bf16[32,16,128]{2,1,0:T(8,128)(2,1)S(1)} %all-to-all-done.2.rec_ref) | copy-start | bytes 393220
  111.3 14.3 %collective-permute-start.12 = (bf16[2,224,448]{2,1,0:T(8,128)(2,1)S(1)}, bf16[2,224,448]{2,1,0:T(8,128)(2,1)S(1)}, u32[]{:S(2)}, u32[]{:S(2)}) collective-permute-start(bf16[2,224,448]{2,1,0:T(8,128)(2,1)S(1)} %pad_maximum_fusion.refs_0_), channel_id=1, source_target_pairs={{0,8},{8,16},{16,24},{24,0},{1,9},{9,17},{17,25},{25,1},{2,10},{10... | collective-permute-start | bytes 1204232 | tf_op jit(solution)/shard_map/ppermute | solution.py:317
  113.1 12.6 %collective-permute-start.13 = (bf16[2,224,448]{2,1,0:T(8,128)(2,1)S(1)}, bf16[2,224,448]{2,1,0:T(8,128)(2,1)S(1)}, u32[]{:S(2)}, u32[]{:S(2)}) collective-permute-start(bf16[2,224,448]{2,1,0:T(8,128)(2,1)S(1)} %pad_maximum_fusion.1.refs_1_), channel_id=1, source_target_pairs={{0,24},{8,0},{16,8},{24,16},{1,25},{9,1},{17,9},{25,17},{2,26},{10... | collective-permute-start | bytes 1204232 | tf_op jit(solution)/shard_map/ppermute | solution.py:317
  125.7 27.5 %copy-start.6 = (bf16[2,224,448]{2,1,0:T(8,128)(2,1)}, bf16[2,224,448]{2,1,0:T(8,128)(2,1)S(1)}, u32[]{:S(2)}) copy-start(bf16[2,224,448]{2,1,0:T(8,128)(2,1)S(1)} %collective-permute-done.12.refs_2_) | copy-start | bytes 1204228
  125.7 27.5 %copy-start.7 = (bf16[2,224,448]{2,1,0:T(8,128)(2,1)}, bf16[2,224,448]{2,1,0:T(8,128)(2,1)S(1)}, u32[]{:S(2)}) copy-start(bf16[2,224,448]{2,1,0:T(8,128)(2,1)S(1)} %collective-permute-done.13.refs_7_) | copy-start | bytes 1204228
  125.7 23.9 %all-to-all-start.3 = ((bf16[32,16,512]{2,1,0:T(8,128)(2,1)}), bf16[32,16,512]{2,1,0:T(8,128)(2,1)S(1)}, u32[]{:S(2)}, u32[]{:S(2)}) async-start(bf16[32,16,512]{2,1,0:T(8,128)(2,1)} %get-tuple-element.65), calls=%async_computation.3 | async-start | bytes 1048576 | tf_op jit(solution)/shard_map/all_to_all | solution.py:403
  129.6 15.5 %collective-permute-start.14 = (bf16[2,224,448]{2,1,0:T(8,128)(2,1)S(1)}, bf16[2,224,448]{2,1,0:T(8,128)(2,1)S(1)}, u32[]{:S(2)}, u32[]{:S(2)}) collective-permute-start(bf16[2,224,448]{2,1,0:T(8,128)(2,1)S(1)} %pad_maximum_fusion.1.refs_1_), channel_id=1, source_target_pairs={{0,8},{8,16},{16,24},{24,0},{1,9},{9,17},{17,25},{25,1},{2,10},{10... | collective-permute-start | bytes 1204232 | tf_op jit(solution)/shard_map/ppermute | solution.py:317
  131.5 13.6 %collective-permute-start.15 = (bf16[2,224,448]{2,1,0:T(8,128)(2,1)S(1)}, bf16[2,224,448]{2,1,0:T(8,128)(2,1)}, u32[]{:S(2)}, u32[]{:S(2)}) collective-permute-start(bf16[2,224,448]{2,1,0:T(8,128)(2,1)S(1)} %pad_maximum_fusion.refs_0_), channel_id=1, source_target_pairs={{0,24},{8,0},{16,8},{24,16},{1,25},{9,1},{17,9},{25,17},{2,26},{10... | collective-permute-start | bytes 1204232 | tf_op jit(solution)/shard_map/ppermute | solution.py:317
  132.5 16.9 %collective-permute-start.16 = (bf16[2,224,448]{2,1,0:T(8,128)(2,1)S(1)}, bf16[2,224,448]{2,1,0:T(8,128)(2,1)}, u32[]{:S(2)}, u32[]{:S(2)}) collective-permute-start(bf16[2,224,448]{2,1,0:T(8,128)(2,1)S(1)} %collective-permute-done.12.refs_2_), channel_id=1, source_target_pairs={{0,8},{8,16},{16,24},{24,0},{1,9},{9,17},{17,25},{25,1},{2,10},{10... | collective-permute-start | bytes 1204232 | tf_op jit(solution)/shard_map/ppermute | solution.py:317
  133.0 16.7 %collective-permute-start.17 = (bf16[2,224,448]{2,1,0:T(8,128)(2,1)S(1)}, bf16[2,224,448]{2,1,0:T(8,128)(2,1)}, u32[]{:S(2)}, u32[]{:S(2)}) collective-permute-start(bf16[2,224,448]{2,1,0:T(8,128)(2,1)S(1)} %collective-permute-done.13.refs_7_), channel_id=1, source_target_pairs={{0,24},{8,0},{16,8},{24,16},{1,25},{9,1},{17,9},{25,17},{2,26},{10... | collective-permute-start | bytes 1204232 | tf_op jit(solution)/shard_map/ppermute | solution.py:317
  145.1 27.8 %copy-start.8 = (bf16[2,224,448]{2,1,0:T(8,128)(2,1)}, bf16[2,224,448]{2,1,0:T(8,128)(2,1)S(1)}, u32[]{:S(2)}) copy-start(bf16[2,224,448]{2,1,0:T(8,128)(2,1)S(1)} %collective-permute-done.14.refs_3_) | copy-start | bytes 1204228
  153.2 37.7 %copy-start.4 = (bf16[256,2,448]{0,2,1:T(8,128)(2,1)S(1)}, bf16[256,2,448]{0,2,1:T(8,128)(2,1)}, u32[]{:S(2)}) copy-start(bf16[256,2,448]{0,2,1:T(8,128)(2,1)} %param.12) | copy-start | bytes 1376260
  164.9 8.0 %collective-permute-start.18 = (bf16[4,256,256]{2,1,0:T(8,128)(2,1)S(1)}, bf16[4,256,256]{2,1,0:T(8,128)(2,1)S(1)}, u32[]{:S(2)}, u32[]{:S(2)}) collective-permute-start(bf16[4,256,256]{2,1,0:T(8,128)(2,1)S(1)} %all_to_all.30.own_ref), channel_id=1, source_target_pairs={{0,4},{4,0},{1,5},{5,1},{2,6},{6,2},{3,7},{7,3},{8,12},{12,8},{9,1... | collective-permute-start | bytes 1572872 | tf_op jit(solution)/shard_map/ppermute | solution.py:420
  176.9 11.8 %collective-permute-start.19 = (bf16[256,448]{1,0:T(8,128)(2,1)}, bf16[256,448]{1,0:T(8,128)(2,1)S(1)}, u32[]{:S(2)}, u32[]{:S(2)}) collective-permute-start(bf16[256,448]{1,0:T(8,128)(2,1)} %get-tuple-element.77), channel_id=1, source_target_pairs={{0,1},{4,3},{8,0},{12,2},{16,5},{20,7},{24,4},{28,6},{1,9},{5,11},... | collective-permute-start | bytes 688136 | tf_op jit(solution)/shard_map/ppermute | solution.py:432
  180.7 9.8 %collective-permute-start.20 = (bf16[256,448]{1,0:T(8,128)(2,1)}, bf16[256,448]{1,0:T(8,128)(2,1)S(1)}, u32[]{:S(2)}, u32[]{:S(2)}) collective-permute-start(bf16[256,448]{1,0:T(8,128)(2,1)} %get-tuple-element.78), channel_id=1, source_target_pairs={{0,0},{4,2},{8,1},{12,3},{16,4},{20,6},{24,5},{28,7},{1,8},{5,10},... | collective-permute-start | bytes 688136 | tf_op jit(solution)/shard_map/ppermute | solution.py:432

commit v7 on v5

--- a/solution.py
+++ b/solution.py
@@ -283,21 +283,19 @@
                 out_ref[half * 2 + part, t * 128 : (t + 1) * 128, :] = out[part * 128 : (part + 1) * 128]
 
 
-def out_kernel(pos_ref, own_ref, oth_ref, *refs):
-    parts, first_ref, second_ref = refs[:8], refs[8], refs[9]
-    y, core, col = pos_ref[0], pos_ref[1], pos_ref[3]
+def out_kernel(pos_ref, own_ref, oth_ref, w_ref, first_ref, second_ref):
+    y, core = pos_ref[0], pos_ref[1]
     acc = [None, None]
-    for shift in range(4):
-        j = lax.rem(y + 4 - shift, 4)
+    for j in range(4):
         for which, ref in enumerate((own_ref, oth_ref)):
-            k = core if which == 0 else 1 - core
+            row = j * 2 + (core if which == 0 else 1 - core)
             heads = ref[j, :, 0:224]
             for e in range(2):
-                part = dot(heads, parts[2 * shift + e][jnp.bitwise_xor(k, lax.rem(col, 2))])
+                part = dot(heads, w_ref[row, e])
                 acc[e] = part if acc[e] is None else acc[e] + part
-    same = lax.rem(y, 2) == lax.div(col, 2)
-    first_ref[...] = jnp.where(same, acc[0], acc[1]).astype(BF)
-    second_ref[...] = jnp.where(same, acc[1], acc[0]).astype(BF)
+    even = lax.rem(y, 2) == 0
+    first_ref[...] = jnp.where(even, acc[0], acc[1]).astype(BF)
+    second_ref[...] = jnp.where(even, acc[1], acc[0]).astype(BF)
 
 
 def body(tokens, w_query, w_key, w_value, w_out, cached_state, cached_norm, slot_prompt, prompt_of, tail_keys, tail_values, tail_length):
@@ -310,17 +308,10 @@
     top, low = tokens[:128].reshape(128, 896), tokens[128:].reshape(128, 896)
     top_1, low_3 = over_y(top, 1), over_y(low, 3)
     low_1, top_3 = over_y(low, 1), over_y(top, 3)
-    top_1, low_3, w_out = lax.optimization_barrier((top_1, low_3, w_out))
     blocks = [top, low, top_1, low_1, over_y(top_1, 1), over_y(low_3, 3), top_3, low_3]
     value_w = jnp.moveaxis(w_value.reshape(2, 448, 112), 0, 1).reshape(448, 224)
     mine = jnp.concatenate([value_w, w_query, w_key], axis=1)
     theirs = lax.ppermute(mine, "core", [(0, 1), (1, 0)])
-    pieces = []
-    for s in range(4):
-        perm = [(k * 4 + c, (c >> 1) * 4 + (s ^ (2 * (c & 1) + k))) for k in range(2) for c in range(4)]
-        pieces.append(lax.ppermute(w_out, ("core", "col"), perm))
-    pieces = [jnp.stack(pieces[:2]), jnp.stack(pieces[2:])]
-
     owner = slot_prompt // 32
     slots = jnp.arange(32, dtype=jnp.int32)
     away = owner != me
@@ -328,6 +319,7 @@
         jnp.where((owner[None, :] == slots[:, None]) & away[None, :], (slots * 32 + slot_prompt % 32 + 1)[None, :], 0), axis=1
     )
     told = lax.all_to_all(code[:, None], ("req", "col"), split_axis=0, concat_axis=0, tiled=True)[:, 0]
+    theirs, told = lax.optimization_barrier((theirs, told))
     here = (slot_prompt[None, :] == (me * 32 + slots)[:, None])
     there = (told[None, :] > 0) & ((told[None, :] - 1) % 32 == slots[:, None])
     at_slot = jnp.max(jnp.where(here, slots[None, :], 0), axis=1)
@@ -349,6 +341,8 @@
         scratch=[pltpu.VMEM((448, 640), BF), pltpu.VMEM((512, 640), BF)],
         free=range(1, 11),
     )
+    partial, w_out = lax.optimization_barrier((partial, w_out))
+    out_w = lax.all_gather(w_out, ("y", "core", "col"), axis=0, tiled=False).reshape(8, 4, 224, 448)
     partial = lax.all_to_all(partial, "col", split_axis=0, concat_axis=0, tiled=True)
     states = jnp.transpose(states, (2, 0, 1))
     partial, states, norms = lax.optimization_barrier((partial, states, norms))
@@ -370,8 +364,6 @@
         scratch=[pltpu.VMEM((512, 128), BF)],
         free=(3, 4),
     )
-    q_send, pieces = lax.optimization_barrier((q_send, pieces))
-    out_w = [over_y(x, step) for step in (1, 3) for x in pieces]
     q_rec = lax.all_to_all(q_send, ("req", "col"), split_axis=0, concat_axis=0, tiled=True)
     shape = jax.ShapeDtypeStruct((2, 512, 256), F32)
     num = call(tail_kernel, shape, 1, pos, own, rec, tail_keys, tail_values, tail_length[:, None])
@@ -395,10 +387,7 @@
         scratch_shapes=[pltpu.VMEM((128, 128), BF)],
         compiler_params=pltpu.CompilerParams(vmem_limit_bytes=VMEM_LIMIT),
     )(pos, owner, in_hbm(q_rec), in_hbm(q_keep), in_hbm(states), in_hbm(norms))
-    r_send, out_w = lax.optimization_barrier((r_send, out_w))
-    far_1, far_3 = over_y(out_w[0], 1), over_y(out_w[3], 3)
     r_rec = lax.all_to_all(r_send, ("req", "col"), split_axis=0, concat_axis=0, tiled=True)
-    r_rec, far_1, far_3 = lax.optimization_barrier((r_rec, far_1, far_3))
     heads = call(
         combine_kernel,
         jax.ShapeDtypeStruct((4, 256, 256), BF),
@@ -415,8 +404,23 @@
     )
     heads = lax.all_to_all(heads, "y", split_axis=0, concat_axis=0, tiled=True)
     heads_oth = lax.ppermute(heads, "core", [(0, 1), (1, 0)])
-    shape = jax.ShapeDtypeStruct((256, 448), BF)
-    mixed = call(out_kernel, (shape, shape), 1, pos, heads, heads_oth, *pieces, out_w[0], out_w[1], far_1, far_3, out_w[2], out_w[3], free=(1, 2))
+    heads_spec = pl.BlockSpec((4, 256, 256), lambda i, pos_ref: (0, 0, 0))
+    half_spec = pl.BlockSpec((256, 448), lambda i, pos_ref: (0, 0))
+    mixed = pl.pallas_call(
+        out_kernel,
+        out_shape=(pltpu.HBM((256, 448), BF), pltpu.HBM((256, 448), BF)),
+        grid_spec=pltpu.PrefetchScalarGridSpec(
+            num_scalar_prefetch=1,
+            grid=(1,),
+            in_specs=[
+                heads_spec,
+                heads_spec,
+                pl.BlockSpec((8, 2, 224, 448), lambda i, pos_ref: (0, pos_ref[1], 0, 0)),
+            ],
+            out_specs=(half_spec, half_spec),
+        ),
+        compiler_params=pltpu.CompilerParams(vmem_limit_bytes=VMEM_LIMIT),
+    )(pos, heads, heads_oth, in_hbm(out_w))
 
     def at(y, core, col):
         return (y * 2 + core) * 4 + col

time: 181 us -> 195 us (1.077); the launches traced: 178 us -> 194 us
  waiting for transfers between devices: 31.8 us -> 51.8 us
  starting transfers between devices: 69.1 us -> 50.4 us
  between operations: 0.4 us -> 13.6 us
    ppermute x4 -> x0, starting transfers between devices: 12.9 us -> none  [body(): pieces.append(lax.ppermute(w_out, ('core', 'col'), perm))]
    all_to_all x1, waiting for transfers between devices: 0.01 us -> 11.5 us  [body(): lax.all_to_all(partial, 'col', split_axis=0, concat_axis=0, tiled=True)]
    all_to_all x1, waiting for transfers between devices: 4.46 us -> 15.4 us  [body(): lax.all_to_all(r_send, ('req', 'col'), split_axis=0, concat_axis=0, tiled...]
    ppermute x12 -> x6, starting transfers between devices: 13.5 us -> 6.3 us  [over_y(): return lax.ppermute(x, 'y', [(i, (i + step) % 4) for i in range(4)])]
    ppermute x12 -> x6, waiting for transfers between devices: 10.2 us -> 3.12 us  [over_y(): return lax.ppermute(x, 'y', [(i, (i + step) % 4) for i in range(4)])]
    pallas_call x0 -> x1, Pallas kernels: none -> 4.61 us  [body(): pl.pallas_call(out_kernel, out_shape=(pltpu.HBM((256, 448), BF), pltpu.HB...]
    ppermute x4 -> x0, waiting for transfers between devices: 4.59 us -> none  [body(): pieces.append(lax.ppermute(w_out, ('core', 'col'), perm))]
    ppermute x1, starting transfers between devices: 0.4 us -> 4.5 us  [body(): rec = lax.ppermute(oth, 'core', [(0, 1), (1, 0)])]
  transfers between devices with their start and end apart: 25 -> 16, of which waited for: 11 -> 9; matrix products, arithmetic and copies ran while one was open for 14% -> 13% of each run, Pallas kernels for 15% -> 15%
where the time goes in v7:
time: 195 us; the launch traced here: 194 us
  waiting for transfers between devices  51.8 us (27%)
  starting transfers between devices  50.4 us (26%)
  Pallas kernels  36.7 us (19%)
  local copies, waits for them, and re-layouts  26 us (13%)
  between operations  13.6 us (7%)
  blocking collectives  12.3 us (6%)
  other arithmetic  3.26 us (2%)
    pallas_call x5, Pallas kernels, call(): pl.pallas_call(kernel, grid=(1,), out_shape=jax.tree.map(lambda x: pltpu....  20.3 us
    all_to_all x1, waiting for transfers between devices, body(): lax.all_to_all(r_send, ('req', 'col'), split_axis=0, concat_axis=0, tiled...  15.4 us
    all_to_all x1, blocking collectives, body(): heads = lax.all_to_all(heads, 'y', split_axis=0, concat_axis=0, tiled=True)  12.3 us
    pallas_call x1, Pallas kernels, body(): pl.pallas_call(slot_kernel, grid=(4,), out_shape=(pltpu.HBM(shape.shape,...  11.8 us
    all_to_all x1, waiting for transfers between devices, body(): lax.all_to_all(partial, 'col', split_axis=0, concat_axis=0, tiled=True)  11.5 us
    all_to_all x1, starting transfers between devices, body(): lax.all_to_all(code[:, None], ('req', 'col'), split_axis=0, concat_axis=0...  11 us
    unnamed x21, local copies, waits for them, and re-layouts  11 us
    ppermute x2, waiting for transfers between devices, body(): lax.ppermute(part, ('y', 'core', 'col'), perm).reshape(2, 128, 448)  9.92 us
  transfers between devices with their start and end apart: 16, of which 9 were waited for; matrix products, arithmetic and copies ran while one was open for 13% of the time, Pallas kernels for 15%

profile of v7, /device:TPU:9, one launch (start us, length us, event | category | flops | bytes accessed | tf_op | source)
XLA Modules:
  0.0 193.9 jit_solution(10318075569180163939)
XLA Ops:
  6.5 1.1 fusion.8
  7.6 0.2 copy.76.refs_1_
  7.8 0.1 collective-permute-start.4
  7.9 1.5 collective-permute-start.2
  9.3 0.2 copy.75.refs_0_
  9.5 1.4 collective-permute-start.1
  10.9 0.2 collective-permute-start.6
  11.1 1.2 reshape.51
  12.4 0.2 copy.84
  12.6 0.1 reshape.52
  12.8 0.9 copy.68
  13.7 0.9 copy.69
  14.6 0.1 pad_maximum_fusion.refs_8_
  14.7 2.1 %collective-permute-start = (bf16[448,288]{1,0:T(8,128)(2,1)S(1)}, bf16[448,288]{1,0:T(8,128)(2,1)S(1)}, u32[]{:S(2)}, u32[]{:S(2)}) collective-permute-start(bf16[448,288]{1,0:T(8,128)(2,1)S(1)} %pad_maximum_fusion.refs_8_), channel_id=1, source_target_pairs={{0,4},{4,0},{1,5},{5,1},{2,6},{6,2},{3,7},{7,3},{8,12},{12,8},{9,1... | collective-permute-start | bytes 774152 | tf_op jit(solution)/shard_map/ppermute | solution.py:314
  16.8 3.1 %collective-permute-done.1.refs_2_ = bf16[128,896]{1,0:T(8,128)(2,1)S(1)} collective-permute-done((bf16[128,896]{1,0:T(8,128)(2,1)S(1)}, bf16[128,896]{1,0:T(8,128)(2,1)S(1)}, u32[]{:S(2)}, u32[]{:S(2)}) %collective-permute-start.1) | collective-permute-done | bytes 229408 | tf_op jit(solution)/shard_map/ppermute | solution.py:306
  19.9 0.3 collective-permute-start.3
  20.2 2.8 %collective-permute-start.5 = (bf16[128,896]{1,0:T(8,128)(2,1)S(1)}, bf16[128,896]{1,0:T(8,128)(2,1)S(1)}, u32[]{:S(2)}, u32[]{:S(2)}) collective-permute-start(bf16[128,896]{1,0:T(8,128)(2,1)S(1)} %collective-permute-done.4.refs_7_), channel_id=1, source_target_pairs={{0,24},{8,0},{16,8},{24,16},{1,25},{9,1},{17,9},{25,17},{2,26},{10... | collective-permute-start | bytes 688136 | tf_op jit(solution)/shard_map/ppermute | solution.py:306
  23.1 0.1 select_reduce_fusion.1
  23.2 0.7 copy.70
  23.9 11.0 %all-to-all-start = ((s32[32,1,1]{2,1,0:T(1,128)}), s32[32,1,1]{2,1,0:T(1,128)S(1)}, u32[]{:S(2)}, u32[]{:S(2)}) async-start(s32[32,1,1]{2,1,0:T(1,128)} %copy.70), calls=%async_computation | async-start | bytes 32768 | tf_op jit(solution)/shard_map/all_to_all | solution.py:321
  34.9 0.0 all-gather.3.cloned.1.call-start
  35.0 0.1 pad_add_fusion.pos_ref
  35.1 8.4 %all-to-all-done = s32[32,1,1]{2,1,0:T(1,128)S(1)} async-done(((s32[32,1,1]{2,1,0:T(1,128)}), s32[32,1,1]{2,1,0:T(1,128)S(1)}, u32[]{:S(2)}, u32[]{:S(2)}) %all-to-all-start) | async-done | bytes 160 | tf_op jit(solution)/shard_map/all_to_all | solution.py:321
  43.5 0.7 reduce
  44.1 0.0 collective-permute-done.refs_9_
  44.1 0.0 collective-permute-done.2.refs_3_
  44.2 3.9 %shard_map.118 = bf16[4,256,1152]{2,1,0:T(8,128)(2,1)} custom-call(s32[4]{0:T(128)S(1)} %pad_add_fusion.pos_ref, bf16[128,896]{1,0:T(8,128)(2,1)S(1)} %copy.75.refs_0_, bf16[128,896]{1,0:T(8,128)(2,1)S(1)} %copy.76.refs_1_, bf16[128,896]{1,0:T(8,128)(2,1)S(1)} %collective-permute-done.1.refs_2_, bf16[128,896]{1,0:T(8,128)(2,1)S(1)} %collective-permute-done.2.refs_3_, ...), custom_call_target="tpu_custom_call" | custom-call | tf_op jit(solution)/shard_map/pallas_call | solution.py:42
  48.1 0.0 all-gather.3.cloned.1.call-update
  48.1 3.6 %all-to-all-start.1 = ((bf16[4,256,1152]{2,1,0:T(8,128)(2,1)}), bf16[4,256,1152]{2,1,0:T(8,128)(2,1)S(1)}, u32[]{:S(2)}, u32[]{:S(2)}) async-start(bf16[4,256,1152]{2,1,0:T(8,128)(2,1)} %shard_map.118), calls=%async_computation.1 | async-start | bytes 4718592 | tf_op jit(solution)/shard_map/all_to_all | solution.py:346
  51.8 7.3 %copy.77 = bf16[1,273,7168]{1,2,0:T(8,128)(2,1)} copy(bf16[1,273,7168]{2,1,0:T(8,128)(2,1)} %param.17) | data formatting | bytes 7827456 | tf_op args[5]
  59.1 8.5 %copy.78 = bf16[273,224,32]{1,0,2:T(8,128)(2,1)} copy(bf16[273,224,32]{0,2,1:T(8,128)(2,1)} %bitcast.23) | data formatting | bytes 7827456 | tf_op jit(solution)/shard_map/reshape;squeeze | solution.py:331
  67.7 0.6 pad.4.norm_ref
  68.3 0.2 compare_reduce_fusion
  68.5 0.2 fusion.2.s_ref
  68.7 0.2 convert_reduce_fusion
  68.9 0.5 multiply_add_fusion
  69.5 11.5 %all-to-all-done.1.p_ref = bf16[4,256,1152]{2,1,0:T(8,128)(2,1)S(1)} async-done(((bf16[4,256,1152]{2,1,0:T(8,128)(2,1)}), bf16[4,256,1152]{2,1,0:T(8,128)(2,1)S(1)}, u32[]{:S(2)}, u32[]{:S(2)}) %all-to-all-start.1) | async-done | bytes 2359328 | tf_op jit(solution)/shard_map/all_to_all | solution.py:346
  81.0 2.0 %shard_map.119 = (bf16[512,288]{1,0:T(8,128)(2,1)}, bf16[512,288]{1,0:T(8,128)(2,1)}) custom-call(s32[4]{0:T(128)S(1)} %pad_add_fusion.pos_ref, bf16[4,256,1152]{2,1,0:T(8,128)(2,1)S(1)} %all-to-all-done.1.p_ref), custom_call_target="tpu_custom_call" | custom-call | tf_op jit(solution)/shard_map/pallas_call | solution.py:42
  83.0 4.5 %collective-permute-start.7 = (bf16[512,288]{1,0:T(8,128)(2,1)}, bf16[512,288]{1,0:T(8,128)(2,1)S(1)}, u32[]{:S(2)}, u32[]{:S(2)}) collective-permute-start(bf16[512,288]{1,0:T(8,128)(2,1)} %get-tuple-element.27), channel_id=1, source_target_pairs={{0,4},{4,0},{1,5},{5,1},{2,6},{6,2},{3,7},{7,3},{8,12},{12,8},{9,1... | collective-permute-start | bytes 884744 | tf_op jit(solution)/shard_map/ppermute | solution.py:351
  87.5 0.1 select_reduce_fusion
  87.7 1.4 collective-permute-done.7.rec_ref
  89.1 1.2 copy-done
  90.3 2.2 %shard_map.120 = (bf16[32,16,128]{2,1,0:T(8,128)(2,1)}, bf16[32,16,128]{2,1,0:T(8,128)(2,1)}) custom-call(s32[4]{0:T(128)S(1)} %pad_add_fusion.pos_ref, s32[32]{0:T(128)S(1)} %broadcast_select_fusion.2.g_ref, s32[32]{0:T(128)S(1)} %fusion.2.s_ref, bf16[512,288]{1,0:T(8,128)(2,1)S(1)} %copy-done, bf16[512,288]{1,0:T(8,128)(2,1)S(1)} %collective-permute-done.7.rec_ref, ...), custom_call_target="tpu_custom_call" | custom-call | tf_op jit(solution)/shard_map/pallas_call | solution.py:42
  92.5 3.8 %all-to-all-start.2 = ((bf16[32,16,128]{2,1,0:T(8,128)(2,1)}), bf16[32,16,128]{2,1,0:T(8,128)(2,1)S(1)}, u32[]{:S(2)}, u32[]{:S(2)}) async-start(bf16[32,16,128]{2,1,0:T(8,128)(2,1)} %get-tuple-element.28), calls=%async_computation.2 | async-start | bytes 262144 | tf_op jit(solution)/shard_map/all_to_all | solution.py:367
  96.4 0.9 copy.79.len_ref
  97.2 8.5 %shard_map.121.num_ref = f32[2,512,256]{2,1,0:T(8,128)} custom-call(s32[4]{0:T(128)S(1)} %pad_add_fusion.pos_ref, bf16[512,288]{1,0:T(8,128)(2,1)} %get-tuple-element.26.own_ref, bf16[512,288]{1,0:T(8,128)(2,1)} %copy-done.1, bf16[512,256]{1,0:T(8,128)(2,1)} %tk_ref.1, bf16[512,1792]{1,0:T(8,128)(2,1)} %tv_ref.1, s32[512,1]{1,0:T(8,128)} %copy.79.len_ref), custom_call_target="tpu_custom_call" | custom-call | tf_op jit(solution)/shard_map/pallas_call | solution.py:42
  105.7 0.5 all-to-all-done.2.rec_ref
  106.2 0.7 copy-done.3
  106.8 11.8 %shard_map.122 = (bf16[32,16,512]{2,1,0:T(8,128)(2,1)}, bf16[32,16,512]{2,1,0:T(8,128)(2,1)}) custom-call(s32[4]{0:T(128)S(1)} %pad_add_fusion.pos_ref, s32[32]{0:T(128)S(1)} %get-tuple-element.40.owner_ref, bf16[32,16,128]{2,1,0:T(8,128)(2,1)} %copy-done.3, bf16[32,16,128]{2,1,0:T(8,128)(2,1)} %get-tuple-element.31.keep_ref, ...), custom_call_target="tpu_custom_call" | custom-call | tf_op jit(solution)/shard_map/pallas_call | solution.py:374
  118.6 8.8 %all-to-all-start.3 = ((bf16[32,16,512]{2,1,0:T(8,128)(2,1)}), bf16[32,16,512]{2,1,0:T(8,128)(2,1)S(1)}, u32[]{:S(2)}, u32[]{:S(2)}) async-start(bf16[32,16,512]{2,1,0:T(8,128)(2,1)} %get-tuple-element.34), calls=%async_computation.3 | async-start | bytes 1048576 | tf_op jit(solution)/shard_map/all_to_all | solution.py:390
  127.4 0.9 copy.80.place_ref
  128.3 15.4 %all-to-all-done.3.rec_ref = bf16[32,16,512]{2,1,0:T(8,128)(2,1)S(1)} async-done(((bf16[32,16,512]{2,1,0:T(8,128)(2,1)}), bf16[32,16,512]{2,1,0:T(8,128)(2,1)S(1)}, u32[]{:S(2)}, u32[]{:S(2)}) %all-to-all-start.3) | async-done | bytes 524320 | tf_op jit(solution)/shard_map/all_to_all | solution.py:390
  143.7 3.6 %shard_map.123 = bf16[4,256,256]{2,1,0:T(8,128)(2,1)} custom-call(s32[4]{0:T(128)S(1)} %pad_add_fusion.pos_ref, s32[32]{0:T(128)S(1)} %broadcast_select_fusion.2.g_ref, s32[32]{0:T(128)S(1)} %fusion.2.s_ref, f32[2,512,256]{2,1,0:T(8,128)} %shard_map.121.num_ref, bf16[32,16,512]{2,1,0:T(8,128)(2,1)S(1)} %all-to-all-done.3.rec_ref, ...), custom_call_target="tpu_custom_call" | custom-call | tf_op jit(solution)/shard_map/pallas_call | solution.py:42
  147.3 12.3 %all_to_all.29.own_ref = bf16[4,256,256]{2,1,0:T(8,128)(2,1)S(1)} all-to-all(bf16[4,256,256]{2,1,0:T(8,128)(2,1)} %shard_map.123), channel_id=1, replica_groups=mesh['req'=8,'y'=4,'core'=2,'col'=4] {'y'}, dimensions={0} | all-to-all | bytes 1048576 | tf_op jit(solution)/shard_map/all_to_all | solution.py:405
  159.6 3.5 %collective-permute-start.8 = (bf16[4,256,256]{2,1,0:T(8,128)(2,1)S(1)}, bf16[4,256,256]{2,1,0:T(8,128)(2,1)S(1)}, u32[]{:S(2)}, u32[]{:S(2)}) collective-permute-start(bf16[4,256,256]{2,1,0:T(8,128)(2,1)S(1)} %all_to_all.29.own_ref), channel_id=1, source_target_pairs={{0,4},{4,0},{1,5},{5,1},{2,6},{6,2},{3,7},{7,3},{8,12},{12,8},{9,1... | collective-permute-start | bytes 1572872 | tf_op jit(solution)/shard_map/ppermute | solution.py:406
  163.1 1.5 collective-permute-done.8.oth_ref
  164.6 4.6 %shard_map.124 = (bf16[256,448]{1,0:T(8,128)(2,1)}, bf16[256,448]{1,0:T(8,128)(2,1)}) custom-call(s32[4]{0:T(128)S(1)} %pad_add_fusion.pos_ref, bf16[4,256,256]{2,1,0:T(8,128)(2,1)S(1)} %all_to_all.29.own_ref, bf16[4,256,256]{2,1,0:T(8,128)(2,1)S(1)} %collective-permute-done.8.oth_ref, bf16[8,4,224,448]{3,2,1,0:T(8,128)(2,1)} %bitcast.25), custom_call_target="tpu_custom_call" | custom-call | tf_op jit(solution)/shard_map/pallas_call | solution.py:409
  169.2 5.1 %collective-permute-start.10 = (bf16[256,448]{1,0:T(8,128)(2,1)}, bf16[256,448]{1,0:T(8,128)(2,1)S(1)}, u32[]{:S(2)}, u32[]{:S(2)}) collective-permute-start(bf16[256,448]{1,0:T(8,128)(2,1)} %get-tuple-element.38), channel_id=1, source_target_pairs={{0,0},{4,2},{8,1},{12,3},{16,4},{20,6},{24,5},{28,7},{1,8},{5,10},... | collective-permute-start | bytes 688136 | tf_op jit(solution)/shard_map/ppermute | solution.py:433
  174.4 1.5 collective-permute-start.9
  175.9 4.3 %collective-permute-done.10 = bf16[256,448]{1,0:T(8,128)(2,1)S(1)} collective-permute-done((bf16[256,448]{1,0:T(8,128)(2,1)}, bf16[256,448]{1,0:T(8,128)(2,1)S(1)}, u32[]{:S(2)}, u32[]{:S(2)}) %collective-permute-start.10) | collective-permute-done | bytes 229408 | tf_op jit(solution)/shard_map/ppermute | solution.py:433
  180.2 5.6 %collective-permute-done.9 = bf16[256,448]{1,0:T(8,128)(2,1)S(1)} collective-permute-done((bf16[256,448]{1,0:T(8,128)(2,1)}, bf16[256,448]{1,0:T(8,128)(2,1)S(1)}, u32[]{:S(2)}, u32[]{:S(2)}) %collective-permute-start.9) | collective-permute-done | bytes 229408 | tf_op jit(solution)/shard_map/ppermute | solution.py:433
  185.8 0.2 copy.81
  186.0 0.2 copy.82
  186.2 0.9 fusion.1
  (29 shorter events, 0.2 us)
Async XLA Ops:
  6.5 10.3 %copy-start.8 = (s32[32]{0:T(128)S(1)}, s32[32]{0:T(128)}, u32[]{:S(2)}) copy-start(s32[32]{0:T(128)} %param.19) | copy-start | bytes 388
  7.8 12.4 %collective-permute-start.4 = (bf16[128,896]{1,0:T(8,128)(2,1)S(1)}, bf16[128,896]{1,0:T(8,128)(2,1)S(1)}, u32[]{:S(2)}, u32[]{:S(2)}) collective-permute-start(bf16[128,896]{1,0:T(8,128)(2,1)S(1)} %copy.76.refs_1_), channel_id=1, source_target_pairs={{0,24},{8,0},{16,8},{24,16},{1,25},{9,1},{17,9},{25,17},{2,26},{10... | collective-permute-start | bytes 688136 | tf_op jit(solution)/shard_map/ppermute | solution.py:306
  7.9 36.2 %collective-permute-start.2 = (bf16[128,896]{1,0:T(8,128)(2,1)S(1)}, bf16[128,896]{1,0:T(8,128)(2,1)S(1)}, u32[]{:S(2)}, u32[]{:S(2)}) collective-permute-start(bf16[128,896]{1,0:T(8,128)(2,1)S(1)} %copy.76.refs_1_), channel_id=1, source_target_pairs={{0,8},{8,16},{16,24},{24,0},{1,9},{9,17},{17,25},{25,1},{2,10},{10... | collective-permute-start | bytes 688136 | tf_op jit(solution)/shard_map/ppermute | solution.py:306
  9.5 10.4 %collective-permute-start.1 = (bf16[128,896]{1,0:T(8,128)(2,1)S(1)}, bf16[128,896]{1,0:T(8,128)(2,1)S(1)}, u32[]{:S(2)}, u32[]{:S(2)}) collective-permute-start(bf16[128,896]{1,0:T(8,128)(2,1)S(1)} %copy.75.refs_0_), channel_id=1, source_target_pairs={{0,8},{8,16},{16,24},{24,0},{1,9},{9,17},{17,25},{25,1},{2,10},{10... | collective-permute-start | bytes 688136 | tf_op jit(solution)/shard_map/ppermute | solution.py:306
  10.9 33.2 %collective-permute-start.6 = (bf16[128,896]{1,0:T(8,128)(2,1)S(1)}, bf16[128,896]{1,0:T(8,128)(2,1)S(1)}, u32[]{:S(2)}, u32[]{:S(2)}) collective-permute-start(bf16[128,896]{1,0:T(8,128)(2,1)S(1)} %copy.75.refs_0_), channel_id=1, source_target_pairs={{0,24},{8,0},{16,8},{24,16},{1,25},{9,1},{17,9},{25,17},{2,26},{10... | collective-permute-start | bytes 688136 | tf_op jit(solution)/shard_map/ppermute | solution.py:306
  14.7 29.4 %collective-permute-start = (bf16[448,288]{1,0:T(8,128)(2,1)S(1)}, bf16[448,288]{1,0:T(8,128)(2,1)S(1)}, u32[]{:S(2)}, u32[]{:S(2)}) collective-permute-start(bf16[448,288]{1,0:T(8,128)(2,1)S(1)} %pad_maximum_fusion.refs_8_), channel_id=1, source_target_pairs={{0,4},{4,0},{1,5},{5,1},{2,6},{6,2},{3,7},{7,3},{8,12},{12,8},{9,1... | collective-permute-start | bytes 774152 | tf_op jit(solution)/shard_map/ppermute | solution.py:314
  19.9 24.2 %collective-permute-start.3 = (bf16[128,896]{1,0:T(8,128)(2,1)S(1)}, bf16[128,896]{1,0:T(8,128)(2,1)S(1)}, u32[]{:S(2)}, u32[]{:S(2)}) collective-permute-start(bf16[128,896]{1,0:T(8,128)(2,1)S(1)} %collective-permute-done.1.refs_2_), channel_id=1, source_target_pairs={{0,8},{8,16},{16,24},{24,0},{1,9},{9,17},{17,25},{25,1},{2,10},{10... | collective-permute-start | bytes 688136 | tf_op jit(solution)/shard_map/ppermute | solution.py:306
  20.2 23.9 %collective-permute-start.5 = (bf16[128,896]{1,0:T(8,128)(2,1)S(1)}, bf16[128,896]{1,0:T(8,128)(2,1)S(1)}, u32[]{:S(2)}, u32[]{:S(2)}) collective-permute-start(bf16[128,896]{1,0:T(8,128)(2,1)S(1)} %collective-permute-done.4.refs_7_), channel_id=1, source_target_pairs={{0,24},{8,0},{16,8},{24,16},{1,25},{9,1},{17,9},{25,17},{2,26},{10... | collective-permute-start | bytes 688136 | tf_op jit(solution)/shard_map/ppermute | solution.py:306
  23.9 19.6 %all-to-all-start = ((s32[32,1,1]{2,1,0:T(1,128)}), s32[32,1,1]{2,1,0:T(1,128)S(1)}, u32[]{:S(2)}, u32[]{:S(2)}) async-start(s32[32,1,1]{2,1,0:T(1,128)} %copy.70), calls=%async_computation | async-start | bytes 32768 | tf_op jit(solution)/shard_map/all_to_all | solution.py:321
  34.9 129.7 %all-gather.3.cloned.1.call-start = ((), (), s32[]{:S(2)}) async-start(), calls=%async_computation.5 | async-start | bytes 7569408 | tf_op jit(solution)/shard_map/all_gather | solution.py:345
  48.1 32.9 %all-to-all-start.1 = ((bf16[4,256,1152]{2,1,0:T(8,128)(2,1)}), bf16[4,256,1152]{2,1,0:T(8,128)(2,1)S(1)}, u32[]{:S(2)}, u32[]{:S(2)}) async-start(bf16[4,256,1152]{2,1,0:T(8,128)(2,1)} %shard_map.118), calls=%async_computation.1 | async-start | bytes 4718592 | tf_op jit(solution)/shard_map/all_to_all | solution.py:346
  59.1 8.5 %copy-start.4 = (bf16[32,273,2]{1,2,0:T(2,128)(2,1)S(1)}, bf16[32,273,2]{1,2,0:T(2,128)(2,1)}, u32[]{:S(2)}) copy-start(bf16[32,273,2]{1,2,0:T(2,128)(2,1)} %param.18) | copy-start | bytes 104836
  59.1 9.6 %copy-start.6 = (s32[512]{0:T(512)S(1)}, s32[512]{0:T(512)}, u32[]{:S(2)}) copy-start(s32[512]{0:T(512)} %param.20) | copy-start | bytes 6148
  59.1 37.3 %copy-start.7 = (s32[512]{0:T(512)S(1)}, s32[512]{0:T(512)}, u32[]{:S(2)}) copy-start(s32[512]{0:T(512)} %param.23) | copy-start | bytes 6148
  83.0 6.1 %collective-permute-start.7 = (bf16[512,288]{1,0:T(8,128)(2,1)}, bf16[512,288]{1,0:T(8,128)(2,1)S(1)}, u32[]{:S(2)}, u32[]{:S(2)}) collective-permute-start(bf16[512,288]{1,0:T(8,128)(2,1)} %get-tuple-element.27), channel_id=1, source_target_pairs={{0,4},{4,0},{1,5},{5,1},{2,6},{6,2},{3,7},{7,3},{8,12},{12,8},{9,1... | collective-permute-start | bytes 884744 | tf_op jit(solution)/shard_map/ppermute | solution.py:351
  89.1 8.1 %copy-start.1 = (bf16[512,288]{1,0:T(8,128)(2,1)}, bf16[512,288]{1,0:T(8,128)(2,1)S(1)}, u32[]{:S(2)}) copy-start(bf16[512,288]{1,0:T(8,128)(2,1)S(1)} %collective-permute-done.7.rec_ref) | copy-start | bytes 884740
  89.1 1.2 copy-start
  92.5 13.7 %all-to-all-start.2 = ((bf16[32,16,128]{2,1,0:T(8,128)(2,1)}), bf16[32,16,128]{2,1,0:T(8,128)(2,1)S(1)}, u32[]{:S(2)}, u32[]{:S(2)}) async-start(bf16[32,16,128]{2,1,0:T(8,128)(2,1)} %get-tuple-element.28), calls=%async_computation.2 | async-start | bytes 262144 | tf_op jit(solution)/shard_map/all_to_all | solution.py:367
  105.7 21.7 %copy-start.5 = (s32[512]{0:T(512)S(1)}, s32[512]{0:T(512)}, u32[]{:S(2)}) copy-start(s32[512]{0:T(512)} %multiply_add_fusion) | copy-start | bytes 6148
  106.2 0.7 copy-start.3
  118.6 25.0 %all-to-all-start.3 = ((bf16[32,16,512]{2,1,0:T(8,128)(2,1)}), bf16[32,16,512]{2,1,0:T(8,128)(2,1)S(1)}, u32[]{:S(2)}, u32[]{:S(2)}) async-start(bf16[32,16,512]{2,1,0:T(8,128)(2,1)} %get-tuple-element.34), calls=%async_computation.3 | async-start | bytes 1048576 | tf_op jit(solution)/shard_map/all_to_all | solution.py:390
  159.6 5.0 %collective-permute-start.8 = (bf16[4,256,256]{2,1,0:T(8,128)(2,1)S(1)}, bf16[4,256,256]{2,1,0:T(8,128)(2,1)S(1)}, u32[]{:S(2)}, u32[]{:S(2)}) collective-permute-start(bf16[4,256,256]{2,1,0:T(8,128)(2,1)S(1)} %all_to_all.29.own_ref), channel_id=1, source_target_pairs={{0,4},{4,0},{1,5},{5,1},{2,6},{6,2},{3,7},{7,3},{8,12},{12,8},{9,1... | collective-permute-start | bytes 1572872 | tf_op jit(solution)/shard_map/ppermute | solution.py:406
  164.6 21.6 %copy-start.2 = (bf16[256,2,448]{0,2,1:T(8,128)(2,1)S(1)}, bf16[256,2,448]{0,2,1:T(8,128)(2,1)}, u32[]{:S(2)}) copy-start(bf16[256,2,448]{0,2,1:T(8,128)(2,1)} %param.12) | copy-start | bytes 1376260
  169.2 11.0 %collective-permute-start.10 = (bf16[256,448]{1,0:T(8,128)(2,1)}, bf16[256,448]{1,0:T(8,128)(2,1)S(1)}, u32[]{:S(2)}, u32[]{:S(2)}) collective-permute-start(bf16[256,448]{1,0:T(8,128)(2,1)} %get-tuple-element.38), channel_id=1, source_target_pairs={{0,0},{4,2},{8,1},{12,3},{16,4},{20,6},{24,5},{28,7},{1,8},{5,10},... | collective-permute-start | bytes 688136 | tf_op jit(solution)/shard_map/ppermute | solution.py:433
  174.4 11.4 %collective-permute-start.9 = (bf16[256,448]{1,0:T(8,128)(2,1)}, bf16[256,448]{1,0:T(8,128)(2,1)S(1)}, u32[]{:S(2)}, u32[]{:S(2)}) collective-permute-start(bf16[256,448]{1,0:T(8,128)(2,1)} %get-tuple-element.37), channel_id=1, source_target_pairs={{0,1},{4,3},{8,0},{12,2},{16,5},{20,7},{24,4},{28,6},{1,9},{5,11},... | collective-permute-start | bytes 688136 | tf_op jit(solution)/shard_map/ppermute | solution.py:433
Sparse Core Ops, SparseCore 0:
  48.2 62.6 all-gather.2

commit v8 on v5

--- a/solution.py
+++ b/solution.py
@@ -284,7 +284,7 @@
 
 
 def out_kernel(pos_ref, own_ref, oth_ref, *refs):
-    parts, first_ref, second_ref = refs[:8], refs[8], refs[9]
+    w0, w1, far_1, far_3, w3, first_ref, second_ref = refs
     y, core, col = pos_ref[0], pos_ref[1], pos_ref[3]
     acc = [None, None]
     for shift in range(4):
@@ -293,7 +293,9 @@
             k = core if which == 0 else 1 - core
             heads = ref[j, :, 0:224]
             for e in range(2):
-                part = dot(heads, parts[2 * shift + e][jnp.bitwise_xor(k, lax.rem(col, 2))])
+                at = jnp.bitwise_xor(k, lax.rem(col, 2))
+                w = (far_1, far_3)[e][at] if shift == 2 else (w0, w1, None, w3)[shift][2 * e + at]
+                part = dot(heads, w)
                 acc[e] = part if acc[e] is None else acc[e] + part
     same = lax.rem(y, 2) == lax.div(col, 2)
     first_ref[...] = jnp.where(same, acc[0], acc[1]).astype(BF)
@@ -310,17 +312,10 @@
     top, low = tokens[:128].reshape(128, 896), tokens[128:].reshape(128, 896)
     top_1, low_3 = over_y(top, 1), over_y(low, 3)
     low_1, top_3 = over_y(low, 1), over_y(top, 3)
-    top_1, low_3, w_out = lax.optimization_barrier((top_1, low_3, w_out))
     blocks = [top, low, top_1, low_1, over_y(top_1, 1), over_y(low_3, 3), top_3, low_3]
     value_w = jnp.moveaxis(w_value.reshape(2, 448, 112), 0, 1).reshape(448, 224)
     mine = jnp.concatenate([value_w, w_query, w_key], axis=1)
     theirs = lax.ppermute(mine, "core", [(0, 1), (1, 0)])
-    pieces = []
-    for s in range(4):
-        perm = [(k * 4 + c, (c >> 1) * 4 + (s ^ (2 * (c & 1) + k))) for k in range(2) for c in range(4)]
-        pieces.append(lax.ppermute(w_out, ("core", "col"), perm))
-    pieces = [jnp.stack(pieces[:2]), jnp.stack(pieces[2:])]
-
     owner = slot_prompt // 32
     slots = jnp.arange(32, dtype=jnp.int32)
     away = owner != me
@@ -349,9 +344,16 @@
         scratch=[pltpu.VMEM((448, 640), BF), pltpu.VMEM((512, 640), BF)],
         free=range(1, 11),
     )
+    partial, w_out = lax.optimization_barrier((partial, w_out))
+    pieces = []
+    for s in range(4):
+        perm = [(k * 4 + c, (c >> 1) * 4 + (s ^ (2 * (c & 1) + k))) for k in range(2) for c in range(4)]
+        pieces.append(lax.ppermute(w_out, ("core", "col"), perm))
+    pieces = jnp.stack(pieces)
+    out_1, out_3 = over_y(pieces, 1), over_y(pieces, 3)
     partial = lax.all_to_all(partial, "col", split_axis=0, concat_axis=0, tiled=True)
+    partial, states, norms = lax.optimization_barrier((partial, states, norms))
     states = jnp.transpose(states, (2, 0, 1))
-    partial, states, norms = lax.optimization_barrier((partial, states, norms))
     shape = jax.ShapeDtypeStruct((512, 288), BF)
     own, oth = call(sum_kernel, (shape, shape), 1, pos, partial, free=(1,))
     rec = lax.ppermute(oth, "core", [(0, 1), (1, 0)])
@@ -370,12 +372,10 @@
         scratch=[pltpu.VMEM((512, 128), BF)],
         free=(3, 4),
     )
-    q_send, pieces = lax.optimization_barrier((q_send, pieces))
-    out_w = [over_y(x, step) for step in (1, 3) for x in pieces]
     q_rec = lax.all_to_all(q_send, ("req", "col"), split_axis=0, concat_axis=0, tiled=True)
     shape = jax.ShapeDtypeStruct((2, 512, 256), F32)
-    num = call(tail_kernel, shape, 1, pos, own, rec, tail_keys, tail_values, tail_length[:, None])
-    q_rec, num = lax.optimization_barrier((q_rec, num))
+    num = call(tail_kernel, shape, 1, pos, own, rec, tail_keys, tail_values, tail_length[:, None], free=(1, 2))
+    q_rec, out_1, out_3 = lax.optimization_barrier((q_rec, out_1, out_3))
     shape = jax.ShapeDtypeStruct((32, 16, 512), BF)
     whole = pl.BlockSpec((32, 16, 128), lambda i: (0, 0, 0))
     whole_out = pl.BlockSpec((32, 16, 512), lambda i: (0, 0, 0))
@@ -395,10 +395,10 @@
         scratch_shapes=[pltpu.VMEM((128, 128), BF)],
         compiler_params=pltpu.CompilerParams(vmem_limit_bytes=VMEM_LIMIT),
     )(pos, owner, in_hbm(q_rec), in_hbm(q_keep), in_hbm(states), in_hbm(norms))
-    r_send, out_w = lax.optimization_barrier((r_send, out_w))
-    far_1, far_3 = over_y(out_w[0], 1), over_y(out_w[3], 3)
+    r_send, near_1, near_3 = lax.optimization_barrier((r_send, out_1, out_3))
+    far_1, far_3 = over_y(near_1[:2], 1), over_y(near_3[2:], 3)
     r_rec = lax.all_to_all(r_send, ("req", "col"), split_axis=0, concat_axis=0, tiled=True)
-    r_rec, far_1, far_3 = lax.optimization_barrier((r_rec, far_1, far_3))
+    r_rec, num, far_1, far_3 = lax.optimization_barrier((r_rec, num, far_1, far_3))
     heads = call(
         combine_kernel,
         jax.ShapeDtypeStruct((4, 256, 256), BF),
@@ -416,7 +416,7 @@
     heads = lax.all_to_all(heads, "y", split_axis=0, concat_axis=0, tiled=True)
     heads_oth = lax.ppermute(heads, "core", [(0, 1), (1, 0)])
     shape = jax.ShapeDtypeStruct((256, 448), BF)
-    mixed = call(out_kernel, (shape, shape), 1, pos, heads, heads_oth, *pieces, out_w[0], out_w[1], far_1, far_3, out_w[2], out_w[3], free=(1, 2))
+    mixed = call(out_kernel, (shape, shape), 1, pos, heads, heads_oth, pieces, out_1, far_1, far_3, out_3, free=(1, 2))
 
     def at(y, core, col):
         return (y * 2 + core) * 4 + col

time: 181 us -> 181 us (level)
  starting transfers between devices: 69.1 us -> 66.9 us
    ppermute x4, waiting for transfers between devices: 4.59 us -> 14.2 us  [body(): pieces.append(lax.ppermute(w_out, ('core', 'col'), perm))]
    ppermute x12 -> x10, waiting for transfers between devices: 10.2 us -> 1.09 us  [over_y(): return lax.ppermute(x, 'y', [(i, (i + step) % 4) for i in range(4)])]
    another operation x1 -> x0, local copies, waits for them, and re-layouts: 8.46 us -> none  [body(): states = cached_state[0].reshape(273, 224, 32)]
    optimization_barrier x0 -> x1, local copies, waits for them, and re-layouts: none -> 8.36 us  [body(): partial, states, norms = lax.optimization_barrier((partial, states, norms))]
    all_to_all x1, waiting for transfers between devices: 4.46 us -> 0.21 us  [body(): lax.all_to_all(r_send, ('req', 'col'), split_axis=0, concat_axis=0, tiled...]
    ppermute x12 -> x10, starting transfers between devices: 13.5 us -> 11.3 us  [over_y(): return lax.ppermute(x, 'y', [(i, (i + step) % 4) for i in range(4)])]
    slice x0 -> x2, local copies, waits for them, and re-layouts: none -> 2.1 us  [body(): far_1, far_3 = (over_y(near_1[:2], 1), over_y(near_3[2:], 3))]
    unnamed x39 -> x29, local copies, waits for them, and re-layouts: 11.1 us -> 10.9 us
  transfers between devices with their start and end apart: 25 -> 23, of which waited for: 11 -> 11; matrix products, arithmetic and copies ran while one was open for 14% -> 16% of each run, Pallas kernels for 15% -> 9%
where the time goes in v8:
time: 181 us; the launch traced here: 178 us
  starting transfers between devices  66.9 us (37%)
  Pallas kernels  35.9 us (20%)
  waiting for transfers between devices  30.6 us (17%)
  local copies, waits for them, and re-layouts  27.8 us (15%)
  blocking collectives  12 us (7%)
  other arithmetic  4.1 us (2%)
    pallas_call x6, Pallas kernels, call(): pl.pallas_call(kernel, grid=(1,), out_shape=jax.tree.map(lambda x: pltpu....  24.1 us
    ppermute x4, starting transfers between devices, body(): pieces.append(lax.ppermute(w_out, ('core', 'col'), perm))  14.4 us
    ppermute x4, waiting for transfers between devices, body(): pieces.append(lax.ppermute(w_out, ('core', 'col'), perm))  14.2 us
    all_to_all x1, blocking collectives, body(): heads = lax.all_to_all(heads, 'y', split_axis=0, concat_axis=0, tiled=True)  12 us
    pallas_call x1, Pallas kernels, body(): pl.pallas_call(slot_kernel, grid=(4,), out_shape=(pltpu.HBM(shape.shape,...  11.8 us
    ppermute x10, starting transfers between devices, over_y(): return lax.ppermute(x, 'y', [(i, (i + step) % 4) for i in range(4)])  11.3 us
    unnamed x29, local copies, waits for them, and re-layouts  10.9 us
    all_to_all x1, starting transfers between devices, body(): lax.all_to_all(code[:, None], ('req', 'col'), split_axis=0, concat_axis=0...  10.8 us
  transfers between devices with their start and end apart: 23, of which 11 were waited for; matrix products, arithmetic and copies ran while one was open for 16% of the time, Pallas kernels for 9%

profile of v8, /device:TPU:9, one launch (start us, length us, event | category | flops | bytes accessed | tf_op | source)
XLA Modules:
  0.0 177.7 jit_solution(4470857293547778083)
XLA Ops:
  0.0 1.1 fusion.8
  1.1 0.2 copy.76.refs_1_
  1.3 1.4 collective-permute-start.1
  2.6 0.2 collective-permute-start.3
  3.0 1.4 collective-permute-start
  4.4 0.3 collective-permute-start.5
  4.7 0.9 copy.74
  5.6 0.9 copy.73
  6.5 1.2 reshape.76
  7.7 0.2 copy.84
  8.3 3.2 %collective-permute-start.6 = (bf16[448,288]{1,0:T(8,128)(2,1)S(1)}, bf16[448,288]{1,0:T(8,128)(2,1)S(1)}, u32[]{:S(2)}, u32[]{:S(2)}) collective-permute-start(bf16[448,288]{1,0:T(8,128)(2,1)S(1)} %pad_maximum_fusion.1.refs_8_), channel_id=1, source_target_pairs={{0,4},{4,0},{1,5},{5,1},{2,6},{6,2},{3,7},{7,3},{8,12},{12,8},{9,1... | collective-permute-start | bytes 774152 | tf_op jit(solution)/shard_map/ppermute | solution.py:318
  11.5 1.1 collective-permute-done.refs_2_
  12.5 1.5 collective-permute-start.2
  14.0 0.5 collective-permute-start.4
  14.7 0.7 copy.67
  15.4 10.8 %all-to-all-start = ((s32[32,1,1]{2,1,0:T(1,128)}), s32[32,1,1]{2,1,0:T(1,128)S(1)}, u32[]{:S(2)}, u32[]{:S(2)}) async-start(s32[32,1,1]{2,1,0:T(1,128)} %copy.67), calls=%async_computation | async-start | bytes 32768 | tf_op jit(solution)/shard_map/all_to_all | solution.py:325
  26.2 4.0 %shard_map.118 = bf16[4,256,1152]{2,1,0:T(8,128)(2,1)} custom-call(s32[4]{0:T(128)S(1)} %pad_add_fusion.pos_ref, bf16[128,896]{1,0:T(8,128)(2,1)S(1)} %copy.75.refs_0_, bf16[128,896]{1,0:T(8,128)(2,1)S(1)} %copy.76.refs_1_, bf16[128,896]{1,0:T(8,128)(2,1)S(1)} %collective-permute-done.refs_2_, bf16[128,896]{1,0:T(8,128)(2,1)S(1)} %collective-permute-done.1.refs_3_, ...), custom_call_target="tpu_custom_call" | custom-call | tf_op jit(solution)/shard_map/pallas_call | solution.py:42
  30.2 4.4 %all-to-all-done = s32[32,1,1]{2,1,0:T(1,128)S(1)} async-done(((s32[32,1,1]{2,1,0:T(1,128)}), s32[32,1,1]{2,1,0:T(1,128)S(1)}, u32[]{:S(2)}, u32[]{:S(2)}) %all-to-all-start) | async-done | bytes 160 | tf_op jit(solution)/shard_map/all_to_all | solution.py:325
  34.6 3.6 %all-to-all-start.1 = ((bf16[4,256,1152]{2,1,0:T(8,128)(2,1)}), bf16[4,256,1152]{2,1,0:T(8,128)(2,1)S(1)}, u32[]{:S(2)}, u32[]{:S(2)}) async-start(bf16[4,256,1152]{2,1,0:T(8,128)(2,1)} %shard_map.118), calls=%async_computation.1 | async-start | bytes 4718592 | tf_op jit(solution)/shard_map/all_to_all | solution.py:354
  38.3 7.4 %copy.77 = bf16[1,273,7168]{1,2,0:T(8,128)(2,1)} copy(bf16[1,273,7168]{2,1,0:T(8,128)(2,1)} %param.17) | data formatting | bytes 7827456 | tf_op args[5]
  45.7 0.6 pad.4.norm_ref
  46.4 0.2 compare_reduce_fusion.1
  46.5 0.2 fusion.2.s_ref
  46.7 0.2 convert_reduce_fusion
  47.0 0.6 multiply_add_fusion
  47.6 8.4 %collective-permute-start.11 = (bf16[224,448]{1,0:T(8,128)(2,1)S(1)}, bf16[224,448]{1,0:T(8,128)(2,1)S(1)}, u32[]{:S(2)}, u32[]{:S(2)}) collective-permute-start(bf16[224,448]{1,0:T(8,128)(2,1)S(1)} %copy-done.12), channel_id=1, source_target_pairs={{0,3},{1,1},{2,7},{3,5},{4,2},{5,0},{6,6},{7,4},{8,11},{9,9},{10,1... | collective-permute-start | bytes 602120 | tf_op jit(solution)/shard_map/ppermute | solution.py:351
  56.1 0.4 collective-permute-start.9
  56.5 5.5 %collective-permute-start.8 = (bf16[224,448]{1,0:T(8,128)(2,1)S(1)}, bf16[224,448]{1,0:T(8,128)(2,1)S(1)}, u32[]{:S(2)}, u32[]{:S(2)}) collective-permute-start(bf16[224,448]{1,0:T(8,128)(2,1)S(1)} %copy-done.12), channel_id=1, source_target_pairs={{0,0},{1,2},{2,4},{3,6},{4,1},{5,3},{6,5},{7,7},{8,8},{9,10},{10,1... | collective-permute-start | bytes 602120 | tf_op jit(solution)/shard_map/ppermute | solution.py:351
  62.0 0.7 add_reduce_fusion
  62.7 0.7 compare_reduce_fusion
  63.3 4.6 %collective-permute-done.11 = bf16[224,448]{1,0:T(8,128)(2,1)S(1)} collective-permute-done((bf16[224,448]{1,0:T(8,128)(2,1)S(1)}, bf16[224,448]{1,0:T(8,128)(2,1)S(1)}, u32[]{:S(2)}, u32[]{:S(2)}) %collective-permute-start.11) | collective-permute-done | bytes 200736 | tf_op jit(solution)/shard_map/ppermute | solution.py:351
  67.9 6.8 %collective-permute-done.10 = bf16[224,448]{1,0:T(8,128)(2,1)S(1)} collective-permute-done((bf16[224,448]{1,0:T(8,128)(2,1)S(1)}, bf16[224,448]{1,0:T(8,128)(2,1)S(1)}, u32[]{:S(2)}, u32[]{:S(2)}) %collective-permute-start.10) | collective-permute-done | bytes 200736 | tf_op jit(solution)/shard_map/ppermute | solution.py:351
  74.7 2.8 %collective-permute-done.8 = bf16[224,448]{1,0:T(8,128)(2,1)S(1)} collective-permute-done((bf16[224,448]{1,0:T(8,128)(2,1)S(1)}, bf16[224,448]{1,0:T(8,128)(2,1)S(1)}, u32[]{:S(2)}, u32[]{:S(2)}) %collective-permute-start.8) | collective-permute-done | bytes 200736 | tf_op jit(solution)/shard_map/ppermute | solution.py:351
  77.7 1.3 collective-permute-start.12
  79.0 1.5 collective-permute-start.13
  80.5 2.0 %shard_map.119 = (bf16[512,288]{1,0:T(8,128)(2,1)}, bf16[512,288]{1,0:T(8,128)(2,1)}) custom-call(s32[4]{0:T(128)S(1)} %pad_add_fusion.pos_ref, bf16[4,256,1152]{2,1,0:T(8,128)(2,1)S(1)} %all-to-all-done.1.p_ref), custom_call_target="tpu_custom_call" | custom-call | tf_op jit(solution)/shard_map/pallas_call | solution.py:42
  82.7 1.8 %collective-permute-done.7.rec_ref = bf16[512,288]{1,0:T(8,128)(2,1)S(1)} collective-permute-done((bf16[512,288]{1,0:T(8,128)(2,1)}, bf16[512,288]{1,0:T(8,128)(2,1)S(1)}, u32[]{:S(2)}, u32[]{:S(2)}) %collective-permute-start.7) | collective-permute-done | bytes 294944 | tf_op jit(solution)/shard_map/ppermute | solution.py:359
  84.5 1.0 copy-done
  85.5 2.3 %shard_map.120 = (bf16[32,16,128]{2,1,0:T(8,128)(2,1)}, bf16[32,16,128]{2,1,0:T(8,128)(2,1)}) custom-call(s32[4]{0:T(128)S(1)} %pad_add_fusion.pos_ref, s32[32]{0:T(128)S(1)} %broadcast_select_fusion.2.g_ref, s32[32]{0:T(128)S(1)} %fusion.2.s_ref, bf16[512,288]{1,0:T(8,128)(2,1)S(1)} %copy-done, bf16[512,288]{1,0:T(8,128)(2,1)S(1)} %collective-permute-done.7.rec_ref, ...), custom_call_target="tpu_custom_call" | custom-call | tf_op jit(solution)/shard_map/pallas_call | solution.py:42
  87.8 3.9 %all-to-all-start.2 = ((bf16[32,16,128]{2,1,0:T(8,128)(2,1)}), bf16[32,16,128]{2,1,0:T(8,128)(2,1)S(1)}, u32[]{:S(2)}, u32[]{:S(2)}) async-start(bf16[32,16,128]{2,1,0:T(8,128)(2,1)} %get-tuple-element.32), calls=%async_computation.2 | async-start | bytes 262144 | tf_op jit(solution)/shard_map/all_to_all | solution.py:375
  91.7 8.4 %copy.78 = bf16[273,224,32]{1,0,2:T(8,128)(2,1)} copy(bf16[273,224,32]{0,2,1:T(8,128)(2,1)} %bitcast.26) | data formatting | bytes 7827456 | tf_op jit(solution)/shard_map/optimization_barrier | solution.py:355
  100.1 1.0 all-to-all-done.2.rec_ref
  101.1 0.7 copy-done.4
  101.7 11.8 %shard_map.121 = (bf16[32,16,512]{2,1,0:T(8,128)(2,1)}, bf16[32,16,512]{2,1,0:T(8,128)(2,1)}) custom-call(s32[4]{0:T(128)S(1)} %pad_add_fusion.pos_ref, s32[32]{0:T(128)S(1)} %get-tuple-element.52.owner_ref, bf16[32,16,128]{2,1,0:T(8,128)(2,1)} %copy-done.4, bf16[32,16,128]{2,1,0:T(8,128)(2,1)} %get-tuple-element.35.keep_ref, ...), custom_call_target="tpu_custom_call" | custom-call | tf_op jit(solution)/shard_map/pallas_call | solution.py:382
  113.5 8.3 %all-to-all-start.3 = ((bf16[32,16,512]{2,1,0:T(8,128)(2,1)}), bf16[32,16,512]{2,1,0:T(8,128)(2,1)S(1)}, u32[]{:S(2)}, u32[]{:S(2)}) async-start(bf16[32,16,512]{2,1,0:T(8,128)(2,1)} %get-tuple-element.41), calls=%async_computation.3 | async-start | bytes 1048576 | tf_op jit(solution)/shard_map/all_to_all | solution.py:400
  121.8 1.0 slice.14
  122.9 0.3 collective-permute-start.14
  123.2 1.0 slice.15
  124.2 3.0 %collective-permute-start.15 = (bf16[2,224,448]{2,1,0:T(8,128)(2,1)S(1)}, bf16[2,224,448]{2,1,0:T(8,128)(2,1)S(1)}, u32[]{:S(2)}, u32[]{:S(2)}) collective-permute-start(bf16[2,224,448]{2,1,0:T(8,128)(2,1)S(1)} %slice.15), channel_id=1, source_target_pairs={{0,24},{8,0},{16,8},{24,16},{1,25},{9,1},{17,9},{25,17},{2,26},{10... | collective-permute-start | bytes 1204232 | tf_op jit(solution)/shard_map/ppermute | solution.py:310
  127.2 0.9 copy.79.len_ref
  128.1 0.9 copy.80.place_ref
  128.9 8.1 %shard_map.122.num_ref = f32[2,512,256]{2,1,0:T(8,128)} custom-call(s32[4]{0:T(128)S(1)} %pad_add_fusion.pos_ref, bf16[512,288]{1,0:T(8,128)(2,1)S(1)} %copy-done.1, bf16[512,288]{1,0:T(8,128)(2,1)S(1)} %collective-permute-done.7.rec_ref, bf16[512,256]{1,0:T(8,128)(2,1)} %tk_ref.1, bf16[512,1792]{1,0:T(8,128)(2,1)} %tv_ref.1, s32[512,1]{1,0:T(8,128)} %copy.79.len_ref), custom_call_target="tpu_custom_call" | custom-call | tf_op jit(solution)/shard_map/pallas_call | solution.py:42
  137.0 0.2 all-to-all-done.3.rec_ref
  137.2 3.7 %shard_map.123 = bf16[4,256,256]{2,1,0:T(8,128)(2,1)} custom-call(s32[4]{0:T(128)S(1)} %pad_add_fusion.pos_ref, s32[32]{0:T(128)S(1)} %broadcast_select_fusion.2.g_ref, s32[32]{0:T(128)S(1)} %fusion.2.s_ref, f32[2,512,256]{2,1,0:T(8,128)} %shard_map.122.num_ref, bf16[32,16,512]{2,1,0:T(8,128)(2,1)S(1)} %all-to-all-done.3.rec_ref, ...), custom_call_target="tpu_custom_call" | custom-call | tf_op jit(solution)/shard_map/pallas_call | solution.py:42
  140.9 12.0 %all_to_all.29.own_ref = bf16[4,256,256]{2,1,0:T(8,128)(2,1)S(1)} all-to-all(bf16[4,256,256]{2,1,0:T(8,128)(2,1)} %shard_map.123), channel_id=1, replica_groups=mesh['req'=8,'y'=4,'core'=2,'col'=4] {'y'}, dimensions={0} | all-to-all | bytes 1048576 | tf_op jit(solution)/shard_map/all_to_all | solution.py:416
  153.0 4.5 %collective-permute-start.16 = (bf16[4,256,256]{2,1,0:T(8,128)(2,1)S(1)}, bf16[4,256,256]{2,1,0:T(8,128)(2,1)S(1)}, u32[]{:S(2)}, u32[]{:S(2)}) collective-permute-start(bf16[4,256,256]{2,1,0:T(8,128)(2,1)S(1)} %all_to_all.29.own_ref), channel_id=1, source_target_pairs={{0,4},{4,0},{1,5},{5,1},{2,6},{6,2},{3,7},{7,3},{8,12},{12,8},{9,1... | collective-permute-start | bytes 1572872 | tf_op jit(solution)/shard_map/ppermute | solution.py:417
  157.5 1.5 collective-permute-done.16.oth_ref
  159.0 4.1 %shard_map.124 = (bf16[256,448]{1,0:T(8,128)(2,1)}, bf16[256,448]{1,0:T(8,128)(2,1)}) custom-call(s32[4]{0:T(128)S(1)} %pad_add_fusion.pos_ref, bf16[4,256,256]{2,1,0:T(8,128)(2,1)S(1)} %all_to_all.29.own_ref, bf16[4,256,256]{2,1,0:T(8,128)(2,1)S(1)} %collective-permute-done.16.oth_ref, bf16[4,224,448]{2,1,0:T(8,128)(2,1)} %copy-done.2, ...), custom_call_target="tpu_custom_call" | custom-call | tf_op jit(solution)/shard_map/pallas_call | solution.py:42
  163.1 3.3 %collective-permute-start.17 = (bf16[256,448]{1,0:T(8,128)(2,1)}, bf16[256,448]{1,0:T(8,128)(2,1)S(1)}, u32[]{:S(2)}, u32[]{:S(2)}) collective-permute-start(bf16[256,448]{1,0:T(8,128)(2,1)} %get-tuple-element.49), channel_id=1, source_target_pairs={{0,1},{4,3},{8,0},{12,2},{16,5},{20,7},{24,4},{28,6},{1,9},{5,11},... | collective-permute-start | bytes 688136 | tf_op jit(solution)/shard_map/ppermute | solution.py:429
  166.4 3.6 %collective-permute-start.18 = (bf16[256,448]{1,0:T(8,128)(2,1)}, bf16[256,448]{1,0:T(8,128)(2,1)S(1)}, u32[]{:S(2)}, u32[]{:S(2)}) collective-permute-start(bf16[256,448]{1,0:T(8,128)(2,1)} %get-tuple-element.50), channel_id=1, source_target_pairs={{0,0},{4,2},{8,1},{12,3},{16,4},{20,6},{24,5},{28,7},{1,8},{5,10},... | collective-permute-start | bytes 688136 | tf_op jit(solution)/shard_map/ppermute | solution.py:429
  170.0 5.0 %collective-permute-done.17 = bf16[256,448]{1,0:T(8,128)(2,1)S(1)} collective-permute-done((bf16[256,448]{1,0:T(8,128)(2,1)}, bf16[256,448]{1,0:T(8,128)(2,1)S(1)}, u32[]{:S(2)}, u32[]{:S(2)}) %collective-permute-start.17) | collective-permute-done | bytes 229408 | tf_op jit(solution)/shard_map/ppermute | solution.py:429
  175.0 1.5 collective-permute-done.18
  176.6 0.2 copy.81
  176.8 0.9 fusion.1
  (53 shorter events, 1.4 us)
Async XLA Ops:
  0.0 11.5 %copy-start.11 = (s32[32]{0:T(128)S(1)}, s32[32]{0:T(128)}, u32[]{:S(2)}) copy-start(s32[32]{0:T(128)} %param.19) | copy-start | bytes 388
  1.3 24.9 %collective-permute-start.1 = (bf16[128,896]{1,0:T(8,128)(2,1)S(1)}, bf16[128,896]{1,0:T(8,128)(2,1)S(1)}, u32[]{:S(2)}, u32[]{:S(2)}) collective-permute-start(bf16[128,896]{1,0:T(8,128)(2,1)S(1)} %copy.76.refs_1_), channel_id=1, source_target_pairs={{0,8},{8,16},{16,24},{24,0},{1,9},{9,17},{17,25},{25,1},{2,10},{10... | collective-permute-start | bytes 688136 | tf_op jit(solution)/shard_map/ppermute | solution.py:310
  2.6 11.4 %collective-permute-start.3 = (bf16[128,896]{1,0:T(8,128)(2,1)S(1)}, bf16[128,896]{1,0:T(8,128)(2,1)S(1)}, u32[]{:S(2)}, u32[]{:S(2)}) collective-permute-start(bf16[128,896]{1,0:T(8,128)(2,1)S(1)} %copy.76.refs_1_), channel_id=1, source_target_pairs={{0,24},{8,0},{16,8},{24,16},{1,25},{9,1},{17,9},{25,17},{2,26},{10... | collective-permute-start | bytes 688136 | tf_op jit(solution)/shard_map/ppermute | solution.py:310
  3.0 9.6 %collective-permute-start = (bf16[128,896]{1,0:T(8,128)(2,1)S(1)}, bf16[128,896]{1,0:T(8,128)(2,1)S(1)}, u32[]{:S(2)}, u32[]{:S(2)}) collective-permute-start(bf16[128,896]{1,0:T(8,128)(2,1)S(1)} %copy.75.refs_0_), channel_id=1, source_target_pairs={{0,8},{8,16},{16,24},{24,0},{1,9},{9,17},{17,25},{25,1},{2,10},{10... | collective-permute-start | bytes 688136 | tf_op jit(solution)/shard_map/ppermute | solution.py:310
  4.4 21.9 %collective-permute-start.5 = (bf16[128,896]{1,0:T(8,128)(2,1)S(1)}, bf16[128,896]{1,0:T(8,128)(2,1)S(1)}, u32[]{:S(2)}, u32[]{:S(2)}) collective-permute-start(bf16[128,896]{1,0:T(8,128)(2,1)S(1)} %copy.75.refs_0_), channel_id=1, source_target_pairs={{0,24},{8,0},{16,8},{24,16},{1,25},{9,1},{17,9},{25,17},{2,26},{10... | collective-permute-start | bytes 688136 | tf_op jit(solution)/shard_map/ppermute | solution.py:310
  8.3 18.0 %collective-permute-start.6 = (bf16[448,288]{1,0:T(8,128)(2,1)S(1)}, bf16[448,288]{1,0:T(8,128)(2,1)S(1)}, u32[]{:S(2)}, u32[]{:S(2)}) collective-permute-start(bf16[448,288]{1,0:T(8,128)(2,1)S(1)} %pad_maximum_fusion.1.refs_8_), channel_id=1, source_target_pairs={{0,4},{4,0},{1,5},{5,1},{2,6},{6,2},{3,7},{7,3},{8,12},{12,8},{9,1... | collective-permute-start | bytes 774152 | tf_op jit(solution)/shard_map/ppermute | solution.py:318
  12.5 13.7 %collective-permute-start.2 = (bf16[128,896]{1,0:T(8,128)(2,1)S(1)}, bf16[128,896]{1,0:T(8,128)(2,1)S(1)}, u32[]{:S(2)}, u32[]{:S(2)}) collective-permute-start(bf16[128,896]{1,0:T(8,128)(2,1)S(1)} %collective-permute-done.refs_2_), channel_id=1, source_target_pairs={{0,8},{8,16},{16,24},{24,0},{1,9},{9,17},{17,25},{25,1},{2,10},{10... | collective-permute-start | bytes 688136 | tf_op jit(solution)/shard_map/ppermute | solution.py:310
  14.0 12.2 %collective-permute-start.4 = (bf16[128,896]{1,0:T(8,128)(2,1)S(1)}, bf16[128,896]{1,0:T(8,128)(2,1)S(1)}, u32[]{:S(2)}, u32[]{:S(2)}) collective-permute-start(bf16[128,896]{1,0:T(8,128)(2,1)S(1)} %collective-permute-done.3.refs_7_), channel_id=1, source_target_pairs={{0,24},{8,0},{16,8},{24,16},{1,25},{9,1},{17,9},{25,17},{2,26},{10... | collective-permute-start | bytes 688136 | tf_op jit(solution)/shard_map/ppermute | solution.py:310
  15.4 19.3 %all-to-all-start = ((s32[32,1,1]{2,1,0:T(1,128)}), s32[32,1,1]{2,1,0:T(1,128)S(1)}, u32[]{:S(2)}, u32[]{:S(2)}) async-start(s32[32,1,1]{2,1,0:T(1,128)} %copy.67), calls=%async_computation | async-start | bytes 32768 | tf_op jit(solution)/shard_map/all_to_all | solution.py:325
  34.6 45.9 %all-to-all-start.1 = ((bf16[4,256,1152]{2,1,0:T(8,128)(2,1)}), bf16[4,256,1152]{2,1,0:T(8,128)(2,1)S(1)}, u32[]{:S(2)}, u32[]{:S(2)}) async-start(bf16[4,256,1152]{2,1,0:T(8,128)(2,1)} %shard_map.118), calls=%async_computation.1 | async-start | bytes 4718592 | tf_op jit(solution)/shard_map/all_to_all | solution.py:354
  38.3 7.4 %copy-start.7 = (bf16[32,273,2]{1,2,0:T(2,128)(2,1)S(1)}, bf16[32,273,2]{1,2,0:T(2,128)(2,1)}, u32[]{:S(2)}) copy-start(bf16[32,273,2]{1,2,0:T(2,128)(2,1)} %param.18) | copy-start | bytes 104836
  38.3 8.4 %copy-start.9 = (s32[512]{0:T(512)S(1)}, s32[512]{0:T(512)}, u32[]{:S(2)}) copy-start(s32[512]{0:T(512)} %param.20) | copy-start | bytes 6148
  38.3 9.3 %copy-start.12 = (bf16[224,448]{1,0:T(8,128)(2,1)S(1)}, bf16[224,448]{1,0:T(8,128)(2,1)}, u32[]{:S(2)}) copy-start(bf16[224,448]{1,0:T(8,128)(2,1)} %param.16) | copy-start | bytes 602116
  47.6 20.3 %collective-permute-start.11 = (bf16[224,448]{1,0:T(8,128)(2,1)S(1)}, bf16[224,448]{1,0:T(8,128)(2,1)S(1)}, u32[]{:S(2)}, u32[]{:S(2)}) collective-permute-start(bf16[224,448]{1,0:T(8,128)(2,1)S(1)} %copy-done.12), channel_id=1, source_target_pairs={{0,3},{1,1},{2,7},{3,5},{4,2},{5,0},{6,6},{7,4},{8,11},{9,9},{10,1... | collective-permute-start | bytes 602120 | tf_op jit(solution)/shard_map/ppermute | solution.py:351
  56.0 18.7 %collective-permute-start.10 = (bf16[224,448]{1,0:T(8,128)(2,1)S(1)}, bf16[224,448]{1,0:T(8,128)(2,1)S(1)}, u32[]{:S(2)}, u32[]{:S(2)}) collective-permute-start(bf16[224,448]{1,0:T(8,128)(2,1)S(1)} %copy-done.12), channel_id=1, source_target_pairs={{0,2},{1,0},{2,6},{3,4},{4,3},{5,1},{6,7},{7,5},{8,10},{9,8},{10,1... | collective-permute-start | bytes 602120 | tf_op jit(solution)/shard_map/ppermute | solution.py:351
  56.1 18.6 %collective-permute-start.9 = (bf16[224,448]{1,0:T(8,128)(2,1)S(1)}, bf16[224,448]{1,0:T(8,128)(2,1)S(1)}, u32[]{:S(2)}, u32[]{:S(2)}) collective-permute-start(bf16[224,448]{1,0:T(8,128)(2,1)S(1)} %copy-done.12), channel_id=1, source_target_pairs={{0,1},{1,3},{2,5},{3,7},{4,0},{5,2},{6,4},{7,6},{8,9},{9,11},{10,1... | collective-permute-start | bytes 602120 | tf_op jit(solution)/shard_map/ppermute | solution.py:351
  56.5 21.0 %collective-permute-start.8 = (bf16[224,448]{1,0:T(8,128)(2,1)S(1)}, bf16[224,448]{1,0:T(8,128)(2,1)S(1)}, u32[]{:S(2)}, u32[]{:S(2)}) collective-permute-start(bf16[224,448]{1,0:T(8,128)(2,1)S(1)} %copy-done.12), channel_id=1, source_target_pairs={{0,0},{1,2},{2,4},{3,6},{4,1},{5,3},{6,5},{7,7},{8,8},{9,10},{10,1... | collective-permute-start | bytes 602120 | tf_op jit(solution)/shard_map/ppermute | solution.py:351
  77.7 22.4 %copy-start.2 = (bf16[4,224,448]{2,1,0:T(8,128)(2,1)}, bf16[4,224,448]{2,1,0:T(8,128)(2,1)S(1)}, u32[]{:S(2)}) copy-start(bf16[4,224,448]{2,1,0:T(8,128)(2,1)S(1)} %pad_maximum_fusion.refs_0_) | copy-start | bytes 2408452
  77.7 22.4 %collective-permute-start.12 = (bf16[4,224,448]{2,1,0:T(8,128)(2,1)S(1)}, bf16[4,224,448]{2,1,0:T(8,128)(2,1)}, u32[]{:S(2)}, u32[]{:S(2)}) collective-permute-start(bf16[4,224,448]{2,1,0:T(8,128)(2,1)S(1)} %pad_maximum_fusion.refs_0_), channel_id=1, source_target_pairs={{0,8},{8,16},{16,24},{24,0},{1,9},{9,17},{17,25},{25,1},{2,10},{10... | collective-permute-start | bytes 2408456 | tf_op jit(solution)/shard_map/ppermute | solution.py:310
  79.0 21.1 %collective-permute-start.13 = (bf16[4,224,448]{2,1,0:T(8,128)(2,1)S(1)}, bf16[4,224,448]{2,1,0:T(8,128)(2,1)}, u32[]{:S(2)}, u32[]{:S(2)}) collective-permute-start(bf16[4,224,448]{2,1,0:T(8,128)(2,1)S(1)} %pad_maximum_fusion.refs_0_), channel_id=1, source_target_pairs={{0,24},{8,0},{16,8},{24,16},{1,25},{9,1},{17,9},{25,17},{2,26},{10... | collective-permute-start | bytes 2408456 | tf_op jit(solution)/shard_map/ppermute | solution.py:310
  82.6 1.9 %collective-permute-start.7 = (bf16[512,288]{1,0:T(8,128)(2,1)}, bf16[512,288]{1,0:T(8,128)(2,1)S(1)}, u32[]{:S(2)}, u32[]{:S(2)}) collective-permute-start(bf16[512,288]{1,0:T(8,128)(2,1)} %get-tuple-element.31), channel_id=1, source_target_pairs={{0,4},{4,0},{1,5},{5,1},{2,6},{6,2},{3,7},{7,3},{8,12},{12,8},{9,1... | collective-permute-start | bytes 884744 | tf_op jit(solution)/shard_map/ppermute | solution.py:359
  84.5 1.0 copy-start
  87.8 13.3 %all-to-all-start.2 = ((bf16[32,16,128]{2,1,0:T(8,128)(2,1)}), bf16[32,16,128]{2,1,0:T(8,128)(2,1)S(1)}, u32[]{:S(2)}, u32[]{:S(2)}) async-start(bf16[32,16,128]{2,1,0:T(8,128)(2,1)} %get-tuple-element.32), calls=%async_computation.2 | async-start | bytes 262144 | tf_op jit(solution)/shard_map/all_to_all | solution.py:375
  100.1 27.1 %copy-start.10 = (s32[512]{0:T(512)S(1)}, s32[512]{0:T(512)}, u32[]{:S(2)}) copy-start(s32[512]{0:T(512)} %param.23) | copy-start | bytes 6148
  101.1 0.7 copy-start.4
  101.7 26.3 %copy-start.8 = (s32[512]{0:T(512)S(1)}, s32[512]{0:T(512)}, u32[]{:S(2)}) copy-start(s32[512]{0:T(512)} %multiply_add_fusion) | copy-start | bytes 6148
  101.7 27.2 %copy-start.1 = (bf16[512,288]{1,0:T(8,128)(2,1)S(1)}, bf16[512,288]{1,0:T(8,128)(2,1)}, u32[]{:S(2)}) copy-start(bf16[512,288]{1,0:T(8,128)(2,1)} %get-tuple-element.30.own_ref) | copy-start | bytes 884740
  113.5 23.7 %all-to-all-start.3 = ((bf16[32,16,512]{2,1,0:T(8,128)(2,1)}), bf16[32,16,512]{2,1,0:T(8,128)(2,1)S(1)}, u32[]{:S(2)}, u32[]{:S(2)}) async-start(bf16[32,16,512]{2,1,0:T(8,128)(2,1)} %get-tuple-element.41), calls=%async_computation.3 | async-start | bytes 1048576 | tf_op jit(solution)/shard_map/all_to_all | solution.py:400
  122.9 14.1 %collective-permute-start.14 = (bf16[2,224,448]{2,1,0:T(8,128)(2,1)S(1)}, bf16[2,224,448]{2,1,0:T(8,128)(2,1)S(1)}, u32[]{:S(2)}, u32[]{:S(2)}) collective-permute-start(bf16[2,224,448]{2,1,0:T(8,128)(2,1)S(1)} %slice.14), channel_id=1, source_target_pairs={{0,8},{8,16},{16,24},{24,0},{1,9},{9,17},{17,25},{25,1},{2,10},{10... | collective-permute-start | bytes 1204232 | tf_op jit(solution)/shard_map/ppermute | solution.py:310
  124.2 12.8 %collective-permute-start.15 = (bf16[2,224,448]{2,1,0:T(8,128)(2,1)S(1)}, bf16[2,224,448]{2,1,0:T(8,128)(2,1)S(1)}, u32[]{:S(2)}, u32[]{:S(2)}) collective-permute-start(bf16[2,224,448]{2,1,0:T(8,128)(2,1)S(1)} %slice.15), channel_id=1, source_target_pairs={{0,24},{8,0},{16,8},{24,16},{1,25},{9,1},{17,9},{25,17},{2,26},{10... | collective-permute-start | bytes 1204232 | tf_op jit(solution)/shard_map/ppermute | solution.py:310
  137.0 22.0 %copy-start.5 = (bf16[2,224,448]{2,1,0:T(8,128)(2,1)}, bf16[2,224,448]{2,1,0:T(8,128)(2,1)S(1)}, u32[]{:S(2)}) copy-start(bf16[2,224,448]{2,1,0:T(8,128)(2,1)S(1)} %collective-permute-done.14.refs_2_) | copy-start | bytes 1204228
  137.0 22.0 %copy-start.6 = (bf16[2,224,448]{2,1,0:T(8,128)(2,1)}, bf16[2,224,448]{2,1,0:T(8,128)(2,1)S(1)}, u32[]{:S(2)}) copy-start(bf16[2,224,448]{2,1,0:T(8,128)(2,1)S(1)} %collective-permute-done.15.refs_3_) | copy-start | bytes 1204228
  140.9 35.9 %copy-start.3 = (bf16[256,2,448]{0,2,1:T(8,128)(2,1)S(1)}, bf16[256,2,448]{0,2,1:T(8,128)(2,1)}, u32[]{:S(2)}) copy-start(bf16[256,2,448]{0,2,1:T(8,128)(2,1)} %param.12) | copy-start | bytes 1376260
  153.0 6.1 %collective-permute-start.16 = (bf16[4,256,256]{2,1,0:T(8,128)(2,1)S(1)}, bf16[4,256,256]{2,1,0:T(8,128)(2,1)S(1)}, u32[]{:S(2)}, u32[]{:S(2)}) collective-permute-start(bf16[4,256,256]{2,1,0:T(8,128)(2,1)S(1)} %all_to_all.29.own_ref), channel_id=1, source_target_pairs={{0,4},{4,0},{1,5},{5,1},{2,6},{6,2},{3,7},{7,3},{8,12},{12,8},{9,1... | collective-permute-start | bytes 1572872 | tf_op jit(solution)/shard_map/ppermute | solution.py:417
  163.1 11.9 %collective-permute-start.17 = (bf16[256,448]{1,0:T(8,128)(2,1)}, bf16[256,448]{1,0:T(8,128)(2,1)S(1)}, u32[]{:S(2)}, u32[]{:S(2)}) collective-permute-start(bf16[256,448]{1,0:T(8,128)(2,1)} %get-tuple-element.49), channel_id=1, source_target_pairs={{0,1},{4,3},{8,0},{12,2},{16,5},{20,7},{24,4},{28,6},{1,9},{5,11},... | collective-permute-start | bytes 688136 | tf_op jit(solution)/shard_map/ppermute | solution.py:429
  166.4 10.0 %collective-permute-start.18 = (bf16[256,448]{1,0:T(8,128)(2,1)}, bf16[256,448]{1,0:T(8,128)(2,1)S(1)}, u32[]{:S(2)}, u32[]{:S(2)}) collective-permute-start(bf16[256,448]{1,0:T(8,128)(2,1)} %get-tuple-element.50), channel_id=1, source_target_pairs={{0,0},{4,2},{8,1},{12,3},{16,4},{20,6},{24,5},{28,7},{1,8},{5,10},... | collective-permute-start | bytes 688136 | tf_op jit(solution)/shard_map/ppermute | solution.py:429

commit v9 on v8

--- a/solution.py
+++ b/solution.py
@@ -34,7 +34,7 @@
     return pltpu.with_memory_space_constraint(x, pltpu.HBM)
 
 
-def call(kernel, out_shapes, n_smem, *args, scratch=(), free=()):
+def call(kernel, out_shapes, n_smem, *args, scratch=(), free=(), pin=True):
     def full(shape):
         zeros = (0,) * len(shape)
         return pl.BlockSpec(shape, lambda i: zeros)
@@ -42,7 +42,7 @@
     return pl.pallas_call(
         kernel,
         grid=(1,),
-        out_shape=jax.tree.map(lambda x: pltpu.HBM(x.shape, x.dtype), out_shapes),
+        out_shape=jax.tree.map(lambda x: pltpu.HBM(x.shape, x.dtype), out_shapes) if pin else out_shapes,
         in_specs=[SM] * n_smem + [full(x.shape) for x in args[n_smem:]],
         out_specs=jax.tree.map(lambda x: full(x.shape), out_shapes),
         scratch_shapes=scratch,
@@ -51,7 +51,7 @@
 
 
 def project_kernel(pos_ref, *refs):
-    blocks, mine_ref, theirs_ref, out_ref, first, second = refs[:8], refs[8], refs[9], refs[10], refs[11], refs[12]
+    blocks, mine_ref, theirs_ref, outs, (first, second, out_ref) = refs[:8], refs[8], refs[9], refs[10:15], refs[15:]
     core = pos_ref[1]
     one = jnp.where(core == 0, mine_ref[...], theirs_ref[...])
     two = jnp.where(core == 0, theirs_ref[...], mine_ref[...])
@@ -63,7 +63,7 @@
     second[64:512, 128:384] = one[:, 0:256]
     second[64:512, 384:640] = two[:, 0:256]
     for shift in range(4):
-        slot = lax.rem(pos_ref[0] + 4 - shift, 4)
+        slot = lax.rem(pos_ref[0] + 8 - shift - pos_ref[3], 4)
         for part in range(2):
             block = blocks[2 * shift + part]
             a = dot(block[:, 0:448], first[...])
@@ -72,15 +72,20 @@
             out_ref[slot, at, 0:512] = a[:, 0:512].astype(BF)
             out_ref[slot, at, 512:640] = (a[:, 512:640] + b[:, 0:128]).astype(BF)
             out_ref[slot, at, 640:1152] = b[:, 128:640].astype(BF)
-
-
-def sum_kernel(pos_ref, p_ref, own_ref, oth_ref):
+    outs[0][...] = out_ref[0]
+    outs[1][...] = out_ref[1]
+    outs[2][...] = out_ref[2, 0:128]
+    outs[3][...] = out_ref[2, 128:256]
+    outs[4][...] = out_ref[3]
+
+
+def sum_kernel(pos_ref, p0, p1, p3, top, low, own_ref, oth_ref):
     core = pos_ref[1]
 
     def total(lo, hi):
-        acc = p_ref[0, :, lo:hi].astype(F32)
-        for i in range(1, 4):
-            acc = acc + p_ref[i, :, lo:hi].astype(F32)
+        acc = jnp.concatenate([top[:, lo:hi], low[:, lo:hi]], axis=0).astype(F32)
+        for ref in (p0, p1, p3):
+            acc = acc + ref[:, lo:hi].astype(F32)
         return acc.astype(BF)
 
     keys = total(512, 640)
@@ -284,7 +289,7 @@
 
 
 def out_kernel(pos_ref, own_ref, oth_ref, *refs):
-    w0, w1, far_1, far_3, w3, first_ref, second_ref = refs
+    parts, first_ref, second_ref = refs[:8], refs[8], refs[9]
     y, core, col = pos_ref[0], pos_ref[1], pos_ref[3]
     acc = [None, None]
     for shift in range(4):
@@ -294,8 +299,7 @@
             heads = ref[j, :, 0:224]
             for e in range(2):
                 at = jnp.bitwise_xor(k, lax.rem(col, 2))
-                w = (far_1, far_3)[e][at] if shift == 2 else (w0, w1, None, w3)[shift][2 * e + at]
-                part = dot(heads, w)
+                part = dot(heads, parts[2 * shift + e][at])
                 acc[e] = part if acc[e] is None else acc[e] + part
     same = lax.rem(y, 2) == lax.div(col, 2)
     first_ref[...] = jnp.where(same, acc[0], acc[1]).astype(BF)
@@ -335,27 +339,35 @@
 
     partial = call(
         project_kernel,
-        jax.ShapeDtypeStruct((4, 256, 1152), BF),
+        [jax.ShapeDtypeStruct((n, 1152), BF) for n in (256, 256, 128, 128, 256)],
         1,
         pos,
         *blocks,
         mine,
         theirs,
-        scratch=[pltpu.VMEM((448, 640), BF), pltpu.VMEM((512, 640), BF)],
+        scratch=[pltpu.VMEM((448, 640), BF), pltpu.VMEM((512, 640), BF), pltpu.VMEM((4, 256, 1152), BF)],
         free=range(1, 11),
     )
-    partial, w_out = lax.optimization_barrier((partial, w_out))
+    here_0, to_1, to_2, to_2_low, to_3 = partial
+
+    def over_x(x, step):
+        return lax.ppermute(x, "col", [(i, (i + step) % 4) for i in range(4)])
+
+    from_1, from_3 = over_x(to_1, 1), over_x(to_3, 3)
+    half_1, half_3 = over_x(to_2, 1), over_x(to_2_low, 3)
+    half_1, half_3, w_out = lax.optimization_barrier((half_1, half_3, w_out))
+    half_1, half_3 = over_x(half_1, 1), over_x(half_3, 3)
     pieces = []
     for s in range(4):
         perm = [(k * 4 + c, (c >> 1) * 4 + (s ^ (2 * (c & 1) + k))) for k in range(2) for c in range(4)]
         pieces.append(lax.ppermute(w_out, ("core", "col"), perm))
-    pieces = jnp.stack(pieces)
-    out_1, out_3 = over_y(pieces, 1), over_y(pieces, 3)
-    partial = lax.all_to_all(partial, "col", split_axis=0, concat_axis=0, tiled=True)
+    pieces = [jnp.stack(pieces[:2]), jnp.stack(pieces[2:])]
+    out_w = [over_y(x, step) for step in (1, 3) for x in pieces]
+    partial = [here_0, from_1, from_3, half_1, half_3]
     partial, states, norms = lax.optimization_barrier((partial, states, norms))
     states = jnp.transpose(states, (2, 0, 1))
     shape = jax.ShapeDtypeStruct((512, 288), BF)
-    own, oth = call(sum_kernel, (shape, shape), 1, pos, partial, free=(1,))
+    own, oth = call(sum_kernel, (shape, shape), 1, pos, *partial, free=range(1, 6))
     rec = lax.ppermute(oth, "core", [(0, 1), (1, 0)])
 
     shape = jax.ShapeDtypeStruct((32, 16, 128), BF)
@@ -374,8 +386,8 @@
     )
     q_rec = lax.all_to_all(q_send, ("req", "col"), split_axis=0, concat_axis=0, tiled=True)
     shape = jax.ShapeDtypeStruct((2, 512, 256), F32)
-    num = call(tail_kernel, shape, 1, pos, own, rec, tail_keys, tail_values, tail_length[:, None], free=(1, 2))
-    q_rec, out_1, out_3 = lax.optimization_barrier((q_rec, out_1, out_3))
+    num = call(tail_kernel, shape, 1, pos, own, rec, tail_keys, tail_values, tail_length[:, None], free=(1, 2), pin=False)
+    q_rec, out_w = lax.optimization_barrier((q_rec, out_w))
     shape = jax.ShapeDtypeStruct((32, 16, 512), BF)
     whole = pl.BlockSpec((32, 16, 128), lambda i: (0, 0, 0))
     whole_out = pl.BlockSpec((32, 16, 512), lambda i: (0, 0, 0))
@@ -395,8 +407,8 @@
         scratch_shapes=[pltpu.VMEM((128, 128), BF)],
         compiler_params=pltpu.CompilerParams(vmem_limit_bytes=VMEM_LIMIT),
     )(pos, owner, in_hbm(q_rec), in_hbm(q_keep), in_hbm(states), in_hbm(norms))
-    r_send, near_1, near_3 = lax.optimization_barrier((r_send, out_1, out_3))
-    far_1, far_3 = over_y(near_1[:2], 1), over_y(near_3[2:], 3)
+    r_send, near_1, near_3 = lax.optimization_barrier((r_send, out_w[0], out_w[3]))
+    far_1, far_3 = over_y(near_1, 1), over_y(near_3, 3)
     r_rec = lax.all_to_all(r_send, ("req", "col"), split_axis=0, concat_axis=0, tiled=True)
     r_rec, num, far_1, far_3 = lax.optimization_barrier((r_rec, num, far_1, far_3))
     heads = call(
@@ -411,12 +423,12 @@
         r_keep,
         place[:, None],
         scratch=[pltpu.VMEM((512, 512), BF)],
-        free=(4,),
+        free=range(3, 7),
     )
     heads = lax.all_to_all(heads, "y", split_axis=0, concat_axis=0, tiled=True)
     heads_oth = lax.ppermute(heads, "core", [(0, 1), (1, 0)])
     shape = jax.ShapeDtypeStruct((256, 448), BF)
-    mixed = call(out_kernel, (shape, shape), 1, pos, heads, heads_oth, pieces, out_1, far_1, far_3, out_3, free=(1, 2))
+    mixed = call(out_kernel, (shape, shape), 1, pos, heads, heads_oth, *pieces, out_w[0], out_w[1], far_1, far_3, out_w[2], out_w[3], free=range(1, 11))
 
     def at(y, core, col):
         return (y * 2 + core) * 4 + col

time: 181 us -> 186 us (1.028)
  starting transfers between devices: 66.9 us -> 71.5 us
  other arithmetic: 4.1 us -> 6.8 us
  Pallas kernels: 35.9 us -> 33.6 us
    ppermute x0 -> x6, waiting for transfers between devices: none -> 8.7 us  [over_x(): return lax.ppermute(x, 'col', [(i, (i + step) % 4) for i in range(4)])]
    ppermute x4, waiting for transfers between devices: 14.2 us -> 6.8 us  [body(): pieces.append(lax.ppermute(w_out, ('core', 'col'), perm))]
    ppermute x0 -> x6, starting transfers between devices: none -> 6.21 us  [over_x(): return lax.ppermute(x, 'col', [(i, (i + step) % 4) for i in range(4)])]
    ppermute x4, starting transfers between devices: 14.4 us -> 8.72 us  [body(): pieces.append(lax.ppermute(w_out, ('core', 'col'), perm))]
    all_to_all x1, waiting for transfers between devices: 4.42 us -> 0.01 us  [body(): lax.all_to_all(code[:, None], ('req', 'col'), split_axis=0, concat_axis=0...]
    ppermute x10 -> x12, waiting for transfers between devices: 1.09 us -> 4.75 us  [over_y(): return lax.ppermute(x, 'y', [(i, (i + step) % 4) for i in range(4)])]
    ppermute x10 -> x12, starting transfers between devices: 11.3 us -> 15 us  [over_y(): return lax.ppermute(x, 'y', [(i, (i + step) % 4) for i in range(4)])]
    all_to_all x1 -> x0, starting transfers between devices: 3.63 us -> none  [body(): lax.all_to_all(partial, 'col', split_axis=0, concat_axis=0, tiled=True)]
  transfers between devices with their start and end apart: 23 -> 30, of which waited for: 11 -> 12; matrix products, arithmetic and copies ran while one was open for 16% -> 15% of each run, Pallas kernels for 9% -> 8%
where the time goes in v9:
time: 186 us; the launch traced here: 183 us
  starting transfers between devices  71.5 us (38%)
  Pallas kernels  33.6 us (18%)
  waiting for transfers between devices  32.3 us (17%)
  local copies, waits for them, and re-layouts  27 us (15%)
  blocking collectives  11.4 us (6%)
  other arithmetic  6.8 us (4%)
    pallas_call x6, Pallas kernels, call(): pl.pallas_call(kernel, grid=(1,), out_shape=jax.tree.map(lambda x: pltpu....  21.9 us
    ppermute x12, starting transfers between devices, over_y(): return lax.ppermute(x, 'y', [(i, (i + step) % 4) for i in range(4)])  15 us
    unnamed x27, local copies, waits for them, and re-layouts  12.9 us
    pallas_call x1, Pallas kernels, body(): pl.pallas_call(slot_kernel, grid=(4,), out_shape=(pltpu.HBM(shape.shape,...  11.7 us
    all_to_all x1, blocking collectives, body(): heads = lax.all_to_all(heads, 'y', split_axis=0, concat_axis=0, tiled=True)  11.4 us
    all_to_all x1, starting transfers between devices, body(): lax.all_to_all(code[:, None], ('req', 'col'), split_axis=0, concat_axis=0...  11 us
    ppermute x4, starting transfers between devices, body(): pieces.append(lax.ppermute(w_out, ('core', 'col'), perm))  8.72 us
    ppermute x6, waiting for transfers between devices, over_x(): return lax.ppermute(x, 'col', [(i, (i + step) % 4) for i in range(4)])  8.7 us
  transfers between devices with their start and end apart: 30, of which 12 were waited for; matrix products, arithmetic and copies ran while one was open for 15% of the time, Pallas kernels for 8%

profile of v9, /device:TPU:9, one launch (start us, length us, event | category | flops | bytes accessed | tf_op | source)
XLA Modules:
  0.0 183.0 jit_solution(16820180155400699143)
XLA Ops:
  0.0 1.1 fusion.8
  1.3 1.4 collective-permute-start.1
  3.0 1.4 collective-permute-start
  4.3 0.3 collective-permute-start.5
  4.7 0.7 fusion.7
  5.3 0.7 broadcast_compare_fusion
  6.1 0.7 copy.67
  6.8 11.0 %all-to-all-start = ((s32[32,1,1]{2,1,0:T(1,128)}), s32[32,1,1]{2,1,0:T(1,128)S(1)}, u32[]{:S(2)}, u32[]{:S(2)}) async-start(s32[32,1,1]{2,1,0:T(1,128)} %copy.67), calls=%async_computation | async-start | bytes 32768 | tf_op jit(solution)/shard_map/all_to_all | solution.py:329
  17.9 0.9 copy.74
  18.7 0.9 copy.73
  19.6 1.2 reshape.76
  21.4 2.0 %collective-permute-start.6 = (bf16[448,288]{1,0:T(8,128)(2,1)S(1)}, bf16[448,288]{1,0:T(8,128)(2,1)S(1)}, u32[]{:S(2)}, u32[]{:S(2)}) collective-permute-start(bf16[448,288]{1,0:T(8,128)(2,1)S(1)} %pad_maximum_fusion.2.refs_8_), channel_id=1, source_target_pairs={{0,4},{4,0},{1,5},{5,1},{2,6},{6,2},{3,7},{7,3},{8,12},{12,8},{9,1... | collective-permute-start | bytes 774152 | tf_op jit(solution)/shard_map/ppermute | solution.py:322
  23.5 1.0 convert_reduce_fusion
  24.5 1.4 collective-permute-start.2
  25.8 1.4 collective-permute-start.4
  27.3 1.3 multiply_add_fusion
  28.6 4.5 %collective-permute-done.2.refs_4_ = bf16[128,896]{1,0:T(8,128)(2,1)S(1)} collective-permute-done((bf16[128,896]{1,0:T(8,128)(2,1)S(1)}, bf16[128,896]{1,0:T(8,128)(2,1)S(1)}, u32[]{:S(2)}, u32[]{:S(2)}) %collective-permute-start.2) | collective-permute-done | bytes 229408 | tf_op jit(solution)/shard_map/ppermute | solution.py:314
  33.1 4.2 %shard_map.118 = (bf16[256,1152]{1,0:T(8,128)(2,1)}, bf16[256,1152]{1,0:T(8,128)(2,1)}, bf16[128,1152]{1,0:T(8,128)(2,1)}, bf16[128,1152]{1,0:T(8,128)(2,1)}, bf16[256,1152]{1,0:T(8,128)(2,1)}) custom-call(s32[4]{0:T(128)S(1)} %pad_add_fusion.pos_ref, bf16[128,896]{1,0:T(8,128)(2,1)S(1)} %copy.75.refs_0_, bf16[128,896]{1,0:T(8,128)(2,1)S(1)} %copy.76.refs_1_, ...), custom_call_target="tpu_custom_call" | custom-call | tf_op jit(solution)/shard_map/pallas_call | solution.py:42
  37.3 1.5 collective-permute-start.7
  38.8 1.2 collective-permute-start.9
  40.0 1.5 collective-permute-start.10
  41.6 7.4 %copy.77 = bf16[1,273,7168]{1,2,0:T(8,128)(2,1)} copy(bf16[1,273,7168]{2,1,0:T(8,128)(2,1)} %param.17) | data formatting | bytes 7827456 | tf_op args[5]
  49.3 0.6 pad.4.norm_ref
  49.9 0.7 add_reduce_fusion
  50.6 8.7 %collective-permute-done.9 = bf16[128,1152]{1,0:T(8,128)(2,1)} collective-permute-done((bf16[128,1152]{1,0:T(8,128)(2,1)}, bf16[128,1152]{1,0:T(8,128)(2,1)}, u32[]{:S(2)}, u32[]{:S(2)}) %collective-permute-start.9) | collective-permute-done | bytes 294944 | tf_op jit(solution)/shard_map/ppermute | solution.py:354
  59.3 1.6 collective-permute-start.15
  60.9 4.1 %collective-permute-start.14 = (bf16[224,448]{1,0:T(8,128)(2,1)}, bf16[224,448]{1,0:T(8,128)(2,1)S(1)}, u32[]{:S(2)}, u32[]{:S(2)}) collective-permute-start(bf16[224,448]{1,0:T(8,128)(2,1)} %param.16), channel_id=1, source_target_pairs={{0,0},{1,2},{2,4},{3,6},{4,1},{5,3},{6,5},{7,7},{8,8},{9,10},{10,1... | collective-permute-start | bytes 602120 | tf_op jit(solution)/shard_map/ppermute | solution.py:363
  65.1 0.8 collective-permute-done.15
  65.9 1.9 %collective-permute-start.12 = (bf16[128,1152]{1,0:T(8,128)(2,1)}, bf16[128,1152]{1,0:T(8,128)(2,1)S(1)}, u32[]{:S(2)}, u32[]{:S(2)}) collective-permute-start(bf16[128,1152]{1,0:T(8,128)(2,1)} %collective-permute-done.10), channel_id=1, source_target_pairs={{0,3},{1,0},{2,1},{3,2},{4,7},{5,4},{6,5},{7,6},{8,11},{9,8},{10,9... | collective-permute-start | bytes 884744 | tf_op jit(solution)/shard_map/ppermute | solution.py:354
  67.8 0.7 compare_reduce_fusion
  68.4 4.0 %collective-permute-done.14 = bf16[224,448]{1,0:T(8,128)(2,1)S(1)} collective-permute-done((bf16[224,448]{1,0:T(8,128)(2,1)}, bf16[224,448]{1,0:T(8,128)(2,1)S(1)}, u32[]{:S(2)}, u32[]{:S(2)}) %collective-permute-start.14) | collective-permute-done | bytes 200736 | tf_op jit(solution)/shard_map/ppermute | solution.py:363
  72.4 2.9 %collective-permute-start.18 = (bf16[224,448]{1,0:T(8,128)(2,1)}, bf16[224,448]{1,0:T(8,128)(2,1)S(1)}, u32[]{:S(2)}, u32[]{:S(2)}) collective-permute-start(bf16[224,448]{1,0:T(8,128)(2,1)} %param.16), channel_id=1, source_target_pairs={{0,3},{1,1},{2,7},{3,5},{4,2},{5,0},{6,6},{7,4},{8,11},{9,9},{10,1... | collective-permute-start | bytes 602120 | tf_op jit(solution)/shard_map/ppermute | solution.py:363
  75.6 2.0 %collective-permute-start.16 = (bf16[2,224,448]{2,1,0:T(8,128)(2,1)S(1)}, bf16[2,224,448]{2,1,0:T(8,128)(2,1)}, u32[]{:S(2)}, u32[]{:S(2)}) collective-permute-start(bf16[2,224,448]{2,1,0:T(8,128)(2,1)S(1)} %pad_maximum_fusion.refs_0_), channel_id=1, source_target_pairs={{0,8},{8,16},{16,24},{24,0},{1,9},{9,17},{17,25},{25,1},{2,10},{10... | collective-permute-start | bytes 1204232 | tf_op jit(solution)/shard_map/ppermute | solution.py:314
  77.6 1.0 collective-permute-start.20
  78.6 2.0 %shard_map.119 = (bf16[512,288]{1,0:T(8,128)(2,1)}, bf16[512,288]{1,0:T(8,128)(2,1)}) custom-call(s32[4]{0:T(128)S(1)} %pad_add_fusion.pos_ref, bf16[256,1152]{1,0:T(8,128)(2,1)S(1)} %copy-done.2, bf16[256,1152]{1,0:T(8,128)(2,1)S(1)} %collective-permute-done.7.p1, bf16[256,1152]{1,0:T(8,128)(2,1)S(1)} %collective-permute-done.8.p3, ...), custom_call_target="tpu_custom_call" | custom-call | tf_op jit(solution)/shard_map/pallas_call | solution.py:42
  80.6 0.4 collective-permute-start.13
  81.3 1.8 collective-permute-done.17
  83.1 1.9 %collective-permute-start.19 = (bf16[2,224,448]{2,1,0:T(8,128)(2,1)S(1)}, bf16[2,224,448]{2,1,0:T(8,128)(2,1)S(1)}, u32[]{:S(2)}, u32[]{:S(2)}) collective-permute-start(bf16[2,224,448]{2,1,0:T(8,128)(2,1)S(1)} %pad_maximum_fusion.1.refs_1_), channel_id=1, source_target_pairs={{0,8},{8,16},{16,24},{24,0},{1,9},{9,17},{17,25},{25,1},{2,10},{10... | collective-permute-start | bytes 1204232 | tf_op jit(solution)/shard_map/ppermute | solution.py:314
  85.0 1.1 collective-permute-start.21
  86.1 1.0 copy-done
  87.1 2.3 %shard_map.120 = (bf16[32,16,128]{2,1,0:T(8,128)(2,1)}, bf16[32,16,128]{2,1,0:T(8,128)(2,1)}) custom-call(s32[4]{0:T(128)S(1)} %pad_add_fusion.pos_ref, s32[32]{0:T(128)S(1)} %broadcast_select_fusion.2.g_ref, s32[32]{0:T(128)S(1)} %fusion.2.s_ref, bf16[512,288]{1,0:T(8,128)(2,1)S(1)} %copy-done, bf16[512,288]{1,0:T(8,128)(2,1)S(1)} %collective-permute-done.13.rec_ref, ...), custom_call_target="tpu_custom_call" | custom-call | tf_op jit(solution)/shard_map/pallas_call | solution.py:42
  89.4 7.1 %all-to-all-start.1 = ((bf16[32,16,128]{2,1,0:T(8,128)(2,1)}), bf16[32,16,128]{2,1,0:T(8,128)(2,1)S(1)}, u32[]{:S(2)}, u32[]{:S(2)}) async-start(bf16[32,16,128]{2,1,0:T(8,128)(2,1)} %get-tuple-element.54), calls=%async_computation.1 | async-start | bytes 262144 | tf_op jit(solution)/shard_map/all_to_all | solution.py:387
  96.6 8.4 %copy.78 = bf16[273,224,32]{1,0,2:T(8,128)(2,1)} copy(bf16[273,224,32]{0,2,1:T(8,128)(2,1)} %bitcast.26) | data formatting | bytes 7827456 | tf_op jit(solution)/shard_map/optimization_barrier | solution.py:367
  105.0 1.0 all-to-all-done.1.rec_ref
  106.0 0.6 copy-done.7
  106.6 11.7 %shard_map.121 = (bf16[32,16,512]{2,1,0:T(8,128)(2,1)}, bf16[32,16,512]{2,1,0:T(8,128)(2,1)}) custom-call(s32[4]{0:T(128)S(1)} %pad_add_fusion.pos_ref, s32[32]{0:T(128)S(1)} %get-tuple-element.76.owner_ref, bf16[32,16,128]{2,1,0:T(8,128)(2,1)} %copy-done.7, bf16[32,16,128]{2,1,0:T(8,128)(2,1)} %get-tuple-element.57.keep_ref, ...), custom_call_target="tpu_custom_call" | custom-call | tf_op jit(solution)/shard_map/pallas_call | solution.py:394
  118.3 8.4 %all-to-all-start.2 = ((bf16[32,16,512]{2,1,0:T(8,128)(2,1)}), bf16[32,16,512]{2,1,0:T(8,128)(2,1)S(1)}, u32[]{:S(2)}, u32[]{:S(2)}) async-start(bf16[32,16,512]{2,1,0:T(8,128)(2,1)} %get-tuple-element.63), calls=%async_computation.2 | async-start | bytes 1048576 | tf_op jit(solution)/shard_map/all_to_all | solution.py:412
  126.7 1.8 %collective-permute-start.22 = (bf16[2,224,448]{2,1,0:T(8,128)(2,1)}, bf16[2,224,448]{2,1,0:T(8,128)(2,1)}, u32[]{:S(2)}, u32[]{:S(2)}) collective-permute-start(bf16[2,224,448]{2,1,0:T(8,128)(2,1)} %collective-permute-done.16.refs_2_), channel_id=1, source_target_pairs={{0,8},{8,16},{16,24},{24,0},{1,9},{9,17},{17,25},{25,1},{2,10},{10... | collective-permute-start | bytes 1204232 | tf_op jit(solution)/shard_map/ppermute | solution.py:314
  128.5 1.1 collective-permute-start.23
  129.7 0.9 copy.79.len_ref
  130.7 7.1 %shard_map.122.num_ref = f32[2,512,256]{2,1,0:T(8,128)S(1)} custom-call(s32[4]{0:T(128)S(1)} %pad_add_fusion.pos_ref, bf16[512,288]{1,0:T(8,128)(2,1)S(1)} %copy-done.1, bf16[512,288]{1,0:T(8,128)(2,1)S(1)} %collective-permute-done.13.rec_ref, bf16[512,256]{1,0:T(8,128)(2,1)} %tk_ref.1, bf16[512,1792]{1,0:T(8,128)(2,1)} %tv_ref.1, s32[512,1]{1,0:T(8,128)} %copy.79.len_ref), custom_call_target="tpu_custom_call" | custom-call | tf_op jit(solution)/shard_map/pallas_call | solution.py:42
  138.0 3.2 %all-to-all-done.2.rec_ref = bf16[32,16,512]{2,1,0:T(8,128)(2,1)S(1)} async-done(((bf16[32,16,512]{2,1,0:T(8,128)(2,1)}), bf16[32,16,512]{2,1,0:T(8,128)(2,1)S(1)}, u32[]{:S(2)}, u32[]{:S(2)}) %all-to-all-start.2) | async-done | bytes 524320 | tf_op jit(solution)/shard_map/all_to_all | solution.py:412
  141.2 1.0 copy-done.3
  142.2 2.7 %shard_map.123 = bf16[4,256,256]{2,1,0:T(8,128)(2,1)} custom-call(s32[4]{0:T(128)S(1)} %pad_add_fusion.pos_ref, s32[32]{0:T(128)S(1)} %broadcast_select_fusion.2.g_ref, s32[32]{0:T(128)S(1)} %fusion.2.s_ref, f32[2,512,256]{2,1,0:T(8,128)S(1)} %shard_map.122.num_ref, bf16[32,16,512]{2,1,0:T(8,128)(2,1)S(1)} %all-to-all-done.2.rec_ref, ...), custom_call_target="tpu_custom_call" | custom-call | tf_op jit(solution)/shard_map/pallas_call | solution.py:42
  144.9 11.4 %all_to_all.24.own_ref = bf16[4,256,256]{2,1,0:T(8,128)(2,1)S(1)} all-to-all(bf16[4,256,256]{2,1,0:T(8,128)(2,1)} %shard_map.123), channel_id=1, replica_groups=mesh['req'=8,'y'=4,'core'=2,'col'=4] {'y'}, dimensions={0} | all-to-all | bytes 1048576 | tf_op jit(solution)/shard_map/all_to_all | solution.py:428
  156.3 6.1 %collective-permute-start.24 = (bf16[4,256,256]{2,1,0:T(8,128)(2,1)S(1)}, bf16[4,256,256]{2,1,0:T(8,128)(2,1)S(1)}, u32[]{:S(2)}, u32[]{:S(2)}) collective-permute-start(bf16[4,256,256]{2,1,0:T(8,128)(2,1)S(1)} %all_to_all.24.own_ref), channel_id=1, source_target_pairs={{0,4},{4,0},{1,5},{5,1},{2,6},{6,2},{3,7},{7,3},{8,12},{12,8},{9,1... | collective-permute-start | bytes 1572872 | tf_op jit(solution)/shard_map/ppermute | solution.py:429
  162.5 1.5 collective-permute-done.24.oth_ref
  164.0 1.0 copy-done.5
  165.0 3.6 %shard_map.124 = (bf16[256,448]{1,0:T(8,128)(2,1)}, bf16[256,448]{1,0:T(8,128)(2,1)}) custom-call(s32[4]{0:T(128)S(1)} %pad_add_fusion.pos_ref, bf16[4,256,256]{2,1,0:T(8,128)(2,1)S(1)} %all_to_all.24.own_ref, bf16[4,256,256]{2,1,0:T(8,128)(2,1)S(1)} %collective-permute-done.24.oth_ref, bf16[2,224,448]{2,1,0:T(8,128)(2,1)S(1)} %pad_maximum_fusion.refs_0_, ...), custom_call_target="tpu_custom_call" | custom-call | tf_op jit(solution)/shard_map/pallas_call | solution.py:42
  168.6 3.0 %collective-permute-start.25 = (bf16[256,448]{1,0:T(8,128)(2,1)}, bf16[256,448]{1,0:T(8,128)(2,1)S(1)}, u32[]{:S(2)}, u32[]{:S(2)}) collective-permute-start(bf16[256,448]{1,0:T(8,128)(2,1)} %get-tuple-element.73), channel_id=1, source_target_pairs={{0,1},{4,3},{8,0},{12,2},{16,5},{20,7},{24,4},{28,6},{1,9},{5,11},... | collective-permute-start | bytes 688136 | tf_op jit(solution)/shard_map/ppermute | solution.py:441
  171.6 3.7 %collective-permute-start.26 = (bf16[256,448]{1,0:T(8,128)(2,1)}, bf16[256,448]{1,0:T(8,128)(2,1)S(1)}, u32[]{:S(2)}, u32[]{:S(2)}) collective-permute-start(bf16[256,448]{1,0:T(8,128)(2,1)} %get-tuple-element.74), channel_id=1, source_target_pairs={{0,0},{4,2},{8,1},{12,3},{16,4},{20,6},{24,5},{28,7},{1,8},{5,10},... | collective-permute-start | bytes 688136 | tf_op jit(solution)/shard_map/ppermute | solution.py:441
  175.3 5.2 %collective-permute-done.25 = bf16[256,448]{1,0:T(8,128)(2,1)S(1)} collective-permute-done((bf16[256,448]{1,0:T(8,128)(2,1)}, bf16[256,448]{1,0:T(8,128)(2,1)S(1)}, u32[]{:S(2)}, u32[]{:S(2)}) %collective-permute-start.25) | collective-permute-done | bytes 229408 | tf_op jit(solution)/shard_map/ppermute | solution.py:441
  180.5 1.3 collective-permute-done.26
  182.1 0.9 fusion.1
  (64 shorter events, 3.2 us)
Async XLA Ops:
  0.0 41.4 %copy-start.11 = (s32[32]{0:T(128)S(1)}, s32[32]{0:T(128)}, u32[]{:S(2)}) copy-start(s32[32]{0:T(128)} %param.19) | copy-start | bytes 388
  1.3 27.3 %collective-permute-start.1 = (bf16[128,896]{1,0:T(8,128)(2,1)S(1)}, bf16[128,896]{1,0:T(8,128)(2,1)S(1)}, u32[]{:S(2)}, u32[]{:S(2)}) collective-permute-start(bf16[128,896]{1,0:T(8,128)(2,1)S(1)} %copy.76.refs_1_), channel_id=1, source_target_pairs={{0,8},{8,16},{16,24},{24,0},{1,9},{9,17},{17,25},{25,1},{2,10},{10... | collective-permute-start | bytes 688136 | tf_op jit(solution)/shard_map/ppermute | solution.py:314
  2.6 23.2 %collective-permute-start.3 = (bf16[128,896]{1,0:T(8,128)(2,1)S(1)}, bf16[128,896]{1,0:T(8,128)(2,1)S(1)}, u32[]{:S(2)}, u32[]{:S(2)}) collective-permute-start(bf16[128,896]{1,0:T(8,128)(2,1)S(1)} %copy.76.refs_1_), channel_id=1, source_target_pairs={{0,24},{8,0},{16,8},{24,16},{1,25},{9,1},{17,9},{25,17},{2,26},{10... | collective-permute-start | bytes 688136 | tf_op jit(solution)/shard_map/ppermute | solution.py:314
  3.0 21.5 %collective-permute-start = (bf16[128,896]{1,0:T(8,128)(2,1)S(1)}, bf16[128,896]{1,0:T(8,128)(2,1)S(1)}, u32[]{:S(2)}, u32[]{:S(2)}) collective-permute-start(bf16[128,896]{1,0:T(8,128)(2,1)S(1)} %copy.75.refs_0_), channel_id=1, source_target_pairs={{0,8},{8,16},{16,24},{24,0},{1,9},{9,17},{17,25},{25,1},{2,10},{10... | collective-permute-start | bytes 688136 | tf_op jit(solution)/shard_map/ppermute | solution.py:314
  4.3 24.3 %collective-permute-start.5 = (bf16[128,896]{1,0:T(8,128)(2,1)S(1)}, bf16[128,896]{1,0:T(8,128)(2,1)S(1)}, u32[]{:S(2)}, u32[]{:S(2)}) collective-permute-start(bf16[128,896]{1,0:T(8,128)(2,1)S(1)} %copy.75.refs_0_), channel_id=1, source_target_pairs={{0,24},{8,0},{16,8},{24,16},{1,25},{9,1},{17,9},{25,17},{2,26},{10... | collective-permute-start | bytes 688136 | tf_op jit(solution)/shard_map/ppermute | solution.py:314
  6.8 43.1 %all-to-all-start = ((s32[32,1,1]{2,1,0:T(1,128)}), s32[32,1,1]{2,1,0:T(1,128)S(1)}, u32[]{:S(2)}, u32[]{:S(2)}) async-start(s32[32,1,1]{2,1,0:T(1,128)} %copy.67), calls=%async_computation | async-start | bytes 32768 | tf_op jit(solution)/shard_map/all_to_all | solution.py:329
  21.4 7.2 %collective-permute-start.6 = (bf16[448,288]{1,0:T(8,128)(2,1)S(1)}, bf16[448,288]{1,0:T(8,128)(2,1)S(1)}, u32[]{:S(2)}, u32[]{:S(2)}) collective-permute-start(bf16[448,288]{1,0:T(8,128)(2,1)S(1)} %pad_maximum_fusion.2.refs_8_), channel_id=1, source_target_pairs={{0,4},{4,0},{1,5},{5,1},{2,6},{6,2},{3,7},{7,3},{8,12},{12,8},{9,1... | collective-permute-start | bytes 774152 | tf_op jit(solution)/shard_map/ppermute | solution.py:322
  24.5 8.6 %collective-permute-start.2 = (bf16[128,896]{1,0:T(8,128)(2,1)S(1)}, bf16[128,896]{1,0:T(8,128)(2,1)S(1)}, u32[]{:S(2)}, u32[]{:S(2)}) collective-permute-start(bf16[128,896]{1,0:T(8,128)(2,1)S(1)} %collective-permute-done.refs_2_), channel_id=1, source_target_pairs={{0,8},{8,16},{16,24},{24,0},{1,9},{9,17},{17,25},{25,1},{2,10},{10... | collective-permute-start | bytes 688136 | tf_op jit(solution)/shard_map/ppermute | solution.py:314
  25.8 7.2 %collective-permute-start.4 = (bf16[128,896]{1,0:T(8,128)(2,1)S(1)}, bf16[128,896]{1,0:T(8,128)(2,1)S(1)}, u32[]{:S(2)}, u32[]{:S(2)}) collective-permute-start(bf16[128,896]{1,0:T(8,128)(2,1)S(1)} %collective-permute-done.3.refs_7_), channel_id=1, source_target_pairs={{0,24},{8,0},{16,8},{24,16},{1,25},{9,1},{17,9},{25,17},{2,26},{10... | collective-permute-start | bytes 688136 | tf_op jit(solution)/shard_map/ppermute | solution.py:314
  37.3 38.1 %collective-permute-start.7 = (bf16[256,1152]{1,0:T(8,128)(2,1)}, bf16[256,1152]{1,0:T(8,128)(2,1)S(1)}, u32[]{:S(2)}, u32[]{:S(2)}) collective-permute-start(bf16[256,1152]{1,0:T(8,128)(2,1)} %get-tuple-element.41), channel_id=1, source_target_pairs={{0,1},{1,2},{2,3},{3,0},{4,5},{5,6},{6,7},{7,4},{8,9},{9,10},{10,1... | collective-permute-start | bytes 1769480 | tf_op jit(solution)/shard_map/ppermute | solution.py:354
  38.8 20.5 %collective-permute-start.9 = (bf16[128,1152]{1,0:T(8,128)(2,1)}, bf16[128,1152]{1,0:T(8,128)(2,1)}, u32[]{:S(2)}, u32[]{:S(2)}) collective-permute-start(bf16[128,1152]{1,0:T(8,128)(2,1)} %get-tuple-element.43), channel_id=1, source_target_pairs={{0,1},{1,2},{2,3},{3,0},{4,5},{5,6},{6,7},{7,4},{8,9},{9,10},{10,1... | collective-permute-start | bytes 884744 | tf_op jit(solution)/shard_map/ppermute | solution.py:354
  40.0 19.3 %collective-permute-start.10 = (bf16[128,1152]{1,0:T(8,128)(2,1)}, bf16[128,1152]{1,0:T(8,128)(2,1)}, u32[]{:S(2)}, u32[]{:S(2)}) collective-permute-start(bf16[128,1152]{1,0:T(8,128)(2,1)} %get-tuple-element.44), channel_id=1, source_target_pairs={{0,3},{1,0},{2,1},{3,2},{4,7},{5,4},{6,5},{7,6},{8,11},{9,8},{10,9... | collective-permute-start | bytes 884744 | tf_op jit(solution)/shard_map/ppermute | solution.py:354
  41.6 7.6 %copy-start.8 = (bf16[32,273,2]{1,2,0:T(2,128)(2,1)S(1)}, bf16[32,273,2]{1,2,0:T(2,128)(2,1)}, u32[]{:S(2)}) copy-start(bf16[32,273,2]{1,2,0:T(2,128)(2,1)} %param.18) | copy-start | bytes 104836
  41.6 37.0 %copy-start.2 = (bf16[256,1152]{1,0:T(8,128)(2,1)S(1)}, bf16[256,1152]{1,0:T(8,128)(2,1)}, u32[]{:S(2)}) copy-start(bf16[256,1152]{1,0:T(8,128)(2,1)} %get-tuple-element.47.p0) | copy-start | bytes 1769476
  49.9 25.7 %collective-permute-start.8 = (bf16[256,1152]{1,0:T(8,128)(2,1)}, bf16[256,1152]{1,0:T(8,128)(2,1)S(1)}, u32[]{:S(2)}, u32[]{:S(2)}) collective-permute-start(bf16[256,1152]{1,0:T(8,128)(2,1)} %get-tuple-element.42), channel_id=1, source_target_pairs={{0,3},{1,0},{2,1},{3,2},{4,7},{5,4},{6,5},{7,6},{8,11},{9,8},{10,9... | collective-permute-start | bytes 1769480 | tf_op jit(solution)/shard_map/ppermute | solution.py:354
  59.3 6.6 %collective-permute-start.15 = (bf16[224,448]{1,0:T(8,128)(2,1)}, bf16[224,448]{1,0:T(8,128)(2,1)S(1)}, u32[]{:S(2)}, u32[]{:S(2)}) collective-permute-start(bf16[224,448]{1,0:T(8,128)(2,1)} %param.16), channel_id=1, source_target_pairs={{0,1},{1,3},{2,5},{3,7},{4,0},{5,2},{6,4},{7,6},{8,9},{9,11},{10,1... | collective-permute-start | bytes 602120 | tf_op jit(solution)/shard_map/ppermute | solution.py:363
  60.9 11.5 %collective-permute-start.14 = (bf16[224,448]{1,0:T(8,128)(2,1)}, bf16[224,448]{1,0:T(8,128)(2,1)S(1)}, u32[]{:S(2)}, u32[]{:S(2)}) collective-permute-start(bf16[224,448]{1,0:T(8,128)(2,1)} %param.16), channel_id=1, source_target_pairs={{0,0},{1,2},{2,4},{3,6},{4,1},{5,3},{6,5},{7,7},{8,8},{9,10},{10,1... | collective-permute-start | bytes 602120 | tf_op jit(solution)/shard_map/ppermute | solution.py:363
  65.0 12.6 %collective-permute-start.11 = (bf16[128,1152]{1,0:T(8,128)(2,1)}, bf16[128,1152]{1,0:T(8,128)(2,1)S(1)}, u32[]{:S(2)}, u32[]{:S(2)}) collective-permute-start(bf16[128,1152]{1,0:T(8,128)(2,1)} %collective-permute-done.9), channel_id=1, source_target_pairs={{0,1},{1,2},{2,3},{3,0},{4,5},{5,6},{6,7},{7,4},{8,9},{9,10},{10,1... | collective-permute-start | bytes 884744 | tf_op jit(solution)/shard_map/ppermute | solution.py:354
  65.9 12.7 %collective-permute-start.12 = (bf16[128,1152]{1,0:T(8,128)(2,1)}, bf16[128,1152]{1,0:T(8,128)(2,1)S(1)}, u32[]{:S(2)}, u32[]{:S(2)}) collective-permute-start(bf16[128,1152]{1,0:T(8,128)(2,1)} %collective-permute-done.10), channel_id=1, source_target_pairs={{0,3},{1,0},{2,1},{3,2},{4,7},{5,4},{6,5},{7,6},{8,11},{9,8},{10,9... | collective-permute-start | bytes 884744 | tf_op jit(solution)/shard_map/ppermute | solution.py:354
  72.4 8.9 %collective-permute-start.18 = (bf16[224,448]{1,0:T(8,128)(2,1)}, bf16[224,448]{1,0:T(8,128)(2,1)S(1)}, u32[]{:S(2)}, u32[]{:S(2)}) collective-permute-start(bf16[224,448]{1,0:T(8,128)(2,1)} %param.16), channel_id=1, source_target_pairs={{0,3},{1,1},{2,7},{3,5},{4,2},{5,0},{6,6},{7,4},{8,11},{9,9},{10,1... | collective-permute-start | bytes 602120 | tf_op jit(solution)/shard_map/ppermute | solution.py:363
  75.3 7.7 %collective-permute-start.17 = (bf16[224,448]{1,0:T(8,128)(2,1)}, bf16[224,448]{1,0:T(8,128)(2,1)S(1)}, u32[]{:S(2)}, u32[]{:S(2)}) collective-permute-start(bf16[224,448]{1,0:T(8,128)(2,1)} %param.16), channel_id=1, source_target_pairs={{0,2},{1,0},{2,6},{3,4},{4,3},{5,1},{6,7},{7,5},{8,10},{9,8},{10,1... | collective-permute-start | bytes 602120 | tf_op jit(solution)/shard_map/ppermute | solution.py:363
  75.6 29.3 %collective-permute-start.16 = (bf16[2,224,448]{2,1,0:T(8,128)(2,1)S(1)}, bf16[2,224,448]{2,1,0:T(8,128)(2,1)}, u32[]{:S(2)}, u32[]{:S(2)}) collective-permute-start(bf16[2,224,448]{2,1,0:T(8,128)(2,1)S(1)} %pad_maximum_fusion.refs_0_), channel_id=1, source_target_pairs={{0,8},{8,16},{16,24},{24,0},{1,9},{9,17},{17,25},{25,1},{2,10},{10... | collective-permute-start | bytes 1204232 | tf_op jit(solution)/shard_map/ppermute | solution.py:314
  77.6 27.4 %collective-permute-start.20 = (bf16[2,224,448]{2,1,0:T(8,128)(2,1)S(1)}, bf16[2,224,448]{2,1,0:T(8,128)(2,1)}, u32[]{:S(2)}, u32[]{:S(2)}) collective-permute-start(bf16[2,224,448]{2,1,0:T(8,128)(2,1)S(1)} %pad_maximum_fusion.refs_0_), channel_id=1, source_target_pairs={{0,24},{8,0},{16,8},{24,16},{1,25},{9,1},{17,9},{25,17},{2,26},{10... | collective-permute-start | bytes 1204232 | tf_op jit(solution)/shard_map/ppermute | solution.py:314
  80.6 5.5 %collective-permute-start.13 = (bf16[512,288]{1,0:T(8,128)(2,1)}, bf16[512,288]{1,0:T(8,128)(2,1)S(1)}, u32[]{:S(2)}, u32[]{:S(2)}) collective-permute-start(bf16[512,288]{1,0:T(8,128)(2,1)} %get-tuple-element.53), channel_id=1, source_target_pairs={{0,4},{4,0},{1,5},{5,1},{2,6},{6,2},{3,7},{7,3},{8,12},{12,8},{9,1... | collective-permute-start | bytes 884744 | tf_op jit(solution)/shard_map/ppermute | solution.py:371
  83.1 21.9 %collective-permute-start.19 = (bf16[2,224,448]{2,1,0:T(8,128)(2,1)S(1)}, bf16[2,224,448]{2,1,0:T(8,128)(2,1)S(1)}, u32[]{:S(2)}, u32[]{:S(2)}) collective-permute-start(bf16[2,224,448]{2,1,0:T(8,128)(2,1)S(1)} %pad_maximum_fusion.1.refs_1_), channel_id=1, source_target_pairs={{0,8},{8,16},{16,24},{24,0},{1,9},{9,17},{17,25},{25,1},{2,10},{10... | collective-permute-start | bytes 1204232 | tf_op jit(solution)/shard_map/ppermute | solution.py:314
  85.0 19.9 %collective-permute-start.21 = (bf16[2,224,448]{2,1,0:T(8,128)(2,1)S(1)}, bf16[2,224,448]{2,1,0:T(8,128)(2,1)}, u32[]{:S(2)}, u32[]{:S(2)}) collective-permute-start(bf16[2,224,448]{2,1,0:T(8,128)(2,1)S(1)} %pad_maximum_fusion.1.refs_1_), channel_id=1, source_target_pairs={{0,24},{8,0},{16,8},{24,16},{1,25},{9,1},{17,9},{25,17},{2,26},{10... | collective-permute-start | bytes 1204232 | tf_op jit(solution)/shard_map/ppermute | solution.py:314
  86.1 1.0 copy-start
  89.4 16.5 %all-to-all-start.1 = ((bf16[32,16,128]{2,1,0:T(8,128)(2,1)}), bf16[32,16,128]{2,1,0:T(8,128)(2,1)S(1)}, u32[]{:S(2)}, u32[]{:S(2)}) async-start(bf16[32,16,128]{2,1,0:T(8,128)(2,1)} %get-tuple-element.54), calls=%async_computation.1 | async-start | bytes 262144 | tf_op jit(solution)/shard_map/all_to_all | solution.py:387
  104.9 24.7 %copy-start.10 = (s32[512]{0:T(512)S(1)}, s32[512]{0:T(512)}, u32[]{:S(2)}) copy-start(s32[512]{0:T(512)} %param.23) | copy-start | bytes 6148
  104.9 25.6 %copy-start.9 = (s32[512]{0:T(512)S(1)}, s32[512]{0:T(512)}, u32[]{:S(2)}) copy-start(s32[512]{0:T(512)} %multiply_add_fusion) | copy-start | bytes 6148
  104.9 25.7 %copy-start.1 = (bf16[512,288]{1,0:T(8,128)(2,1)S(1)}, bf16[512,288]{1,0:T(8,128)(2,1)}, u32[]{:S(2)}) copy-start(bf16[512,288]{1,0:T(8,128)(2,1)} %get-tuple-element.52.own_ref) | copy-start | bytes 884740
  105.0 25.5 %copy-start.4 = (bf16[2,224,448]{2,1,0:T(8,128)(2,1)}, bf16[2,224,448]{2,1,0:T(8,128)(2,1)S(1)}, u32[]{:S(2)}) copy-start(bf16[2,224,448]{2,1,0:T(8,128)(2,1)S(1)} %collective-permute-done.19.refs_3_) | copy-start | bytes 1204228
  106.0 0.6 copy-start.7
  118.3 22.8 %all-to-all-start.2 = ((bf16[32,16,512]{2,1,0:T(8,128)(2,1)}), bf16[32,16,512]{2,1,0:T(8,128)(2,1)S(1)}, u32[]{:S(2)}, u32[]{:S(2)}) async-start(bf16[32,16,512]{2,1,0:T(8,128)(2,1)} %get-tuple-element.63), calls=%async_computation.2 | async-start | bytes 1048576 | tf_op jit(solution)/shard_map/all_to_all | solution.py:412
  126.7 11.3 %collective-permute-start.22 = (bf16[2,224,448]{2,1,0:T(8,128)(2,1)}, bf16[2,224,448]{2,1,0:T(8,128)(2,1)}, u32[]{:S(2)}, u32[]{:S(2)}) collective-permute-start(bf16[2,224,448]{2,1,0:T(8,128)(2,1)} %collective-permute-done.16.refs_2_), channel_id=1, source_target_pairs={{0,8},{8,16},{16,24},{24,0},{1,9},{9,17},{17,25},{25,1},{2,10},{10... | collective-permute-start | bytes 1204232 | tf_op jit(solution)/shard_map/ppermute | solution.py:314
  128.5 9.5 %collective-permute-start.23 = (bf16[2,224,448]{2,1,0:T(8,128)(2,1)}, bf16[2,224,448]{2,1,0:T(8,128)(2,1)}, u32[]{:S(2)}, u32[]{:S(2)}) collective-permute-start(bf16[2,224,448]{2,1,0:T(8,128)(2,1)} %collective-permute-done.21.refs_7_), channel_id=1, source_target_pairs={{0,24},{8,0},{16,8},{24,16},{1,25},{9,1},{17,9},{25,17},{2,26},{10... | collective-permute-start | bytes 1204232 | tf_op jit(solution)/shard_map/ppermute | solution.py:314
  141.2 1.0 copy-start.3
  144.9 37.2 %copy-start.6 = (bf16[256,2,448]{0,2,1:T(8,128)(2,1)S(1)}, bf16[256,2,448]{0,2,1:T(8,128)(2,1)}, u32[]{:S(2)}) copy-start(bf16[256,2,448]{0,2,1:T(8,128)(2,1)} %param.12) | copy-start | bytes 1376260
  156.3 7.7 %collective-permute-start.24 = (bf16[4,256,256]{2,1,0:T(8,128)(2,1)S(1)}, bf16[4,256,256]{2,1,0:T(8,128)(2,1)S(1)}, u32[]{:S(2)}, u32[]{:S(2)}) collective-permute-start(bf16[4,256,256]{2,1,0:T(8,128)(2,1)S(1)} %all_to_all.24.own_ref), channel_id=1, source_target_pairs={{0,4},{4,0},{1,5},{5,1},{2,6},{6,2},{3,7},{7,3},{8,12},{12,8},{9,1... | collective-permute-start | bytes 1572872 | tf_op jit(solution)/shard_map/ppermute | solution.py:429
  164.0 1.0 copy-start.5
  168.6 11.8 %collective-permute-start.25 = (bf16[256,448]{1,0:T(8,128)(2,1)}, bf16[256,448]{1,0:T(8,128)(2,1)S(1)}, u32[]{:S(2)}, u32[]{:S(2)}) collective-permute-start(bf16[256,448]{1,0:T(8,128)(2,1)} %get-tuple-element.73), channel_id=1, source_target_pairs={{0,1},{4,3},{8,0},{12,2},{16,5},{20,7},{24,4},{28,6},{1,9},{5,11},... | collective-permute-start | bytes 688136 | tf_op jit(solution)/shard_map/ppermute | solution.py:441
  171.6 10.1 %collective-permute-start.26 = (bf16[256,448]{1,0:T(8,128)(2,1)}, bf16[256,448]{1,0:T(8,128)(2,1)S(1)}, u32[]{:S(2)}, u32[]{:S(2)}) collective-permute-start(bf16[256,448]{1,0:T(8,128)(2,1)} %get-tuple-element.74), channel_id=1, source_target_pairs={{0,0},{4,2},{8,1},{12,3},{16,4},{20,6},{24,5},{28,7},{1,8},{5,10},... | collective-permute-start | bytes 688136 | tf_op jit(solution)/shard_map/ppermute | solution.py:441

commit v10 on v8

--- a/solution.py
+++ b/solution.py
@@ -34,7 +34,7 @@
     return pltpu.with_memory_space_constraint(x, pltpu.HBM)
 
 
-def call(kernel, out_shapes, n_smem, *args, scratch=(), free=()):
+def call(kernel, out_shapes, n_smem, *args, scratch=(), free=(), pin=True):
     def full(shape):
         zeros = (0,) * len(shape)
         return pl.BlockSpec(shape, lambda i: zeros)
@@ -42,7 +42,7 @@
     return pl.pallas_call(
         kernel,
         grid=(1,),
-        out_shape=jax.tree.map(lambda x: pltpu.HBM(x.shape, x.dtype), out_shapes),
+        out_shape=jax.tree.map(lambda x: pltpu.HBM(x.shape, x.dtype), out_shapes) if pin else out_shapes,
         in_specs=[SM] * n_smem + [full(x.shape) for x in args[n_smem:]],
         out_specs=jax.tree.map(lambda x: full(x.shape), out_shapes),
         scratch_shapes=scratch,
@@ -312,10 +312,16 @@
     top, low = tokens[:128].reshape(128, 896), tokens[128:].reshape(128, 896)
     top_1, low_3 = over_y(top, 1), over_y(low, 3)
     low_1, top_3 = over_y(low, 1), over_y(top, 3)
+    top_1, low_3, w_out = lax.optimization_barrier((top_1, low_3, w_out))
     blocks = [top, low, top_1, low_1, over_y(top_1, 1), over_y(low_3, 3), top_3, low_3]
     value_w = jnp.moveaxis(w_value.reshape(2, 448, 112), 0, 1).reshape(448, 224)
     mine = jnp.concatenate([value_w, w_query, w_key], axis=1)
     theirs = lax.ppermute(mine, "core", [(0, 1), (1, 0)])
+    pieces = []
+    for s in range(4):
+        perm = [(k * 4 + c, (c >> 1) * 4 + (s ^ (2 * (c & 1) + k))) for k in range(2) for c in range(4)]
+        pieces.append(lax.ppermute(w_out, ("core", "col"), perm))
+    mine, pieces = lax.optimization_barrier((mine, pieces))
     owner = slot_prompt // 32
     slots = jnp.arange(32, dtype=jnp.int32)
     away = owner != me
@@ -344,11 +350,7 @@
         scratch=[pltpu.VMEM((448, 640), BF), pltpu.VMEM((512, 640), BF)],
         free=range(1, 11),
     )
-    partial, w_out = lax.optimization_barrier((partial, w_out))
-    pieces = []
-    for s in range(4):
-        perm = [(k * 4 + c, (c >> 1) * 4 + (s ^ (2 * (c & 1) + k))) for k in range(2) for c in range(4)]
-        pieces.append(lax.ppermute(w_out, ("core", "col"), perm))
+    partial, pieces = lax.optimization_barrier((partial, pieces))
     pieces = jnp.stack(pieces)
     out_1, out_3 = over_y(pieces, 1), over_y(pieces, 3)
     partial = lax.all_to_all(partial, "col", split_axis=0, concat_axis=0, tiled=True)
@@ -374,7 +376,7 @@
     )
     q_rec = lax.all_to_all(q_send, ("req", "col"), split_axis=0, concat_axis=0, tiled=True)
     shape = jax.ShapeDtypeStruct((2, 512, 256), F32)
-    num = call(tail_kernel, shape, 1, pos, own, rec, tail_keys, tail_values, tail_length[:, None], free=(1, 2))
+    num = call(tail_kernel, shape, 1, pos, own, rec, tail_keys, tail_values, tail_length[:, None], free=(1, 2), pin=False)
     q_rec, out_1, out_3 = lax.optimization_barrier((q_rec, out_1, out_3))
     shape = jax.ShapeDtypeStruct((32, 16, 512), BF)
     whole = pl.BlockSpec((32, 16, 128), lambda i: (0, 0, 0))
@@ -411,12 +413,12 @@
         r_keep,
         place[:, None],
         scratch=[pltpu.VMEM((512, 512), BF)],
-        free=(4,),
+        free=range(3, 7),
     )
     heads = lax.all_to_all(heads, "y", split_axis=0, concat_axis=0, tiled=True)
     heads_oth = lax.ppermute(heads, "core", [(0, 1), (1, 0)])
     shape = jax.ShapeDtypeStruct((256, 448), BF)
-    mixed = call(out_kernel, (shape, shape), 1, pos, heads, heads_oth, pieces, out_1, far_1, far_3, out_3, free=(1, 2))
+    mixed = call(out_kernel, (shape, shape), 1, pos, heads, heads_oth, pieces, out_1, far_1, far_3, out_3, free=range(1, 8))
 
     def at(y, core, col):
         return (y * 2 + core) * 4 + col

time: 181 us -> 183 us (1.011)
  waiting for transfers between devices: 30.6 us -> 36.2 us
  starting transfers between devices: 66.9 us -> 63 us
  Pallas kernels: 35.9 us -> 33.7 us
  local copies, waits for them, and re-layouts: 27.8 us -> 29.7 us
    all_to_all x1, waiting for transfers between devices: 0.01 us -> 12.5 us  [body(): lax.all_to_all(partial, 'col', split_axis=0, concat_axis=0, tiled=True)]
    ppermute x4, waiting for transfers between devices: 14.2 us -> 5.69 us  [body(): pieces.append(lax.ppermute(w_out, ('core', 'col'), perm))]
    ppermute x4, starting transfers between devices: 14.4 us -> 10.7 us  [body(): pieces.append(lax.ppermute(w_out, ('core', 'col'), perm))]
    ppermute x1, starting transfers between devices: 3.19 us -> 0.01 us  [body(): theirs = lax.ppermute(mine, 'core', [(0, 1), (1, 0)])]
    ppermute x1, starting transfers between devices: 0.01 us -> 2.72 us  [body(): rec = lax.ppermute(oth, 'core', [(0, 1), (1, 0)])]
    pallas_call x6, Pallas kernels: 24.1 us -> 21.8 us  [call(): pl.pallas_call(kernel, grid=(1,), out_shape=jax.tree.map(lambda x: pltpu....]
    unnamed x29 -> x25, local copies, waits for them, and re-layouts: 10.9 us -> 11.9 us
  transfers between devices with their start and end apart: 23 -> 23, of which waited for: 11 -> 14; matrix products, arithmetic and copies ran while one was open for 16% -> 16% of each run, Pallas kernels for 9% -> 8%
where the time goes in v10:
time: 183 us; the launch traced here: 180 us
  starting transfers between devices  63 us (34%)
  waiting for transfers between devices  36.2 us (20%)
  Pallas kernels  33.7 us (18%)
  local copies, waits for them, and re-layouts  29.7 us (16%)
  blocking collectives  12.1 us (7%)
  other arithmetic  5.29 us (3%)
    pallas_call x6, Pallas kernels, call(): pl.pallas_call(kernel, grid=(1,), out_shape=jax.tree.map(lambda x: pltpu....  21.8 us
    all_to_all x1, waiting for transfers between devices, body(): lax.all_to_all(partial, 'col', split_axis=0, concat_axis=0, tiled=True)  12.5 us
    all_to_all x1, starting transfers between devices, body(): lax.all_to_all(code[:, None], ('req', 'col'), split_axis=0, concat_axis=0...  12.3 us
    all_to_all x1, blocking collectives, body(): heads = lax.all_to_all(heads, 'y', split_axis=0, concat_axis=0, tiled=True)  12.1 us
    pallas_call x1, Pallas kernels, body(): pl.pallas_call(slot_kernel, grid=(4,), out_shape=(pltpu.HBM(shape.shape,...  11.9 us
    unnamed x25, local copies, waits for them, and re-layouts  11.9 us
    ppermute x4, starting transfers between devices, body(): pieces.append(lax.ppermute(w_out, ('core', 'col'), perm))  10.7 us
    ppermute x10, starting transfers between devices, over_y(): return lax.ppermute(x, 'y', [(i, (i + step) % 4) for i in range(4)])  10.7 us
  transfers between devices with their start and end apart: 23, of which 14 were waited for; matrix products, arithmetic and copies ran while one was open for 16% of the time, Pallas kernels for 8%

profile of v10, /device:TPU:9, one launch (start us, length us, event | category | flops | bytes accessed | tf_op | source)
XLA Modules:
  0.0 180.2 jit_solution(7297421534875074919)
XLA Ops:
  0.0 1.1 fusion.8
  1.3 1.4 collective-permute-start
  2.8 0.2 collective-permute-start.1
  3.1 1.3 collective-permute-start.2
  4.4 1.2 reshape.76
  5.6 0.2 copy.84
  6.0 0.9 copy.73
  6.9 0.9 copy.74
  8.0 1.1 collective-permute-done.1.refs_7_
  9.1 4.9 %collective-permute-start.6 = (bf16[224,448]{1,0:T(8,128)(2,1)S(1)}, bf16[224,448]{1,0:T(8,128)(2,1)S(1)}, u32[]{:S(2)}, u32[]{:S(2)}) collective-permute-start(bf16[224,448]{1,0:T(8,128)(2,1)S(1)} %copy-done.10), channel_id=1, source_target_pairs={{0,0},{1,2},{2,4},{3,6},{4,1},{5,3},{6,5},{7,7},{8,8},{9,10},{10,1... | collective-permute-start | bytes 602120 | tf_op jit(solution)/shard_map/ppermute | solution.py:323
  14.0 1.4 collective-permute-start.8
  15.4 4.4 %collective-permute-start.9 = (bf16[224,448]{1,0:T(8,128)(2,1)S(1)}, bf16[224,448]{1,0:T(8,128)(2,1)}, u32[]{:S(2)}, u32[]{:S(2)}) collective-permute-start(bf16[224,448]{1,0:T(8,128)(2,1)S(1)} %copy-done.10), channel_id=1, source_target_pairs={{0,3},{1,1},{2,7},{3,5},{4,2},{5,0},{6,6},{7,4},{8,11},{9,9},{10,1... | collective-permute-start | bytes 602120 | tf_op jit(solution)/shard_map/ppermute | solution.py:323
  19.9 0.6 collective-permute-done.6
  20.4 1.0 collective-permute-start.5
  21.4 0.4 collective-permute-done.7
  21.8 4.7 %collective-permute-done.8 = bf16[224,448]{1,0:T(8,128)(2,1)} collective-permute-done((bf16[224,448]{1,0:T(8,128)(2,1)S(1)}, bf16[224,448]{1,0:T(8,128)(2,1)}, u32[]{:S(2)}, u32[]{:S(2)}) %collective-permute-start.8) | collective-permute-done | bytes 200736 | tf_op jit(solution)/shard_map/ppermute | solution.py:323
  26.5 1.0 collective-permute-start.3
  27.5 0.5 collective-permute-start.4
  28.1 0.7 copy.67
  28.8 12.3 %all-to-all-start = ((s32[32,1,1]{2,1,0:T(1,128)}), s32[32,1,1]{2,1,0:T(1,128)S(1)}, u32[]{:S(2)}, u32[]{:S(2)}) async-start(s32[32,1,1]{2,1,0:T(1,128)} %copy.67), calls=%async_computation | async-start | bytes 32768 | tf_op jit(solution)/shard_map/all_to_all | solution.py:331
  41.3 4.0 %shard_map.118 = bf16[4,256,1152]{2,1,0:T(8,128)(2,1)} custom-call(s32[4]{0:T(128)S(1)} %pad_add_fusion.pos_ref, bf16[128,896]{1,0:T(8,128)(2,1)S(1)} %copy.75.refs_0_, bf16[128,896]{1,0:T(8,128)(2,1)S(1)} %copy.76.refs_1_, bf16[128,896]{1,0:T(8,128)(2,1)S(1)} %collective-permute-done.refs_2_, bf16[128,896]{1,0:T(8,128)(2,1)S(1)} %collective-permute-done.2.refs_3_, ...), custom_call_target="tpu_custom_call" | custom-call | tf_op jit(solution)/shard_map/pallas_call | solution.py:42
  45.2 4.4 %all-to-all-done = s32[32,1,1]{2,1,0:T(1,128)S(1)} async-done(((s32[32,1,1]{2,1,0:T(1,128)}), s32[32,1,1]{2,1,0:T(1,128)S(1)}, u32[]{:S(2)}, u32[]{:S(2)}) %all-to-all-start) | async-done | bytes 160 | tf_op jit(solution)/shard_map/all_to_all | solution.py:331
  49.6 3.8 %all-to-all-start.1 = ((bf16[4,256,1152]{2,1,0:T(8,128)(2,1)}), bf16[4,256,1152]{2,1,0:T(8,128)(2,1)S(1)}, u32[]{:S(2)}, u32[]{:S(2)}) async-start(bf16[4,256,1152]{2,1,0:T(8,128)(2,1)} %shard_map.118), calls=%async_computation.1 | async-start | bytes 4718592 | tf_op jit(solution)/shard_map/all_to_all | solution.py:356
  53.5 7.3 %copy.77 = bf16[1,273,7168]{1,2,0:T(8,128)(2,1)} copy(bf16[1,273,7168]{2,1,0:T(8,128)(2,1)} %param.17) | data formatting | bytes 7827456 | tf_op args[5]
  60.9 0.6 pad.4.norm_ref
  61.5 0.2 compare_reduce_fusion.1
  61.7 0.2 fusion.2.s_ref
  61.9 0.2 convert_reduce_fusion
  62.1 0.6 multiply_add_fusion
  62.7 0.7 add_reduce_fusion
  63.4 0.7 compare_reduce_fusion
  64.1 1.3 pad_maximum_fusion.refs_0_
  65.5 2.7 %collective-permute-start.13 = (bf16[4,224,448]{2,1,0:T(8,128)(2,1)S(1)}, bf16[4,224,448]{2,1,0:T(8,128)(2,1)}, u32[]{:S(2)}, u32[]{:S(2)}) collective-permute-start(bf16[4,224,448]{2,1,0:T(8,128)(2,1)S(1)} %pad_maximum_fusion.refs_0_), channel_id=1, source_target_pairs={{0,24},{8,0},{16,8},{24,16},{1,25},{9,1},{17,9},{25,17},{2,26},{10... | collective-permute-start | bytes 2408456 | tf_op jit(solution)/shard_map/ppermute | solution.py:310
  68.1 12.5 %all-to-all-done.1.p_ref = bf16[4,256,1152]{2,1,0:T(8,128)(2,1)S(1)} async-done(((bf16[4,256,1152]{2,1,0:T(8,128)(2,1)}), bf16[4,256,1152]{2,1,0:T(8,128)(2,1)S(1)}, u32[]{:S(2)}, u32[]{:S(2)}) %all-to-all-start.1) | async-done | bytes 2359328 | tf_op jit(solution)/shard_map/all_to_all | solution.py:356
  80.6 2.0 %shard_map.119 = (bf16[512,288]{1,0:T(8,128)(2,1)}, bf16[512,288]{1,0:T(8,128)(2,1)}) custom-call(s32[4]{0:T(128)S(1)} %pad_add_fusion.pos_ref, bf16[4,256,1152]{2,1,0:T(8,128)(2,1)S(1)} %all-to-all-done.1.p_ref), custom_call_target="tpu_custom_call" | custom-call | tf_op jit(solution)/shard_map/pallas_call | solution.py:42
  82.6 2.7 %collective-permute-start.11 = (bf16[512,288]{1,0:T(8,128)(2,1)}, bf16[512,288]{1,0:T(8,128)(2,1)S(1)}, u32[]{:S(2)}, u32[]{:S(2)}) collective-permute-start(bf16[512,288]{1,0:T(8,128)(2,1)} %get-tuple-element.50), channel_id=1, source_target_pairs={{0,4},{4,0},{1,5},{5,1},{2,6},{6,2},{3,7},{7,3},{8,12},{12,8},{9,1... | collective-permute-start | bytes 884744 | tf_op jit(solution)/shard_map/ppermute | solution.py:361
  85.5 1.4 collective-permute-done.11.rec_ref
  86.9 1.0 copy-done
  87.9 2.3 %shard_map.120 = (bf16[32,16,128]{2,1,0:T(8,128)(2,1)}, bf16[32,16,128]{2,1,0:T(8,128)(2,1)}) custom-call(s32[4]{0:T(128)S(1)} %pad_add_fusion.pos_ref, s32[32]{0:T(128)S(1)} %broadcast_select_fusion.2.g_ref, s32[32]{0:T(128)S(1)} %fusion.2.s_ref, bf16[512,288]{1,0:T(8,128)(2,1)S(1)} %copy-done, bf16[512,288]{1,0:T(8,128)(2,1)S(1)} %collective-permute-done.11.rec_ref, ...), custom_call_target="tpu_custom_call" | custom-call | tf_op jit(solution)/shard_map/pallas_call | solution.py:42
  90.2 3.9 %all-to-all-start.2 = ((bf16[32,16,128]{2,1,0:T(8,128)(2,1)}), bf16[32,16,128]{2,1,0:T(8,128)(2,1)S(1)}, u32[]{:S(2)}, u32[]{:S(2)}) async-start(bf16[32,16,128]{2,1,0:T(8,128)(2,1)} %get-tuple-element.51), calls=%async_computation.2 | async-start | bytes 262144 | tf_op jit(solution)/shard_map/all_to_all | solution.py:377
  94.1 8.4 %copy.78 = bf16[273,224,32]{1,0,2:T(8,128)(2,1)} copy(bf16[273,224,32]{0,2,1:T(8,128)(2,1)} %bitcast.26) | data formatting | bytes 7827456 | tf_op jit(solution)/shard_map/optimization_barrier | solution.py:357
  102.4 1.5 all-to-all-done.2.rec_ref
  103.9 0.7 copy-done.4
  104.6 11.9 %shard_map.121 = (bf16[32,16,512]{2,1,0:T(8,128)(2,1)}, bf16[32,16,512]{2,1,0:T(8,128)(2,1)}) custom-call(s32[4]{0:T(128)S(1)} %pad_add_fusion.pos_ref, s32[32]{0:T(128)S(1)} %get-tuple-element.74.owner_ref, bf16[32,16,128]{2,1,0:T(8,128)(2,1)} %copy-done.4, bf16[32,16,128]{2,1,0:T(8,128)(2,1)} %get-tuple-element.57.keep_ref, ...), custom_call_target="tpu_custom_call" | custom-call | tf_op jit(solution)/shard_map/pallas_call | solution.py:384
  116.4 7.7 %all-to-all-start.3 = ((bf16[32,16,512]{2,1,0:T(8,128)(2,1)}), bf16[32,16,512]{2,1,0:T(8,128)(2,1)S(1)}, u32[]{:S(2)}, u32[]{:S(2)}) async-start(bf16[32,16,512]{2,1,0:T(8,128)(2,1)} %get-tuple-element.63), calls=%async_computation.3 | async-start | bytes 1048576 | tf_op jit(solution)/shard_map/all_to_all | solution.py:402
  124.1 1.8 %slice.14 = bf16[2,224,448]{2,1,0:T(8,128)(2,1)} slice(bf16[4,224,448]{2,1,0:T(8,128)(2,1)} %collective-permute-done.12.refs_1_), slice={[0:2], [0:224], [0:448]} | slice | bytes 802816 | tf_op jit(solution)/shard_map/slice | solution.py:401
  126.0 1.8 %slice.15 = bf16[2,224,448]{2,1,0:T(8,128)(2,1)} slice(bf16[4,224,448]{2,1,0:T(8,128)(2,1)} %collective-permute-done.13.refs_4_), slice={[2:4], [0:224], [0:448]} | slice | bytes 802816 | tf_op jit(solution)/shard_map/slice | solution.py:401
  127.8 2.6 %collective-permute-start.15 = (bf16[2,224,448]{2,1,0:T(8,128)(2,1)}, bf16[2,224,448]{2,1,0:T(8,128)(2,1)}, u32[]{:S(2)}, u32[]{:S(2)}) collective-permute-start(bf16[2,224,448]{2,1,0:T(8,128)(2,1)} %slice.15), channel_id=1, source_target_pairs={{0,24},{8,0},{16,8},{24,16},{1,25},{9,1},{17,9},{25,17},{2,26},{10... | collective-permute-start | bytes 1204232 | tf_op jit(solution)/shard_map/ppermute | solution.py:310
  130.4 0.9 copy.79.len_ref
  131.4 7.1 %shard_map.122.num_ref = f32[2,512,256]{2,1,0:T(8,128)S(1)} custom-call(s32[4]{0:T(128)S(1)} %pad_add_fusion.pos_ref, bf16[512,288]{1,0:T(8,128)(2,1)S(1)} %copy-done.1, bf16[512,288]{1,0:T(8,128)(2,1)S(1)} %collective-permute-done.11.rec_ref, bf16[512,256]{1,0:T(8,128)(2,1)} %tk_ref.1, bf16[512,1792]{1,0:T(8,128)(2,1)} %tv_ref.1, s32[512,1]{1,0:T(8,128)} %copy.79.len_ref), custom_call_target="tpu_custom_call" | custom-call | tf_op jit(solution)/shard_map/pallas_call | solution.py:42
  138.5 0.3 collective-permute-done.14.refs_2_
  138.8 0.9 collective-permute-done.15.refs_3_
  139.7 0.7 all-to-all-done.3.rec_ref
  140.4 1.0 copy-done.2
  141.5 2.7 %shard_map.123 = bf16[4,256,256]{2,1,0:T(8,128)(2,1)} custom-call(s32[4]{0:T(128)S(1)} %pad_add_fusion.pos_ref, s32[32]{0:T(128)S(1)} %broadcast_select_fusion.2.g_ref, s32[32]{0:T(128)S(1)} %fusion.2.s_ref, f32[2,512,256]{2,1,0:T(8,128)S(1)} %shard_map.122.num_ref, bf16[32,16,512]{2,1,0:T(8,128)(2,1)S(1)} %all-to-all-done.3.rec_ref, ...), custom_call_target="tpu_custom_call" | custom-call | tf_op jit(solution)/shard_map/pallas_call | solution.py:42
  144.2 12.1 %all_to_all.29.own_ref = bf16[4,256,256]{2,1,0:T(8,128)(2,1)S(1)} all-to-all(bf16[4,256,256]{2,1,0:T(8,128)(2,1)} %shard_map.123), channel_id=1, replica_groups=mesh['req'=8,'y'=4,'core'=2,'col'=4] {'y'}, dimensions={0} | all-to-all | bytes 1048576 | tf_op jit(solution)/shard_map/all_to_all | solution.py:418
  156.3 3.5 %collective-permute-start.16 = (bf16[4,256,256]{2,1,0:T(8,128)(2,1)S(1)}, bf16[4,256,256]{2,1,0:T(8,128)(2,1)S(1)}, u32[]{:S(2)}, u32[]{:S(2)}) collective-permute-start(bf16[4,256,256]{2,1,0:T(8,128)(2,1)S(1)} %all_to_all.29.own_ref), channel_id=1, source_target_pairs={{0,4},{4,0},{1,5},{5,1},{2,6},{6,2},{3,7},{7,3},{8,12},{12,8},{9,1... | collective-permute-start | bytes 1572872 | tf_op jit(solution)/shard_map/ppermute | solution.py:419
  159.9 1.5 collective-permute-done.16.oth_ref
  161.4 3.8 %shard_map.124 = (bf16[256,448]{1,0:T(8,128)(2,1)}, bf16[256,448]{1,0:T(8,128)(2,1)}) custom-call(s32[4]{0:T(128)S(1)} %pad_add_fusion.pos_ref, bf16[4,256,256]{2,1,0:T(8,128)(2,1)S(1)} %all_to_all.29.own_ref, bf16[4,256,256]{2,1,0:T(8,128)(2,1)S(1)} %collective-permute-done.16.oth_ref, bf16[4,224,448]{2,1,0:T(8,128)(2,1)S(1)} %pad_maximum_fusion.refs_0_, ...), custom_call_target="tpu_custom_call" | custom-call | tf_op jit(solution)/shard_map/pallas_call | solution.py:42
  165.2 3.9 %collective-permute-start.17 = (bf16[256,448]{1,0:T(8,128)(2,1)}, bf16[256,448]{1,0:T(8,128)(2,1)S(1)}, u32[]{:S(2)}, u32[]{:S(2)}) collective-permute-start(bf16[256,448]{1,0:T(8,128)(2,1)} %get-tuple-element.71), channel_id=1, source_target_pairs={{0,1},{4,3},{8,0},{12,2},{16,5},{20,7},{24,4},{28,6},{1,9},{5,11},... | collective-permute-start | bytes 688136 | tf_op jit(solution)/shard_map/ppermute | solution.py:431
  169.1 3.7 %collective-permute-start.18 = (bf16[256,448]{1,0:T(8,128)(2,1)}, bf16[256,448]{1,0:T(8,128)(2,1)S(1)}, u32[]{:S(2)}, u32[]{:S(2)}) collective-permute-start(bf16[256,448]{1,0:T(8,128)(2,1)} %get-tuple-element.72), channel_id=1, source_target_pairs={{0,0},{4,2},{8,1},{12,3},{16,4},{20,6},{24,5},{28,7},{1,8},{5,10},... | collective-permute-start | bytes 688136 | tf_op jit(solution)/shard_map/ppermute | solution.py:431
  172.8 4.4 %collective-permute-done.17 = bf16[256,448]{1,0:T(8,128)(2,1)S(1)} collective-permute-done((bf16[256,448]{1,0:T(8,128)(2,1)}, bf16[256,448]{1,0:T(8,128)(2,1)S(1)}, u32[]{:S(2)}, u32[]{:S(2)}) %collective-permute-start.17) | collective-permute-done | bytes 229408 | tf_op jit(solution)/shard_map/ppermute | solution.py:431
  177.2 1.7 collective-permute-done.18
  179.3 0.9 fusion.1
  (49 shorter events, 1.8 us)
Async XLA Ops:
  0.0 9.1 %copy-start.10 = (bf16[224,448]{1,0:T(8,128)(2,1)S(1)}, bf16[224,448]{1,0:T(8,128)(2,1)}, u32[]{:S(2)}) copy-start(bf16[224,448]{1,0:T(8,128)(2,1)} %param.16) | copy-start | bytes 602116
  0.0 19.8 %copy-start.9 = (s32[32]{0:T(128)S(1)}, s32[32]{0:T(128)}, u32[]{:S(2)}) copy-start(s32[32]{0:T(128)} %param.19) | copy-start | bytes 388
  1.3 6.7 %collective-permute-start = (bf16[128,896]{1,0:T(8,128)(2,1)S(1)}, bf16[128,896]{1,0:T(8,128)(2,1)S(1)}, u32[]{:S(2)}, u32[]{:S(2)}) collective-permute-start(bf16[128,896]{1,0:T(8,128)(2,1)S(1)} %copy.75.refs_0_), channel_id=1, source_target_pairs={{0,8},{8,16},{16,24},{24,0},{1,9},{9,17},{17,25},{25,1},{2,10},{10... | collective-permute-start | bytes 688136 | tf_op jit(solution)/shard_map/ppermute | solution.py:310
  2.8 6.2 %collective-permute-start.1 = (bf16[128,896]{1,0:T(8,128)(2,1)S(1)}, bf16[128,896]{1,0:T(8,128)(2,1)S(1)}, u32[]{:S(2)}, u32[]{:S(2)}) collective-permute-start(bf16[128,896]{1,0:T(8,128)(2,1)S(1)} %copy.76.refs_1_), channel_id=1, source_target_pairs={{0,24},{8,0},{16,8},{24,16},{1,25},{9,1},{17,9},{25,17},{2,26},{10... | collective-permute-start | bytes 688136 | tf_op jit(solution)/shard_map/ppermute | solution.py:310
  3.1 38.1 %collective-permute-start.2 = (bf16[128,896]{1,0:T(8,128)(2,1)S(1)}, bf16[128,896]{1,0:T(8,128)(2,1)S(1)}, u32[]{:S(2)}, u32[]{:S(2)}) collective-permute-start(bf16[128,896]{1,0:T(8,128)(2,1)S(1)} %copy.76.refs_1_), channel_id=1, source_target_pairs={{0,8},{8,16},{16,24},{24,0},{1,9},{9,17},{17,25},{25,1},{2,10},{10... | collective-permute-start | bytes 688136 | tf_op jit(solution)/shard_map/ppermute | solution.py:310
  9.1 11.4 %collective-permute-start.6 = (bf16[224,448]{1,0:T(8,128)(2,1)S(1)}, bf16[224,448]{1,0:T(8,128)(2,1)S(1)}, u32[]{:S(2)}, u32[]{:S(2)}) collective-permute-start(bf16[224,448]{1,0:T(8,128)(2,1)S(1)} %copy-done.10), channel_id=1, source_target_pairs={{0,0},{1,2},{2,4},{3,6},{4,1},{5,3},{6,5},{7,7},{8,8},{9,10},{10,1... | collective-permute-start | bytes 602120 | tf_op jit(solution)/shard_map/ppermute | solution.py:323
  13.9 7.9 %collective-permute-start.7 = (bf16[224,448]{1,0:T(8,128)(2,1)S(1)}, bf16[224,448]{1,0:T(8,128)(2,1)}, u32[]{:S(2)}, u32[]{:S(2)}) collective-permute-start(bf16[224,448]{1,0:T(8,128)(2,1)S(1)} %copy-done.10), channel_id=1, source_target_pairs={{0,1},{1,3},{2,5},{3,7},{4,0},{5,2},{6,4},{7,6},{8,9},{9,11},{10,1... | collective-permute-start | bytes 602120 | tf_op jit(solution)/shard_map/ppermute | solution.py:323
  14.0 12.5 %collective-permute-start.8 = (bf16[224,448]{1,0:T(8,128)(2,1)S(1)}, bf16[224,448]{1,0:T(8,128)(2,1)}, u32[]{:S(2)}, u32[]{:S(2)}) collective-permute-start(bf16[224,448]{1,0:T(8,128)(2,1)S(1)} %copy-done.10), channel_id=1, source_target_pairs={{0,2},{1,0},{2,6},{3,4},{4,3},{5,1},{6,7},{7,5},{8,10},{9,8},{10,1... | collective-permute-start | bytes 602120 | tf_op jit(solution)/shard_map/ppermute | solution.py:323
  15.4 12.1 %collective-permute-start.9 = (bf16[224,448]{1,0:T(8,128)(2,1)S(1)}, bf16[224,448]{1,0:T(8,128)(2,1)}, u32[]{:S(2)}, u32[]{:S(2)}) collective-permute-start(bf16[224,448]{1,0:T(8,128)(2,1)S(1)} %copy-done.10), channel_id=1, source_target_pairs={{0,3},{1,1},{2,7},{3,5},{4,2},{5,0},{6,6},{7,4},{8,11},{9,9},{10,1... | collective-permute-start | bytes 602120 | tf_op jit(solution)/shard_map/ppermute | solution.py:323
  20.4 20.8 %collective-permute-start.5 = (bf16[128,896]{1,0:T(8,128)(2,1)S(1)}, bf16[128,896]{1,0:T(8,128)(2,1)S(1)}, u32[]{:S(2)}, u32[]{:S(2)}) collective-permute-start(bf16[128,896]{1,0:T(8,128)(2,1)S(1)} %copy.75.refs_0_), channel_id=1, source_target_pairs={{0,24},{8,0},{16,8},{24,16},{1,25},{9,1},{17,9},{25,17},{2,26},{10... | collective-permute-start | bytes 688136 | tf_op jit(solution)/shard_map/ppermute | solution.py:310
  21.8 19.4 %collective-permute-start.10 = (bf16[448,288]{1,0:T(8,128)(2,1)S(1)}, bf16[448,288]{1,0:T(8,128)(2,1)S(1)}, u32[]{:S(2)}, u32[]{:S(2)}) collective-permute-start(bf16[448,288]{1,0:T(8,128)(2,1)S(1)} %pad_maximum_fusion.1.refs_8_), channel_id=1, source_target_pairs={{0,4},{4,0},{1,5},{5,1},{2,6},{6,2},{3,7},{7,3},{8,12},{12,8},{9,1... | collective-permute-start | bytes 774152 | tf_op jit(solution)/shard_map/ppermute | solution.py:319
  26.5 14.7 %collective-permute-start.3 = (bf16[128,896]{1,0:T(8,128)(2,1)S(1)}, bf16[128,896]{1,0:T(8,128)(2,1)S(1)}, u32[]{:S(2)}, u32[]{:S(2)}) collective-permute-start(bf16[128,896]{1,0:T(8,128)(2,1)S(1)} %collective-permute-done.refs_2_), channel_id=1, source_target_pairs={{0,8},{8,16},{16,24},{24,0},{1,9},{9,17},{17,25},{25,1},{2,10},{10... | collective-permute-start | bytes 688136 | tf_op jit(solution)/shard_map/ppermute | solution.py:310
  27.5 13.7 %collective-permute-start.4 = (bf16[128,896]{1,0:T(8,128)(2,1)S(1)}, bf16[128,896]{1,0:T(8,128)(2,1)S(1)}, u32[]{:S(2)}, u32[]{:S(2)}) collective-permute-start(bf16[128,896]{1,0:T(8,128)(2,1)S(1)} %collective-permute-done.1.refs_7_), channel_id=1, source_target_pairs={{0,24},{8,0},{16,8},{24,16},{1,25},{9,1},{17,9},{25,17},{2,26},{10... | collective-permute-start | bytes 688136 | tf_op jit(solution)/shard_map/ppermute | solution.py:310
  28.8 20.8 %all-to-all-start = ((s32[32,1,1]{2,1,0:T(1,128)}), s32[32,1,1]{2,1,0:T(1,128)S(1)}, u32[]{:S(2)}, u32[]{:S(2)}) async-start(s32[32,1,1]{2,1,0:T(1,128)} %copy.67), calls=%async_computation | async-start | bytes 32768 | tf_op jit(solution)/shard_map/all_to_all | solution.py:331
  49.6 31.0 %all-to-all-start.1 = ((bf16[4,256,1152]{2,1,0:T(8,128)(2,1)}), bf16[4,256,1152]{2,1,0:T(8,128)(2,1)S(1)}, u32[]{:S(2)}, u32[]{:S(2)}) async-start(bf16[4,256,1152]{2,1,0:T(8,128)(2,1)} %shard_map.118), calls=%async_computation.1 | async-start | bytes 4718592 | tf_op jit(solution)/shard_map/all_to_all | solution.py:356
  53.5 7.4 %copy-start.5 = (bf16[32,273,2]{1,2,0:T(2,128)(2,1)S(1)}, bf16[32,273,2]{1,2,0:T(2,128)(2,1)}, u32[]{:S(2)}) copy-start(bf16[32,273,2]{1,2,0:T(2,128)(2,1)} %param.18) | copy-start | bytes 104836
  53.5 8.4 %copy-start.7 = (s32[512]{0:T(512)S(1)}, s32[512]{0:T(512)}, u32[]{:S(2)}) copy-start(s32[512]{0:T(512)} %param.20) | copy-start | bytes 6148
  65.4 37.1 %collective-permute-start.12 = (bf16[4,224,448]{2,1,0:T(8,128)(2,1)S(1)}, bf16[4,224,448]{2,1,0:T(8,128)(2,1)}, u32[]{:S(2)}, u32[]{:S(2)}) collective-permute-start(bf16[4,224,448]{2,1,0:T(8,128)(2,1)S(1)} %pad_maximum_fusion.refs_0_), channel_id=1, source_target_pairs={{0,8},{8,16},{16,24},{24,0},{1,9},{9,17},{17,25},{25,1},{2,10},{10... | collective-permute-start | bytes 2408456 | tf_op jit(solution)/shard_map/ppermute | solution.py:310
  65.5 37.0 %collective-permute-start.13 = (bf16[4,224,448]{2,1,0:T(8,128)(2,1)S(1)}, bf16[4,224,448]{2,1,0:T(8,128)(2,1)}, u32[]{:S(2)}, u32[]{:S(2)}) collective-permute-start(bf16[4,224,448]{2,1,0:T(8,128)(2,1)S(1)} %pad_maximum_fusion.refs_0_), channel_id=1, source_target_pairs={{0,24},{8,0},{16,8},{24,16},{1,25},{9,1},{17,9},{25,17},{2,26},{10... | collective-permute-start | bytes 2408456 | tf_op jit(solution)/shard_map/ppermute | solution.py:310
  82.6 4.3 %collective-permute-start.11 = (bf16[512,288]{1,0:T(8,128)(2,1)}, bf16[512,288]{1,0:T(8,128)(2,1)S(1)}, u32[]{:S(2)}, u32[]{:S(2)}) collective-permute-start(bf16[512,288]{1,0:T(8,128)(2,1)} %get-tuple-element.50), channel_id=1, source_target_pairs={{0,4},{4,0},{1,5},{5,1},{2,6},{6,2},{3,7},{7,3},{8,12},{12,8},{9,1... | collective-permute-start | bytes 884744 | tf_op jit(solution)/shard_map/ppermute | solution.py:361
  86.9 1.0 copy-start
  90.2 13.7 %all-to-all-start.2 = ((bf16[32,16,128]{2,1,0:T(8,128)(2,1)}), bf16[32,16,128]{2,1,0:T(8,128)(2,1)S(1)}, u32[]{:S(2)}, u32[]{:S(2)}) async-start(bf16[32,16,128]{2,1,0:T(8,128)(2,1)} %get-tuple-element.51), calls=%async_computation.2 | async-start | bytes 262144 | tf_op jit(solution)/shard_map/all_to_all | solution.py:377
  102.4 28.0 %copy-start.8 = (s32[512]{0:T(512)S(1)}, s32[512]{0:T(512)}, u32[]{:S(2)}) copy-start(s32[512]{0:T(512)} %param.23) | copy-start | bytes 6148
  103.9 0.7 copy-start.4
  104.5 26.7 %copy-start.6 = (s32[512]{0:T(512)S(1)}, s32[512]{0:T(512)}, u32[]{:S(2)}) copy-start(s32[512]{0:T(512)} %multiply_add_fusion) | copy-start | bytes 6148
  104.5 26.9 %copy-start.1 = (bf16[512,288]{1,0:T(8,128)(2,1)S(1)}, bf16[512,288]{1,0:T(8,128)(2,1)}, u32[]{:S(2)}) copy-start(bf16[512,288]{1,0:T(8,128)(2,1)} %get-tuple-element.49.own_ref) | copy-start | bytes 884740
  116.4 24.0 %all-to-all-start.3 = ((bf16[32,16,512]{2,1,0:T(8,128)(2,1)}), bf16[32,16,512]{2,1,0:T(8,128)(2,1)S(1)}, u32[]{:S(2)}, u32[]{:S(2)}) async-start(bf16[32,16,512]{2,1,0:T(8,128)(2,1)} %get-tuple-element.63), calls=%async_computation.3 | async-start | bytes 1048576 | tf_op jit(solution)/shard_map/all_to_all | solution.py:402
  126.0 12.8 %collective-permute-start.14 = (bf16[2,224,448]{2,1,0:T(8,128)(2,1)}, bf16[2,224,448]{2,1,0:T(8,128)(2,1)}, u32[]{:S(2)}, u32[]{:S(2)}) collective-permute-start(bf16[2,224,448]{2,1,0:T(8,128)(2,1)} %slice.14), channel_id=1, source_target_pairs={{0,8},{8,16},{16,24},{24,0},{1,9},{9,17},{17,25},{25,1},{2,10},{10... | collective-permute-start | bytes 1204232 | tf_op jit(solution)/shard_map/ppermute | solution.py:310
  127.8 11.9 %collective-permute-start.15 = (bf16[2,224,448]{2,1,0:T(8,128)(2,1)}, bf16[2,224,448]{2,1,0:T(8,128)(2,1)}, u32[]{:S(2)}, u32[]{:S(2)}) collective-permute-start(bf16[2,224,448]{2,1,0:T(8,128)(2,1)} %slice.15), channel_id=1, source_target_pairs={{0,24},{8,0},{16,8},{24,16},{1,25},{9,1},{17,9},{25,17},{2,26},{10... | collective-permute-start | bytes 1204232 | tf_op jit(solution)/shard_map/ppermute | solution.py:310
  140.4 1.0 copy-start.2
  144.2 35.1 %copy-start.3 = (bf16[256,2,448]{0,2,1:T(8,128)(2,1)S(1)}, bf16[256,2,448]{0,2,1:T(8,128)(2,1)}, u32[]{:S(2)}) copy-start(bf16[256,2,448]{0,2,1:T(8,128)(2,1)} %param.12) | copy-start | bytes 1376260
  156.3 5.1 %collective-permute-start.16 = (bf16[4,256,256]{2,1,0:T(8,128)(2,1)S(1)}, bf16[4,256,256]{2,1,0:T(8,128)(2,1)S(1)}, u32[]{:S(2)}, u32[]{:S(2)}) collective-permute-start(bf16[4,256,256]{2,1,0:T(8,128)(2,1)S(1)} %all_to_all.29.own_ref), channel_id=1, source_target_pairs={{0,4},{4,0},{1,5},{5,1},{2,6},{6,2},{3,7},{7,3},{8,12},{12,8},{9,1... | collective-permute-start | bytes 1572872 | tf_op jit(solution)/shard_map/ppermute | solution.py:419
  165.2 12.0 %collective-permute-start.17 = (bf16[256,448]{1,0:T(8,128)(2,1)}, bf16[256,448]{1,0:T(8,128)(2,1)S(1)}, u32[]{:S(2)}, u32[]{:S(2)}) collective-permute-start(bf16[256,448]{1,0:T(8,128)(2,1)} %get-tuple-element.71), channel_id=1, source_target_pairs={{0,1},{4,3},{8,0},{12,2},{16,5},{20,7},{24,4},{28,6},{1,9},{5,11},... | collective-permute-start | bytes 688136 | tf_op jit(solution)/shard_map/ppermute | solution.py:431
  169.1 9.8 %collective-permute-start.18 = (bf16[256,448]{1,0:T(8,128)(2,1)}, bf16[256,448]{1,0:T(8,128)(2,1)S(1)}, u32[]{:S(2)}, u32[]{:S(2)}) collective-permute-start(bf16[256,448]{1,0:T(8,128)(2,1)} %get-tuple-element.72), channel_id=1, source_target_pairs={{0,0},{4,2},{8,1},{12,3},{16,4},{20,6},{24,5},{28,7},{1,8},{5,10},... | collective-permute-start | bytes 688136 | tf_op jit(solution)/shard_map/ppermute | solution.py:431

commit v11 on v8

--- a/solution.py
+++ b/solution.py
@@ -34,7 +34,7 @@
     return pltpu.with_memory_space_constraint(x, pltpu.HBM)
 
 
-def call(kernel, out_shapes, n_smem, *args, scratch=(), free=()):
+def call(kernel, out_shapes, n_smem, *args, scratch=(), free=(), pin=True):
     def full(shape):
         zeros = (0,) * len(shape)
         return pl.BlockSpec(shape, lambda i: zeros)
@@ -42,7 +42,7 @@
     return pl.pallas_call(
         kernel,
         grid=(1,),
-        out_shape=jax.tree.map(lambda x: pltpu.HBM(x.shape, x.dtype), out_shapes),
+        out_shape=jax.tree.map(lambda x: pltpu.HBM(x.shape, x.dtype), out_shapes) if pin else out_shapes,
         in_specs=[SM] * n_smem + [full(x.shape) for x in args[n_smem:]],
         out_specs=jax.tree.map(lambda x: full(x.shape), out_shapes),
         scratch_shapes=scratch,
@@ -284,7 +284,7 @@
 
 
 def out_kernel(pos_ref, own_ref, oth_ref, *refs):
-    w0, w1, far_1, far_3, w3, first_ref, second_ref = refs
+    parts, first_ref, second_ref = refs[:8], refs[8], refs[9]
     y, core, col = pos_ref[0], pos_ref[1], pos_ref[3]
     acc = [None, None]
     for shift in range(4):
@@ -294,8 +294,7 @@
             heads = ref[j, :, 0:224]
             for e in range(2):
                 at = jnp.bitwise_xor(k, lax.rem(col, 2))
-                w = (far_1, far_3)[e][at] if shift == 2 else (w0, w1, None, w3)[shift][2 * e + at]
-                part = dot(heads, w)
+                part = dot(heads, parts[2 * shift + e][at])
                 acc[e] = part if acc[e] is None else acc[e] + part
     same = lax.rem(y, 2) == lax.div(col, 2)
     first_ref[...] = jnp.where(same, acc[0], acc[1]).astype(BF)
@@ -349,8 +348,8 @@
     for s in range(4):
         perm = [(k * 4 + c, (c >> 1) * 4 + (s ^ (2 * (c & 1) + k))) for k in range(2) for c in range(4)]
         pieces.append(lax.ppermute(w_out, ("core", "col"), perm))
-    pieces = jnp.stack(pieces)
-    out_1, out_3 = over_y(pieces, 1), over_y(pieces, 3)
+    pieces = [jnp.stack(pieces[:2]), jnp.stack(pieces[2:])]
+    out_w = [over_y(x, step) for step in (1, 3) for x in pieces]
     partial = lax.all_to_all(partial, "col", split_axis=0, concat_axis=0, tiled=True)
     partial, states, norms = lax.optimization_barrier((partial, states, norms))
     states = jnp.transpose(states, (2, 0, 1))
@@ -374,8 +373,8 @@
     )
     q_rec = lax.all_to_all(q_send, ("req", "col"), split_axis=0, concat_axis=0, tiled=True)
     shape = jax.ShapeDtypeStruct((2, 512, 256), F32)
-    num = call(tail_kernel, shape, 1, pos, own, rec, tail_keys, tail_values, tail_length[:, None], free=(1, 2))
-    q_rec, out_1, out_3 = lax.optimization_barrier((q_rec, out_1, out_3))
+    num = call(tail_kernel, shape, 1, pos, own, rec, tail_keys, tail_values, tail_length[:, None], free=(1, 2), pin=False)
+    q_rec, out_w = lax.optimization_barrier((q_rec, out_w))
     shape = jax.ShapeDtypeStruct((32, 16, 512), BF)
     whole = pl.BlockSpec((32, 16, 128), lambda i: (0, 0, 0))
     whole_out = pl.BlockSpec((32, 16, 512), lambda i: (0, 0, 0))
@@ -395,8 +394,8 @@
         scratch_shapes=[pltpu.VMEM((128, 128), BF)],
         compiler_params=pltpu.CompilerParams(vmem_limit_bytes=VMEM_LIMIT),
     )(pos, owner, in_hbm(q_rec), in_hbm(q_keep), in_hbm(states), in_hbm(norms))
-    r_send, near_1, near_3 = lax.optimization_barrier((r_send, out_1, out_3))
-    far_1, far_3 = over_y(near_1[:2], 1), over_y(near_3[2:], 3)
+    r_send, near_1, near_3 = lax.optimization_barrier((r_send, out_w[0], out_w[3]))
+    far_1, far_3 = over_y(near_1, 1), over_y(near_3, 3)
     r_rec = lax.all_to_all(r_send, ("req", "col"), split_axis=0, concat_axis=0, tiled=True)
     r_rec, num, far_1, far_3 = lax.optimization_barrier((r_rec, num, far_1, far_3))
     heads = call(
@@ -411,12 +410,12 @@
         r_keep,
         place[:, None],
         scratch=[pltpu.VMEM((512, 512), BF)],
-        free=(4,),
+        free=range(3, 7),
     )
     heads = lax.all_to_all(heads, "y", split_axis=0, concat_axis=0, tiled=True)
     heads_oth = lax.ppermute(heads, "core", [(0, 1), (1, 0)])
     shape = jax.ShapeDtypeStruct((256, 448), BF)
-    mixed = call(out_kernel, (shape, shape), 1, pos, heads, heads_oth, pieces, out_1, far_1, far_3, out_3, free=(1, 2))
+    mixed = call(out_kernel, (shape, shape), 1, pos, heads, heads_oth, *pieces, out_w[0], out_w[1], far_1, far_3, out_w[2], out_w[3], free=range(1, 11))
 
     def at(y, core, col):
         return (y * 2 + core) * 4 + col

time: 181 us -> 181 us (level)
  starting transfers between devices: 66.9 us -> 71 us
  Pallas kernels: 35.9 us -> 33.3 us
    all_to_all x1, waiting for transfers between devices: 0.21 us -> 3.06 us  [body(): lax.all_to_all(r_send, ('req', 'col'), split_axis=0, concat_axis=0, tiled...]
    pallas_call x6, Pallas kernels: 24.1 us -> 21.6 us  [call(): pl.pallas_call(kernel, grid=(1,), out_shape=jax.tree.map(lambda x: pltpu....]
    ppermute x10 -> x12, starting transfers between devices: 11.3 us -> 13.8 us  [over_y(): return lax.ppermute(x, 'y', [(i, (i + step) % 4) for i in range(4)])]
    all_to_all x1, starting transfers between devices: 3.95 us -> 6.28 us  [body(): lax.all_to_all(q_send, ('req', 'col'), split_axis=0, concat_axis=0, tiled...]
    unnamed x29 -> x31, local copies, waits for them, and re-layouts: 10.9 us -> 13 us
    slice x2 -> x0, local copies, waits for them, and re-layouts: 2.1 us -> none  [body(): far_1, far_3 = (over_y(near_1[:2], 1), over_y(near_3[2:], 3))]
  transfers between devices with their start and end apart: 23 -> 25, of which waited for: 11 -> 10; matrix products, arithmetic and copies ran while one was open for 16% -> 14% of each run, Pallas kernels for 9% -> 9%
where the time goes in v11:
time: 181 us; the launch traced here: 178 us
  starting transfers between devices  71 us (39%)
  Pallas kernels  33.3 us (18%)
  waiting for transfers between devices  30.4 us (17%)
  local copies, waits for them, and re-layouts  27.1 us (15%)
  blocking collectives  11.7 us (6%)
  other arithmetic  4.06 us (2%)
    pallas_call x6, Pallas kernels, call(): pl.pallas_call(kernel, grid=(1,), out_shape=jax.tree.map(lambda x: pltpu....  21.6 us
    ppermute x12, starting transfers between devices, over_y(): return lax.ppermute(x, 'y', [(i, (i + step) % 4) for i in range(4)])  13.8 us
    ppermute x4, starting transfers between devices, body(): pieces.append(lax.ppermute(w_out, ('core', 'col'), perm))  13.7 us
    unnamed x31, local copies, waits for them, and re-layouts  13 us
    ppermute x4, waiting for transfers between devices, body(): pieces.append(lax.ppermute(w_out, ('core', 'col'), perm))  12.4 us
    all_to_all x1, blocking collectives, body(): heads = lax.all_to_all(heads, 'y', split_axis=0, concat_axis=0, tiled=True)  11.7 us
    pallas_call x1, Pallas kernels, body(): pl.pallas_call(slot_kernel, grid=(4,), out_shape=(pltpu.HBM(shape.shape,...  11.7 us
    all_to_all x1, starting transfers between devices, body(): lax.all_to_all(code[:, None], ('req', 'col'), split_axis=0, concat_axis=0...  10.8 us
  transfers between devices with their start and end apart: 25, of which 10 were waited for; matrix products, arithmetic and copies ran while one was open for 14% of the time, Pallas kernels for 9%

profile of v11, /device:TPU:9, one launch (start us, length us, event | category | flops | bytes accessed | tf_op | source)
XLA Modules:
  0.0 177.8 jit_solution(11331525763687571901)
XLA Ops:
  0.0 1.1 fusion.8
  1.1 0.2 copy.76.refs_1_
  1.3 1.4 collective-permute-start.1
  2.6 0.2 collective-permute-start.3
  2.8 0.2 copy.75.refs_0_
  3.0 1.4 collective-permute-start
  4.3 0.3 collective-permute-start.5
  4.7 0.9 copy.74
  5.6 0.9 copy.73
  6.5 1.2 reshape.76
  7.7 0.2 copy.84
  8.3 3.2 %collective-permute-start.6 = (bf16[448,288]{1,0:T(8,128)(2,1)S(1)}, bf16[448,288]{1,0:T(8,128)(2,1)S(1)}, u32[]{:S(2)}, u32[]{:S(2)}) collective-permute-start(bf16[448,288]{1,0:T(8,128)(2,1)S(1)} %pad_maximum_fusion.2.refs_8_), channel_id=1, source_target_pairs={{0,4},{4,0},{1,5},{5,1},{2,6},{6,2},{3,7},{7,3},{8,12},{12,8},{9,1... | collective-permute-start | bytes 774152 | tf_op jit(solution)/shard_map/ppermute | solution.py:317
  11.5 1.1 collective-permute-done.refs_2_
  12.5 1.5 collective-permute-start.2
  14.0 0.5 collective-permute-start.4
  14.7 0.7 copy.67
  15.3 10.8 %all-to-all-start = ((s32[32,1,1]{2,1,0:T(1,128)}), s32[32,1,1]{2,1,0:T(1,128)S(1)}, u32[]{:S(2)}, u32[]{:S(2)}) async-start(s32[32,1,1]{2,1,0:T(1,128)} %copy.67), calls=%async_computation | async-start | bytes 32768 | tf_op jit(solution)/shard_map/all_to_all | solution.py:324
  26.2 3.9 %shard_map.118 = bf16[4,256,1152]{2,1,0:T(8,128)(2,1)} custom-call(s32[4]{0:T(128)S(1)} %pad_add_fusion.pos_ref, bf16[128,896]{1,0:T(8,128)(2,1)S(1)} %copy.75.refs_0_, bf16[128,896]{1,0:T(8,128)(2,1)S(1)} %copy.76.refs_1_, bf16[128,896]{1,0:T(8,128)(2,1)S(1)} %collective-permute-done.refs_2_, bf16[128,896]{1,0:T(8,128)(2,1)S(1)} %collective-permute-done.1.refs_3_, ...), custom_call_target="tpu_custom_call" | custom-call | tf_op jit(solution)/shard_map/pallas_call | solution.py:42
  30.1 4.5 %all-to-all-done = s32[32,1,1]{2,1,0:T(1,128)S(1)} async-done(((s32[32,1,1]{2,1,0:T(1,128)}), s32[32,1,1]{2,1,0:T(1,128)S(1)}, u32[]{:S(2)}, u32[]{:S(2)}) %all-to-all-start) | async-done | bytes 160 | tf_op jit(solution)/shard_map/all_to_all | solution.py:324
  34.6 3.6 %all-to-all-start.1 = ((bf16[4,256,1152]{2,1,0:T(8,128)(2,1)}), bf16[4,256,1152]{2,1,0:T(8,128)(2,1)S(1)}, u32[]{:S(2)}, u32[]{:S(2)}) async-start(bf16[4,256,1152]{2,1,0:T(8,128)(2,1)} %shard_map.118), calls=%async_computation.1 | async-start | bytes 4718592 | tf_op jit(solution)/shard_map/all_to_all | solution.py:353
  38.3 7.3 %copy.77 = bf16[1,273,7168]{1,2,0:T(8,128)(2,1)} copy(bf16[1,273,7168]{2,1,0:T(8,128)(2,1)} %param.17) | data formatting | bytes 7827456 | tf_op args[5]
  45.7 0.6 pad.4.norm_ref
  46.3 0.2 compare_reduce_fusion.1
  46.5 0.2 fusion.2.s_ref
  46.7 0.2 convert_reduce_fusion
  46.9 0.6 multiply_add_fusion
  47.5 0.7 add_reduce_fusion
  48.2 3.6 %collective-permute-start.9 = (bf16[224,448]{1,0:T(8,128)(2,1)}, bf16[224,448]{1,0:T(8,128)(2,1)S(1)}, u32[]{:S(2)}, u32[]{:S(2)}) collective-permute-start(bf16[224,448]{1,0:T(8,128)(2,1)} %param.16), channel_id=1, source_target_pairs={{0,1},{1,3},{2,5},{3,7},{4,0},{5,2},{6,4},{7,6},{8,9},{9,11},{10,1... | collective-permute-start | bytes 602120 | tf_op jit(solution)/shard_map/ppermute | solution.py:350
  51.8 5.5 %collective-permute-start.8 = (bf16[224,448]{1,0:T(8,128)(2,1)}, bf16[224,448]{1,0:T(8,128)(2,1)S(1)}, u32[]{:S(2)}, u32[]{:S(2)}) collective-permute-start(bf16[224,448]{1,0:T(8,128)(2,1)} %param.16), channel_id=1, source_target_pairs={{0,0},{1,2},{2,4},{3,6},{4,1},{5,3},{6,5},{7,7},{8,8},{9,10},{10,1... | collective-permute-start | bytes 602120 | tf_op jit(solution)/shard_map/ppermute | solution.py:350
  57.3 0.7 compare_reduce_fusion
  58.0 1.9 %collective-permute-start.12 = (bf16[224,448]{1,0:T(8,128)(2,1)}, bf16[224,448]{1,0:T(8,128)(2,1)S(1)}, u32[]{:S(2)}, u32[]{:S(2)}) collective-permute-start(bf16[224,448]{1,0:T(8,128)(2,1)} %param.16), channel_id=1, source_target_pairs={{0,3},{1,1},{2,7},{3,5},{4,2},{5,0},{6,6},{7,4},{8,11},{9,9},{10,1... | collective-permute-start | bytes 602120 | tf_op jit(solution)/shard_map/ppermute | solution.py:350
  59.9 2.7 %collective-permute-start.11 = (bf16[224,448]{1,0:T(8,128)(2,1)}, bf16[224,448]{1,0:T(8,128)(2,1)S(1)}, u32[]{:S(2)}, u32[]{:S(2)}) collective-permute-start(bf16[224,448]{1,0:T(8,128)(2,1)} %param.16), channel_id=1, source_target_pairs={{0,2},{1,0},{2,6},{3,4},{4,3},{5,1},{6,7},{7,5},{8,10},{9,8},{10,1... | collective-permute-start | bytes 602120 | tf_op jit(solution)/shard_map/ppermute | solution.py:350
  62.7 6.2 %collective-permute-done.9 = bf16[224,448]{1,0:T(8,128)(2,1)S(1)} collective-permute-done((bf16[224,448]{1,0:T(8,128)(2,1)}, bf16[224,448]{1,0:T(8,128)(2,1)S(1)}, u32[]{:S(2)}, u32[]{:S(2)}) %collective-permute-start.9) | collective-permute-done | bytes 200736 | tf_op jit(solution)/shard_map/ppermute | solution.py:350
  68.9 6.2 %collective-permute-done.8 = bf16[224,448]{1,0:T(8,128)(2,1)S(1)} collective-permute-done((bf16[224,448]{1,0:T(8,128)(2,1)}, bf16[224,448]{1,0:T(8,128)(2,1)S(1)}, u32[]{:S(2)}, u32[]{:S(2)}) %collective-permute-start.8) | collective-permute-done | bytes 200736 | tf_op jit(solution)/shard_map/ppermute | solution.py:350
  75.2 1.3 collective-permute-start.10
  76.5 1.5 collective-permute-start.14
  78.0 2.0 %shard_map.119 = (bf16[512,288]{1,0:T(8,128)(2,1)}, bf16[512,288]{1,0:T(8,128)(2,1)}) custom-call(s32[4]{0:T(128)S(1)} %pad_add_fusion.pos_ref, bf16[4,256,1152]{2,1,0:T(8,128)(2,1)S(1)} %all-to-all-done.1.p_ref), custom_call_target="tpu_custom_call" | custom-call | tf_op jit(solution)/shard_map/pallas_call | solution.py:42
  80.2 2.7 %collective-permute-start.15 = (bf16[2,224,448]{2,1,0:T(8,128)(2,1)S(1)}, bf16[2,224,448]{2,1,0:T(8,128)(2,1)}, u32[]{:S(2)}, u32[]{:S(2)}) collective-permute-start(bf16[2,224,448]{2,1,0:T(8,128)(2,1)S(1)} %pad_maximum_fusion.1.refs_1_), channel_id=1, source_target_pairs={{0,24},{8,0},{16,8},{24,16},{1,25},{9,1},{17,9},{25,17},{2,26},{10... | collective-permute-start | bytes 1204232 | tf_op jit(solution)/shard_map/ppermute | solution.py:309
  82.9 1.1 copy-done
  84.0 2.3 %shard_map.120 = (bf16[32,16,128]{2,1,0:T(8,128)(2,1)}, bf16[32,16,128]{2,1,0:T(8,128)(2,1)}) custom-call(s32[4]{0:T(128)S(1)} %pad_add_fusion.pos_ref, s32[32]{0:T(128)S(1)} %broadcast_select_fusion.2.g_ref, s32[32]{0:T(128)S(1)} %fusion.2.s_ref, bf16[512,288]{1,0:T(8,128)(2,1)S(1)} %copy-done, bf16[512,288]{1,0:T(8,128)(2,1)S(1)} %collective-permute-done.7.rec_ref, ...), custom_call_target="tpu_custom_call" | custom-call | tf_op jit(solution)/shard_map/pallas_call | solution.py:42
  86.3 6.3 %all-to-all-start.2 = ((bf16[32,16,128]{2,1,0:T(8,128)(2,1)}), bf16[32,16,128]{2,1,0:T(8,128)(2,1)S(1)}, u32[]{:S(2)}, u32[]{:S(2)}) async-start(bf16[32,16,128]{2,1,0:T(8,128)(2,1)} %get-tuple-element.34), calls=%async_computation.2 | async-start | bytes 262144 | tf_op jit(solution)/shard_map/all_to_all | solution.py:374
  92.6 8.4 %copy.78 = bf16[273,224,32]{1,0,2:T(8,128)(2,1)} copy(bf16[273,224,32]{0,2,1:T(8,128)(2,1)} %bitcast.26) | data formatting | bytes 7827456 | tf_op jit(solution)/shard_map/optimization_barrier | solution.py:354
  101.0 1.0 all-to-all-done.2.rec_ref
  102.0 0.6 copy-done.8
  102.7 11.7 %shard_map.121 = (bf16[32,16,512]{2,1,0:T(8,128)(2,1)}, bf16[32,16,512]{2,1,0:T(8,128)(2,1)}) custom-call(s32[4]{0:T(128)S(1)} %pad_add_fusion.pos_ref, s32[32]{0:T(128)S(1)} %get-tuple-element.56.owner_ref, bf16[32,16,128]{2,1,0:T(8,128)(2,1)} %copy-done.8, bf16[32,16,128]{2,1,0:T(8,128)(2,1)} %get-tuple-element.37.keep_ref, ...), custom_call_target="tpu_custom_call" | custom-call | tf_op jit(solution)/shard_map/pallas_call | solution.py:381
  114.4 8.2 %all-to-all-start.3 = ((bf16[32,16,512]{2,1,0:T(8,128)(2,1)}), bf16[32,16,512]{2,1,0:T(8,128)(2,1)S(1)}, u32[]{:S(2)}, u32[]{:S(2)}) async-start(bf16[32,16,512]{2,1,0:T(8,128)(2,1)} %get-tuple-element.43), calls=%async_computation.3 | async-start | bytes 1048576 | tf_op jit(solution)/shard_map/all_to_all | solution.py:399
  122.7 2.9 %collective-permute-start.17 = (bf16[2,224,448]{2,1,0:T(8,128)(2,1)}, bf16[2,224,448]{2,1,0:T(8,128)(2,1)}, u32[]{:S(2)}, u32[]{:S(2)}) collective-permute-start(bf16[2,224,448]{2,1,0:T(8,128)(2,1)} %collective-permute-done.15.refs_7_), channel_id=1, source_target_pairs={{0,24},{8,0},{16,8},{24,16},{1,25},{9,1},{17,9},{25,17},{2,26},{10... | collective-permute-start | bytes 1204232 | tf_op jit(solution)/shard_map/ppermute | solution.py:309
  125.6 0.9 copy.79.len_ref
  126.6 1.0 copy-done.3
  127.6 7.1 %shard_map.122.num_ref = f32[2,512,256]{2,1,0:T(8,128)S(1)} custom-call(s32[4]{0:T(128)S(1)} %pad_add_fusion.pos_ref, bf16[512,288]{1,0:T(8,128)(2,1)S(1)} %copy-done.1, bf16[512,288]{1,0:T(8,128)(2,1)S(1)} %copy-done.3, bf16[512,256]{1,0:T(8,128)(2,1)} %tk_ref.1, bf16[512,1792]{1,0:T(8,128)(2,1)} %tv_ref.1, s32[512,1]{1,0:T(8,128)} %copy.79.len_ref), custom_call_target="tpu_custom_call" | custom-call | tf_op jit(solution)/shard_map/pallas_call | solution.py:42
  134.7 0.4 collective-permute-done.16.refs_4_
  135.0 3.1 %all-to-all-done.3.rec_ref = bf16[32,16,512]{2,1,0:T(8,128)(2,1)S(1)} async-done(((bf16[32,16,512]{2,1,0:T(8,128)(2,1)}), bf16[32,16,512]{2,1,0:T(8,128)(2,1)S(1)}, u32[]{:S(2)}, u32[]{:S(2)}) %all-to-all-start.3) | async-done | bytes 524320 | tf_op jit(solution)/shard_map/all_to_all | solution.py:399
  138.1 1.0 copy-done.4
  139.1 2.7 %shard_map.123 = bf16[4,256,256]{2,1,0:T(8,128)(2,1)} custom-call(s32[4]{0:T(128)S(1)} %pad_add_fusion.pos_ref, s32[32]{0:T(128)S(1)} %broadcast_select_fusion.2.g_ref, s32[32]{0:T(128)S(1)} %fusion.2.s_ref, f32[2,512,256]{2,1,0:T(8,128)S(1)} %shard_map.122.num_ref, bf16[32,16,512]{2,1,0:T(8,128)(2,1)S(1)} %all-to-all-done.3.rec_ref, ...), custom_call_target="tpu_custom_call" | custom-call | tf_op jit(solution)/shard_map/pallas_call | solution.py:42
  141.9 11.7 %all_to_all.29.own_ref = bf16[4,256,256]{2,1,0:T(8,128)(2,1)S(1)} all-to-all(bf16[4,256,256]{2,1,0:T(8,128)(2,1)} %shard_map.123), channel_id=1, replica_groups=mesh['req'=8,'y'=4,'core'=2,'col'=4] {'y'}, dimensions={0} | all-to-all | bytes 1048576 | tf_op jit(solution)/shard_map/all_to_all | solution.py:415
  153.6 4.6 %collective-permute-start.18 = (bf16[4,256,256]{2,1,0:T(8,128)(2,1)S(1)}, bf16[4,256,256]{2,1,0:T(8,128)(2,1)S(1)}, u32[]{:S(2)}, u32[]{:S(2)}) collective-permute-start(bf16[4,256,256]{2,1,0:T(8,128)(2,1)S(1)} %all_to_all.29.own_ref), channel_id=1, source_target_pairs={{0,4},{4,0},{1,5},{5,1},{2,6},{6,2},{3,7},{7,3},{8,12},{12,8},{9,1... | collective-permute-start | bytes 1572872 | tf_op jit(solution)/shard_map/ppermute | solution.py:416
  158.2 1.5 collective-permute-done.18.oth_ref
  159.7 3.6 %shard_map.124 = (bf16[256,448]{1,0:T(8,128)(2,1)}, bf16[256,448]{1,0:T(8,128)(2,1)}) custom-call(s32[4]{0:T(128)S(1)} %pad_add_fusion.pos_ref, bf16[4,256,256]{2,1,0:T(8,128)(2,1)S(1)} %all_to_all.29.own_ref, bf16[4,256,256]{2,1,0:T(8,128)(2,1)S(1)} %collective-permute-done.18.oth_ref, bf16[2,224,448]{2,1,0:T(8,128)(2,1)S(1)} %pad_maximum_fusion.refs_0_, ...), custom_call_target="tpu_custom_call" | custom-call | tf_op jit(solution)/shard_map/pallas_call | solution.py:42
  163.3 3.2 %collective-permute-start.19 = (bf16[256,448]{1,0:T(8,128)(2,1)}, bf16[256,448]{1,0:T(8,128)(2,1)S(1)}, u32[]{:S(2)}, u32[]{:S(2)}) collective-permute-start(bf16[256,448]{1,0:T(8,128)(2,1)} %get-tuple-element.53), channel_id=1, source_target_pairs={{0,1},{4,3},{8,0},{12,2},{16,5},{20,7},{24,4},{28,6},{1,9},{5,11},... | collective-permute-start | bytes 688136 | tf_op jit(solution)/shard_map/ppermute | solution.py:428
  166.5 3.7 %collective-permute-start.20 = (bf16[256,448]{1,0:T(8,128)(2,1)}, bf16[256,448]{1,0:T(8,128)(2,1)S(1)}, u32[]{:S(2)}, u32[]{:S(2)}) collective-permute-start(bf16[256,448]{1,0:T(8,128)(2,1)} %get-tuple-element.54), channel_id=1, source_target_pairs={{0,0},{4,2},{8,1},{12,3},{16,4},{20,6},{24,5},{28,7},{1,8},{5,10},... | collective-permute-start | bytes 688136 | tf_op jit(solution)/shard_map/ppermute | solution.py:428
  170.2 5.0 %collective-permute-done.19 = bf16[256,448]{1,0:T(8,128)(2,1)S(1)} collective-permute-done((bf16[256,448]{1,0:T(8,128)(2,1)}, bf16[256,448]{1,0:T(8,128)(2,1)S(1)}, u32[]{:S(2)}, u32[]{:S(2)}) %collective-permute-start.19) | collective-permute-done | bytes 229408 | tf_op jit(solution)/shard_map/ppermute | solution.py:428
  175.2 1.4 collective-permute-done.20
  176.8 0.2 copy.81
  177.0 0.9 fusion.1
  (58 shorter events, 1.4 us)
Async XLA Ops:
  0.0 11.4 %copy-start.13 = (s32[32]{0:T(128)S(1)}, s32[32]{0:T(128)}, u32[]{:S(2)}) copy-start(s32[32]{0:T(128)} %param.19) | copy-start | bytes 388
  1.3 24.9 %collective-permute-start.1 = (bf16[128,896]{1,0:T(8,128)(2,1)S(1)}, bf16[128,896]{1,0:T(8,128)(2,1)S(1)}, u32[]{:S(2)}, u32[]{:S(2)}) collective-permute-start(bf16[128,896]{1,0:T(8,128)(2,1)S(1)} %copy.76.refs_1_), channel_id=1, source_target_pairs={{0,8},{8,16},{16,24},{24,0},{1,9},{9,17},{17,25},{25,1},{2,10},{10... | collective-permute-start | bytes 688136 | tf_op jit(solution)/shard_map/ppermute | solution.py:309
  2.6 11.4 %collective-permute-start.3 = (bf16[128,896]{1,0:T(8,128)(2,1)S(1)}, bf16[128,896]{1,0:T(8,128)(2,1)S(1)}, u32[]{:S(2)}, u32[]{:S(2)}) collective-permute-start(bf16[128,896]{1,0:T(8,128)(2,1)S(1)} %copy.76.refs_1_), channel_id=1, source_target_pairs={{0,24},{8,0},{16,8},{24,16},{1,25},{9,1},{17,9},{25,17},{2,26},{10... | collective-permute-start | bytes 688136 | tf_op jit(solution)/shard_map/ppermute | solution.py:309
  3.0 9.6 %collective-permute-start = (bf16[128,896]{1,0:T(8,128)(2,1)S(1)}, bf16[128,896]{1,0:T(8,128)(2,1)S(1)}, u32[]{:S(2)}, u32[]{:S(2)}) collective-permute-start(bf16[128,896]{1,0:T(8,128)(2,1)S(1)} %copy.75.refs_0_), channel_id=1, source_target_pairs={{0,8},{8,16},{16,24},{24,0},{1,9},{9,17},{17,25},{25,1},{2,10},{10... | collective-permute-start | bytes 688136 | tf_op jit(solution)/shard_map/ppermute | solution.py:309
  4.3 21.9 %collective-permute-start.5 = (bf16[128,896]{1,0:T(8,128)(2,1)S(1)}, bf16[128,896]{1,0:T(8,128)(2,1)S(1)}, u32[]{:S(2)}, u32[]{:S(2)}) collective-permute-start(bf16[128,896]{1,0:T(8,128)(2,1)S(1)} %copy.75.refs_0_), channel_id=1, source_target_pairs={{0,24},{8,0},{16,8},{24,16},{1,25},{9,1},{17,9},{25,17},{2,26},{10... | collective-permute-start | bytes 688136 | tf_op jit(solution)/shard_map/ppermute | solution.py:309
  8.3 18.0 %collective-permute-start.6 = (bf16[448,288]{1,0:T(8,128)(2,1)S(1)}, bf16[448,288]{1,0:T(8,128)(2,1)S(1)}, u32[]{:S(2)}, u32[]{:S(2)}) collective-permute-start(bf16[448,288]{1,0:T(8,128)(2,1)S(1)} %pad_maximum_fusion.2.refs_8_), channel_id=1, source_target_pairs={{0,4},{4,0},{1,5},{5,1},{2,6},{6,2},{3,7},{7,3},{8,12},{12,8},{9,1... | collective-permute-start | bytes 774152 | tf_op jit(solution)/shard_map/ppermute | solution.py:317
  12.5 13.7 %collective-permute-start.2 = (bf16[128,896]{1,0:T(8,128)(2,1)S(1)}, bf16[128,896]{1,0:T(8,128)(2,1)S(1)}, u32[]{:S(2)}, u32[]{:S(2)}) collective-permute-start(bf16[128,896]{1,0:T(8,128)(2,1)S(1)} %collective-permute-done.refs_2_), channel_id=1, source_target_pairs={{0,8},{8,16},{16,24},{24,0},{1,9},{9,17},{17,25},{25,1},{2,10},{10... | collective-permute-start | bytes 688136 | tf_op jit(solution)/shard_map/ppermute | solution.py:309
  14.0 12.2 %collective-permute-start.4 = (bf16[128,896]{1,0:T(8,128)(2,1)S(1)}, bf16[128,896]{1,0:T(8,128)(2,1)S(1)}, u32[]{:S(2)}, u32[]{:S(2)}) collective-permute-start(bf16[128,896]{1,0:T(8,128)(2,1)S(1)} %collective-permute-done.3.refs_7_), channel_id=1, source_target_pairs={{0,24},{8,0},{16,8},{24,16},{1,25},{9,1},{17,9},{25,17},{2,26},{10... | collective-permute-start | bytes 688136 | tf_op jit(solution)/shard_map/ppermute | solution.py:309
  15.3 19.3 %all-to-all-start = ((s32[32,1,1]{2,1,0:T(1,128)}), s32[32,1,1]{2,1,0:T(1,128)S(1)}, u32[]{:S(2)}, u32[]{:S(2)}) async-start(s32[32,1,1]{2,1,0:T(1,128)} %copy.67), calls=%async_computation | async-start | bytes 32768 | tf_op jit(solution)/shard_map/all_to_all | solution.py:324
  34.6 43.4 %all-to-all-start.1 = ((bf16[4,256,1152]{2,1,0:T(8,128)(2,1)}), bf16[4,256,1152]{2,1,0:T(8,128)(2,1)S(1)}, u32[]{:S(2)}, u32[]{:S(2)}) async-start(bf16[4,256,1152]{2,1,0:T(8,128)(2,1)} %shard_map.118), calls=%async_computation.1 | async-start | bytes 4718592 | tf_op jit(solution)/shard_map/all_to_all | solution.py:353
  38.3 7.4 %copy-start.9 = (bf16[32,273,2]{1,2,0:T(2,128)(2,1)S(1)}, bf16[32,273,2]{1,2,0:T(2,128)(2,1)}, u32[]{:S(2)}) copy-start(bf16[32,273,2]{1,2,0:T(2,128)(2,1)} %param.18) | copy-start | bytes 104836
  38.3 8.4 %copy-start.11 = (s32[512]{0:T(512)S(1)}, s32[512]{0:T(512)}, u32[]{:S(2)}) copy-start(s32[512]{0:T(512)} %param.20) | copy-start | bytes 6148
  48.2 20.7 %collective-permute-start.9 = (bf16[224,448]{1,0:T(8,128)(2,1)}, bf16[224,448]{1,0:T(8,128)(2,1)S(1)}, u32[]{:S(2)}, u32[]{:S(2)}) collective-permute-start(bf16[224,448]{1,0:T(8,128)(2,1)} %param.16), channel_id=1, source_target_pairs={{0,1},{1,3},{2,5},{3,7},{4,0},{5,2},{6,4},{7,6},{8,9},{9,11},{10,1... | collective-permute-start | bytes 602120 | tf_op jit(solution)/shard_map/ppermute | solution.py:350
  51.8 23.3 %collective-permute-start.8 = (bf16[224,448]{1,0:T(8,128)(2,1)}, bf16[224,448]{1,0:T(8,128)(2,1)S(1)}, u32[]{:S(2)}, u32[]{:S(2)}) collective-permute-start(bf16[224,448]{1,0:T(8,128)(2,1)} %param.16), channel_id=1, source_target_pairs={{0,0},{1,2},{2,4},{3,6},{4,1},{5,3},{6,5},{7,7},{8,8},{9,10},{10,1... | collective-permute-start | bytes 602120 | tf_op jit(solution)/shard_map/ppermute | solution.py:350
  58.0 22.0 %collective-permute-start.12 = (bf16[224,448]{1,0:T(8,128)(2,1)}, bf16[224,448]{1,0:T(8,128)(2,1)S(1)}, u32[]{:S(2)}, u32[]{:S(2)}) collective-permute-start(bf16[224,448]{1,0:T(8,128)(2,1)} %param.16), channel_id=1, source_target_pairs={{0,3},{1,1},{2,7},{3,5},{4,2},{5,0},{6,6},{7,4},{8,11},{9,9},{10,1... | collective-permute-start | bytes 602120 | tf_op jit(solution)/shard_map/ppermute | solution.py:350
  59.9 20.1 %collective-permute-start.11 = (bf16[224,448]{1,0:T(8,128)(2,1)}, bf16[224,448]{1,0:T(8,128)(2,1)S(1)}, u32[]{:S(2)}, u32[]{:S(2)}) collective-permute-start(bf16[224,448]{1,0:T(8,128)(2,1)} %param.16), channel_id=1, source_target_pairs={{0,2},{1,0},{2,6},{3,4},{4,3},{5,1},{6,7},{7,5},{8,10},{9,8},{10,1... | collective-permute-start | bytes 602120 | tf_op jit(solution)/shard_map/ppermute | solution.py:350
  75.2 25.8 %collective-permute-start.10 = (bf16[2,224,448]{2,1,0:T(8,128)(2,1)S(1)}, bf16[2,224,448]{2,1,0:T(8,128)(2,1)}, u32[]{:S(2)}, u32[]{:S(2)}) collective-permute-start(bf16[2,224,448]{2,1,0:T(8,128)(2,1)S(1)} %pad_maximum_fusion.refs_0_), channel_id=1, source_target_pairs={{0,8},{8,16},{16,24},{24,0},{1,9},{9,17},{17,25},{25,1},{2,10},{10... | collective-permute-start | bytes 1204232 | tf_op jit(solution)/shard_map/ppermute | solution.py:309
  76.5 24.5 %collective-permute-start.14 = (bf16[2,224,448]{2,1,0:T(8,128)(2,1)S(1)}, bf16[2,224,448]{2,1,0:T(8,128)(2,1)}, u32[]{:S(2)}, u32[]{:S(2)}) collective-permute-start(bf16[2,224,448]{2,1,0:T(8,128)(2,1)S(1)} %pad_maximum_fusion.refs_0_), channel_id=1, source_target_pairs={{0,24},{8,0},{16,8},{24,16},{1,25},{9,1},{17,9},{25,17},{2,26},{10... | collective-permute-start | bytes 1204232 | tf_op jit(solution)/shard_map/ppermute | solution.py:309
  80.0 2.8 %collective-permute-start.7 = (bf16[512,288]{1,0:T(8,128)(2,1)}, bf16[512,288]{1,0:T(8,128)(2,1)S(1)}, u32[]{:S(2)}, u32[]{:S(2)}) collective-permute-start(bf16[512,288]{1,0:T(8,128)(2,1)} %get-tuple-element.33), channel_id=1, source_target_pairs={{0,4},{4,0},{1,5},{5,1},{2,6},{6,2},{3,7},{7,3},{8,12},{12,8},{9,1... | collective-permute-start | bytes 884744 | tf_op jit(solution)/shard_map/ppermute | solution.py:358
  80.1 20.9 %collective-permute-start.13 = (bf16[2,224,448]{2,1,0:T(8,128)(2,1)S(1)}, bf16[2,224,448]{2,1,0:T(8,128)(2,1)S(1)}, u32[]{:S(2)}, u32[]{:S(2)}) collective-permute-start(bf16[2,224,448]{2,1,0:T(8,128)(2,1)S(1)} %pad_maximum_fusion.1.refs_1_), channel_id=1, source_target_pairs={{0,8},{8,16},{16,24},{24,0},{1,9},{9,17},{17,25},{25,1},{2,10},{10... | collective-permute-start | bytes 1204232 | tf_op jit(solution)/shard_map/ppermute | solution.py:309
  80.2 20.8 %collective-permute-start.15 = (bf16[2,224,448]{2,1,0:T(8,128)(2,1)S(1)}, bf16[2,224,448]{2,1,0:T(8,128)(2,1)}, u32[]{:S(2)}, u32[]{:S(2)}) collective-permute-start(bf16[2,224,448]{2,1,0:T(8,128)(2,1)S(1)} %pad_maximum_fusion.1.refs_1_), channel_id=1, source_target_pairs={{0,24},{8,0},{16,8},{24,16},{1,25},{9,1},{17,9},{25,17},{2,26},{10... | collective-permute-start | bytes 1204232 | tf_op jit(solution)/shard_map/ppermute | solution.py:309
  82.9 3.4 %copy-start.2 = (bf16[512,288]{1,0:T(8,128)(2,1)}, bf16[512,288]{1,0:T(8,128)(2,1)S(1)}, u32[]{:S(2)}) copy-start(bf16[512,288]{1,0:T(8,128)(2,1)S(1)} %collective-permute-done.7.rec_ref) | copy-start | bytes 884740
  82.9 1.1 copy-start
  86.3 15.7 %all-to-all-start.2 = ((bf16[32,16,128]{2,1,0:T(8,128)(2,1)}), bf16[32,16,128]{2,1,0:T(8,128)(2,1)S(1)}, u32[]{:S(2)}, u32[]{:S(2)}) async-start(bf16[32,16,128]{2,1,0:T(8,128)(2,1)} %get-tuple-element.34), calls=%async_computation.2 | async-start | bytes 262144 | tf_op jit(solution)/shard_map/all_to_all | solution.py:374
  100.9 24.6 %copy-start.12 = (s32[512]{0:T(512)S(1)}, s32[512]{0:T(512)}, u32[]{:S(2)}) copy-start(s32[512]{0:T(512)} %param.23) | copy-start | bytes 6148
  100.9 25.5 %copy-start.10 = (s32[512]{0:T(512)S(1)}, s32[512]{0:T(512)}, u32[]{:S(2)}) copy-start(s32[512]{0:T(512)} %multiply_add_fusion) | copy-start | bytes 6148
  100.9 25.6 %copy-start.1 = (bf16[512,288]{1,0:T(8,128)(2,1)S(1)}, bf16[512,288]{1,0:T(8,128)(2,1)}, u32[]{:S(2)}) copy-start(bf16[512,288]{1,0:T(8,128)(2,1)} %get-tuple-element.32.own_ref) | copy-start | bytes 884740
  101.0 25.5 %copy-start.5 = (bf16[2,224,448]{2,1,0:T(8,128)(2,1)}, bf16[2,224,448]{2,1,0:T(8,128)(2,1)S(1)}, u32[]{:S(2)}) copy-start(bf16[2,224,448]{2,1,0:T(8,128)(2,1)S(1)} %collective-permute-done.13.refs_3_) | copy-start | bytes 1204228
  102.0 0.6 copy-start.8
  114.4 23.7 %all-to-all-start.3 = ((bf16[32,16,512]{2,1,0:T(8,128)(2,1)}), bf16[32,16,512]{2,1,0:T(8,128)(2,1)S(1)}, u32[]{:S(2)}, u32[]{:S(2)}) async-start(bf16[32,16,512]{2,1,0:T(8,128)(2,1)} %get-tuple-element.43), calls=%async_computation.3 | async-start | bytes 1048576 | tf_op jit(solution)/shard_map/all_to_all | solution.py:399
  122.6 12.4 %collective-permute-start.16 = (bf16[2,224,448]{2,1,0:T(8,128)(2,1)}, bf16[2,224,448]{2,1,0:T(8,128)(2,1)}, u32[]{:S(2)}, u32[]{:S(2)}) collective-permute-start(bf16[2,224,448]{2,1,0:T(8,128)(2,1)} %collective-permute-done.10.refs_2_), channel_id=1, source_target_pairs={{0,8},{8,16},{16,24},{24,0},{1,9},{9,17},{17,25},{25,1},{2,10},{10... | collective-permute-start | bytes 1204232 | tf_op jit(solution)/shard_map/ppermute | solution.py:309
  122.7 12.3 %collective-permute-start.17 = (bf16[2,224,448]{2,1,0:T(8,128)(2,1)}, bf16[2,224,448]{2,1,0:T(8,128)(2,1)}, u32[]{:S(2)}, u32[]{:S(2)}) collective-permute-start(bf16[2,224,448]{2,1,0:T(8,128)(2,1)} %collective-permute-done.15.refs_7_), channel_id=1, source_target_pairs={{0,24},{8,0},{16,8},{24,16},{1,25},{9,1},{17,9},{25,17},{2,26},{10... | collective-permute-start | bytes 1204232 | tf_op jit(solution)/shard_map/ppermute | solution.py:309
  126.6 1.0 copy-start.3
  138.1 1.0 copy-start.4
  139.1 20.6 %copy-start.6 = (bf16[2,224,448]{2,1,0:T(8,128)(2,1)S(1)}, bf16[2,224,448]{2,1,0:T(8,128)(2,1)}, u32[]{:S(2)}) copy-start(bf16[2,224,448]{2,1,0:T(8,128)(2,1)} %copy-done.5) | copy-start | bytes 1204228
  141.8 35.1 %copy-start.7 = (bf16[256,2,448]{0,2,1:T(8,128)(2,1)S(1)}, bf16[256,2,448]{0,2,1:T(8,128)(2,1)}, u32[]{:S(2)}) copy-start(bf16[256,2,448]{0,2,1:T(8,128)(2,1)} %param.12) | copy-start | bytes 1376260
  153.6 6.1 %collective-permute-start.18 = (bf16[4,256,256]{2,1,0:T(8,128)(2,1)S(1)}, bf16[4,256,256]{2,1,0:T(8,128)(2,1)S(1)}, u32[]{:S(2)}, u32[]{:S(2)}) collective-permute-start(bf16[4,256,256]{2,1,0:T(8,128)(2,1)S(1)} %all_to_all.29.own_ref), channel_id=1, source_target_pairs={{0,4},{4,0},{1,5},{5,1},{2,6},{6,2},{3,7},{7,3},{8,12},{12,8},{9,1... | collective-permute-start | bytes 1572872 | tf_op jit(solution)/shard_map/ppermute | solution.py:416
  163.3 11.9 %collective-permute-start.19 = (bf16[256,448]{1,0:T(8,128)(2,1)}, bf16[256,448]{1,0:T(8,128)(2,1)S(1)}, u32[]{:S(2)}, u32[]{:S(2)}) collective-permute-start(bf16[256,448]{1,0:T(8,128)(2,1)} %get-tuple-element.53), channel_id=1, source_target_pairs={{0,1},{4,3},{8,0},{12,2},{16,5},{20,7},{24,4},{28,6},{1,9},{5,11},... | collective-permute-start | bytes 688136 | tf_op jit(solution)/shard_map/ppermute | solution.py:428
  166.5 10.0 %collective-permute-start.20 = (bf16[256,448]{1,0:T(8,128)(2,1)}, bf16[256,448]{1,0:T(8,128)(2,1)S(1)}, u32[]{:S(2)}, u32[]{:S(2)}) collective-permute-start(bf16[256,448]{1,0:T(8,128)(2,1)} %get-tuple-element.54), channel_id=1, source_target_pairs={{0,0},{4,2},{8,1},{12,3},{16,4},{20,6},{24,5},{28,7},{1,8},{5,10},... | collective-permute-start | bytes 688136 | tf_op jit(solution)/shard_map/ppermute | solution.py:428
